TPU v7x, 32 devices: a whole 2x2x4 slice. The times are simulated.
32 devices in a mesh: dp: 8 (over z, x), shard: 4 (over y, core).
Axes of the slice: x: 2, y: 2, z: 4, core: 2. Of those that a mesh axis runs over, the one named last changes fastest.
Arguments:
- tokens: bfloat16 [8, 2048, 2048], P('dp', 'shard'), may hold values from -6 to 6
- cotangent: bfloat16 [8, 2048, 2048], P('dp', 'shard'), may hold values from -6 to 6
- lengths: int32 [8], replicated, may hold values from 1024 to 2048, as said below
- slot_sequence: int32 [8], P('dp'), may hold values from 0 to 7, each once
- attn_gain: float32 [2048], P(('dp', 'shard')), may hold values from 0.1 to 1.9
- w_qkv: float32 [2048, 1536], P(('dp', 'shard')), may hold values from -0.125 to 0.125
- q_gain: float32 [64], replicated, may hold values from 0.6 to 1.8
- k_gain: float32 [64], replicated, may hold values from 0.6 to 1.8
- w_out: float32 [1024, 2048], P(None, ('dp', 'shard')), may hold values from -1.5 to 1.5
- ffn_gain: float32 [2048], P(('dp', 'shard')), may hold values from 0.1 to 1.9
- w_gate: float32 [2048, 1024], P(('dp', 'shard')), may hold values from -0.125 to 0.125
- w_up: float32 [2048, 1024], P(('dp', 'shard')), may hold values from -0.125 to 0.125
- w_down: float32 [1024, 2048], P(None, ('dp', 'shard')), may hold values from -0.1875 to 0.1875
Outputs:
- output: bfloat16 [8, 2048, 2048], P('dp', 'shard')
- input_grad: float32 [8, 2048, 2048], P('dp', 'shard')
- grad_attn_gain: float32 [2048], P(('dp', 'shard'))
- grad_w_qkv: float32 [2048, 1536], P(('dp', 'shard'))
- grad_q_gain: float32 [64], replicated
- grad_k_gain: float32 [64], replicated
- grad_w_out: float32 [1024, 2048], P(None, ('dp', 'shard'))
- grad_ffn_gain: float32 [2048], P(('dp', 'shard'))
- grad_w_gate: float32 [2048, 1024], P(('dp', 'shard'))
- grad_w_up: float32 [2048, 1024], P(('dp', 'shard'))
- grad_w_down: float32 [1024, 2048], P(None, ('dp', 'shard'))
Inputs may be any that keep to these rules, and one draw needn't show every extreme that they name: `lengths`: some sequence has exactly 2048 tokens. `slot_sequence`: each row holds a different sequence.
All inputs are finite; a program needn't handle non-finite values.
Results may differ from a plain program's by a relative error of at most 0.015.
The roundings to bfloat16 on the way count: a program that leaves them out, or rounds other values in their place, can miss the bound.
Values may be sent and summed in bfloat16 or wider, within the bound.
No kernel may reach another device: no remote copies, remote signals or barrier semaphores. Data moves between devices by JAX's collectives and lax.ppermute only.
A program may use at most 192 MiB of HBM per device.

v0:
```python
import math

import jax
import jax.numpy as jnp
from jax import lax
from jax.sharding import PartitionSpec as P

HEADS = 16
KV = 4
HD = 64


EPS = 1e-06


def normalize(values):
    inverse = lax.rsqrt(jnp.mean(values * values, axis=-1, keepdims=True) + EPS)
    return (values * inverse, inverse)


def norm_back(values, inverse, grad_normed):
    cubed = inverse * inverse * inverse
    return inverse * grad_normed - values * cubed * jnp.mean(
        grad_normed * values, axis=-1, keepdims=True
    )


def rotate(values, cos_t, sin_t):
    half_len = values.shape[-1] // 2
    turned = jnp.concatenate([-values[..., half_len:], values[..., :half_len]], axis=-1)
    return values * cos_t + turned * sin_t


def rotate_back(grad_in, cos_t, sin_t):
    half_len = grad_in.shape[-1] // 2
    along = grad_in * sin_t
    return grad_in * cos_t + jnp.concatenate(
        [along[..., half_len:], -along[..., :half_len]], axis=-1
    )


def tables(positions):
    freq = 10000.0 ** (-(2.0 * jnp.arange(HD // 2, dtype=jnp.float32)) / HD)
    angles = positions.astype(jnp.float32)[:, None] * freq[None, :]
    angles = jnp.concatenate([angles, angles], axis=-1)
    return (jnp.cos(angles), jnp.sin(angles))


def unchanged(running):
    return running


def local(
    tokens,
    cotangent,
    lengths,
    slot_sequence,
    attn_gain,
    w_qkv,
    q_gain,
    k_gain,
    w_out,
    ffn_gain,
    w_gate,
    w_up,
    w_down,
):
    row_count, piece_len, model_width = tokens.shape
    group_size = HEADS // KV
    q_width = HEADS * HD
    kv_width = KV * HD
    total_rows = lengths.shape[0]
    row_len = piece_len * lax.axis_size("shard")
    scale_factor = 1.0 / math.sqrt(HD)
    row_valid = jnp.sum(
        jnp.where(
            slot_sequence[:, None] == jnp.arange(total_rows, dtype=jnp.int32)[None, :],
            lengths[None, :],
            0,
        ),
        axis=1,
    )
    longest = jnp.max(row_valid)
    positions = lax.axis_index("shard") * piece_len + jnp.arange(piece_len, dtype=jnp.int32)
    last_query = lax.axis_index("shard") * piece_len + piece_len - 1
    live_mask = (positions[None, :] < row_valid[:, None]).astype(jnp.float32)
    cos_t, sin_t = tables(positions)
    cos_h = cos_t[None, :, None, :]
    sin_h = sin_t[None, :, None, :]
    query_pos = jnp.tile(positions, group_size)
    attn_pack = (
        attn_gain.astype(jnp.bfloat16),
        w_qkv.astype(jnp.bfloat16),
        w_out.astype(jnp.bfloat16),
    )
    gain_attn, wqkv_low, wout_low = (
        lax.all_gather(attn_pack[0], ("dp", "shard"), axis=0, tiled=True),
        lax.all_gather(attn_pack[1], ("dp", "shard"), axis=0, tiled=True),
        lax.all_gather(attn_pack[2], ("dp", "shard"), axis=1, tiled=True),
    )
    gain_attn_f = gain_attn.astype(jnp.float32)
    x_float = tokens.astype(jnp.float32)
    normed_one, inverse_one = normalize(x_float)
    normed_low = (normed_one * gain_attn_f).astype(jnp.bfloat16)
    projected = jnp.einsum("rtd,de->rte", normed_low, wqkv_low, preferred_element_type=jnp.float32)
    q_raw = projected[..., :q_width].reshape(row_count, piece_len, HEADS, HD)
    k_raw = projected[..., q_width : q_width + kv_width].reshape(row_count, piece_len, KV, HD)
    v_raw = projected[..., q_width + kv_width :]
    q_unit, q_inverse = normalize(q_raw)
    k_unit, k_inverse = normalize(k_raw)
    q_low = rotate(q_unit * q_gain, cos_h, sin_h).astype(jnp.bfloat16)
    k_low = (
        rotate(k_unit * k_gain, cos_h, sin_h)
        .astype(jnp.bfloat16)
        .reshape(row_count, piece_len, kv_width)
    )
    v_low = v_raw.astype(jnp.bfloat16)
    q_group = (
        q_low.reshape(row_count, piece_len, KV, group_size, HD)
        .transpose(0, 2, 3, 1, 4)
        .reshape(row_count, KV, group_size * piece_len, HD)
    )

    def block_scores(key_piece, value_piece, offset, block_len):
        k_block = lax.dynamic_slice_in_dim(key_piece, offset, block_len, 1).reshape(
            row_count, block_len, KV, HD
        )
        v_block = lax.dynamic_slice_in_dim(value_piece, offset, block_len, 1).reshape(
            row_count, block_len, KV, HD
        )
        scores = scale_factor * jnp.einsum(
            "rgqh,rkgh->rgqk", q_group, k_block, preferred_element_type=jnp.float32
        )
        key_pos = offset + jnp.arange(block_len, dtype=jnp.int32)
        allowed = (key_pos[None, None, None, :] <= query_pos[None, None, :, None]) & (
            key_pos[None, None, None, :] < row_valid[:, None, None, None]
        )
        return (k_block, v_block, jnp.where(allowed, jnp.exp(scores), 0.0))

    def block_used(key_start):
        return (key_start <= last_query) & (key_start < longest)

    zero_accum = jnp.zeros((row_count, KV, group_size * piece_len, HD), jnp.float32)
    zero_sums = jnp.zeros((row_count, KV, group_size * piece_len), jnp.float32)
    key_piece = lax.all_gather(k_low, "shard", axis=1, tiled=True)
    value_piece = lax.all_gather(v_low, "shard", axis=1, tiled=True)
    block_len = math.gcd(key_piece.shape[1], piece_len)
    block_count = key_piece.shape[1] // block_len

    def fold_block(block_index, running):
        offset = block_index * block_len

        def compute(state):
            accum_out, row_sums = state
            k_block, v_block, exps = block_scores(key_piece, value_piece, offset, block_len)
            row_sums = row_sums + jnp.sum(exps, axis=-1)
            accum_out = accum_out + jnp.einsum(
                "rgqk,rkgh->rgqh",
                exps.astype(jnp.bfloat16),
                v_block,
                preferred_element_type=jnp.float32,
            )
            return (accum_out, row_sums)

        return lax.cond(block_used(offset), compute, unchanged, running)

    accum_out, denominator = lax.fori_loop(0, block_count, fold_block, (zero_accum, zero_sums))
    o_group = accum_out / denominator[..., None]
    att_low = (
        o_group.reshape(row_count, KV, group_size, piece_len, HD)
        .transpose(0, 3, 1, 2, 4)
        .reshape(row_count, piece_len, q_width)
        .astype(jnp.bfloat16)
    )
    x_mid = x_float + jnp.einsum(
        "rtc,cd->rtd", att_low, wout_low, preferred_element_type=jnp.float32
    )
    ffn_pack = (
        ffn_gain.astype(jnp.bfloat16),
        w_gate.astype(jnp.bfloat16),
        w_up.astype(jnp.bfloat16),
        w_down.astype(jnp.bfloat16),
    )
    gain_ffn, wgate_low, wup_low, wdown_low = (
        lax.all_gather(ffn_pack[0], ("dp", "shard"), axis=0, tiled=True),
        lax.all_gather(ffn_pack[1], ("dp", "shard"), axis=0, tiled=True),
        lax.all_gather(ffn_pack[2], ("dp", "shard"), axis=0, tiled=True),
        lax.all_gather(ffn_pack[3], ("dp", "shard"), axis=1, tiled=True),
    )
    gain_ffn_f = gain_ffn.astype(jnp.float32)
    normed_two, inverse_two = normalize(x_mid)
    ffn_in = (normed_two * gain_ffn_f).astype(jnp.bfloat16)
    gate_proj = jnp.einsum("rtd,df->rtf", ffn_in, wgate_low, preferred_element_type=jnp.float32)
    up_proj = jnp.einsum("rtd,df->rtf", ffn_in, wup_low, preferred_element_type=jnp.float32)
    gate_sig = jax.nn.sigmoid(gate_proj)
    silu_gate = gate_proj * gate_sig
    activated = (silu_gate * up_proj).astype(jnp.bfloat16)
    result = x_mid + jnp.einsum(
        "rtf,fd->rtd", activated, wdown_low, preferred_element_type=jnp.float32
    )
    output = result.astype(jnp.bfloat16)
    grad_out = cotangent.astype(jnp.float32) * live_mask[..., None]
    grad_low = grad_out.astype(jnp.bfloat16)
    gain_again, wgate_k, wup_k, wdown_k = (
        lax.all_gather(ffn_pack[0], ("dp", "shard"), axis=0, tiled=True),
        lax.all_gather(ffn_pack[1], ("dp", "shard"), axis=0, tiled=True),
        lax.all_gather(ffn_pack[2], ("dp", "shard"), axis=0, tiled=True),
        lax.all_gather(ffn_pack[3], ("dp", "shard"), axis=1, tiled=True),
    )
    gain_ffn_k = gain_again.astype(jnp.float32)
    grad_down = jnp.einsum("rtf,rtd->fd", activated, grad_low, preferred_element_type=jnp.float32)
    grad_act = jnp.einsum("rtd,fd->rtf", grad_low, wdown_k, preferred_element_type=jnp.float32)
    grad_gate = (grad_act * up_proj * gate_sig * (1.0 + gate_proj * (1.0 - gate_sig))).astype(
        jnp.bfloat16
    )
    grad_up = (grad_act * silu_gate).astype(jnp.bfloat16)
    grad_wgate = jnp.einsum("rtd,rtf->df", ffn_in, grad_gate, preferred_element_type=jnp.float32)
    grad_wup = jnp.einsum("rtd,rtf->df", ffn_in, grad_up, preferred_element_type=jnp.float32)
    grad_ffn_in = jnp.einsum(
        "rtf,df->rtd", grad_gate, wgate_k, preferred_element_type=jnp.float32
    ) + jnp.einsum("rtf,df->rtd", grad_up, wup_k, preferred_element_type=jnp.float32)
    grad_gain_two = jnp.sum(grad_ffn_in * normed_two, axis=(0, 1))
    grad_mid = grad_out + norm_back(x_mid, inverse_two, grad_ffn_in * gain_ffn_k)
    summed_gain_two, summed_wgate, summed_wup, summed_down = (
        lax.psum_scatter(grad_gain_two, ("dp", "shard"), scatter_dimension=0, tiled=True),
        lax.psum_scatter(grad_wgate, ("dp", "shard"), scatter_dimension=0, tiled=True),
        lax.psum_scatter(grad_wup, ("dp", "shard"), scatter_dimension=0, tiled=True),
        lax.psum_scatter(grad_down, ("dp", "shard"), scatter_dimension=1, tiled=True),
    )
    gain_back, wqkv_k, wout_k = (
        lax.all_gather(attn_pack[0], ("dp", "shard"), axis=0, tiled=True),
        lax.all_gather(attn_pack[1], ("dp", "shard"), axis=0, tiled=True),
        lax.all_gather(attn_pack[2], ("dp", "shard"), axis=1, tiled=True),
    )
    gain_attn_k = gain_back.astype(jnp.float32)
    mid_low = grad_mid.astype(jnp.bfloat16)
    grad_wout = jnp.einsum("rtc,rtd->cd", att_low, mid_low, preferred_element_type=jnp.float32)
    grad_att = jnp.einsum("rtd,cd->rtc", mid_low, wout_k, preferred_element_type=jnp.float32)
    grad_group = (
        grad_att.reshape(row_count, piece_len, KV, group_size, HD)
        .transpose(0, 2, 3, 1, 4)
        .reshape(row_count, KV, group_size * piece_len, HD)
    )
    grad_sums = -jnp.sum(grad_group * o_group, axis=-1) / denominator
    grad_accum = (grad_group / denominator[..., None]).astype(jnp.bfloat16)
    zero_keys = jnp.zeros((row_count, row_len, kv_width), jnp.float32)
    attend_key_piece = lax.all_gather(k_low, "shard", axis=1, tiled=True)
    attend_value_piece = lax.all_gather(v_low, "shard", axis=1, tiled=True)
    attend_block_len = math.gcd(attend_key_piece.shape[1], piece_len)
    block_count = attend_key_piece.shape[1] // attend_block_len

    def fold_block(block_index, running):
        offset = block_index * attend_block_len
        key_start = offset

        def compute(state):
            grad_query, grad_keys, grad_values = state
            k_block, v_block, exps = block_scores(
                attend_key_piece, attend_value_piece, offset, attend_block_len
            )
            grad_exps = (
                jnp.einsum(
                    "rgqh,rkgh->rgqk", grad_accum, v_block, preferred_element_type=jnp.float32
                )
                + grad_sums[..., None]
            )
            grad_scores = (exps * grad_exps).astype(jnp.bfloat16)
            grad_query = grad_query + scale_factor * jnp.einsum(
                "rgqk,rkgh->rgqh", grad_scores, k_block, preferred_element_type=jnp.float32
            )
            part_keys = scale_factor * jnp.einsum(
                "rgqk,rgqh->rkgh", grad_scores, q_group, preferred_element_type=jnp.float32
            )
            part_values = jnp.einsum(
                "rgqk,rgqh->rkgh",
                exps.astype(jnp.bfloat16),
                grad_accum,
                preferred_element_type=jnp.float32,
            )
            old_keys = lax.dynamic_slice_in_dim(grad_keys, key_start, attend_block_len, 1)
            old_values = lax.dynamic_slice_in_dim(grad_values, key_start, attend_block_len, 1)
            grad_keys = lax.dynamic_update_slice_in_dim(
                grad_keys,
                old_keys + part_keys.reshape(row_count, attend_block_len, kv_width),
                key_start,
                1,
            )
            grad_values = lax.dynamic_update_slice_in_dim(
                grad_values,
                old_values + part_values.reshape(row_count, attend_block_len, kv_width),
                key_start,
                1,
            )
            return (grad_query, grad_keys, grad_values)

        return lax.cond(block_used(key_start), compute, unchanged, running)

    grad_query, grad_keys_all, grad_values_all = lax.fori_loop(
        0, block_count, fold_block, (zero_accum, zero_keys, zero_keys)
    )
    grad_keys, grad_values = (
        lax.psum_scatter(grad_keys_all, "shard", scatter_dimension=1, tiled=True),
        lax.psum_scatter(grad_values_all, "shard", scatter_dimension=1, tiled=True),
    )
    grad_q_heads = (
        grad_query.reshape(row_count, KV, group_size, piece_len, HD)
        .transpose(0, 3, 1, 2, 4)
        .reshape(row_count, piece_len, HEADS, HD)
    )
    grad_q_scaled = rotate_back(grad_q_heads, cos_h, sin_h)
    grad_qgain = jnp.sum(grad_q_scaled * q_unit, axis=(0, 1, 2))
    grad_q_raw = norm_back(q_raw, q_inverse, grad_q_scaled * q_gain)
    grad_k_scaled = rotate_back(grad_keys.reshape(row_count, piece_len, KV, HD), cos_h, sin_h)
    grad_kgain = jnp.sum(grad_k_scaled * k_unit, axis=(0, 1, 2))
    grad_k_raw = norm_back(k_raw, k_inverse, grad_k_scaled * k_gain)
    grad_projected = jnp.concatenate(
        [
            grad_q_raw.reshape(row_count, piece_len, q_width),
            grad_k_raw.reshape(row_count, piece_len, kv_width),
            grad_values,
        ],
        axis=-1,
    ).astype(jnp.bfloat16)
    grad_wqkv = jnp.einsum(
        "rtd,rte->de", normed_low, grad_projected, preferred_element_type=jnp.float32
    )
    grad_normed = jnp.einsum(
        "rte,de->rtd", grad_projected, wqkv_k, preferred_element_type=jnp.float32
    )
    grad_gain_one = jnp.sum(grad_normed * normed_one, axis=(0, 1))
    input_grad = grad_mid + norm_back(x_float, inverse_one, grad_normed * gain_attn_k)
    summed_gain_one, summed_wqkv, summed_wout = (
        lax.psum_scatter(grad_gain_one, ("dp", "shard"), scatter_dimension=0, tiled=True),
        lax.psum_scatter(grad_wqkv, ("dp", "shard"), scatter_dimension=0, tiled=True),
        lax.psum_scatter(grad_wout, ("dp", "shard"), scatter_dimension=1, tiled=True),
    )
    summed_qgain, summed_kgain = lax.psum((grad_qgain, grad_kgain), ("dp", "shard"))
    return (
        output,
        input_grad,
        summed_gain_one,
        summed_wqkv,
        summed_qgain,
        summed_kgain,
        summed_wout,
        summed_gain_two,
        summed_wgate,
        summed_wup,
        summed_down,
    )


def solution(mesh):
    in_specs = (
        P("dp", "shard", None),
        P("dp", "shard", None),
        P(),
        P("dp"),
        P(("dp", "shard")),
        P(("dp", "shard"), None),
        P(),
        P(),
        P(None, ("dp", "shard")),
        P(("dp", "shard")),
        P(("dp", "shard"), None),
        P(("dp", "shard"), None),
        P(None, ("dp", "shard")),
    )
    out_specs = (
        P("dp", "shard", None),
        P("dp", "shard", None),
        P(("dp", "shard")),
        P(("dp", "shard"), None),
        P(),
        P(),
        P(None, ("dp", "shard")),
        P(("dp", "shard")),
        P(("dp", "shard"), None),
        P(("dp", "shard"), None),
        P(None, ("dp", "shard")),
    )
    return jax.shard_map(local, mesh=mesh, in_specs=in_specs, out_specs=out_specs, check_vma=False)
```

profile of v0, /device:TPU:0, one launch (start us, length us, event | category | flops | bytes accessed | tf_op | source)
XLA Modules:
  0.0 1401.9 jit_solution(8994772418632828310)
XLA Ops:
  12.6 42.5 %all-reduce.5 = (bf16[2048]{0:T(1024)(128)(2,1)S(1)}, bf16[2048]{0:T(1024)(128)(2,1)S(1)}) all-reduce(bf16[2048]{0:T(1024)(128)(2,1)S(1)} %dynamic-update-slice, bf16[2048]{0:T(1024)(128)(2,1)S(1)} %dynamic-update-slice.1), channel_id=1, replica_groups=mesh['dp'=8,'shard'=4] {'dp','shard'}, use_global_device_ids=true, to_apply=%add | all-reduce | flops 4096 | bytes 16384
  58.7 25.3 %all-gather.8.cloned.1.call-done = bf16[2048,1536]{1,0:T(8,128)(2,1)} async-done(((bf16[64,1536]{1,0:T(8,128)(2,1)}), bf16[2048,1536]{1,0:T(8,128)(2,1)}) %all-gather.8.cloned.1.call-update) | async-done | bytes 6291472 | tf_op jit(solution)/shard_map/all_gather | solution.py:98
  84.0 6.3 convolution_bitcast_fusion
  112.9 35.1 %all-gather.14.cloned.1.call-done = bf16[1024,2048]{0,1:T(8,128)(2,1)} async-done(((bf16[1024,64]{0,1:T(8,128)(2,1)}), bf16[1024,2048]{0,1:T(8,128)(2,1)}) %all-gather.14.cloned.1.call-update) | async-done | bytes 4194320 | tf_op jit(solution)/shard_map/all_gather | solution.py:99
  148.0 6.5 copy.151
  161.4 4.1 all-gather.10.cloned.1.call-done
  167.7 16.5 %all-gather.12.cloned.1.call-done = bf16[1,2048,256]{2,1,0:T(8,128)(2,1)} async-done(((bf16[1,512,256]{2,1,0:T(8,128)(2,1)}), bf16[1,2048,256]{2,1,0:T(8,128)(2,1)}) %all-gather.12.cloned.1.call-update) | async-done | bytes 1048592 | tf_op jit(solution)/shard_map/all_gather | solution.py:146
  186.7 14.9 %while.34 = (s32[]{:T(128)}, f32[1,4,2048,64]{2,3,1,0:T(8,128)S(1)}, f32[1,4,2048]{2,1,0:T(4,128)S(1)}, s32[]{:T(128)}, s32[]{:T(128)}, /*index=5*/s32[1]{0:T(12...) while((s32[]{:T(128)}, ...), condition=%wide.region_8.0_spmd.clone, body=%wide.region_4.8_spmd.clone.sunk | while | flops 1101530624 | bytes 47881560 | solution.py:167
  187.4 12.0 conditional.6
  190.0 4.6 fusion.4
  194.7 4.8 fusion.14
  202.8 3.0 convert_element_type.167
  207.7 4.9 multiply_reduce_fusion
  216.4 33.2 %all-gather.16.cloned.1.call-done = bf16[2048,1024]{1,0:T(8,128)(2,1)} async-done(((bf16[64,1024]{1,0:T(8,128)(2,1)}), bf16[2048,1024]{1,0:T(8,128)(2,1)}) %all-gather.16.cloned.1.call-update) | async-done | bytes 4194320 | tf_op jit(solution)/shard_map/all_gather | solution.py:186
  249.6 6.5 fusion.88
  256.1 57.4 %all-gather.18.cloned.1.call-done = bf16[2048,1024]{1,0:T(8,128)(2,1)} async-done(((bf16[64,1024]{1,0:T(8,128)(2,1)}), bf16[2048,1024]{1,0:T(8,128)(2,1)}) %all-gather.18.cloned.1.call-update) | async-done | bytes 4194320 | tf_op jit(solution)/shard_map/all_gather | solution.py:187
  313.6 6.5 fusion.89
  320.1 57.0 %all-gather.20.cloned.1.call-done = bf16[1024,2048]{0,1:T(8,128)(2,1)} async-done(((bf16[1024,64]{0,1:T(8,128)(2,1)}), bf16[1024,2048]{0,1:T(8,128)(2,1)}) %all-gather.20.cloned.1.call-update) | async-done | bytes 4194320 | tf_op jit(solution)/shard_map/all_gather | solution.py:188
  377.0 8.3 multiply_convert_fusion.1
  389.5 3.9 fusion.46
  403.2 45.3 %while.35 = (s32[]{:T(128)}, f32[1,4,2048,64]{2,3,1,0:T(8,128)S(1)}, f32[1,2048,256]{1,2,0:T(8,128)}, f32[1,2048,256]{1,2,0:T(8,128)}, s32[]{:T(128)}, /*index=5...) while((s32[]{:T(128)}, ...), condition=%wide.region_15.16_spmd.clone, body=%wide.region_12.0_spmd.clone.sunk | while | flops 2721449472 | bytes 137174512 | solution.py:298
  403.9 42.5 %conditional.7 = ((f32[1,4,2048,64]{2,3,1,0:T(8,128)S(1)}, f32[1,2048,256]{1,2,0:T(8,128)}, f32[1,2048,256]{1,2,0:T(8,128)})) conditional(s32[]{:T(128)} %convert_element_type.273, (f32[1,4,2048,64]{2,3,1,0:T(8,128)S(1)}, f32[1,2048,256]{1,2,0:T(8,128)}, f32[1,2048,256]{1,2,0:T(8,128)}) %tuple.118, (s32[]{:T(128)}, s32[512]{0:T(512)S(1)}, ...), branch_computations={%region_13.13_spmd, %region_14.14_spmd} | conditional | flops 2721449472 | bytes 137174208 | solution.py:296
  404.9 8.2 fusion.31
  415.8 8.6 fusion.21
  427.7 10.1 fusion.23
  437.8 6.1 convolution_multiply_fusion.1
  448.6 2.9 copy.162
  452.0 2.9 copy.169
  456.1 7.8 fusion.60
  465.1 7.3 fusion.91
  473.6 7.3 fusion.92
  482.2 7.3 fusion.70
  492.0 2.9 copy.157
  497.8 3.0 copy.160
  512.0 3.0 copy.161
  520.8 7.9 fusion.66
  528.7 80.1 %reduce-scatter.8.cloned.1.call-done = f32[1,512,256]{2,1,0:T(8,128)} async-done(((f32[1,2048,256]{2,1,0:T(8,128)}), f32[1,512,256]{2,1,0:T(8,128)}) %reduce-scatter.8.cloned.1.call-update) | async-done | bytes 524304 | tf_op jit(solution)/shard_map/reduce_scatter | solution.py:302
  618.2 24.8 %reduce-scatter.10.cloned.1.call-done = f32[1,512,256]{2,1,0:T(8,128)} async-done(((f32[1,2048,256]{2,1,0:T(8,128)}), f32[1,512,256]{2,1,0:T(8,128)}) %reduce-scatter.10.cloned.1.call-update) | async-done | bytes 524304 | tf_op jit(solution)/shard_map/reduce_scatter | solution.py:303
  647.2 6.9 fusion.75
  658.3 6.1 fusion.49
  664.6 8.6 fusion.40
  673.2 66.0 %all-reduce.4 = (f32[2048]{0:T(1024)S(1)}, f32[64]{0:T(128)}, f32[64]{0:T(128)}, f32[2048]{0:T(1024)S(1)}) all-reduce(f32[2048]{0:T(1024)S(1)} %get-tuple-element.660, f32[64]{0:T(128)S(1)} %fusion.57, f32[64]{0:T(128)S(1)} %reduce_sum.161, f32[2048]{0:T(1024)S(1)} %copy-done.44), channel_id=4, replica_groups=mesh['dp'=8,'shard'=4] {'dp','shard'}, use_global_device_ids=true, to_apply=%region_22.23.clone | all-reduce | flops 4224 | bytes 33792
  740.4 6.7 fusion.44
  747.1 47.7 %reduce-scatter.14.cloned.1.call-done = f32[1024,64]{0,1:T(8,128)} async-done(((f32[1024,2048]{0,1:T(8,128)}), f32[1024,64]{0,1:T(8,128)}) %reduce-scatter.14.cloned.1.call-update) | async-done | bytes 262160 | tf_op jit(solution)/shard_map/reduce_scatter | solution.py:335
  794.8 147.6 %reduce-scatter.16.cloned.1.call-done = f32[64,1024]{1,0:T(8,128)} async-done(((f32[2048,1024]{1,0:T(8,128)}), f32[64,1024]{1,0:T(8,128)}) %reduce-scatter.16.cloned.1.call-update) | async-done | bytes 262160 | tf_op jit(solution)/shard_map/reduce_scatter | solution.py:226
  942.3 147.5 %reduce-scatter.18.cloned.1.call-done = f32[64,1024]{1,0:T(8,128)} async-done(((f32[2048,1024]{1,0:T(8,128)}), f32[64,1024]{1,0:T(8,128)}) %reduce-scatter.18.cloned.1.call-update) | async-done | bytes 262160 | tf_op jit(solution)/shard_map/reduce_scatter | solution.py:227
  1089.9 147.5 %reduce-scatter.20.cloned.1.call-done = f32[1024,64]{0,1:T(8,128)} async-done(((f32[1024,2048]{0,1:T(8,128)}), f32[1024,64]{0,1:T(8,128)}) %reduce-scatter.20.cloned.1.call-update) | async-done | bytes 262160 | tf_op jit(solution)/shard_map/reduce_scatter | solution.py:228
  1237.4 157.7 %reduce-scatter.12.cloned.1.call-done = f32[64,1536]{1,0:T(8,128)} async-done(((f32[2048,1536]{1,0:T(8,128)}), f32[64,1536]{1,0:T(8,128)}) %reduce-scatter.12.cloned.1.call-update) | async-done | bytes 393232 | tf_op jit(solution)/shard_map/reduce_scatter | solution.py:334
  (273 shorter events, 121.6 us)
Async XLA Ops:
  7.2 76.8 %all-gather.8.cloned.1.call-start = ((), (), s32[]{:S(2)}) async-start(), calls=%async_computation.7 | async-start | bytes 6488064 | tf_op jit(solution)/shard_map/all_gather | solution.py:98
  8.9 139.1 %all-gather.14.cloned.1.call-start = ((), (), s32[]{:S(2)}) async-start(), calls=%async_computation.10 | async-start | bytes 4325376 | tf_op jit(solution)/shard_map/all_gather | solution.py:99
  10.6 46.9 %copy-start.54 = (f32[64]{0:T(128)S(1)}, f32[64]{0:T(128)}, u32[]{:S(2)}) copy-start(f32[64]{0:T(128)} %param.28) | copy-start | bytes 772
  10.6 47.0 %copy-start.14 = (bf16[1,512,2048]{2,1,0:T(8,128)(2,1)S(1)}, bf16[1,512,2048]{2,1,0:T(8,128)(2,1)}, u32[]{:S(2)}) copy-start(bf16[1,512,2048]{2,1,0:T(8,128)(2,1)} %param.21) | copy-start | bytes 6291460
  10.6 154.8 %all-gather.10.cloned.1.call-start = ((), (), s32[]{:S(2)}) async-start(), calls=%async_computation.8 | async-start | bytes 1310720 | tf_op jit(solution)/shard_map/all_gather | solution.py:145
  55.1 28.9 %copy-start.42 = (f32[2048]{0:T(1024)}, f32[2048]{0:T(1024)S(1)}, u32[]{:S(2)}) copy-start(f32[2048]{0:T(1024)S(1)} %convert_element_type.160) | copy-start | bytes 24580
  55.4 105.1 %copy-start.18 = (f32[512,64]{0,1:T(8,128)}, f32[512,64]{0,1:T(8,128)S(1)}, u32[]{:S(2)}) copy-start(f32[512,64]{0,1:T(8,128)S(1)} %get-tuple-element.739) | copy-start | bytes 393220
  55.4 105.1 %copy-start.25 = (f32[512,64]{0,1:T(8,128)}, f32[512,64]{0,1:T(8,128)S(1)}, u32[]{:S(2)}) copy-start(f32[512,64]{0,1:T(8,128)S(1)} %get-tuple-element.740) | copy-start | bytes 393220
  57.6 44.6 %copy-start.45 = (f32[256]{0:T(256)}, f32[256]{0:T(256)S(1)}, u32[]{:S(2)}) copy-start(f32[256]{0:T(256)S(1)} %mul.793) | copy-start | bytes 3076
  58.7 31.5 %copy-start.50 = (f32[512]{0:T(512)}, f32[512]{0:T(512)S(1)}, u32[]{:S(2)}) copy-start(f32[512]{0:T(512)S(1)} %get-tuple-element.746) | copy-start | bytes 6148
  90.3 64.2 %copy-start.11 = (f32[1,512,1536]{2,1,0:T(8,128)}, f32[1,512,1536]{2,1,0:T(8,128)S(1)}, u32[]{:S(2)}) copy-start(f32[1,512,1536]{2,1,0:T(8,128)S(1)} %convolution_bitcast_fusion) | copy-start | bytes 9437188
  102.3 9.3 copy-start.57
  104.7 79.5 %all-gather.12.cloned.1.call-start = ((), (), s32[]{:S(2)}) async-start(), calls=%async_computation.9 | async-start | bytes 1310720 | tf_op jit(solution)/shard_map/all_gather | solution.py:146
  105.5 144.1 %all-gather.16.cloned.1.call-start = ((), (), s32[]{:S(2)}) async-start(), calls=%async_computation.11 | async-start | bytes 4325376 | tf_op jit(solution)/shard_map/all_gather | solution.py:186
  107.2 206.3 %all-gather.18.cloned.1.call-start = ((), (), s32[]{:S(2)}) async-start(), calls=%async_computation.12 | async-start | bytes 4325376 | tf_op jit(solution)/shard_map/all_gather | solution.py:187
  108.9 268.1 %all-gather.20.cloned.1.call-start = ((), (), s32[]{:S(2)}) async-start(), calls=%async_computation.13 | async-start | bytes 4325376 | tf_op jit(solution)/shard_map/all_gather | solution.py:188
  110.6 498.2 %reduce-scatter.8.cloned.1.call-start = ((), (), s32[]{:S(2)}) async-start(), calls=%async_computation.14 | async-start | bytes 2621440 | tf_op jit(solution)/shard_map/reduce_scatter | solution.py:302
  112.9 280.5 %copy-start.52 = (f32[512]{0:T(512)}, f32[512]{0:T(512)S(1)}, u32[]{:S(2)}) copy-start(f32[512]{0:T(512)S(1)} %compare_convert_fusion) | copy-start | bytes 6148
  190.0 4.6 copy-start.1
  207.4 5.3 copy-start.23
  377.0 8.3 copy-start.56
  385.3 4.2 copy-start.22
  389.5 3.9 copy-start.27
  404.9 10.9 copy-start.32
  414.6 9.8 copy-start.9
  424.4 3.3 copy-start
  437.8 6.1 copy-start.10
  451.5 191.4 %reduce-scatter.10.cloned.1.call-start = ((), (), s32[]{:S(2)}) async-start(), calls=%async_computation.15 | async-start | bytes 2621440 | tf_op jit(solution)/shard_map/reduce_scatter | solution.py:303
  454.9 339.9 %reduce-scatter.14.cloned.1.call-start = ((), (), s32[]{:S(2)}) async-start(), calls=%async_computation.17 | async-start | bytes 8650752 | tf_op jit(solution)/shard_map/reduce_scatter | solution.py:335
  463.9 478.4 %reduce-scatter.16.cloned.1.call-start = ((), (), s32[]{:S(2)}) async-start(), calls=%async_computation.18 | async-start | bytes 8650752 | tf_op jit(solution)/shard_map/reduce_scatter | solution.py:226
  472.4 617.4 %reduce-scatter.18.cloned.1.call-start = ((), (), s32[]{:S(2)}) async-start(), calls=%async_computation.19 | async-start | bytes 8650752 | tf_op jit(solution)/shard_map/reduce_scatter | solution.py:227
  481.0 756.4 %reduce-scatter.20.cloned.1.call-start = ((), (), s32[]{:S(2)}) async-start(), calls=%async_computation.20 | async-start | bytes 8650752 | tf_op jit(solution)/shard_map/reduce_scatter | solution.py:228
  489.6 905.6 %reduce-scatter.12.cloned.1.call-start = ((), (), s32[]{:S(2)}) async-start(), calls=%async_computation.16 | async-start | bytes 12976128 | tf_op jit(solution)/shard_map/reduce_scatter | solution.py:334
  492.0 4.1 copy-start.40
  506.7 3.8 copy-start.12
  528.7 83.4 %copy-start.55 = (f32[64]{0:T(128)S(1)}, f32[64]{0:T(128)}, u32[]{:S(2)}) copy-start(f32[64]{0:T(128)} %param.28) | copy-start | bytes 772
  613.1 30.9 %copy-start.46 = (f32[256]{0:T(256)S(1)}, f32[256]{0:T(256)}, u32[]{:S(2)}) copy-start(f32[256]{0:T(256)} %copy-done.45) | copy-start | bytes 3076
  644.0 3.2 copy-start.16
  644.0 3.2 copy-start.30
  644.1 3.1 copy-start.43
  644.1 3.1 copy-start.51
  654.9 3.1 copy-start.6
  654.9 3.4 copy-start.61
  658.3 6.3 copy-start.17
  658.3 6.3 copy-start.31
  658.3 6.3 copy-start.38
  664.6 8.6 copy-start.44
  664.6 75.8 %copy-start.49 = (f32[512]{0:T(512)S(1)}, f32[512]{0:T(512)}, u32[]{:S(2)}) copy-start(f32[512]{0:T(512)} %get-tuple-element.745) | copy-start | bytes 6148
  (28 other events, 48.6 us)
Sparse Core Ops, SparseCore 0:
  11.5 72.4 all-gather.7
  87.4 60.5 all-gather.13
  150.1 15.2 all-gather.9
  167.4 16.7 all-gather.11
  187.5 62.1 all-gather.15
  252.9 60.5 all-gather.17
  316.4 60.5 all-gather.19
  451.6 157.1 reduce-scatter.7
  611.5 31.3 reduce-scatter.9
  645.7 149.0 reduce-scatter.13
  797.6 144.6 reduce-scatter.15
  945.1 144.7 reduce-scatter.17
  1092.7 144.5 reduce-scatter.19
  1243.8 151.2 reduce-scatter.11
where the time goes:
time: 1410 us; the launch traced here: 1400 us
  waiting for transfers between devices  982 us (70%)
  matrix products  137 us (10%)
  blocking collectives  109 us (8%)
  local copies, waits for them, and re-layouts  93.9 us (7%)
  other arithmetic  58.4 us (4%)
  between operations  15.5 us (1%)
    reduce_scatter x1, waiting for transfers between devices, local(): lax.psum_scatter(grad_wqkv, ('dp', 'shard'), scatter_dimension=0, tiled=T...  158 us
    reduce_scatter x1, waiting for transfers between devices, local(): lax.psum_scatter(grad_wgate, ('dp', 'shard'), scatter_dimension=0, tiled=...  148 us
    reduce_scatter x1, waiting for transfers between devices, local(): lax.psum_scatter(grad_wup, ('dp', 'shard'), scatter_dimension=0, tiled=True)  148 us
    reduce_scatter x1, waiting for transfers between devices, local(): lax.psum_scatter(grad_down, ('dp', 'shard'), scatter_dimension=1, tiled=T...  148 us
    unnamed x2, blocking collectives  109 us
    reduce_scatter x1, waiting for transfers between devices, local(): lax.psum_scatter(grad_keys_all, 'shard', scatter_dimension=1, tiled=True)  80.1 us
    all_gather x1, waiting for transfers between devices, local(): lax.all_gather(ffn_pack[2], ('dp', 'shard'), axis=0, tiled=True)  57.4 us
    all_gather x1, waiting for transfers between devices, local(): lax.all_gather(ffn_pack[3], ('dp', 'shard'), axis=1, tiled=True)  57 us
  transfers between devices with their start and end apart: 14, of which 14 were waited for; matrix products, arithmetic and copies ran while one was open for 14% of the time, Pallas kernels for 0%

commit v1 on v0

--- a/solution.py
+++ b/solution.py
@@ -3,6 +3,8 @@
 import jax
 import jax.numpy as jnp
 from jax import lax
+from jax.experimental import pallas as pl
+from jax.experimental.pallas import tpu as pltpu
 from jax.sharding import PartitionSpec as P
 
 HEADS = 16
@@ -44,6 +46,161 @@
     angles = positions.astype(jnp.float32)[:, None] * freq[None, :]
     angles = jnp.concatenate([angles, angles], axis=-1)
     return (jnp.cos(angles), jnp.sin(angles))
+
+
+ANY = pl.BlockSpec(memory_space=pl.ANY)
+
+
+def swap(values, mask, devices):
+    return lax.ppermute(values, ("dp", "shard"), [(i, i ^ mask) for i in range(devices)])
+
+
+def place(blocks, masks, me, total_rows):
+    count = len(blocks)
+    sizes = [array.shape[0] // len(own) for array, own in zip(blocks, masks)]
+    copies = sum(len(own) for own in masks)
+
+    def kernel(me_ref, *refs):
+        sources, out_ref, sems = refs[:count], refs[count], refs[count + 1]
+        started = []
+        for array, own, size in zip(sources, masks, sizes):
+            for at, mask in enumerate(own):
+                row = pl.multiple_of((me_ref[0] ^ mask) * size, size)
+                copy = pltpu.make_async_copy(
+                    array.at[pl.ds(at * size, size)], out_ref.at[pl.ds(row, size)], sems.at[len(started)]
+                )
+                copy.start()
+                started.append(copy)
+        for copy in started:
+            copy.wait()
+
+    return pl.pallas_call(
+        kernel,
+        out_shape=jax.ShapeDtypeStruct((total_rows,) + blocks[0].shape[1:], blocks[0].dtype),
+        in_specs=[pl.BlockSpec(memory_space=pltpu.SMEM)] + [ANY] * count,
+        out_specs=ANY,
+        scratch_shapes=[pltpu.SemaphoreType.DMA((copies,))],
+    )(me, *blocks)
+
+
+def pick(array, orders, me, size):
+    copies = sum(len(own) for own in orders)
+
+    def kernel(me_ref, in_ref, *refs):
+        outs, sems = refs[:-1], refs[-1]
+        started = []
+        for out, own in zip(outs, orders):
+            for at, mask in enumerate(own):
+                row = pl.multiple_of((me_ref[0] ^ mask) * size, size)
+                copy = pltpu.make_async_copy(
+                    in_ref.at[pl.ds(row, size)], out.at[pl.ds(at * size, size)], sems.at[len(started)]
+                )
+                copy.start()
+                started.append(copy)
+        for copy in started:
+            copy.wait()
+
+    return pl.pallas_call(
+        kernel,
+        out_shape=[jax.ShapeDtypeStruct((len(own) * size,) + array.shape[1:], array.dtype) for own in orders],
+        in_specs=[pl.BlockSpec(memory_space=pltpu.SMEM), ANY],
+        out_specs=[ANY] * len(orders),
+        scratch_shapes=[pltpu.SemaphoreType.DMA((copies,))],
+    )(me, array)
+
+
+def gather_rows(part, me, devices):
+    if devices != 32:
+        return lax.all_gather(part, ("dp", "shard"), axis=0, tiled=True)
+    zs = [part] + [swap(part, m, devices) for m in (8, 16, 24)]
+    near, far = jnp.concatenate(zs[:2]), jnp.concatenate(zs[2:])
+    near_x, far_x = swap(near, 4, devices), swap(far, 4, devices)
+    near_y, far_y = swap(near, 2, devices), swap(far, 2, devices)
+    near_xy, far_xy = swap(near_x, 2, devices), swap(far_y, 4, devices)
+    blocks, masks = [], []
+    for array, shift, base in (
+        (near, 0, 0), (far, 0, 16), (near_x, 4, 0), (far_y, 2, 16),
+        (near_y, 2, 0), (far_x, 4, 16), (near_xy, 6, 0), (far_xy, 6, 16),
+    ):
+        blocks += [array, swap(array, 1, devices)]
+        masks += [(base | shift, (base + 8) | shift), (base | shift | 1, (base + 8) | shift | 1)]
+    return place(blocks, masks, me, part.shape[0] * devices)
+
+
+def reduce_rows(grad, me, devices):
+    if devices != 32:
+        return lax.psum_scatter(
+            grad.astype(jnp.float32), ("dp", "shard"), scatter_dimension=0, tiled=True
+        )
+    size = grad.shape[0] // devices
+    order = [2, 10, 6, 14, 20, 28, 22, 30, 0, 8, 4, 12, 16, 24, 18, 26]
+    keep, send = pick(grad, [order, [m | 1 for m in order]], me, size)
+    came = swap(send, 1, devices)
+    low = jnp.bfloat16
+    def both(lo, hi):
+        return keep[lo * size : hi * size].astype(jnp.float32) + came[lo * size : hi * size].astype(
+            jnp.float32
+        )
+    from_y = swap(both(0, 4).astype(low), 2, devices)
+    from_x = swap(both(4, 8).astype(low), 4, devices)
+    near = both(8, 12) + from_y.astype(jnp.float32)
+    far = both(12, 16) + from_x.astype(jnp.float32)
+    from_x = swap(near[2 * size :].astype(low), 4, devices)
+    from_y = swap(far[2 * size :].astype(low), 2, devices)
+    near = near[: 2 * size] + from_x.astype(jnp.float32)
+    far = far[: 2 * size] + from_y.astype(jnp.float32)
+    one = swap(near[size:].astype(low), 8, devices)
+    two = swap(far[:size].astype(low), 16, devices)
+    three = swap(far[size:].astype(low), 24, devices)
+    return (
+        near[:size]
+        + one.astype(jnp.float32)
+        + (two.astype(jnp.float32) + three.astype(jnp.float32))
+    )
+
+
+def gather_row(part, devices, shards):
+    if shards != 4:
+        return lax.all_gather(part, "shard", axis=1, tiled=True)
+    at = lax.axis_index("shard").reshape(1)
+    flat = part[0]
+    over = swap(flat, 2, devices)
+    blocks = [flat, swap(flat, 1, devices), over, swap(over, 1, devices)]
+    return place(blocks, [(0,), (1,), (2,), (3,)], at, 4 * flat.shape[0])[None]
+
+
+def reduce_row(grad, devices, shards):
+    if shards != 4:
+        return lax.psum_scatter(grad, "shard", scatter_dimension=1, tiled=True)
+    at = lax.axis_index("shard").reshape(1)
+    size = grad.shape[1] // 4
+    low = grad[0].astype(jnp.bfloat16)
+    keep, send = pick(low, [(0, 2), (1, 3)], at, size)
+    both = keep.astype(jnp.float32) + swap(send, 1, devices).astype(jnp.float32)
+    over = swap(both[size:].astype(jnp.bfloat16), 2, devices)
+    return (both[:size] + over.astype(jnp.float32))[None]
+
+
+def small_gather(part, devices):
+    if devices != 32:
+        return lax.all_gather(part, ("dp", "shard"), axis=0)
+    rows = part[None]
+    for mask in (1, 2, 4, 8, 16):
+        rows = jnp.concatenate([rows, swap(rows, mask, devices)])
+    me = lax.axis_index("dp") * 4 + lax.axis_index("shard")
+    return rows[jnp.arange(devices) ^ me]
+
+
+def small_reduce(rows, shared, devices):
+    if devices != 32:
+        own = lax.psum_scatter(rows, ("dp", "shard"), scatter_dimension=0)
+        return own, lax.psum(shared, ("dp", "shard"))
+    me = lax.axis_index("dp") * 4 + lax.axis_index("shard")
+    rows = rows[jnp.arange(devices) ^ me]
+    for mask in (16, 8, 4, 2, 1):
+        came = swap(jnp.concatenate([rows[mask:], shared]), mask, devices)
+        rows, shared = rows[:mask] + came[:mask], shared + came[mask:]
+    return rows[0], shared
 
 
 def unchanged(running):
@@ -88,16 +245,19 @@
     cos_h = cos_t[None, :, None, :]
     sin_h = sin_t[None, :, None, :]
     query_pos = jnp.tile(positions, group_size)
-    attn_pack = (
-        attn_gain.astype(jnp.bfloat16),
-        w_qkv.astype(jnp.bfloat16),
-        w_out.astype(jnp.bfloat16),
-    )
-    gain_attn, wqkv_low, wout_low = (
-        lax.all_gather(attn_pack[0], ("dp", "shard"), axis=0, tiled=True),
-        lax.all_gather(attn_pack[1], ("dp", "shard"), axis=0, tiled=True),
-        lax.all_gather(attn_pack[2], ("dp", "shard"), axis=1, tiled=True),
-    )
+    shards = lax.axis_size("shard")
+    devices = lax.axis_size("dp") * shards
+    me = (lax.axis_index("dp") * shards + lax.axis_index("shard")).reshape(1)
+    gains = small_gather(jnp.concatenate([attn_gain, ffn_gain]).astype(jnp.bfloat16), devices)
+    part_len = attn_gain.shape[0]
+    gain_attn = gains[:, :part_len].reshape(model_width)
+    gain_ffn = gains[:, part_len:].reshape(model_width)
+    low = jnp.bfloat16
+    wqkv_low = gather_rows(w_qkv.astype(low), me, devices)
+    wout_low = gather_rows(w_out.astype(low).T, me, devices)
+    wgate_low = gather_rows(w_gate.astype(low), me, devices)
+    wup_low = gather_rows(w_up.astype(low), me, devices)
+    wdown_low = gather_rows(w_down.astype(low).T, me, devices)
     gain_attn_f = gain_attn.astype(jnp.float32)
     x_float = tokens.astype(jnp.float32)
     normed_one, inverse_one = normalize(x_float)
@@ -142,8 +302,8 @@
 
     zero_accum = jnp.zeros((row_count, KV, group_size * piece_len, HD), jnp.float32)
     zero_sums = jnp.zeros((row_count, KV, group_size * piece_len), jnp.float32)
-    key_piece = lax.all_gather(k_low, "shard", axis=1, tiled=True)
-    value_piece = lax.all_gather(v_low, "shard", axis=1, tiled=True)
+    both_piece = gather_row(jnp.concatenate([k_low, v_low], axis=-1), devices, shards)
+    key_piece, value_piece = both_piece[..., :kv_width], both_piece[..., kv_width:]
     block_len = math.gcd(key_piece.shape[1], piece_len)
     block_count = key_piece.shape[1] // block_len
 
@@ -173,19 +333,7 @@
         .astype(jnp.bfloat16)
     )
     x_mid = x_float + jnp.einsum(
-        "rtc,cd->rtd", att_low, wout_low, preferred_element_type=jnp.float32
-    )
-    ffn_pack = (
-        ffn_gain.astype(jnp.bfloat16),
-        w_gate.astype(jnp.bfloat16),
-        w_up.astype(jnp.bfloat16),
-        w_down.astype(jnp.bfloat16),
-    )
-    gain_ffn, wgate_low, wup_low, wdown_low = (
-        lax.all_gather(ffn_pack[0], ("dp", "shard"), axis=0, tiled=True),
-        lax.all_gather(ffn_pack[1], ("dp", "shard"), axis=0, tiled=True),
-        lax.all_gather(ffn_pack[2], ("dp", "shard"), axis=0, tiled=True),
-        lax.all_gather(ffn_pack[3], ("dp", "shard"), axis=1, tiled=True),
+        "rtc,dc->rtd", att_low, wout_low, preferred_element_type=jnp.float32
     )
     gain_ffn_f = gain_ffn.astype(jnp.float32)
     normed_two, inverse_two = normalize(x_mid)
@@ -196,46 +344,34 @@
     silu_gate = gate_proj * gate_sig
     activated = (silu_gate * up_proj).astype(jnp.bfloat16)
     result = x_mid + jnp.einsum(
-        "rtf,fd->rtd", activated, wdown_low, preferred_element_type=jnp.float32
+        "rtf,df->rtd", activated, wdown_low, preferred_element_type=jnp.float32
     )
     output = result.astype(jnp.bfloat16)
     grad_out = cotangent.astype(jnp.float32) * live_mask[..., None]
     grad_low = grad_out.astype(jnp.bfloat16)
-    gain_again, wgate_k, wup_k, wdown_k = (
-        lax.all_gather(ffn_pack[0], ("dp", "shard"), axis=0, tiled=True),
-        lax.all_gather(ffn_pack[1], ("dp", "shard"), axis=0, tiled=True),
-        lax.all_gather(ffn_pack[2], ("dp", "shard"), axis=0, tiled=True),
-        lax.all_gather(ffn_pack[3], ("dp", "shard"), axis=1, tiled=True),
-    )
-    gain_ffn_k = gain_again.astype(jnp.float32)
-    grad_down = jnp.einsum("rtf,rtd->fd", activated, grad_low, preferred_element_type=jnp.float32)
-    grad_act = jnp.einsum("rtd,fd->rtf", grad_low, wdown_k, preferred_element_type=jnp.float32)
+    gain_ffn_k = gain_ffn_f
+    wgate_k, wup_k, wdown_k = wgate_low, wup_low, wdown_low
+    grad_down = jnp.einsum("rtd,rtf->df", grad_low, activated, preferred_element_type=jnp.float32).astype(low)
+    grad_act = jnp.einsum("rtd,df->rtf", grad_low, wdown_k, preferred_element_type=jnp.float32)
     grad_gate = (grad_act * up_proj * gate_sig * (1.0 + gate_proj * (1.0 - gate_sig))).astype(
         jnp.bfloat16
     )
     grad_up = (grad_act * silu_gate).astype(jnp.bfloat16)
-    grad_wgate = jnp.einsum("rtd,rtf->df", ffn_in, grad_gate, preferred_element_type=jnp.float32)
-    grad_wup = jnp.einsum("rtd,rtf->df", ffn_in, grad_up, preferred_element_type=jnp.float32)
+    grad_wgate = jnp.einsum("rtd,rtf->df", ffn_in, grad_gate, preferred_element_type=jnp.float32).astype(low)
+    grad_wup = jnp.einsum("rtd,rtf->df", ffn_in, grad_up, preferred_element_type=jnp.float32).astype(low)
     grad_ffn_in = jnp.einsum(
         "rtf,df->rtd", grad_gate, wgate_k, preferred_element_type=jnp.float32
     ) + jnp.einsum("rtf,df->rtd", grad_up, wup_k, preferred_element_type=jnp.float32)
     grad_gain_two = jnp.sum(grad_ffn_in * normed_two, axis=(0, 1))
     grad_mid = grad_out + norm_back(x_mid, inverse_two, grad_ffn_in * gain_ffn_k)
-    summed_gain_two, summed_wgate, summed_wup, summed_down = (
-        lax.psum_scatter(grad_gain_two, ("dp", "shard"), scatter_dimension=0, tiled=True),
-        lax.psum_scatter(grad_wgate, ("dp", "shard"), scatter_dimension=0, tiled=True),
-        lax.psum_scatter(grad_wup, ("dp", "shard"), scatter_dimension=0, tiled=True),
-        lax.psum_scatter(grad_down, ("dp", "shard"), scatter_dimension=1, tiled=True),
-    )
-    gain_back, wqkv_k, wout_k = (
-        lax.all_gather(attn_pack[0], ("dp", "shard"), axis=0, tiled=True),
-        lax.all_gather(attn_pack[1], ("dp", "shard"), axis=0, tiled=True),
-        lax.all_gather(attn_pack[2], ("dp", "shard"), axis=1, tiled=True),
-    )
-    gain_attn_k = gain_back.astype(jnp.float32)
+    summed_down = reduce_rows(grad_down, me, devices).T
+    summed_wgate = reduce_rows(grad_wgate, me, devices)
+    summed_wup = reduce_rows(grad_wup, me, devices)
+    wqkv_k, wout_k, gain_attn_k = wqkv_low, wout_low, gain_attn_f
     mid_low = grad_mid.astype(jnp.bfloat16)
-    grad_wout = jnp.einsum("rtc,rtd->cd", att_low, mid_low, preferred_element_type=jnp.float32)
-    grad_att = jnp.einsum("rtd,cd->rtc", mid_low, wout_k, preferred_element_type=jnp.float32)
+    grad_wout = jnp.einsum("rtd,rtc->dc", mid_low, att_low, preferred_element_type=jnp.float32).astype(low)
+    summed_wout = reduce_rows(grad_wout, me, devices).T
+    grad_att = jnp.einsum("rtd,dc->rtc", mid_low, wout_k, preferred_element_type=jnp.float32)
     grad_group = (
         grad_att.reshape(row_count, piece_len, KV, group_size, HD)
         .transpose(0, 2, 3, 1, 4)
@@ -244,8 +380,7 @@
     grad_sums = -jnp.sum(grad_group * o_group, axis=-1) / denominator
     grad_accum = (grad_group / denominator[..., None]).astype(jnp.bfloat16)
     zero_keys = jnp.zeros((row_count, row_len, kv_width), jnp.float32)
-    attend_key_piece = lax.all_gather(k_low, "shard", axis=1, tiled=True)
-    attend_value_piece = lax.all_gather(v_low, "shard", axis=1, tiled=True)
+    attend_key_piece, attend_value_piece = key_piece, value_piece
     attend_block_len = math.gcd(attend_key_piece.shape[1], piece_len)
     block_count = attend_key_piece.shape[1] // attend_block_len
 
@@ -298,10 +433,8 @@
     grad_query, grad_keys_all, grad_values_all = lax.fori_loop(
         0, block_count, fold_block, (zero_accum, zero_keys, zero_keys)
     )
-    grad_keys, grad_values = (
-        lax.psum_scatter(grad_keys_all, "shard", scatter_dimension=1, tiled=True),
-        lax.psum_scatter(grad_values_all, "shard", scatter_dimension=1, tiled=True),
-    )
+    grad_both = reduce_row(jnp.concatenate([grad_keys_all, grad_values_all], axis=-1), devices, shards)
+    grad_keys, grad_values = grad_both[..., :kv_width], grad_both[..., kv_width:]
     grad_q_heads = (
         grad_query.reshape(row_count, KV, group_size, piece_len, HD)
         .transpose(0, 3, 1, 2, 4)
@@ -323,18 +456,22 @@
     ).astype(jnp.bfloat16)
     grad_wqkv = jnp.einsum(
         "rtd,rte->de", normed_low, grad_projected, preferred_element_type=jnp.float32
-    )
+    ).astype(low)
     grad_normed = jnp.einsum(
         "rte,de->rtd", grad_projected, wqkv_k, preferred_element_type=jnp.float32
     )
     grad_gain_one = jnp.sum(grad_normed * normed_one, axis=(0, 1))
     input_grad = grad_mid + norm_back(x_float, inverse_one, grad_normed * gain_attn_k)
-    summed_gain_one, summed_wqkv, summed_wout = (
-        lax.psum_scatter(grad_gain_one, ("dp", "shard"), scatter_dimension=0, tiled=True),
-        lax.psum_scatter(grad_wqkv, ("dp", "shard"), scatter_dimension=0, tiled=True),
-        lax.psum_scatter(grad_wout, ("dp", "shard"), scatter_dimension=1, tiled=True),
-    )
-    summed_qgain, summed_kgain = lax.psum((grad_qgain, grad_kgain), ("dp", "shard"))
+    summed_wqkv = reduce_rows(grad_wqkv, me, devices)
+    own, shared = small_reduce(
+        jnp.concatenate(
+            [grad_gain_one.reshape(devices, part_len), grad_gain_two.reshape(devices, part_len)], axis=1
+        ),
+        jnp.concatenate([grad_qgain, grad_kgain])[None],
+        devices,
+    )
+    summed_gain_one, summed_gain_two = own[:part_len], own[part_len:]
+    summed_qgain, summed_kgain = shared[0, :HD], shared[0, HD:]
     return (
         output,
         input_grad,

time: 1410 us -> 2350 us (1.67)
  Pallas kernels: 0 us -> 1540 us
  waiting for transfers between devices: 982 us -> 230 us
  starting transfers between devices: 1.34 us -> 277 us
  blocking collectives: 109 us -> 0 us
    pallas_call x0 -> x12, Pallas kernels: none -> 1540 us  [the longest x6 770 us: place(): pl.pallas_call(kernel, out_shape=jax.ShapeDtypeStruct((total_rows,) + blo...]
    reduce_scatter x7 -> x0, waiting for transfers between devices: 753 us -> none  [the longest x1 158 us: local(): lax.psum_scatter(grad_wqkv, ('dp', 'shard'), scatter_dimension=0, tiled=T...]
    ppermute x0 -> x140, starting transfers between devices: none -> 277 us  [swap(): lax.ppermute(values, ('dp', 'shard'), [(i, i ^ mask) for i in range(devic...]
    ppermute x0 -> x140, waiting for transfers between devices: none -> 230 us  [swap(): lax.ppermute(values, ('dp', 'shard'), [(i, i ^ mask) for i in range(devic...]
    all_gather x7 -> x0, waiting for transfers between devices: 228 us -> none  [the longest x1 57.4 us: local(): lax.all_gather(ffn_pack[2], ('dp', 'shard'), axis=0, tiled=True)]
    unnamed x2 -> x0, blocking collectives: 109 us -> none
  transfers between devices with their start and end apart: 14 -> 140, of which waited for: 14 -> 48; matrix products, arithmetic and copies ran while one was open for 14% -> 5% of each run, Pallas kernels for 0% -> 52%
where the time goes in v1:
time: 2350 us; the launch traced here: 2340 us
  Pallas kernels  1540 us (66%)
  starting transfers between devices  277 us (12%)
  waiting for transfers between devices  230 us (10%)
  matrix products  119 us (5%)
  local copies, waits for them, and re-layouts  82.9 us (4%)
  other arithmetic  69.3 us (3%)
    pallas_call x6, Pallas kernels, place(): pl.pallas_call(kernel, out_shape=jax.ShapeDtypeStruct((total_rows,) + blo...  770 us
    pallas_call x6, Pallas kernels, pick(): pl.pallas_call(kernel, out_shape=[jax.ShapeDtypeStruct((len(own) * size,)...  770 us
    ppermute x140, starting transfers between devices, swap(): lax.ppermute(values, ('dp', 'shard'), [(i, i ^ mask) for i in range(devic...  277 us
    ppermute x140, waiting for transfers between devices, swap(): lax.ppermute(values, ('dp', 'shard'), [(i, i ^ mask) for i in range(devic...  230 us
  transfers between devices with their start and end apart: 140, of which 48 were waited for; matrix products, arithmetic and copies ran while one was open for 5% of the time, Pallas kernels for 52%

profile of v1, /device:TPU:0, one launch (start us, length us, event | category | flops | bytes accessed | tf_op | source)
XLA Modules:
  0.0 2344.7 jit_solution(5981978604743839468)
XLA Ops:
  15.7 5.8 collective-permute-done.3
  38.5 7.5 collective-permute-start.5
  53.2 18.9 collective-permute-done.44
  126.7 5.7 collective-permute-done.10.refs_4_
  135.5 5.7 collective-permute-done.38.refs_12_
  183.3 128.4 %shard_map.214 = bf16[2048,1024]{1,0:T(8,128)(2,1)} custom-call(s32[1]{0:T(128)} %bitcast.31.me_ref, bf16[128,1024]{1,0:T(8,128)(2,1)} %copy-done.46, bf16[128,1024]{1,0:T(8,128)(2,1)} %copy-done.68, bf16[128,1024]{1,0:T(8,128)(2,1)} %copy-done.57, bf16[128,1024]{1,0:T(8,128)(2,1)} %copy-done.70, bf16[128,1024]{1,0:T(8,128)(2,1)} %copy-done.69, ...), custom_call_target="tpu_custom_call" | custom-call | tf_op jit(solution)/shard_map/pallas_call | solution.py:77
  311.7 6.6 copy.117
  318.3 128.4 %shard_map.217 = bf16[2048,1024]{1,0:T(8,128)(2,1)} custom-call(s32[1]{0:T(128)} %bitcast.31.me_ref, bf16[128,1024]{1,0:T(8,128)(2,1)} %copy-done.47, bf16[128,1024]{1,0:T(8,128)(2,1)} %copy-done.73, bf16[128,1024]{1,0:T(8,128)(2,1)} %copy-done.58, bf16[128,1024]{1,0:T(8,128)(2,1)} %copy-done.76, bf16[128,1024]{1,0:T(8,128)(2,1)} %copy-done.75, ...), custom_call_target="tpu_custom_call" | custom-call | tf_op jit(solution)/shard_map/pallas_call | solution.py:77
  446.8 128.5 %shard_map.216 = bf16[2048,1024]{1,0:T(8,128)(2,1)} custom-call(s32[1]{0:T(128)} %bitcast.31.me_ref, bf16[128,1024]{1,0:T(8,128)(2,1)} %copy-done.48, bf16[128,1024]{1,0:T(8,128)(2,1)} %copy-done.79, bf16[128,1024]{1,0:T(8,128)(2,1)} %copy-done.59, bf16[128,1024]{1,0:T(8,128)(2,1)} %copy-done.81, bf16[128,1024]{1,0:T(8,128)(2,1)} %copy-done.82, ...), custom_call_target="tpu_custom_call" | custom-call | tf_op jit(solution)/shard_map/pallas_call | solution.py:77
  575.3 128.5 %shard_map.215 = bf16[2048,1024]{1,0:T(8,128)(2,1)} custom-call(s32[1]{0:T(128)} %bitcast.31.me_ref, bf16[128,1024]{1,0:T(8,128)(2,1)} %copy-done.49, bf16[128,1024]{1,0:T(8,128)(2,1)} %copy-done.84, bf16[128,1024]{1,0:T(8,128)(2,1)} %copy-done.56, bf16[128,1024]{1,0:T(8,128)(2,1)} %copy-done.85, bf16[128,1024]{1,0:T(8,128)(2,1)} %copy-done.86, ...), custom_call_target="tpu_custom_call" | custom-call | tf_op jit(solution)/shard_map/pallas_call | solution.py:77
  704.9 5.9 fusion.71
  711.6 192.0 %shard_map.212 = bf16[2048,1536]{1,0:T(8,128)(2,1)} custom-call(s32[1]{0:T(128)} %bitcast.31.me_ref, bf16[128,1536]{1,0:T(8,128)(2,1)} %copy-done.42, bf16[128,1536]{1,0:T(8,128)(2,1)} %copy-done.60, bf16[128,1536]{1,0:T(8,128)(2,1)} %copy-done.55, bf16[128,1536]{1,0:T(8,128)(2,1)} %copy-done.61, bf16[128,1536]{1,0:T(8,128)(2,1)} %copy-done.62, ...), custom_call_target="tpu_custom_call" | custom-call | tf_op jit(solution)/shard_map/pallas_call | solution.py:77
  903.6 6.3 convolution_bitcast_fusion
  930.3 8.9 collective-permute-done.23.refs_2_
  945.6 64.7 %shard_map.213 = bf16[2048,512]{1,0:T(8,128)(2,1)} custom-call(s32[1]{0:T(128)} %bitcast.26.me_ref, bf16[512,512]{1,0:T(8,128)(2,1)} %maximum_bitcast_fusion.1.refs_0_, bf16[512,512]{1,0:T(8,128)(2,1)} %collective-permute-done.22.refs_1_, bf16[512,512]{1,0:T(8,128)(2,1)} %collective-permute-done.23.refs_2_, bf16[512,512]{1,0:T(8,128)(2,1)} %collective-permute-done.24.refs_3_), custom_call_target="tpu_custom_call" | custom-call | tf_op jit(solution)/shard_map/pallas_call | solution.py:77
  1015.1 29.9 %while.34 = (s32[]{:T(128)}, f32[1,4,2048,64]{2,3,1,0:T(8,128)S(1)}, f32[1,4,2048]{2,1,0:T(4,128)S(1)}, s32[]{:T(128)}, s32[]{:T(128)}, /*index=5*/s32[1]{0:T(12...) while((s32[]{:T(128)}, ...), condition=%wide.region_8.0_spmd.clone, body=%wide.region_4.8_spmd.clone.sunk | while | flops 1101530624 | bytes 47881560 | solution.py:327
  1031.0 12.0 conditional.6
  1083.2 45.3 %while.35 = (s32[]{:T(128)}, f32[1,4,2048,64]{2,3,1,0:T(8,128)S(1)}, f32[1,2048,256]{1,2,0:T(8,128)}, f32[1,2048,256]{1,2,0:T(8,128)}, s32[]{:T(128)}, /*index=5...) while((s32[]{:T(128)}, ...), condition=%wide.region_15.16_spmd.clone, body=%wide.region_12.0_spmd.clone.sunk | while | flops 2721449472 | bytes 137174512 | solution.py:433
  1084.2 42.2 %conditional.7 = ((f32[1,4,2048,64]{2,3,1,0:T(8,128)S(1)}, f32[1,2048,256]{1,2,0:T(8,128)}, f32[1,2048,256]{1,2,0:T(8,128)})) conditional(s32[]{:T(128)} %convert_element_type.784, (f32[1,4,2048,64]{2,3,1,0:T(8,128)S(1)}, f32[1,2048,256]{1,2,0:T(8,128)}, f32[1,2048,256]{1,2,0:T(8,128)}) %tuple.133, (s32[]{:T(128)}, s32[512]{0:T(512)S(1)}, ...), branch_computations={%region_13.13_spmd, %region_14.14_spmd} | conditional | flops 2721449472 | bytes 137174208 | solution.py:431
  1085.2 8.1 fusion.31
  1096.0 8.6 fusion.21
  1107.8 10.1 fusion.23
  1118.0 6.1 convolution_multiply_fusion.1
  1135.7 64.7 %shard_map.218 = (bf16[1024,512]{1,0:T(8,128)(2,1)}, bf16[1024,512]{1,0:T(8,128)(2,1)}) custom-call(s32[1]{0:T(128)} %bitcast.26.me_ref, bf16[2048,512]{1,0:T(8,128)(2,1)} %maximum_bitcast_fusion.in_ref), custom_call_target="tpu_custom_call" | custom-call | tf_op jit(solution)/shard_map/pallas_call | solution.py:103
  1200.4 54.7 %collective-permute-start.93 = (bf16[1024,512]{1,0:T(8,128)(2,1)}, bf16[1024,512]{1,0:T(8,128)(2,1)}, u32[]{:S(2)}, u32[]{:S(2)}) collective-permute-start(bf16[1024,512]{1,0:T(8,128)(2,1)} %get-tuple-element.497), channel_id=1, source_target_pairs={{0,1},{1,0},{2,3},{3,2},{4,5},{5,4},{6,7},{7,6},{8,9},{9,8},{10,11... | collective-permute-start | bytes 3145736 | tf_op jit(solution)/shard_map/ppermute | solution.py:55
  1270.9 6.6 convolution_convert_fusion.1.in_ref
  1284.1 6.0 fusion.49
  1291.9 55.3 %collective-permute-start.94 = (bf16[512,512]{1,0:T(8,128)(2,1)S(1)}, bf16[512,512]{1,0:T(8,128)(2,1)S(1)}, u32[]{:S(2)}, u32[]{:S(2)}) collective-permute-start(bf16[512,512]{1,0:T(8,128)(2,1)S(1)} %slice.758), channel_id=1, source_target_pairs={{0,2},{1,3},{2,0},{3,1},{4,6},{5,7},{6,4},{7,5},{8,10},{9,11},{10,... | collective-permute-start | bytes 1572872 | tf_op jit(solution)/shard_map/ppermute | solution.py:55
  1351.6 7.7 collective-permute-done.94
  1366.1 9.2 fusion.40
  1381.9 5.9 convolution_convert_fusion.3.in_ref
  1387.9 52.5 %collective-permute-start.96 = (f32[9,128]{1,0:T(8,128)S(1)}, f32[9,128]{1,0:T(8,128)S(1)}, u32[]{:S(2)}, u32[]{:S(2)}) collective-permute-start(f32[9,128]{1,0:T(8,128)S(1)} %pad_maximum_fusion.14), channel_id=1, source_target_pairs={{0,8},{1,9},{2,10},{3,11},{4,12},{5,13},{6,14},{7,15},{8,0},{9,1},... | collective-permute-start | bytes 13832 | tf_op jit(solution)/shard_map/ppermute | solution.py:55
  1444.7 128.4 %shard_map.220 = (bf16[1024,1024]{1,0:T(8,128)(2,1)}, bf16[1024,1024]{1,0:T(8,128)(2,1)}) custom-call(s32[1]{0:T(128)} %bitcast.31.me_ref, bf16[2048,1024]{1,0:T(8,128)(2,1)} %convolution_convert_fusion.4.in_ref), custom_call_target="tpu_custom_call" | custom-call | tf_op jit(solution)/shard_map/pallas_call | solution.py:103
  1573.3 128.4 %shard_map.221 = (bf16[1024,1024]{1,0:T(8,128)(2,1)}, bf16[1024,1024]{1,0:T(8,128)(2,1)}) custom-call(s32[1]{0:T(128)} %bitcast.31.me_ref, bf16[2048,1024]{1,0:T(8,128)(2,1)} %convolution_convert_fusion.3.in_ref), custom_call_target="tpu_custom_call" | custom-call | tf_op jit(solution)/shard_map/pallas_call | solution.py:103
  1702.3 128.4 %shard_map.222 = (bf16[1024,1024]{1,0:T(8,128)(2,1)}, bf16[1024,1024]{1,0:T(8,128)(2,1)}) custom-call(s32[1]{0:T(128)} %bitcast.31.me_ref, bf16[2048,1024]{1,0:T(8,128)(2,1)} %convolution_convert_fusion.2.in_ref), custom_call_target="tpu_custom_call" | custom-call | tf_op jit(solution)/shard_map/pallas_call | solution.py:103
  1830.8 128.4 %shard_map.223 = (bf16[1024,1024]{1,0:T(8,128)(2,1)}, bf16[1024,1024]{1,0:T(8,128)(2,1)}) custom-call(s32[1]{0:T(128)} %bitcast.31.me_ref, bf16[2048,1024]{1,0:T(8,128)(2,1)} %convolution_convert_fusion.1.in_ref), custom_call_target="tpu_custom_call" | custom-call | tf_op jit(solution)/shard_map/pallas_call | solution.py:103
  1965.4 6.6 fusion.44
  1972.2 5.9 convolution_convert_fusion.in_ref
  1978.1 192.0 %shard_map.219 = (bf16[1024,1536]{1,0:T(8,128)(2,1)}, bf16[1024,1536]{1,0:T(8,128)(2,1)}) custom-call(s32[1]{0:T(128)} %bitcast.31.me_ref, bf16[2048,1536]{1,0:T(8,128)(2,1)} %convolution_convert_fusion.in_ref), custom_call_target="tpu_custom_call" | custom-call | tf_op jit(solution)/shard_map/pallas_call | solution.py:103
  2181.5 6.6 collective-permute-done.112
  2190.2 9.2 collective-permute-done.120
  2201.4 9.3 collective-permute-done.128
  2212.6 8.3 collective-permute-done.136
  2236.2 14.6 collective-permute-done.137
  2290.9 5.8 collective-permute-done.104
  2311.2 13.9 collective-permute-done.105
  2327.4 6.1 collective-permute-done.102
  2336.0 7.5 collective-permute-done.106
  (773 shorter events, 382.6 us)
Async XLA Ops:
  6.5 22.1 collective-permute-start.25
  8.2 22.4 collective-permute-start.27
  10.8 20.4 collective-permute-start.28
  13.5 19.6 collective-permute-start.76
  30.5 15.5 collective-permute-start.59
  31.2 17.1 collective-permute-start.61
  33.1 15.8 collective-permute-start.62
  37.5 15.5 collective-permute-start.42
  38.5 34.5 %collective-permute-start.5 = (bf16[64,1536]{1,0:T(8,128)(2,1)S(1)}, bf16[64,1536]{1,0:T(8,128)(2,1)S(1)}, u32[]{:S(2)}, u32[]{:S(2)}) collective-permute-start(bf16[64,1536]{1,0:T(8,128)(2,1)S(1)} %convert_element_type.484), channel_id=1, source_target_pairs={{0,8},{1,9},{2,10},{3,11},{4,12},{5,13},{6,14},{7,15},{8,0},{9,1},... | collective-permute-start | bytes 589832 | tf_op jit(solution)/shard_map/ppermute | solution.py:55
  46.0 27.3 %collective-permute-start.7 = (bf16[64,1536]{1,0:T(8,128)(2,1)S(1)}, bf16[64,1536]{1,0:T(8,128)(2,1)S(1)}, u32[]{:S(2)}, u32[]{:S(2)}) collective-permute-start(bf16[64,1536]{1,0:T(8,128)(2,1)S(1)} %convert_element_type.484), channel_id=1, source_target_pairs={{0,16},{1,17},{2,18},{3,19},{4,20},{5,21},{6,22},{7,23},{8,24},{9,... | collective-permute-start | bytes 589832 | tf_op jit(solution)/shard_map/ppermute | solution.py:55
  48.2 23.9 %collective-permute-start.44 = (bf16[64,1024]{1,0:T(8,128)(2,1)S(1)}, bf16[64,1024]{1,0:T(8,128)(2,1)S(1)}, u32[]{:S(2)}, u32[]{:S(2)}) collective-permute-start(bf16[64,1024]{1,0:T(8,128)(2,1)S(1)} %convert_element_type.496), channel_id=1, source_target_pairs={{0,16},{1,17},{2,18},{3,19},{4,20},{5,21},{6,22},{7,23},{8,24},{9,... | collective-permute-start | bytes 393224 | tf_op jit(solution)/shard_map/ppermute | solution.py:55
  48.9 23.2 collective-permute-start.45
  53.1 20.2 collective-permute-start.8
  172.4 531.4 %collective-permute-start.14 = (bf16[128,1536]{1,0:T(8,128)(2,1)S(1)}, bf16[128,1536]{1,0:T(8,128)(2,1)}, u32[]{:S(2)}, u32[]{:S(2)}) collective-permute-start(bf16[128,1536]{1,0:T(8,128)(2,1)S(1)} %pad_maximum_fusion.6.refs_0_), channel_id=1, source_target_pairs={{0,2},{1,3},{2,0},{3,1},{4,6},{5,7},{6,4},{7,5},{8,10},{9,11},{10,... | collective-permute-start | bytes 1179656 | tf_op jit(solution)/shard_map/ppermute | solution.py:55
  173.4 530.4 %collective-permute-start.16 = (bf16[128,1536]{1,0:T(8,128)(2,1)}, bf16[128,1536]{1,0:T(8,128)(2,1)}, u32[]{:S(2)}, u32[]{:S(2)}) collective-permute-start(bf16[128,1536]{1,0:T(8,128)(2,1)} %copy-done.55), channel_id=1, source_target_pairs={{0,4},{1,5},{2,6},{3,7},{4,0},{5,1},{6,2},{7,3},{8,12},{9,13},{10,... | collective-permute-start | bytes 1179656 | tf_op jit(solution)/shard_map/ppermute | solution.py:55
  174.5 529.8 %collective-permute-start.11 = (bf16[128,1536]{1,0:T(8,128)(2,1)}, bf16[128,1536]{1,0:T(8,128)(2,1)}, u32[]{:S(2)}, u32[]{:S(2)}) collective-permute-start(bf16[128,1536]{1,0:T(8,128)(2,1)} %copy-done.62), channel_id=1, source_target_pairs={{0,1},{1,0},{2,3},{3,2},{4,5},{5,4},{6,7},{7,6},{8,9},{9,8},{10,11... | collective-permute-start | bytes 1179656 | tf_op jit(solution)/shard_map/ppermute | solution.py:55
  174.5 529.9 %collective-permute-start.18 = (bf16[128,1536]{1,0:T(8,128)(2,1)}, bf16[128,1536]{1,0:T(8,128)(2,1)}, u32[]{:S(2)}, u32[]{:S(2)}) collective-permute-start(bf16[128,1536]{1,0:T(8,128)(2,1)} %copy-done.62), channel_id=1, source_target_pairs={{0,2},{1,3},{2,0},{3,1},{4,6},{5,7},{6,4},{7,5},{8,10},{9,11},{10,... | collective-permute-start | bytes 1179656 | tf_op jit(solution)/shard_map/ppermute | solution.py:55
  175.6 529.3 %collective-permute-start.20 = (bf16[128,1536]{1,0:T(8,128)(2,1)}, bf16[128,1536]{1,0:T(8,128)(2,1)}, u32[]{:S(2)}, u32[]{:S(2)}) collective-permute-start(bf16[128,1536]{1,0:T(8,128)(2,1)} %copy-done.63), channel_id=1, source_target_pairs={{0,4},{1,5},{2,6},{3,7},{4,0},{5,1},{6,2},{7,3},{8,12},{9,13},{10,... | collective-permute-start | bytes 1179656 | tf_op jit(solution)/shard_map/ppermute | solution.py:55
  924.5 21.1 collective-permute-start.22
  1200.4 89.7 %collective-permute-start.93 = (bf16[1024,512]{1,0:T(8,128)(2,1)}, bf16[1024,512]{1,0:T(8,128)(2,1)}, u32[]{:S(2)}, u32[]{:S(2)}) collective-permute-start(bf16[1024,512]{1,0:T(8,128)(2,1)} %get-tuple-element.497), channel_id=1, source_target_pairs={{0,1},{1,0},{2,3},{3,2},{4,5},{5,4},{6,7},{7,6},{8,9},{9,8},{10,11... | collective-permute-start | bytes 3145736 | tf_op jit(solution)/shard_map/ppermute | solution.py:55
  1291.9 67.4 %collective-permute-start.94 = (bf16[512,512]{1,0:T(8,128)(2,1)S(1)}, bf16[512,512]{1,0:T(8,128)(2,1)S(1)}, u32[]{:S(2)}, u32[]{:S(2)}) collective-permute-start(bf16[512,512]{1,0:T(8,128)(2,1)S(1)} %slice.758), channel_id=1, source_target_pairs={{0,2},{1,3},{2,0},{3,1},{4,6},{5,7},{6,4},{7,5},{8,10},{9,11},{10,... | collective-permute-start | bytes 1572872 | tf_op jit(solution)/shard_map/ppermute | solution.py:55
  1387.9 571.9 %collective-permute-start.96 = (f32[9,128]{1,0:T(8,128)S(1)}, f32[9,128]{1,0:T(8,128)S(1)}, u32[]{:S(2)}, u32[]{:S(2)}) collective-permute-start(f32[9,128]{1,0:T(8,128)S(1)} %pad_maximum_fusion.14), channel_id=1, source_target_pairs={{0,8},{1,9},{2,10},{3,11},{4,12},{5,13},{6,14},{7,15},{8,0},{9,1},... | collective-permute-start | bytes 13832 | tf_op jit(solution)/shard_map/ppermute | solution.py:55
  1573.2 598.6 %collective-permute-start.108 = (bf16[1024,1024]{1,0:T(8,128)(2,1)}, bf16[1024,1024]{1,0:T(8,128)(2,1)}, u32[]{:S(2)}, u32[]{:S(2)}) collective-permute-start(bf16[1024,1024]{1,0:T(8,128)(2,1)} %get-tuple-element.501), channel_id=1, source_target_pairs={{0,1},{1,0},{2,3},{3,2},{4,5},{5,4},{6,7},{7,6},{8,9},{9,8},{10,11... | collective-permute-start | bytes 6291464 | tf_op jit(solution)/shard_map/ppermute | solution.py:55
  1701.7 471.7 %collective-permute-start.116 = (bf16[1024,1024]{1,0:T(8,128)(2,1)}, bf16[1024,1024]{1,0:T(8,128)(2,1)}, u32[]{:S(2)}, u32[]{:S(2)}) collective-permute-start(bf16[1024,1024]{1,0:T(8,128)(2,1)} %get-tuple-element.503), channel_id=1, source_target_pairs={{0,1},{1,0},{2,3},{3,2},{4,5},{5,4},{6,7},{7,6},{8,9},{9,8},{10,11... | collective-permute-start | bytes 6291464 | tf_op jit(solution)/shard_map/ppermute | solution.py:55
  1830.7 346.1 %collective-permute-start.124 = (bf16[1024,1024]{1,0:T(8,128)(2,1)}, bf16[1024,1024]{1,0:T(8,128)(2,1)}, u32[]{:S(2)}, u32[]{:S(2)}) collective-permute-start(bf16[1024,1024]{1,0:T(8,128)(2,1)} %get-tuple-element.505), channel_id=1, source_target_pairs={{0,1},{1,0},{2,3},{3,2},{4,5},{5,4},{6,7},{7,6},{8,9},{9,8},{10,11... | collective-permute-start | bytes 6291464 | tf_op jit(solution)/shard_map/ppermute | solution.py:55
  1959.3 218.9 %collective-permute-start.132 = (bf16[1024,1024]{1,0:T(8,128)(2,1)}, bf16[1024,1024]{1,0:T(8,128)(2,1)}, u32[]{:S(2)}, u32[]{:S(2)}) collective-permute-start(bf16[1024,1024]{1,0:T(8,128)(2,1)} %get-tuple-element.507), channel_id=1, source_target_pairs={{0,1},{1,0},{2,3},{3,2},{4,5},{5,4},{6,7},{7,6},{8,9},{9,8},{10,11... | collective-permute-start | bytes 6291464 | tf_op jit(solution)/shard_map/ppermute | solution.py:55
  1972.1 198.0 %collective-permute-start.99 = (f32[2,128]{1,0:T(2,128)S(1)}, f32[2,128]{1,0:T(2,128)S(1)}, u32[]{:S(2)}, u32[]{:S(2)}) collective-permute-start(f32[2,128]{1,0:T(2,128)S(1)} %pad_maximum_fusion.19), channel_id=1, source_target_pairs={{0,1},{1,0},{2,3},{3,2},{4,5},{5,4},{6,7},{7,6},{8,9},{9,8},{10,11... | collective-permute-start | bytes 3080 | tf_op jit(solution)/shard_map/ppermute | solution.py:55
  2170.1 96.4 %collective-permute-start.100 = (bf16[1024,1536]{1,0:T(8,128)(2,1)}, bf16[1024,1536]{1,0:T(8,128)(2,1)S(1)}, u32[]{:S(2)}, u32[]{:S(2)}) collective-permute-start(bf16[1024,1536]{1,0:T(8,128)(2,1)} %get-tuple-element.499), channel_id=1, source_target_pairs={{0,1},{1,0},{2,3},{3,2},{4,5},{5,4},{6,7},{7,6},{8,9},{9,8},{10,11... | collective-permute-start | bytes 9437192 | tf_op jit(solution)/shard_map/ppermute | solution.py:55
  2174.8 24.6 %collective-permute-start.120 = (bf16[256,1024]{1,0:T(8,128)(2,1)S(1)}, bf16[256,1024]{1,0:T(8,128)(2,1)S(1)}, u32[]{:S(2)}, u32[]{:S(2)}) collective-permute-start(bf16[256,1024]{1,0:T(8,128)(2,1)S(1)} %add_convert_fusion.6), channel_id=1, source_target_pairs={{0,4},{1,5},{2,6},{3,7},{4,0},{5,1},{6,2},{7,3},{8,12},{9,13},{10,... | collective-permute-start | bytes 1572872 | tf_op jit(solution)/shard_map/ppermute | solution.py:55
  2178.1 32.5 %collective-permute-start.128 = (bf16[256,1024]{1,0:T(8,128)(2,1)S(1)}, bf16[256,1024]{1,0:T(8,128)(2,1)S(1)}, u32[]{:S(2)}, u32[]{:S(2)}) collective-permute-start(bf16[256,1024]{1,0:T(8,128)(2,1)S(1)} %add_convert_fusion.4), channel_id=1, source_target_pairs={{0,4},{1,5},{2,6},{3,7},{4,0},{5,1},{6,2},{7,3},{8,12},{9,13},{10,... | collective-permute-start | bytes 1572872 | tf_op jit(solution)/shard_map/ppermute | solution.py:55
  2179.5 41.5 %collective-permute-start.136 = (bf16[256,1024]{1,0:T(8,128)(2,1)S(1)}, bf16[256,1024]{1,0:T(8,128)(2,1)S(1)}, u32[]{:S(2)}, u32[]{:S(2)}) collective-permute-start(bf16[256,1024]{1,0:T(8,128)(2,1)S(1)} %add_convert_fusion.2), channel_id=1, source_target_pairs={{0,4},{1,5},{2,6},{3,7},{4,0},{5,1},{6,2},{7,3},{8,12},{9,13},{10,... | collective-permute-start | bytes 1572872 | tf_op jit(solution)/shard_map/ppermute | solution.py:55
  2189.8 61.4 %collective-permute-start.109 = (bf16[256,1024]{1,0:T(8,128)(2,1)S(1)}, bf16[256,1024]{1,0:T(8,128)(2,1)S(1)}, u32[]{:S(2)}, u32[]{:S(2)}) collective-permute-start(bf16[256,1024]{1,0:T(8,128)(2,1)S(1)} %get-tuple-element.726), channel_id=1, source_target_pairs={{0,2},{1,3},{2,0},{3,1},{4,6},{5,7},{6,4},{7,5},{8,10},{9,11},{10,... | collective-permute-start | bytes 1572872 | tf_op jit(solution)/shard_map/ppermute | solution.py:55
  2199.4 23.6 %collective-permute-start.113 = (bf16[128,1024]{1,0:T(8,128)(2,1)S(1)}, bf16[128,1024]{1,0:T(8,128)(2,1)S(1)}, u32[]{:S(2)}, u32[]{:S(2)}) collective-permute-start(bf16[128,1024]{1,0:T(8,128)(2,1)S(1)} %slice.767), channel_id=1, source_target_pairs={{0,2},{1,3},{2,0},{3,1},{4,6},{5,7},{6,4},{7,5},{8,10},{9,11},{10,... | collective-permute-start | bytes 786440 | tf_op jit(solution)/shard_map/ppermute | solution.py:55
  2210.6 42.2 %collective-permute-start.117 = (bf16[256,1024]{1,0:T(8,128)(2,1)S(1)}, bf16[256,1024]{1,0:T(8,128)(2,1)S(1)}, u32[]{:S(2)}, u32[]{:S(2)}) collective-permute-start(bf16[256,1024]{1,0:T(8,128)(2,1)S(1)} %get-tuple-element.724), channel_id=1, source_target_pairs={{0,2},{1,3},{2,0},{3,1},{4,6},{5,7},{6,4},{7,5},{8,10},{9,11},{10,... | collective-permute-start | bytes 1572872 | tf_op jit(solution)/shard_map/ppermute | solution.py:55
  2230.2 25.4 %collective-permute-start.125 = (bf16[256,1024]{1,0:T(8,128)(2,1)S(1)}, bf16[256,1024]{1,0:T(8,128)(2,1)S(1)}, u32[]{:S(2)}, u32[]{:S(2)}) collective-permute-start(bf16[256,1024]{1,0:T(8,128)(2,1)S(1)} %get-tuple-element.722), channel_id=1, source_target_pairs={{0,2},{1,3},{2,0},{3,1},{4,6},{5,7},{6,4},{7,5},{8,10},{9,11},{10,... | collective-permute-start | bytes 1572872 | tf_op jit(solution)/shard_map/ppermute | solution.py:55
  2251.2 32.6 %collective-permute-start.115 = (bf16[64,1024]{1,0:T(8,128)(2,1)S(1)}, bf16[64,1024]{1,0:T(8,128)(2,1)S(1)}, u32[]{:S(2)}, u32[]{:S(2)}) collective-permute-start(bf16[64,1024]{1,0:T(8,128)(2,1)S(1)} %get-tuple-element.755), channel_id=1, source_target_pairs={{0,24},{1,25},{2,26},{3,27},{4,28},{5,29},{6,30},{7,31},{8,16},{9,... | collective-permute-start | bytes 393224 | tf_op jit(solution)/shard_map/ppermute | solution.py:55
  2252.9 31.8 %collective-permute-start.114 = (bf16[64,1024]{1,0:T(8,128)(2,1)S(1)}, bf16[64,1024]{1,0:T(8,128)(2,1)S(1)}, u32[]{:S(2)}, u32[]{:S(2)}) collective-permute-start(bf16[64,1024]{1,0:T(8,128)(2,1)S(1)} %get-tuple-element.754), channel_id=1, source_target_pairs={{0,16},{1,17},{2,18},{3,19},{4,20},{5,21},{6,22},{7,23},{8,24},{9,... | collective-permute-start | bytes 393224 | tf_op jit(solution)/shard_map/ppermute | solution.py:55
  2266.5 17.0 collective-permute-start.134
  2272.2 24.4 %collective-permute-start.104 = (bf16[256,1536]{1,0:T(8,128)(2,1)S(1)}, bf16[256,1536]{1,0:T(8,128)(2,1)S(1)}, u32[]{:S(2)}, u32[]{:S(2)}) collective-permute-start(bf16[256,1536]{1,0:T(8,128)(2,1)S(1)} %add_convert_fusion), channel_id=1, source_target_pairs={{0,4},{1,5},{2,6},{3,7},{4,0},{5,1},{6,2},{7,3},{8,12},{9,13},{10,... | collective-permute-start | bytes 2359304 | tf_op jit(solution)/shard_map/ppermute | solution.py:55
  2277.8 21.3 collective-permute-start.123
  2283.8 15.4 collective-permute-start.122
  2284.7 21.3 collective-permute-start.131
  2290.1 17.8 collective-permute-start.130
  2299.2 25.9 %collective-permute-start.101 = (bf16[256,1536]{1,0:T(8,128)(2,1)S(1)}, bf16[256,1536]{1,0:T(8,128)(2,1)S(1)}, u32[]{:S(2)}, u32[]{:S(2)}) collective-permute-start(bf16[256,1536]{1,0:T(8,128)(2,1)S(1)} %get-tuple-element.716), channel_id=1, source_target_pairs={{0,2},{1,3},{2,0},{3,1},{4,6},{5,7},{6,4},{7,5},{8,10},{9,11},{10,... | collective-permute-start | bytes 2359304 | tf_op jit(solution)/shard_map/ppermute | solution.py:55
  2304.2 20.8 collective-permute-start.105
  2306.0 27.8 %collective-permute-start.139 = (bf16[64,1024]{1,0:T(8,128)(2,1)S(1)}, bf16[64,1024]{1,0:T(8,128)(2,1)S(1)}, u32[]{:S(2)}, u32[]{:S(2)}) collective-permute-start(bf16[64,1024]{1,0:T(8,128)(2,1)S(1)} %get-tuple-element.749), channel_id=1, source_target_pairs={{0,24},{1,25},{2,26},{3,27},{4,28},{5,29},{6,30},{7,31},{8,16},{9,... | collective-permute-start | bytes 393224 | tf_op jit(solution)/shard_map/ppermute | solution.py:55
  2307.9 27.3 %collective-permute-start.138 = (bf16[64,1024]{1,0:T(8,128)(2,1)S(1)}, bf16[64,1024]{1,0:T(8,128)(2,1)S(1)}, u32[]{:S(2)}, u32[]{:S(2)}) collective-permute-start(bf16[64,1024]{1,0:T(8,128)(2,1)S(1)} %get-tuple-element.748), channel_id=1, source_target_pairs={{0,16},{1,17},{2,18},{3,19},{4,20},{5,21},{6,22},{7,23},{8,24},{9,... | collective-permute-start | bytes 393224 | tf_op jit(solution)/shard_map/ppermute | solution.py:55
  2307.9 27.3 %collective-permute-start.135 = (bf16[64,1024]{1,0:T(8,128)(2,1)S(1)}, bf16[64,1024]{1,0:T(8,128)(2,1)S(1)}, u32[]{:S(2)}, u32[]{:S(2)}) collective-permute-start(bf16[64,1024]{1,0:T(8,128)(2,1)S(1)} %slice.771), channel_id=1, source_target_pairs={{0,8},{1,9},{2,10},{3,11},{4,12},{5,13},{6,14},{7,15},{8,0},{9,1},... | collective-permute-start | bytes 393224 | tf_op jit(solution)/shard_map/ppermute | solution.py:55
  (230 other events, 8549.6 us)

commit v2 on v1

--- a/solution.py
+++ b/solution.py
@@ -78,8 +78,9 @@
         kernel,
         out_shape=jax.ShapeDtypeStruct((total_rows,) + blocks[0].shape[1:], blocks[0].dtype),
         in_specs=[pl.BlockSpec(memory_space=pltpu.SMEM)] + [ANY] * count,
-        out_specs=ANY,
+        out_specs=pl.BlockSpec(memory_space=pltpu.VMEM),
         scratch_shapes=[pltpu.SemaphoreType.DMA((copies,))],
+        compiler_params=pltpu.CompilerParams(vmem_limit_bytes=20 << 20),
     )(me, *blocks)
 
 
@@ -103,9 +104,10 @@
     return pl.pallas_call(
         kernel,
         out_shape=[jax.ShapeDtypeStruct((len(own) * size,) + array.shape[1:], array.dtype) for own in orders],
-        in_specs=[pl.BlockSpec(memory_space=pltpu.SMEM), ANY],
+        in_specs=[pl.BlockSpec(memory_space=pltpu.SMEM), pl.BlockSpec(memory_space=pltpu.VMEM)],
         out_specs=[ANY] * len(orders),
         scratch_shapes=[pltpu.SemaphoreType.DMA((copies,))],
+        compiler_params=pltpu.CompilerParams(vmem_limit_bytes=20 << 20),
     )(me, array)
 
 

time: 2350 us -> 917 us (0.39)
  Pallas kernels: 1540 us -> 77.8 us
  local copies, waits for them, and re-layouts: 82.9 us -> 144 us
  waiting for transfers between devices: 230 us -> 206 us
    pallas_call x6, Pallas kernels: 770 us -> 32.5 us  [pick(): pl.pallas_call(kernel, out_shape=[jax.ShapeDtypeStruct((len(own) * size,)...]
    pallas_call x6, Pallas kernels: 770 us -> 45.4 us  [place(): pl.pallas_call(kernel, out_shape=jax.ShapeDtypeStruct((total_rows,) + blo...]
    unnamed x273 -> x323, local copies, waits for them, and re-layouts: 17.3 us -> 55.5 us
    ppermute x140, waiting for transfers between devices: 230 us -> 206 us  [swap(): lax.ppermute(values, ('dp', 'shard'), [(i, i ^ mask) for i in range(devic...]
  transfers between devices with their start and end apart: 140 -> 140, of which waited for: 48 -> 47; matrix products, arithmetic and copies ran while one was open for 5% -> 16% of each run, Pallas kernels for 52% -> 6%
where the time goes in v2:
time: 917 us; the launch traced here: 907 us
  starting transfers between devices  285 us (31%)
  waiting for transfers between devices  206 us (22%)
  local copies, waits for them, and re-layouts  144 us (16%)
  matrix products  107 us (12%)
  other arithmetic  77.8 us (8%)
  Pallas kernels  77.8 us (8%)
    ppermute x140, starting transfers between devices, swap(): lax.ppermute(values, ('dp', 'shard'), [(i, i ^ mask) for i in range(devic...  285 us
    ppermute x140, waiting for transfers between devices, swap(): lax.ppermute(values, ('dp', 'shard'), [(i, i ^ mask) for i in range(devic...  206 us
    unnamed x323, local copies, waits for them, and re-layouts  55.5 us
    pallas_call x6, Pallas kernels, place(): pl.pallas_call(kernel, out_shape=jax.ShapeDtypeStruct((total_rows,) + blo...  45.4 us
    pallas_call x6, Pallas kernels, pick(): pl.pallas_call(kernel, out_shape=[jax.ShapeDtypeStruct((len(own) * size,)...  32.5 us
  transfers between devices with their start and end apart: 140, of which 47 were waited for; matrix products, arithmetic and copies ran while one was open for 16% of the time, Pallas kernels for 6%

profile of v2, /device:TPU:0, one launch (start us, length us, event | category | flops | bytes accessed | tf_op | source)
XLA Modules:
  0.0 907.1 jit_solution(9268553675711977320)
XLA Ops:
  15.7 5.8 collective-permute-done.3
  38.5 7.5 collective-permute-start.5
  53.2 18.9 %collective-permute-done.44 = bf16[64,1024]{1,0:T(8,128)(2,1)S(1)} collective-permute-done((bf16[64,1024]{1,0:T(8,128)(2,1)S(1)}, bf16[64,1024]{1,0:T(8,128)(2,1)S(1)}, u32[]{:S(2)}, u32[]{:S(2)}) %collective-permute-start.44) | collective-permute-done | bytes 131104 | tf_op jit(solution)/shard_map/ppermute | solution.py:55
  82.5 4.9 collective-permute-done.34.refs_8_
  105.2 4.9 collective-permute-done.66.refs_6_
  127.6 5.6 collective-permute-done.10.refs_4_
  216.9 6.1 shard_map.214
  225.0 6.6 copy.117
  240.2 6.3 shard_map.217
  253.3 5.8 shard_map.215
  266.0 6.6 shard_map.212
  316.8 16.1 %shard_map.213 = bf16[2048,512]{1,0:T(8,128)(2,1)S(1)} custom-call(s32[1]{0:T(128)} %bitcast.26.me_ref, bf16[512,512]{1,0:T(8,128)(2,1)S(1)} %maximum_bitcast_fusion.1.refs_0_, bf16[512,512]{1,0:T(8,128)(2,1)S(1)} %collective-permute-done.22.refs_1_, bf16[512,512]{1,0:T(8,128)(2,1)S(1)} %collective-permute-done.23.refs_2_, ...), custom_call_target="tpu_custom_call" | custom-call | tf_op jit(solution)/shard_map/pallas_call | solution.py:77
  336.2 14.3 %while.34 = (s32[]{:T(128)}, f32[1,4,2048,64]{2,3,1,0:T(8,128)S(1)}, f32[1,4,2048]{2,1,0:T(4,128)S(1)}, s32[]{:T(128)}, s32[]{:T(128)}, /*index=5*/s32[1]{0:T(12...) while((s32[]{:T(128)}, ...), condition=%wide.region_8.0_spmd.clone, body=%wide.region_4.8_spmd.clone.sunk | while | flops 1101530624 | bytes 47881560 | solution.py:329
  336.8 11.9 %conditional.6 = ((f32[1,4,2048,64]{2,3,1,0:T(8,128)S(1)}, f32[1,4,2048]{2,1,0:T(4,128)S(1)})) conditional(s32[]{:T(128)} %convert_element_type.783, (f32[1,4,2048,64]{2,3,1,0:T(8,128)S(1)}, f32[1,4,2048]{2,1,0:T(4,128)S(1)}) %tuple.130, (s32[]{:T(128)}, s32[512]{0:T(512)S(1)}, s32[1]{0:T(128)}, bf16[1,2048,256]{1,2,0:T(8,128)(2,1)}, ...), branch_computations={%region_5.5_spmd, %region_6.0_spmd} | conditional | flops 1101530624 | bytes 47881320 | solution.py:327
  339.3 4.6 fusion.4
  343.9 4.7 fusion.14
  356.3 4.9 multiply_reduce_fusion
  388.8 45.0 %while.35 = (s32[]{:T(128)}, f32[1,4,2048,64]{2,3,1,0:T(8,128)S(1)}, f32[1,2048,256]{1,2,0:T(8,128)}, f32[1,2048,256]{1,2,0:T(8,128)}, s32[]{:T(128)}, /*index=5...) while((s32[]{:T(128)}, ...), condition=%wide.region_15.16_spmd.clone, body=%wide.region_12.0_spmd.clone.sunk | while | flops 2721449472 | bytes 137174512 | solution.py:435
  389.8 42.2 %conditional.7 = ((f32[1,4,2048,64]{2,3,1,0:T(8,128)S(1)}, f32[1,2048,256]{1,2,0:T(8,128)}, f32[1,2048,256]{1,2,0:T(8,128)})) conditional(s32[]{:T(128)} %convert_element_type.784, (f32[1,4,2048,64]{2,3,1,0:T(8,128)S(1)}, f32[1,2048,256]{1,2,0:T(8,128)}, f32[1,2048,256]{1,2,0:T(8,128)}) %tuple.133, (s32[]{:T(128)}, s32[512]{0:T(512)S(1)}, ...), branch_computations={%region_13.13_spmd, %region_14.14_spmd} | conditional | flops 2721449472 | bytes 137174208 | solution.py:433
  390.8 8.1 fusion.31
  401.4 8.6 fusion.21
  413.4 10.1 %fusion.23 = f32[4,512,64]{1,2,0:T(8,128)} fusion(f32[4,512,2048]{2,1,0:T(8,128)} %fusion.31, pred[2048,512]{0,1:T(8,128)(4,1)} %copy-done.101, bf16[1,4,2048,64]{2,3,1,0:T(8,128)(2,1)} %get-tuple-element.442), kind=kOutput, calls=%fused_computation.28 | convolution fusion | flops 549453824 | bytes 19398656 | tf_op jit(solution)/shard_map/while/body/eval_jaxpr/cond/branch_1_fun/rgqk,rgqh->rkgh/dot_general | solution.py:411
  423.5 6.1 convolution_multiply_fusion.1
  440.7 54.6 %collective-permute-start.93 = (bf16[1024,512]{1,0:T(8,128)(2,1)S(1)}, bf16[1024,512]{1,0:T(8,128)(2,1)}, u32[]{:S(2)}, u32[]{:S(2)}) collective-permute-start(bf16[1024,512]{1,0:T(8,128)(2,1)S(1)} %get-tuple-element.497), channel_id=1, source_target_pairs={{0,1},{1,0},{2,3},{3,2},{4,5},{5,4},{6,7},{7,6},{8,9},{9,8},{10,11... | collective-permute-start | bytes 3145736 | tf_op jit(solution)/shard_map/ppermute | solution.py:55
  511.1 6.5 convolution_convert_fusion.1.in_ref
  517.7 5.7 fusion.65
  531.5 109.3 %collective-permute-start.94 = (bf16[512,512]{1,0:T(8,128)(2,1)S(1)}, bf16[512,512]{1,0:T(8,128)(2,1)S(1)}, u32[]{:S(2)}, u32[]{:S(2)}) collective-permute-start(bf16[512,512]{1,0:T(8,128)(2,1)S(1)} %slice.758), channel_id=1, source_target_pairs={{0,2},{1,3},{2,0},{3,1},{4,6},{5,7},{6,4},{7,5},{8,10},{9,11},{10,... | collective-permute-start | bytes 1572872 | tf_op jit(solution)/shard_map/ppermute | solution.py:55
  645.1 7.8 collective-permute-done.94
  660.0 9.3 %fusion.40 = (f32[2048]{0:T(1024)S(1)}, f32[512]{0:T(512)S(1)}, f32[512,2048]{1,0:T(8,128)}) fusion(bf16[1,512,2048]{2,1,0:T(8,128)(2,1)S(1)} %copy-done.116, f32[512]{0:T(512)S(1)} %copy-done.148, f32[2048]{0:T(1024)S(1)} %copy-done.139, bf16[2048,1536]{1,0:T(8,128)(2,1)} %copy-done.3, bf16[512,256]{1,0:T(8,128)(2,1)} %fusion.84, ...), kind=kOutput, calls=%fused_computation.60 | convolution fusion | flops 3233281536 | bytes 14176256 | tf_op jit(solution)/shard_map/rte,de->rtd/dot_general | solution.py:462
  670.3 5.6 collective-permute-start.95
  682.8 5.9 shard_map.220
  688.8 5.9 shard_map.221
  695.2 5.9 shard_map.222
  701.2 5.9 shard_map.223
  713.6 5.3 fusion.44
  719.1 5.1 convolution_convert_fusion.in_ref
  724.3 8.8 shard_map.219
  744.0 6.8 collective-permute-done.112
  752.6 9.4 %collective-permute-done.120 = bf16[256,1024]{1,0:T(8,128)(2,1)S(1)} collective-permute-done((bf16[256,1024]{1,0:T(8,128)(2,1)S(1)}, bf16[256,1024]{1,0:T(8,128)(2,1)S(1)}, u32[]{:S(2)}, u32[]{:S(2)}) %collective-permute-start.120) | collective-permute-done | bytes 524320 | tf_op jit(solution)/shard_map/ppermute | solution.py:55
  763.8 9.5 %collective-permute-done.128 = bf16[256,1024]{1,0:T(8,128)(2,1)S(1)} collective-permute-done((bf16[256,1024]{1,0:T(8,128)(2,1)S(1)}, bf16[256,1024]{1,0:T(8,128)(2,1)S(1)}, u32[]{:S(2)}, u32[]{:S(2)}) %collective-permute-start.128) | collective-permute-done | bytes 524320 | tf_op jit(solution)/shard_map/ppermute | solution.py:55
  775.1 8.6 collective-permute-done.136
  787.5 5.4 collective-permute-done.121
  793.0 5.5 collective-permute-done.129
  798.7 14.9 %collective-permute-done.137 = bf16[128,1024]{1,0:T(8,128)(2,1)S(1)} collective-permute-done((bf16[128,1024]{1,0:T(8,128)(2,1)S(1)}, bf16[128,1024]{1,0:T(8,128)(2,1)S(1)}, u32[]{:S(2)}, u32[]{:S(2)}) %collective-permute-start.137) | collective-permute-done | bytes 262176 | tf_op jit(solution)/shard_map/ppermute | solution.py:55
  854.0 6.4 collective-permute-done.104
  874.6 13.7 %collective-permute-done.105 = bf16[128,1536]{1,0:T(8,128)(2,1)S(1)} collective-permute-done((bf16[128,1536]{1,0:T(8,128)(2,1)S(1)}, bf16[128,1536]{1,0:T(8,128)(2,1)S(1)}, u32[]{:S(2)}, u32[]{:S(2)}) %collective-permute-start.105) | collective-permute-done | bytes 393248 | tf_op jit(solution)/shard_map/ppermute | solution.py:55
  890.9 5.7 collective-permute-done.102
  899.6 6.4 collective-permute-done.106
  (823 shorter events, 421.7 us)
Async XLA Ops:
  6.5 22.1 %collective-permute-start.25 = (bf16[64,1024]{1,0:T(8,128)(2,1)S(1)}, bf16[64,1024]{1,0:T(8,128)(2,1)S(1)}, u32[]{:S(2)}, u32[]{:S(2)}) collective-permute-start(bf16[64,1024]{1,0:T(8,128)(2,1)S(1)} %convert_bitcast_fusion.1), channel_id=1, source_target_pairs={{0,8},{1,9},{2,10},{3,11},{4,12},{5,13},{6,14},{7,15},{8,0},{9,1},... | collective-permute-start | bytes 393224 | tf_op jit(solution)/shard_map/ppermute | solution.py:55
  8.2 22.4 %collective-permute-start.27 = (bf16[64,1024]{1,0:T(8,128)(2,1)S(1)}, bf16[64,1024]{1,0:T(8,128)(2,1)S(1)}, u32[]{:S(2)}, u32[]{:S(2)}) collective-permute-start(bf16[64,1024]{1,0:T(8,128)(2,1)S(1)} %convert_bitcast_fusion.1), channel_id=1, source_target_pairs={{0,16},{1,17},{2,18},{3,19},{4,20},{5,21},{6,22},{7,23},{8,24},{9,... | collective-permute-start | bytes 393224 | tf_op jit(solution)/shard_map/ppermute | solution.py:55
  10.8 20.4 %collective-permute-start.28 = (bf16[64,1024]{1,0:T(8,128)(2,1)S(1)}, bf16[64,1024]{1,0:T(8,128)(2,1)S(1)}, u32[]{:S(2)}, u32[]{:S(2)}) collective-permute-start(bf16[64,1024]{1,0:T(8,128)(2,1)S(1)} %convert_bitcast_fusion.1), channel_id=1, source_target_pairs={{0,24},{1,25},{2,26},{3,27},{4,28},{5,29},{6,30},{7,31},{8,16},{9,... | collective-permute-start | bytes 393224 | tf_op jit(solution)/shard_map/ppermute | solution.py:55
  13.5 19.6 %collective-permute-start.76 = (bf16[64,1024]{1,0:T(8,128)(2,1)S(1)}, bf16[64,1024]{1,0:T(8,128)(2,1)S(1)}, u32[]{:S(2)}, u32[]{:S(2)}) collective-permute-start(bf16[64,1024]{1,0:T(8,128)(2,1)S(1)} %convert_bitcast_fusion), channel_id=1, source_target_pairs={{0,8},{1,9},{2,10},{3,11},{4,12},{5,13},{6,14},{7,15},{8,0},{9,1},... | collective-permute-start | bytes 393224 | tf_op jit(solution)/shard_map/ppermute | solution.py:55
  30.5 15.5 %collective-permute-start.59 = (bf16[64,1024]{1,0:T(8,128)(2,1)S(1)}, bf16[64,1024]{1,0:T(8,128)(2,1)S(1)}, u32[]{:S(2)}, u32[]{:S(2)}) collective-permute-start(bf16[64,1024]{1,0:T(8,128)(2,1)S(1)} %convert_element_type.497), channel_id=1, source_target_pairs={{0,8},{1,9},{2,10},{3,11},{4,12},{5,13},{6,14},{7,15},{8,0},{9,1},... | collective-permute-start | bytes 393224 | tf_op jit(solution)/shard_map/ppermute | solution.py:55
  31.2 17.1 %collective-permute-start.61 = (bf16[64,1024]{1,0:T(8,128)(2,1)S(1)}, bf16[64,1024]{1,0:T(8,128)(2,1)S(1)}, u32[]{:S(2)}, u32[]{:S(2)}) collective-permute-start(bf16[64,1024]{1,0:T(8,128)(2,1)S(1)} %convert_element_type.497), channel_id=1, source_target_pairs={{0,16},{1,17},{2,18},{3,19},{4,20},{5,21},{6,22},{7,23},{8,24},{9,... | collective-permute-start | bytes 393224 | tf_op jit(solution)/shard_map/ppermute | solution.py:55
  33.1 15.8 %collective-permute-start.62 = (bf16[64,1024]{1,0:T(8,128)(2,1)S(1)}, bf16[64,1024]{1,0:T(8,128)(2,1)S(1)}, u32[]{:S(2)}, u32[]{:S(2)}) collective-permute-start(bf16[64,1024]{1,0:T(8,128)(2,1)S(1)} %convert_element_type.497), channel_id=1, source_target_pairs={{0,24},{1,25},{2,26},{3,27},{4,28},{5,29},{6,30},{7,31},{8,16},{9,... | collective-permute-start | bytes 393224 | tf_op jit(solution)/shard_map/ppermute | solution.py:55
  37.5 15.5 %collective-permute-start.42 = (bf16[64,1024]{1,0:T(8,128)(2,1)S(1)}, bf16[64,1024]{1,0:T(8,128)(2,1)S(1)}, u32[]{:S(2)}, u32[]{:S(2)}) collective-permute-start(bf16[64,1024]{1,0:T(8,128)(2,1)S(1)} %convert_element_type.496), channel_id=1, source_target_pairs={{0,8},{1,9},{2,10},{3,11},{4,12},{5,13},{6,14},{7,15},{8,0},{9,1},... | collective-permute-start | bytes 393224 | tf_op jit(solution)/shard_map/ppermute | solution.py:55
  38.5 34.5 %collective-permute-start.5 = (bf16[64,1536]{1,0:T(8,128)(2,1)S(1)}, bf16[64,1536]{1,0:T(8,128)(2,1)S(1)}, u32[]{:S(2)}, u32[]{:S(2)}) collective-permute-start(bf16[64,1536]{1,0:T(8,128)(2,1)S(1)} %convert_element_type.484), channel_id=1, source_target_pairs={{0,8},{1,9},{2,10},{3,11},{4,12},{5,13},{6,14},{7,15},{8,0},{9,1},... | collective-permute-start | bytes 589832 | tf_op jit(solution)/shard_map/ppermute | solution.py:55
  46.0 27.3 %collective-permute-start.7 = (bf16[64,1536]{1,0:T(8,128)(2,1)S(1)}, bf16[64,1536]{1,0:T(8,128)(2,1)S(1)}, u32[]{:S(2)}, u32[]{:S(2)}) collective-permute-start(bf16[64,1536]{1,0:T(8,128)(2,1)S(1)} %convert_element_type.484), channel_id=1, source_target_pairs={{0,16},{1,17},{2,18},{3,19},{4,20},{5,21},{6,22},{7,23},{8,24},{9,... | collective-permute-start | bytes 589832 | tf_op jit(solution)/shard_map/ppermute | solution.py:55
  48.2 23.9 %collective-permute-start.44 = (bf16[64,1024]{1,0:T(8,128)(2,1)S(1)}, bf16[64,1024]{1,0:T(8,128)(2,1)S(1)}, u32[]{:S(2)}, u32[]{:S(2)}) collective-permute-start(bf16[64,1024]{1,0:T(8,128)(2,1)S(1)} %convert_element_type.496), channel_id=1, source_target_pairs={{0,16},{1,17},{2,18},{3,19},{4,20},{5,21},{6,22},{7,23},{8,24},{9,... | collective-permute-start | bytes 393224 | tf_op jit(solution)/shard_map/ppermute | solution.py:55
  48.9 23.2 %collective-permute-start.45 = (bf16[64,1024]{1,0:T(8,128)(2,1)S(1)}, bf16[64,1024]{1,0:T(8,128)(2,1)S(1)}, u32[]{:S(2)}, u32[]{:S(2)}) collective-permute-start(bf16[64,1024]{1,0:T(8,128)(2,1)S(1)} %convert_element_type.496), channel_id=1, source_target_pairs={{0,24},{1,25},{2,26},{3,27},{4,28},{5,29},{6,30},{7,31},{8,16},{9,... | collective-permute-start | bytes 393224 | tf_op jit(solution)/shard_map/ppermute | solution.py:55
  53.1 20.2 %collective-permute-start.8 = (bf16[64,1536]{1,0:T(8,128)(2,1)S(1)}, bf16[64,1536]{1,0:T(8,128)(2,1)S(1)}, u32[]{:S(2)}, u32[]{:S(2)}) collective-permute-start(bf16[64,1536]{1,0:T(8,128)(2,1)S(1)} %convert_element_type.484), channel_id=1, source_target_pairs={{0,24},{1,25},{2,26},{3,27},{4,28},{5,29},{6,30},{7,31},{8,16},{9,... | collective-permute-start | bytes 589832 | tf_op jit(solution)/shard_map/ppermute | solution.py:55
  176.2 84.8 %collective-permute-start.14 = (bf16[128,1536]{1,0:T(8,128)(2,1)S(1)}, bf16[128,1536]{1,0:T(8,128)(2,1)}, u32[]{:S(2)}, u32[]{:S(2)}) collective-permute-start(bf16[128,1536]{1,0:T(8,128)(2,1)S(1)} %pad_maximum_fusion.6.refs_0_), channel_id=1, source_target_pairs={{0,2},{1,3},{2,0},{3,1},{4,6},{5,7},{6,4},{7,5},{8,10},{9,11},{10,... | collective-permute-start | bytes 1179656 | tf_op jit(solution)/shard_map/ppermute | solution.py:55
  177.2 83.9 %collective-permute-start.16 = (bf16[128,1536]{1,0:T(8,128)(2,1)S(1)}, bf16[128,1536]{1,0:T(8,128)(2,1)}, u32[]{:S(2)}, u32[]{:S(2)}) collective-permute-start(bf16[128,1536]{1,0:T(8,128)(2,1)S(1)} %constant_dynamic-update-slice_fusion.refs_2_), channel_id=1, source_target_pairs={{0,4},{1,5},{2,6},{3,7},{4,0},{5,1},{6,2},{7,3},{8,12},{9,13},{10,... | collective-permute-start | bytes 1179656 | tf_op jit(solution)/shard_map/ppermute | solution.py:55
  178.3 83.3 %collective-permute-start.11 = (bf16[128,1536]{1,0:T(8,128)(2,1)}, bf16[128,1536]{1,0:T(8,128)(2,1)}, u32[]{:S(2)}, u32[]{:S(2)}) collective-permute-start(bf16[128,1536]{1,0:T(8,128)(2,1)} %copy-done.12), channel_id=1, source_target_pairs={{0,1},{1,0},{2,3},{3,2},{4,5},{5,4},{6,7},{7,6},{8,9},{9,8},{10,11... | collective-permute-start | bytes 1179656 | tf_op jit(solution)/shard_map/ppermute | solution.py:55
  178.3 83.4 %collective-permute-start.18 = (bf16[128,1536]{1,0:T(8,128)(2,1)}, bf16[128,1536]{1,0:T(8,128)(2,1)}, u32[]{:S(2)}, u32[]{:S(2)}) collective-permute-start(bf16[128,1536]{1,0:T(8,128)(2,1)} %copy-done.12), channel_id=1, source_target_pairs={{0,2},{1,3},{2,0},{3,1},{4,6},{5,7},{6,4},{7,5},{8,10},{9,11},{10,... | collective-permute-start | bytes 1179656 | tf_op jit(solution)/shard_map/ppermute | solution.py:55
  178.9 83.2 %collective-permute-start.20 = (bf16[128,1536]{1,0:T(8,128)(2,1)}, bf16[128,1536]{1,0:T(8,128)(2,1)}, u32[]{:S(2)}, u32[]{:S(2)}) collective-permute-start(bf16[128,1536]{1,0:T(8,128)(2,1)} %copy-done.14), channel_id=1, source_target_pairs={{0,4},{1,5},{2,6},{3,7},{4,0},{5,1},{6,2},{7,3},{8,12},{9,13},{10,... | collective-permute-start | bytes 1179656 | tf_op jit(solution)/shard_map/ppermute | solution.py:55
  289.4 27.4 %collective-permute-start.22 = (bf16[512,512]{1,0:T(8,128)(2,1)S(1)}, bf16[512,512]{1,0:T(8,128)(2,1)S(1)}, u32[]{:S(2)}, u32[]{:S(2)}) collective-permute-start(bf16[512,512]{1,0:T(8,128)(2,1)S(1)} %maximum_bitcast_fusion.1.refs_0_), channel_id=1, source_target_pairs={{0,1},{1,0},{2,3},{3,2},{4,5},{5,4},{6,7},{7,6},{8,9},{9,8},{10,11... | collective-permute-start | bytes 1572872 | tf_op jit(solution)/shard_map/ppermute | solution.py:55
  440.7 89.0 %collective-permute-start.93 = (bf16[1024,512]{1,0:T(8,128)(2,1)S(1)}, bf16[1024,512]{1,0:T(8,128)(2,1)}, u32[]{:S(2)}, u32[]{:S(2)}) collective-permute-start(bf16[1024,512]{1,0:T(8,128)(2,1)S(1)} %get-tuple-element.497), channel_id=1, source_target_pairs={{0,1},{1,0},{2,3},{3,2},{4,5},{5,4},{6,7},{7,6},{8,9},{9,8},{10,11... | collective-permute-start | bytes 3145736 | tf_op jit(solution)/shard_map/ppermute | solution.py:55
  531.5 121.5 %collective-permute-start.94 = (bf16[512,512]{1,0:T(8,128)(2,1)S(1)}, bf16[512,512]{1,0:T(8,128)(2,1)S(1)}, u32[]{:S(2)}, u32[]{:S(2)}) collective-permute-start(bf16[512,512]{1,0:T(8,128)(2,1)S(1)} %slice.758), channel_id=1, source_target_pairs={{0,2},{1,3},{2,0},{3,1},{4,6},{5,7},{6,4},{7,5},{8,10},{9,11},{10,... | collective-permute-start | bytes 1572872 | tf_op jit(solution)/shard_map/ppermute | solution.py:55
  680.3 27.3 %collective-permute-start.96 = (f32[9,128]{1,0:T(8,128)S(1)}, f32[9,128]{1,0:T(8,128)S(1)}, u32[]{:S(2)}, u32[]{:S(2)}) collective-permute-start(f32[9,128]{1,0:T(8,128)S(1)} %pad_maximum_fusion.14), channel_id=1, source_target_pairs={{0,8},{1,9},{2,10},{3,11},{4,12},{5,13},{6,14},{7,15},{8,0},{9,1},... | collective-permute-start | bytes 13832 | tf_op jit(solution)/shard_map/ppermute | solution.py:55
  688.7 46.1 %collective-permute-start.108 = (bf16[1024,1024]{1,0:T(8,128)(2,1)S(1)}, bf16[1024,1024]{1,0:T(8,128)(2,1)}, u32[]{:S(2)}, u32[]{:S(2)}) collective-permute-start(bf16[1024,1024]{1,0:T(8,128)(2,1)S(1)} %get-tuple-element.501), channel_id=1, source_target_pairs={{0,1},{1,0},{2,3},{3,2},{4,5},{5,4},{6,7},{7,6},{8,9},{9,8},{10,11... | collective-permute-start | bytes 6291464 | tf_op jit(solution)/shard_map/ppermute | solution.py:55
  694.7 41.4 %collective-permute-start.116 = (bf16[1024,1024]{1,0:T(8,128)(2,1)S(1)}, bf16[1024,1024]{1,0:T(8,128)(2,1)}, u32[]{:S(2)}, u32[]{:S(2)}) collective-permute-start(bf16[1024,1024]{1,0:T(8,128)(2,1)S(1)} %get-tuple-element.503), channel_id=1, source_target_pairs={{0,1},{1,0},{2,3},{3,2},{4,5},{5,4},{6,7},{7,6},{8,9},{9,8},{10,11... | collective-permute-start | bytes 6291464 | tf_op jit(solution)/shard_map/ppermute | solution.py:55
  701.1 38.3 %collective-permute-start.124 = (bf16[1024,1024]{1,0:T(8,128)(2,1)S(1)}, bf16[1024,1024]{1,0:T(8,128)(2,1)}, u32[]{:S(2)}, u32[]{:S(2)}) collective-permute-start(bf16[1024,1024]{1,0:T(8,128)(2,1)S(1)} %get-tuple-element.505), channel_id=1, source_target_pairs={{0,1},{1,0},{2,3},{3,2},{4,5},{5,4},{6,7},{7,6},{8,9},{9,8},{10,11... | collective-permute-start | bytes 6291464 | tf_op jit(solution)/shard_map/ppermute | solution.py:55
  707.1 33.6 %collective-permute-start.132 = (bf16[1024,1024]{1,0:T(8,128)(2,1)S(1)}, bf16[1024,1024]{1,0:T(8,128)(2,1)}, u32[]{:S(2)}, u32[]{:S(2)}) collective-permute-start(bf16[1024,1024]{1,0:T(8,128)(2,1)S(1)} %get-tuple-element.507), channel_id=1, source_target_pairs={{0,1},{1,0},{2,3},{3,2},{4,5},{5,4},{6,7},{7,6},{8,9},{9,8},{10,11... | collective-permute-start | bytes 6291464 | tf_op jit(solution)/shard_map/ppermute | solution.py:55
  733.1 96.1 %collective-permute-start.100 = (bf16[1024,1536]{1,0:T(8,128)(2,1)S(1)}, bf16[1024,1536]{1,0:T(8,128)(2,1)S(1)}, u32[]{:S(2)}, u32[]{:S(2)}) collective-permute-start(bf16[1024,1536]{1,0:T(8,128)(2,1)S(1)} %get-tuple-element.499), channel_id=1, source_target_pairs={{0,1},{1,0},{2,3},{3,2},{4,5},{5,4},{6,7},{7,6},{8,9},{9,8},{10,11... | collective-permute-start | bytes 9437192 | tf_op jit(solution)/shard_map/ppermute | solution.py:55
  736.0 14.8 %collective-permute-start.112 = (bf16[256,1024]{1,0:T(8,128)(2,1)S(1)}, bf16[256,1024]{1,0:T(8,128)(2,1)S(1)}, u32[]{:S(2)}, u32[]{:S(2)}) collective-permute-start(bf16[256,1024]{1,0:T(8,128)(2,1)S(1)} %add_convert_fusion.8), channel_id=1, source_target_pairs={{0,4},{1,5},{2,6},{3,7},{4,0},{5,1},{6,2},{7,3},{8,12},{9,13},{10,... | collective-permute-start | bytes 1572872 | tf_op jit(solution)/shard_map/ppermute | solution.py:55
  737.3 24.8 %collective-permute-start.120 = (bf16[256,1024]{1,0:T(8,128)(2,1)S(1)}, bf16[256,1024]{1,0:T(8,128)(2,1)S(1)}, u32[]{:S(2)}, u32[]{:S(2)}) collective-permute-start(bf16[256,1024]{1,0:T(8,128)(2,1)S(1)} %add_convert_fusion.6), channel_id=1, source_target_pairs={{0,4},{1,5},{2,6},{3,7},{4,0},{5,1},{6,2},{7,3},{8,12},{9,13},{10,... | collective-permute-start | bytes 1572872 | tf_op jit(solution)/shard_map/ppermute | solution.py:55
  740.6 32.7 %collective-permute-start.128 = (bf16[256,1024]{1,0:T(8,128)(2,1)S(1)}, bf16[256,1024]{1,0:T(8,128)(2,1)S(1)}, u32[]{:S(2)}, u32[]{:S(2)}) collective-permute-start(bf16[256,1024]{1,0:T(8,128)(2,1)S(1)} %add_convert_fusion.4), channel_id=1, source_target_pairs={{0,4},{1,5},{2,6},{3,7},{4,0},{5,1},{6,2},{7,3},{8,12},{9,13},{10,... | collective-permute-start | bytes 1572872 | tf_op jit(solution)/shard_map/ppermute | solution.py:55
  742.0 41.7 %collective-permute-start.136 = (bf16[256,1024]{1,0:T(8,128)(2,1)S(1)}, bf16[256,1024]{1,0:T(8,128)(2,1)S(1)}, u32[]{:S(2)}, u32[]{:S(2)}) collective-permute-start(bf16[256,1024]{1,0:T(8,128)(2,1)S(1)} %add_convert_fusion.2), channel_id=1, source_target_pairs={{0,4},{1,5},{2,6},{3,7},{4,0},{5,1},{6,2},{7,3},{8,12},{9,13},{10,... | collective-permute-start | bytes 1572872 | tf_op jit(solution)/shard_map/ppermute | solution.py:55
  752.5 61.4 %collective-permute-start.109 = (bf16[256,1024]{1,0:T(8,128)(2,1)S(1)}, bf16[256,1024]{1,0:T(8,128)(2,1)S(1)}, u32[]{:S(2)}, u32[]{:S(2)}) collective-permute-start(bf16[256,1024]{1,0:T(8,128)(2,1)S(1)} %get-tuple-element.726), channel_id=1, source_target_pairs={{0,2},{1,3},{2,0},{3,1},{4,6},{5,7},{6,4},{7,5},{8,10},{9,11},{10,... | collective-permute-start | bytes 1572872 | tf_op jit(solution)/shard_map/ppermute | solution.py:55
  762.1 23.3 %collective-permute-start.113 = (bf16[128,1024]{1,0:T(8,128)(2,1)S(1)}, bf16[128,1024]{1,0:T(8,128)(2,1)S(1)}, u32[]{:S(2)}, u32[]{:S(2)}) collective-permute-start(bf16[128,1024]{1,0:T(8,128)(2,1)S(1)} %slice.767), channel_id=1, source_target_pairs={{0,2},{1,3},{2,0},{3,1},{4,6},{5,7},{6,4},{7,5},{8,10},{9,11},{10,... | collective-permute-start | bytes 786440 | tf_op jit(solution)/shard_map/ppermute | solution.py:55
  773.3 43.8 %collective-permute-start.117 = (bf16[256,1024]{1,0:T(8,128)(2,1)S(1)}, bf16[256,1024]{1,0:T(8,128)(2,1)S(1)}, u32[]{:S(2)}, u32[]{:S(2)}) collective-permute-start(bf16[256,1024]{1,0:T(8,128)(2,1)S(1)} %get-tuple-element.724), channel_id=1, source_target_pairs={{0,2},{1,3},{2,0},{3,1},{4,6},{5,7},{6,4},{7,5},{8,10},{9,11},{10,... | collective-permute-start | bytes 1572872 | tf_op jit(solution)/shard_map/ppermute | solution.py:55
  792.9 27.3 %collective-permute-start.125 = (bf16[256,1024]{1,0:T(8,128)(2,1)S(1)}, bf16[256,1024]{1,0:T(8,128)(2,1)S(1)}, u32[]{:S(2)}, u32[]{:S(2)}) collective-permute-start(bf16[256,1024]{1,0:T(8,128)(2,1)S(1)} %get-tuple-element.722), channel_id=1, source_target_pairs={{0,2},{1,3},{2,0},{3,1},{4,6},{5,7},{6,4},{7,5},{8,10},{9,11},{10,... | collective-permute-start | bytes 1572872 | tf_op jit(solution)/shard_map/ppermute | solution.py:55
  798.5 15.0 %collective-permute-start.137 = (bf16[128,1024]{1,0:T(8,128)(2,1)S(1)}, bf16[128,1024]{1,0:T(8,128)(2,1)S(1)}, u32[]{:S(2)}, u32[]{:S(2)}) collective-permute-start(bf16[128,1024]{1,0:T(8,128)(2,1)S(1)} %slice.761), channel_id=1, source_target_pairs={{0,2},{1,3},{2,0},{3,1},{4,6},{5,7},{6,4},{7,5},{8,10},{9,11},{10,... | collective-permute-start | bytes 786440 | tf_op jit(solution)/shard_map/ppermute | solution.py:55
  813.9 34.3 %collective-permute-start.115 = (bf16[64,1024]{1,0:T(8,128)(2,1)S(1)}, bf16[64,1024]{1,0:T(8,128)(2,1)S(1)}, u32[]{:S(2)}, u32[]{:S(2)}) collective-permute-start(bf16[64,1024]{1,0:T(8,128)(2,1)S(1)} %get-tuple-element.755), channel_id=1, source_target_pairs={{0,24},{1,25},{2,26},{3,27},{4,28},{5,29},{6,30},{7,31},{8,16},{9,... | collective-permute-start | bytes 393224 | tf_op jit(solution)/shard_map/ppermute | solution.py:55
  817.1 31.5 %collective-permute-start.114 = (bf16[64,1024]{1,0:T(8,128)(2,1)S(1)}, bf16[64,1024]{1,0:T(8,128)(2,1)S(1)}, u32[]{:S(2)}, u32[]{:S(2)}) collective-permute-start(bf16[64,1024]{1,0:T(8,128)(2,1)S(1)} %get-tuple-element.754), channel_id=1, source_target_pairs={{0,16},{1,17},{2,18},{3,19},{4,20},{5,21},{6,22},{7,23},{8,24},{9,... | collective-permute-start | bytes 393224 | tf_op jit(solution)/shard_map/ppermute | solution.py:55
  829.2 17.0 %collective-permute-start.134 = (bf16[128,1024]{1,0:T(8,128)(2,1)S(1)}, bf16[128,1024]{1,0:T(8,128)(2,1)S(1)}, u32[]{:S(2)}, u32[]{:S(2)}) collective-permute-start(bf16[128,1024]{1,0:T(8,128)(2,1)S(1)} %slice.762), channel_id=1, source_target_pairs={{0,4},{1,5},{2,6},{3,7},{4,0},{5,1},{6,2},{7,3},{8,12},{9,13},{10,... | collective-permute-start | bytes 786440 | tf_op jit(solution)/shard_map/ppermute | solution.py:55
  834.9 25.5 %collective-permute-start.104 = (bf16[256,1536]{1,0:T(8,128)(2,1)S(1)}, bf16[256,1536]{1,0:T(8,128)(2,1)S(1)}, u32[]{:S(2)}, u32[]{:S(2)}) collective-permute-start(bf16[256,1536]{1,0:T(8,128)(2,1)S(1)} %add_convert_fusion), channel_id=1, source_target_pairs={{0,4},{1,5},{2,6},{3,7},{4,0},{5,1},{6,2},{7,3},{8,12},{9,13},{10,... | collective-permute-start | bytes 2359304 | tf_op jit(solution)/shard_map/ppermute | solution.py:55
  840.5 21.3 %collective-permute-start.123 = (bf16[64,1024]{1,0:T(8,128)(2,1)S(1)}, bf16[64,1024]{1,0:T(8,128)(2,1)S(1)}, u32[]{:S(2)}, u32[]{:S(2)}) collective-permute-start(bf16[64,1024]{1,0:T(8,128)(2,1)S(1)} %get-tuple-element.753), channel_id=1, source_target_pairs={{0,24},{1,25},{2,26},{3,27},{4,28},{5,29},{6,30},{7,31},{8,16},{9,... | collective-permute-start | bytes 393224 | tf_op jit(solution)/shard_map/ppermute | solution.py:55
  848.6 20.8 %collective-permute-start.131 = (bf16[64,1024]{1,0:T(8,128)(2,1)S(1)}, bf16[64,1024]{1,0:T(8,128)(2,1)S(1)}, u32[]{:S(2)}, u32[]{:S(2)}) collective-permute-start(bf16[64,1024]{1,0:T(8,128)(2,1)S(1)} %get-tuple-element.751), channel_id=1, source_target_pairs={{0,24},{1,25},{2,26},{3,27},{4,28},{5,29},{6,30},{7,31},{8,16},{9,... | collective-permute-start | bytes 393224 | tf_op jit(solution)/shard_map/ppermute | solution.py:55
  852.1 19.2 %collective-permute-start.130 = (bf16[64,1024]{1,0:T(8,128)(2,1)S(1)}, bf16[64,1024]{1,0:T(8,128)(2,1)S(1)}, u32[]{:S(2)}, u32[]{:S(2)}) collective-permute-start(bf16[64,1024]{1,0:T(8,128)(2,1)S(1)} %get-tuple-element.750), channel_id=1, source_target_pairs={{0,16},{1,17},{2,18},{3,19},{4,20},{5,21},{6,22},{7,23},{8,24},{9,... | collective-permute-start | bytes 393224 | tf_op jit(solution)/shard_map/ppermute | solution.py:55
  863.0 25.4 %collective-permute-start.101 = (bf16[256,1536]{1,0:T(8,128)(2,1)S(1)}, bf16[256,1536]{1,0:T(8,128)(2,1)S(1)}, u32[]{:S(2)}, u32[]{:S(2)}) collective-permute-start(bf16[256,1536]{1,0:T(8,128)(2,1)S(1)} %get-tuple-element.716), channel_id=1, source_target_pairs={{0,2},{1,3},{2,0},{3,1},{4,6},{5,7},{6,4},{7,5},{8,10},{9,11},{10,... | collective-permute-start | bytes 2359304 | tf_op jit(solution)/shard_map/ppermute | solution.py:55
  867.1 21.2 %collective-permute-start.105 = (bf16[128,1536]{1,0:T(8,128)(2,1)S(1)}, bf16[128,1536]{1,0:T(8,128)(2,1)S(1)}, u32[]{:S(2)}, u32[]{:S(2)}) collective-permute-start(bf16[128,1536]{1,0:T(8,128)(2,1)S(1)} %slice.759), channel_id=1, source_target_pairs={{0,2},{1,3},{2,0},{3,1},{4,6},{5,7},{6,4},{7,5},{8,10},{9,11},{10,... | collective-permute-start | bytes 1179656 | tf_op jit(solution)/shard_map/ppermute | solution.py:55
  869.4 28.6 %collective-permute-start.139 = (bf16[64,1024]{1,0:T(8,128)(2,1)S(1)}, bf16[64,1024]{1,0:T(8,128)(2,1)S(1)}, u32[]{:S(2)}, u32[]{:S(2)}) collective-permute-start(bf16[64,1024]{1,0:T(8,128)(2,1)S(1)} %get-tuple-element.749), channel_id=1, source_target_pairs={{0,24},{1,25},{2,26},{3,27},{4,28},{5,29},{6,30},{7,31},{8,16},{9,... | collective-permute-start | bytes 393224 | tf_op jit(solution)/shard_map/ppermute | solution.py:55
  871.3 27.2 %collective-permute-start.138 = (bf16[64,1024]{1,0:T(8,128)(2,1)S(1)}, bf16[64,1024]{1,0:T(8,128)(2,1)S(1)}, u32[]{:S(2)}, u32[]{:S(2)}) collective-permute-start(bf16[64,1024]{1,0:T(8,128)(2,1)S(1)} %get-tuple-element.748), channel_id=1, source_target_pairs={{0,16},{1,17},{2,18},{3,19},{4,20},{5,21},{6,22},{7,23},{8,24},{9,... | collective-permute-start | bytes 393224 | tf_op jit(solution)/shard_map/ppermute | solution.py:55
  871.3 27.1 %collective-permute-start.135 = (bf16[64,1024]{1,0:T(8,128)(2,1)S(1)}, bf16[64,1024]{1,0:T(8,128)(2,1)S(1)}, u32[]{:S(2)}, u32[]{:S(2)}) collective-permute-start(bf16[64,1024]{1,0:T(8,128)(2,1)S(1)} %slice.771), channel_id=1, source_target_pairs={{0,8},{1,9},{2,10},{3,11},{4,12},{5,13},{6,14},{7,15},{8,0},{9,1},... | collective-permute-start | bytes 393224 | tf_op jit(solution)/shard_map/ppermute | solution.py:55
  (255 other events, 2319.3 us)

commit v3 on v0

v3 whole, which is shorter than its diff:
```python
import functools
import math

import jax
import jax.numpy as jnp
from jax import lax
from jax.experimental import pallas as pl
from jax.experimental.pallas import tpu as pltpu
from jax.sharding import PartitionSpec as P

HEADS = 16
KV = 4
HD = 64
GROUP = HEADS // KV
EPS = 1e-06
LOW = jnp.bfloat16
ANY = pl.BlockSpec(memory_space=pl.ANY)
VMEM = pl.BlockSpec(memory_space=pltpu.VMEM)
SMEM = pl.BlockSpec(memory_space=pltpu.SMEM)
FIRST_FIRST = (((0,), (0,)), ((), ()))
LAST_FIRST = (((1,), (0,)), ((), ()))
LAST_LAST = (((1,), (1,)), ((), ()))


def dot(left, right, dims):
    return lax.dot_general(left, right, dims, preferred_element_type=jnp.float32)


def normalize(values, axis=-1):
    inverse = lax.rsqrt(jnp.mean(values * values, axis=axis, keepdims=True) + EPS)
    return (values * inverse, inverse)


def norm_back(values, inverse, grad_normed, axis=-1):
    cubed = inverse * inverse * inverse
    return inverse * grad_normed - values * cubed * jnp.mean(
        grad_normed * values, axis=axis, keepdims=True
    )


def rotate(values, cos_t, sin_t):
    half_len = HD // 2
    turned = jnp.concatenate([-values[:, :, half_len:], values[:, :, :half_len]], axis=2)
    return values * cos_t + turned * sin_t


def rotate_back(grad_in, cos_t, sin_t):
    half_len = HD // 2
    along = grad_in * sin_t
    return grad_in * cos_t + jnp.concatenate([along[:, :, half_len:], -along[:, :, :half_len]], axis=2)


def tables(positions):
    freq = 10000.0 ** (-(2.0 * jnp.arange(HD // 2, dtype=jnp.float32)) / HD)
    angles = freq[:, None] * positions.astype(jnp.float32)[None, :]
    angles = jnp.concatenate([angles, angles], axis=0)
    return (jnp.cos(angles), jnp.sin(angles))


def swap(values, mask, devices):
    return lax.ppermute(values, ("dp", "shard"), [(i, i ^ mask) for i in range(devices)])


def place(blocks, masks, widths, me, total_rows):
    count = len(blocks)
    size = blocks[0].shape[0] // len(masks[0])
    copies = sum(len(own) for own in masks) * len(widths)

    def kernel(me_ref, *refs):
        sources, outs, sems = refs[:count], refs[count:-1], refs[-1]
        started = []
        for array, own in zip(sources, masks):
            for at, mask in enumerate(own):
                row = pl.multiple_of((me_ref[0] ^ mask) * size, size)
                column = 0
                for out, width in zip(outs, widths):
                    copy = pltpu.make_async_copy(
                        array.at[pl.ds(at * size, size), pl.ds(column, width)],
                        out.at[pl.ds(row, size)],
                        sems.at[len(started)],
                    )
                    copy.start()
                    started.append(copy)
                    column += width
        for copy in started:
            copy.wait()

    return pl.pallas_call(
        kernel,
        out_shape=[jax.ShapeDtypeStruct((total_rows, width), blocks[0].dtype) for width in widths],
        in_specs=[SMEM] + [ANY] * count,
        out_specs=[VMEM] * len(widths),
        scratch_shapes=[pltpu.SemaphoreType.DMA((copies,))],
        compiler_params=pltpu.CompilerParams(vmem_limit_bytes=24 << 20),
    )(me, *blocks)


def pick(arrays, orders, me, size):
    count = len(arrays)
    copies = sum(len(own) for own in orders) * count
    width = sum(array.shape[1] for array in arrays)

    def kernel(me_ref, *refs):
        sources, outs, sems = refs[:count], refs[count:-1], refs[-1]
        started = []
        for out, own in zip(outs, orders):
            for at, mask in enumerate(own):
                row = pl.multiple_of((me_ref[0] ^ mask) * size, size)
                column = 0
                for array in sources:
                    copy = pltpu.make_async_copy(
                        array.at[pl.ds(row, size)],
                        out.at[pl.ds(at * size, size), pl.ds(column, array.shape[1])],
                        sems.at[len(started)],
                    )
                    copy.start()
                    started.append(copy)
                    column += array.shape[1]
        for copy in started:
            copy.wait()

    return pl.pallas_call(
        kernel,
        out_shape=[jax.ShapeDtypeStruct((len(own) * size, width), arrays[0].dtype) for own in orders],
        in_specs=[SMEM] + [VMEM] * count,
        out_specs=[ANY] * len(orders),
        scratch_shapes=[pltpu.SemaphoreType.DMA((copies,))],
        compiler_params=pltpu.CompilerParams(vmem_limit_bytes=24 << 20),
    )(me, *arrays)


def gather_rows(parts, me, devices):
    part = jnp.concatenate(parts, axis=1)
    widths = [one.shape[1] for one in parts]
    if devices != 32:
        whole = lax.all_gather(part, ("dp", "shard"), axis=0, tiled=True)
        return jnp.split(whole, [sum(widths[:i]) for i in range(1, len(widths))], axis=1)
    near = jnp.concatenate([part, swap(part, 8, devices)])
    far = jnp.concatenate([swap(part, 16, devices), swap(part, 24, devices)])
    near = jnp.concatenate([near, swap(near, 4, devices)])
    far = jnp.concatenate([far, swap(far, 2, devices)])
    near_masks, far_masks = (0, 8, 4, 12), (16, 24, 18, 26)
    blocks, masks = [near, far], [near_masks, far_masks]
    blocks += [swap(near, 2, devices), swap(far, 4, devices)]
    masks += [tuple(m | 2 for m in near_masks), tuple(m | 4 for m in far_masks)]
    blocks += [swap(block, 1, devices) for block in blocks]
    masks += [tuple(m | 1 for m in own) for own in masks]
    return place(blocks, masks, widths, me, part.shape[0] * devices)


def reduce_rows(grads, me, devices):
    if devices != 32:
        grad = jnp.concatenate([one.astype(jnp.float32) for one in grads], axis=1)
        return lax.psum_scatter(grad, ("dp", "shard"), scatter_dimension=0, tiled=True)
    size = grads[0].shape[0] // devices
    order = [2, 10, 6, 14, 20, 28, 22, 30, 0, 8, 4, 12, 16, 24, 18, 26]
    keep, send = pick(grads, [order, [m | 1 for m in order]], me, size)
    came = swap(send, 1, devices)

    def both(low, high):
        rows = slice(low * size, high * size)
        return keep[rows].astype(jnp.float32) + came[rows].astype(jnp.float32)

    from_y = swap(both(0, 4).astype(LOW), 2, devices)
    from_x = swap(both(4, 8).astype(LOW), 4, devices)
    near = both(8, 12) + from_y.astype(jnp.float32)
    far = both(12, 16) + from_x.astype(jnp.float32)
    from_x = swap(near[2 * size :].astype(LOW), 4, devices)
    from_y = swap(far[2 * size :].astype(LOW), 2, devices)
    near = near[: 2 * size] + from_x.astype(jnp.float32)
    far = far[: 2 * size] + from_y.astype(jnp.float32)
    one = swap(near[size:].astype(LOW), 8, devices)
    two = swap(far[:size].astype(LOW), 16, devices)
    three = swap(far[size:].astype(LOW), 24, devices)
    return (near[:size] + one.astype(jnp.float32)) + (two.astype(jnp.float32) + three.astype(jnp.float32))


def gather_pieces(part, devices, shards):
    at = lax.axis_index("shard")
    if shards != 4 or devices != 32:
        return lax.all_gather(part, "shard", axis=0), jnp.arange(shards, dtype=jnp.int32)
    over = swap(part, 2, devices)
    pieces = jnp.stack([part, swap(part, 1, devices), over, swap(over, 1, devices)])
    return pieces, jnp.arange(4, dtype=jnp.int32) ^ at


def reduce_pieces(grad, devices, shards):
    if shards != 4 or devices != 32:
        return lax.psum_scatter(grad, "shard", scatter_dimension=0)
    came = swap(jnp.stack([grad[1], grad[3]]).astype(LOW), 1, devices).astype(jnp.float32)
    over = swap((grad[2] + came[1]).astype(LOW), 2, devices)
    return grad[0] + came[0] + over.astype(jnp.float32)


def sum_over_devices(values, devices):
    if devices != 32:
        return lax.psum(values, ("dp", "shard"))
    for mask in (16, 8, 4, 2, 1):
        values = values + swap(values, mask, devices)
    return values


def allowed(base, start, valid, key_axis, shape):
    key = base + lax.broadcasted_iota(jnp.int32, shape, key_axis)
    query = start + lax.broadcasted_iota(jnp.int32, shape, 1 - key_axis)
    return (key <= query) & (key < valid)


def over_pieces(info_ref, pieces, length, row, tile, before=None, after=None):
    start, valid = info_ref[0], info_ref[1 + pieces + row]

    def one(piece, carry):
        base = info_ref[1 + piece]
        if before is not None:
            before()
        used = (base < start + length) & (base < valid)
        full = (base + length <= start) & (base + length <= valid)
        pl.when(used & full)(lambda: tile(piece, None))
        pl.when(used & jnp.logical_not(full))(lambda: tile(piece, (base, start, valid)))
        if after is not None:
            after(piece)
        return carry

    lax.fori_loop(0, pieces, one, 0)


def attention(info, queries, keys_values):
    rows, _, length = queries.shape
    pieces = keys_values.shape[0]
    group_width = GROUP * HD

    def kernel(info_ref, q_ref, k_ref, v_ref, out_ref, low_ref, sums_ref, accum_ref, part_ref):
        accum_ref[...] = jnp.zeros_like(accum_ref)
        part_ref[...] = jnp.zeros_like(part_ref)

        def tile(piece, bounds):
            key_t, value_t = k_ref[piece, 0], v_ref[piece, 0]
            if bounds is not None:
                mask = allowed(*bounds, 1, (length, length))
            for head in range(GROUP):
                exps = jnp.exp(dot(q_ref[0, head * HD : (head + 1) * HD, :], key_t, FIRST_FIRST))
                if bounds is not None:
                    exps = jnp.where(mask, exps, 0.0)
                width = min(128, length)
                part = exps[:, :width]
                for at in range(width, length, width):
                    part = part + exps[:, at : at + width]
                part_ref[head] += part
                accum_ref[head] += dot(exps.astype(LOW), value_t, LAST_LAST)

        over_pieces(info_ref, pieces, length, pl.program_id(0), tile)
        for head in range(GROUP):
            own = slice(head * HD, (head + 1) * HD)
            sums = jnp.sum(part_ref[head].T, axis=0, keepdims=True)
            sums_ref[0, 0, head : head + 1, :] = sums
            out = accum_ref[head].T / sums
            out_ref[0, own, :] = out
            low_ref[0, own, :] = out.astype(LOW)

    q_spec = pl.BlockSpec((1, group_width, length), lambda row, group, *_: (row, group, 0))
    k_spec = pl.BlockSpec((pieces, 1, HD, length), lambda row, group, *_: (0, row, group, 0))
    v_spec = pl.BlockSpec((pieces, 1, HD, length), lambda row, group, *_: (0, row, group + KV, 0))
    s_spec = pl.BlockSpec((1, 1, GROUP, length), lambda row, group, *_: (row, group, 0, 0))
    work = rows * HEADS * length * length * pieces
    return pl.pallas_call(
        kernel,
        out_shape=[
            jax.ShapeDtypeStruct(queries.shape, jnp.float32),
            jax.ShapeDtypeStruct(queries.shape, LOW),
            jax.ShapeDtypeStruct((rows, KV, GROUP, length), jnp.float32),
        ],
        grid_spec=pltpu.PrefetchScalarGridSpec(
            num_scalar_prefetch=1,
            grid=(rows, KV),
            in_specs=[q_spec, k_spec, v_spec],
            out_specs=[q_spec, q_spec, s_spec],
            scratch_shapes=[
                pltpu.VMEM((GROUP, length, HD), jnp.float32),
                pltpu.VMEM((GROUP, length, min(128, length)), jnp.float32),
            ],
        ),
        compiler_params=pltpu.CompilerParams(vmem_limit_bytes=40 << 20),
        cost_estimate=pl.CostEstimate(flops=work * 1000, transcendentals=work, bytes_accessed=10 << 20),
    )(info, queries, keys_values, keys_values)


def attention_back(info, queries, keys_values, out, sums, grad_out, first, groups):
    rows, _, length = queries.shape
    pieces = keys_values.shape[0]
    group_width = GROUP * HD

    def kernel(
        info_ref, q_ref, k_ref, v_ref, out_ref, sums_ref, grad_ref, dq_ref, dk_ref, dv_ref,
        grad_low, grad_sums, q_rows, grad_rows, k_accum, v_accum,
    ):
        dq_ref[...] = jnp.zeros_like(dq_ref)
        for head in range(GROUP):
            own = slice(head * HD, (head + 1) * HD)
            inverse = 1.0 / sums_ref[0, 0, head : head + 1, :]
            grad = grad_ref[0, own, :]
            grad_sums[head] = -jnp.sum(grad * out_ref[0, own, :], axis=0, keepdims=True) * inverse
            scaled = grad * inverse
            grad_low[own, :] = scaled.astype(LOW)
            grad_rows[head] = scaled.T.astype(LOW)
            q_rows[head] = q_ref[0, own, :].T

        def tile(piece, bounds):
            key_t, value_t = k_ref[piece, 0], v_ref[piece, 0]
            if bounds is not None:
                mask = allowed(*bounds, 0, (length, length))
            for head in range(GROUP):
                own = slice(head * HD, (head + 1) * HD)
                exps = jnp.exp(dot(key_t, q_ref[0, own, :], FIRST_FIRST))
                if bounds is not None:
                    exps = jnp.where(mask, exps, 0.0)
                grad_exps = dot(value_t, grad_low[own, :], FIRST_FIRST) + grad_sums[head]
                grad_scores = (exps * grad_exps).astype(LOW)
                v_accum[...] += dot(exps.astype(LOW), grad_rows[head], LAST_FIRST)
                k_accum[...] += dot(grad_scores, q_rows[head], LAST_FIRST)
                dq_ref[0, own, :] += dot(key_t, grad_scores, LAST_FIRST)

        def before():
            k_accum[...] = jnp.zeros_like(k_accum)
            v_accum[...] = jnp.zeros_like(v_accum)

        def after(piece):
            dk_ref[piece, 0] = k_accum[...].T
            dv_ref[piece, 0] = v_accum[...].T

        over_pieces(info_ref, pieces, length, pl.program_id(0), tile, before, after)

    q_spec = pl.BlockSpec((1, group_width, length), lambda row, group, *_: (row, group + first, 0))
    k_spec = pl.BlockSpec((pieces, 1, HD, length), lambda row, group, *_: (0, row, group + first, 0))
    v_spec = pl.BlockSpec(
        (pieces, 1, HD, length), lambda row, group, *_: (0, row, group + first + KV, 0)
    )
    s_spec = pl.BlockSpec((1, 1, GROUP, length), lambda row, group, *_: (row, group + first, 0, 0))
    dq_spec = pl.BlockSpec((1, group_width, length), lambda row, group, *_: (row, group, 0))
    dk_spec = pl.BlockSpec((pieces, 1, HD, length), lambda row, group, *_: (0, row, group, 0))
    work = rows * groups * GROUP * length * length * pieces
    pieces_shape = jax.ShapeDtypeStruct((pieces, rows, groups * HD, length), jnp.float32)
    return pl.pallas_call(
        kernel,
        out_shape=[
            jax.ShapeDtypeStruct((rows, groups * group_width, length), jnp.float32),
            pieces_shape,
            pieces_shape,
        ],
        grid_spec=pltpu.PrefetchScalarGridSpec(
            num_scalar_prefetch=1,
            grid=(rows, groups),
            in_specs=[q_spec, k_spec, v_spec, q_spec, s_spec, q_spec],
            out_specs=[dq_spec, dk_spec, dk_spec],
            scratch_shapes=[
                pltpu.VMEM((group_width, length), LOW),
                pltpu.VMEM((GROUP, 1, length), jnp.float32),
                pltpu.VMEM((GROUP, length, HD), LOW),
                pltpu.VMEM((GROUP, length, HD), LOW),
                pltpu.VMEM((length, HD), jnp.float32),
                pltpu.VMEM((length, HD), jnp.float32),
            ],
        ),
        compiler_params=pltpu.CompilerParams(vmem_limit_bytes=40 << 20),
        cost_estimate=pl.CostEstimate(flops=work * 2500, transcendentals=work, bytes_accessed=10 << 20),
    )(info, queries, keys_values, keys_values, out, sums, grad_out)


def local(
    tokens,
    cotangent,
    lengths,
    slot_sequence,
    attn_gain,
    w_qkv,
    q_gain,
    k_gain,
    w_out,
    ffn_gain,
    w_gate,
    w_up,
    w_down,
):
    row_count, piece_len, model_width = tokens.shape
    q_width = HEADS * HD
    kv_width = KV * HD
    total_rows = lengths.shape[0]
    scale_factor = 1.0 / math.sqrt(HD)
    shards = lax.axis_size("shard")
    devices = lax.axis_size("dp") * shards
    part_len = attn_gain.shape[0]
    shard_at = lax.axis_index("shard")
    me = (lax.axis_index("dp") * shards + shard_at).astype(jnp.int32).reshape(1)
    row_valid = jnp.sum(
        jnp.where(
            slot_sequence[:, None] == jnp.arange(total_rows, dtype=jnp.int32)[None, :],
            lengths[None, :],
            0,
        ),
        axis=1,
    )
    start = (shard_at * piece_len).astype(jnp.int32)
    positions = start + jnp.arange(piece_len, dtype=jnp.int32)
    live_mask = (positions[None, :] < row_valid[:, None]).astype(jnp.float32)
    cos_t, sin_t = tables(positions)
    cos_h = cos_t[None, None]
    sin_h = sin_t[None, None]
    q_gain_h = q_gain[None, None, :, None]
    k_gain_h = k_gain[None, None, :, None]

    gain_columns = jnp.concatenate(
        [attn_gain[:, None], ffn_gain[:, None], jnp.zeros((part_len, 126), jnp.float32)], axis=1
    )
    wqkv, gains = gather_rows([w_qkv.astype(LOW), gain_columns.astype(LOW)], me, devices)
    wout, wgate = gather_rows([w_out.astype(LOW).T, w_gate.astype(LOW)], me, devices)
    wup, wdown = gather_rows([w_up.astype(LOW), w_down.astype(LOW).T], me, devices)
    gain_attn = gains[:, 0].astype(jnp.float32)
    gain_ffn = gains[:, 1].astype(jnp.float32)

    x_float = tokens.astype(jnp.float32)
    normed_one, inverse_one = normalize(x_float)
    normed_low = (normed_one * gain_attn).astype(LOW)
    projected = jnp.einsum("rtd,de->ret", normed_low, wqkv, preferred_element_type=jnp.float32)
    q_raw = projected[:, :q_width].reshape(row_count, HEADS, HD, piece_len)
    k_raw = projected[:, q_width : q_width + kv_width].reshape(row_count, KV, HD, piece_len)
    v_raw = projected[:, q_width + kv_width :]
    q_unit, q_inverse = normalize(q_raw, 2)
    k_unit, k_inverse = normalize(k_raw, 2)
    q_low = (
        rotate(q_unit * q_gain_h, cos_h, sin_h).astype(LOW) * jnp.array(scale_factor, LOW)
    ).reshape(row_count, q_width, piece_len)
    k_low = rotate(k_unit * k_gain_h, cos_h, sin_h).astype(LOW).reshape(row_count, kv_width, piece_len)
    own_kv = jnp.concatenate([k_low, v_raw.astype(LOW)], axis=1)
    pieces, piece_at = gather_pieces(own_kv, devices, shards)
    info = jnp.concatenate([start.reshape(1), piece_at * piece_len, row_valid]).astype(jnp.int32)
    o_heads, att_low, sums = attention(info, q_low, pieces)
    x_mid = x_float + jnp.einsum("rct,dc->rtd", att_low, wout, preferred_element_type=jnp.float32)
    normed_two, inverse_two = normalize(x_mid)
    ffn_in = (normed_two * gain_ffn).astype(LOW)
    gate_proj = jnp.einsum("rtd,df->rtf", ffn_in, wgate, preferred_element_type=jnp.float32)
    up_proj = jnp.einsum("rtd,df->rtf", ffn_in, wup, preferred_element_type=jnp.float32)
    gate_sig = jax.nn.sigmoid(gate_proj)
    silu_gate = gate_proj * gate_sig
    activated = (silu_gate * up_proj).astype(LOW)
    output = (
        x_mid + jnp.einsum("rtf,df->rtd", activated, wdown, preferred_element_type=jnp.float32)
    ).astype(LOW)

    grad_out = cotangent.astype(jnp.float32) * live_mask[..., None]
    grad_low = grad_out.astype(LOW)
    grad_down = jnp.einsum("rtd,rtf->df", grad_low, activated, preferred_element_type=jnp.float32)
    grad_act = jnp.einsum("rtd,df->rtf", grad_low, wdown, preferred_element_type=jnp.float32)
    grad_gate = (grad_act * up_proj * gate_sig * (1.0 + gate_proj * (1.0 - gate_sig))).astype(LOW)
    grad_up = (grad_act * silu_gate).astype(LOW)
    grad_wgate = jnp.einsum("rtd,rtf->df", ffn_in, grad_gate, preferred_element_type=jnp.float32)
    grad_wup = jnp.einsum("rtd,rtf->df", ffn_in, grad_up, preferred_element_type=jnp.float32)
    one = reduce_rows([grad_down.astype(LOW), grad_wgate.astype(LOW)], me, devices)
    width = grad_down.shape[1]
    summed_down, summed_wgate = one[:, :width].T, one[:, width:]
    grad_ffn_in = jnp.einsum(
        "rtf,df->rtd", grad_gate, wgate, preferred_element_type=jnp.float32
    ) + jnp.einsum("rtf,df->rtd", grad_up, wup, preferred_element_type=jnp.float32)
    grad_gain_two = jnp.sum(grad_ffn_in * normed_two, axis=(0, 1))
    grad_mid = grad_out + norm_back(x_mid, inverse_two, grad_ffn_in * gain_ffn)
    mid_low = grad_mid.astype(LOW)
    grad_wout = jnp.einsum("rtd,rct->dc", mid_low, att_low, preferred_element_type=jnp.float32)
    two = reduce_rows([grad_wup.astype(LOW), grad_wout.astype(LOW)], me, devices)
    summed_wup, summed_wout = two[:, :width], two[:, width:].T
    grad_att = jnp.einsum("rtd,dc->rct", mid_low, wout, preferred_element_type=jnp.float32)
    dq_parts, dk_parts, dv_parts = [], [], []
    for group in range(KV):
        dq, dk, dv = attention_back(info, q_low, pieces, o_heads, sums, grad_att, group, 1)
        dq_parts.append(dq)
        dk_parts.append(dk)
        dv_parts.append(dv)
    grad_query = jnp.concatenate(dq_parts, axis=1)
    grad_pieces = jnp.concatenate(dk_parts + dv_parts, axis=2)
    grad_kv = reduce_pieces(grad_pieces, devices, shards)
    grad_q_scaled = rotate_back(
        scale_factor * grad_query.reshape(row_count, HEADS, HD, piece_len), cos_h, sin_h
    )
    grad_qgain = jnp.sum(grad_q_scaled * q_unit, axis=(0, 1, 3))
    grad_q_raw = norm_back(q_raw, q_inverse, grad_q_scaled * q_gain_h, 2)
    grad_k_scaled = rotate_back(
        grad_kv[:, :kv_width].reshape(row_count, KV, HD, piece_len), cos_h, sin_h
    )
    grad_kgain = jnp.sum(grad_k_scaled * k_unit, axis=(0, 1, 3))
    grad_k_raw = norm_back(k_raw, k_inverse, grad_k_scaled * k_gain_h, 2)
    shared = sum_over_devices(jnp.concatenate([grad_qgain, grad_kgain])[None], devices)
    grad_projected = jnp.concatenate(
        [
            grad_q_raw.reshape(row_count, q_width, piece_len),
            grad_k_raw.reshape(row_count, kv_width, piece_len),
            grad_kv[:, kv_width:],
        ],
        axis=1,
    ).astype(LOW)
    grad_wqkv = jnp.einsum("rtd,ret->de", normed_low, grad_projected, preferred_element_type=jnp.float32)
    grad_normed = jnp.einsum("ret,de->rtd", grad_projected, wqkv, preferred_element_type=jnp.float32)
    grad_gain_one = jnp.sum(grad_normed * normed_one, axis=(0, 1))
    input_grad = grad_mid + norm_back(x_float, inverse_one, grad_normed * gain_attn)
    grad_gains = jnp.concatenate(
        [grad_gain_one[:, None], grad_gain_two[:, None], jnp.zeros((model_width, 126), jnp.float32)],
        axis=1,
    )
    three = reduce_rows([grad_wqkv.astype(LOW), grad_gains.astype(LOW)], me, devices)
    qkv_width = w_qkv.shape[1]
    return (
        output,
        input_grad,
        three[:, qkv_width],
        three[:, :qkv_width],
        shared[0, :HD],
        shared[0, HD:],
        summed_wout,
        three[:, qkv_width + 1],
        summed_wgate,
        summed_wup,
        summed_down,
    )


def solution(mesh):
    in_specs = (
        P("dp", "shard", None),
        P("dp", "shard", None),
        P(),
        P("dp"),
        P(("dp", "shard")),
        P(("dp", "shard"), None),
        P(),
        P(),
        P(None, ("dp", "shard")),
        P(("dp", "shard")),
        P(("dp", "shard"), None),
        P(("dp", "shard"), None),
        P(None, ("dp", "shard")),
    )
    out_specs = (
        P("dp", "shard", None),
        P("dp", "shard", None),
        P(("dp", "shard")),
        P(("dp", "shard"), None),
        P(),
        P(),
        P(None, ("dp", "shard")),
        P(("dp", "shard")),
        P(("dp", "shard"), None),
        P(("dp", "shard"), None),
        P(None, ("dp", "shard")),
    )
    return jax.shard_map(local, mesh=mesh, in_specs=in_specs, out_specs=out_specs, check_vma=False)
```

time: 1410 us -> 574 us (0.41)
  waiting for transfers between devices: 982 us -> 247 us
  starting transfers between devices: 1.34 us -> 116 us
  blocking collectives: 109 us -> 0 us
  matrix products: 137 us -> 66.2 us
  local copies, waits for them, and re-layouts: 93.9 us -> 30.5 us
  Pallas kernels: 0 us -> 48.2 us
    reduce_scatter x7 -> x0, waiting for transfers between devices: 753 us -> none  [the longest x1 158 us: local(): lax.psum_scatter(grad_wqkv, ('dp', 'shard'), scatter_dimension=0, tiled=T...]
    ppermute x0 -> x67, waiting for transfers between devices: none -> 247 us  [swap(): lax.ppermute(values, ('dp', 'shard'), [(i, i ^ mask) for i in range(devic...]
    all_gather x7 -> x0, waiting for transfers between devices: 228 us -> none  [the longest x1 57.4 us: local(): lax.all_gather(ffn_pack[2], ('dp', 'shard'), axis=0, tiled=True)]
    ppermute x0 -> x67, starting transfers between devices: none -> 116 us  [swap(): lax.ppermute(values, ('dp', 'shard'), [(i, i ^ mask) for i in range(devic...]
    unnamed x2 -> x0, blocking collectives: 109 us -> none
    dot_general x20 -> x13, matrix products: 122 us -> 57.6 us  [the longest x1 7.6 us: local(): jnp.einsum('rtf,df->rtd', activated, wdown, preferred_element_type=jnp.fl...]
    pallas_call x0 -> x11, Pallas kernels: none -> 48.2 us  [the longest x4 20.2 us: attention_back(): pl.pallas_call(kernel, out_shape=[jax.ShapeDtypeStruct((rows, groups * gr...]
  transfers between devices with their start and end apart: 14 -> 67, of which waited for: 14 -> 24; matrix products, arithmetic and copies ran while one was open for 14% -> 16% of each run, Pallas kernels for 0% -> 3%
where the time goes in v3:
time: 574 us; the launch traced here: 569 us
  waiting for transfers between devices  247 us (43%)
  starting transfers between devices  116 us (20%)
  matrix products  66.2 us (12%)
  other arithmetic  57.7 us (10%)
  Pallas kernels  48.2 us (8%)
  local copies, waits for them, and re-layouts  30.5 us (5%)
    ppermute x67, waiting for transfers between devices, swap(): lax.ppermute(values, ('dp', 'shard'), [(i, i ^ mask) for i in range(devic...  247 us
    ppermute x67, starting transfers between devices, swap(): lax.ppermute(values, ('dp', 'shard'), [(i, i ^ mask) for i in range(devic...  116 us
    unnamed x150, local copies, waits for them, and re-layouts  22 us
    pallas_call x4, Pallas kernels, attention_back(): pl.pallas_call(kernel, out_shape=[jax.ShapeDtypeStruct((rows, groups * gr...  20.2 us
  transfers between devices with their start and end apart: 67, of which 24 were waited for; matrix products, arithmetic and copies ran while one was open for 16% of the time, Pallas kernels for 3%

profile of v3, /device:TPU:0, one launch (start us, length us, event | category | flops | bytes accessed | tf_op | source)
XLA Modules:
  0.0 569.2 jit_solution(7127815522112499783)
XLA Ops:
  12.8 3.5 collective-permute-start.2
  23.8 5.5 collective-permute-done
  32.6 14.9 %collective-permute-done.2 = bf16[64,1664]{1,0:T(8,128)(2,1)} collective-permute-done((bf16[64,1664]{1,0:T(8,128)(2,1)S(1)}, bf16[64,1664]{1,0:T(8,128)(2,1)}, u32[]{:S(2)}, u32[]{:S(2)}) %collective-permute-start.2) | collective-permute-done | bytes 213024 | tf_op jit(solution)/shard_map/ppermute | solution.py:61
  47.6 4.6 collective-permute-start.27
  60.6 9.6 %collective-permute-done.27 = bf16[64,2048]{1,0:T(8,128)(2,1)S(1)} collective-permute-done((bf16[64,2048]{1,0:T(8,128)(2,1)S(1)}, bf16[64,2048]{1,0:T(8,128)(2,1)S(1)}, u32[]{:S(2)}, u32[]{:S(2)}) %collective-permute-start.27) | collective-permute-done | bytes 262176 | tf_op jit(solution)/shard_map/ppermute | solution.py:61
  77.2 7.8 %collective-permute-done.15 = bf16[128,2048]{1,0:T(8,128)(2,1)S(1)} collective-permute-done((bf16[128,2048]{1,0:T(8,128)(2,1)S(1)}, bf16[128,2048]{1,0:T(8,128)(2,1)S(1)}, u32[]{:S(2)}, u32[]{:S(2)}) %collective-permute-start.15) | collective-permute-done | bytes 524320 | tf_op jit(solution)/shard_map/ppermute | solution.py:61
  86.5 25.1 %collective-permute-done.29 = bf16[128,2048]{1,0:T(8,128)(2,1)S(1)} collective-permute-done((bf16[128,2048]{1,0:T(8,128)(2,1)S(1)}, bf16[128,2048]{1,0:T(8,128)(2,1)S(1)}, u32[]{:S(2)}, u32[]{:S(2)}) %collective-permute-start.29) | collective-permute-done | bytes 524320 | tf_op jit(solution)/shard_map/ppermute | solution.py:61
  120.8 3.6 convolution_bitcast_fusion
  125.5 14.0 %collective-permute-done.19.refs_2_ = bf16[256,2048]{1,0:T(8,128)(2,1)S(1)} collective-permute-done((bf16[256,2048]{1,0:T(8,128)(2,1)S(1)}, bf16[256,2048]{1,0:T(8,128)(2,1)S(1)}, u32[]{:S(2)}, u32[]{:S(2)}) %collective-permute-start.19) | collective-permute-done | bytes 1048608 | tf_op jit(solution)/shard_map/ppermute | solution.py:61
  143.6 17.8 %collective-permute-done.30.refs_2_ = bf16[256,2048]{1,0:T(8,128)(2,1)S(1)} collective-permute-done((bf16[256,2048]{1,0:T(8,128)(2,1)S(1)}, bf16[256,2048]{1,0:T(8,128)(2,1)S(1)}, u32[]{:S(2)}, u32[]{:S(2)}) %collective-permute-start.30) | collective-permute-done | bytes 1048608 | tf_op jit(solution)/shard_map/ppermute | solution.py:61
  172.4 7.3 %collective-permute-done.12 = bf16[1,512,512]{2,1,0:T(8,128)(2,1)} collective-permute-done((bf16[1,512,512]{2,1,0:T(8,128)(2,1)}, bf16[1,512,512]{2,1,0:T(8,128)(2,1)}, u32[]{:S(2)}, u32[]{:S(2)}) %collective-permute-start.12) | collective-permute-done | bytes 524320 | tf_op jit(solution)/shard_map/ppermute | solution.py:61
  182.0 3.9 fusion.40
  187.3 11.0 %shard_map.213 = (f32[1,1024,512]{2,1,0:T(8,128)S(1)}, bf16[1,1024,512]{2,1,0:T(8,128)(2,1)S(1)}, f32[1,4,4,512]{3,2,1,0:T(4,128)S(1)}) custom-call(s32[6]{0:T(128)S(1)} %pad_add_fusion.info_ref, bf16[1,1024,512]{2,1,0:T(8,128)(2,1)S(1)} %fusion.28.q_ref, bf16[4,1,512,512]{3,2,1,0:T(8,128)(2,1)S(1)} %pad_maximum_fusion.1.k_ref.v_ref, ...), custom_call_target="tpu_custom_call" | custom-call | flops 16777216000 | bytes 10485760 | tf_op jit(solution)/shard_map/pallas_call | solution.py:265
  198.3 4.2 multiply_reduce_fusion
  203.0 4.0 copy-done.10
  209.3 4.3 multiply_convert_fusion.2
  213.6 4.3 fusion.74
  217.9 7.4 %fusion.9 = (bf16[2048]{0:T(1024)(128)(2,1)S(1)}, f32[512]{0:T(512)S(1)}, f32[512,2048]{1,0:T(8,128)}) fusion(f32[1,512,2048]{2,1,0:T(8,128)S(1)} %get-tuple-element.127, f32[512]{0:T(512)S(1)} %get-tuple-element.123, f32[2048]{0:T(1024)S(1)} %get-tuple-element.69, f32[512,2048]{1,0:T(8,128)} %fusion.74, bf16[512,1024]{1,0:T(8,128)(2,1)S(1)} %get-tuple-element.83, ...), kind=kOutput, calls=%fused_computation.16 | convolution fusion | flops 2154821120 | bytes 17842176 | tf_op jit(solution)/shard_map/rtf,df->rtd/dot_general | solution.py:459
  225.2 3.5 fusion.11
  231.2 4.9 shard_map.216
  236.1 5.3 shard_map.217
  241.4 4.9 shard_map.218
  246.3 5.1 shard_map.219
  251.4 4.4 convolution_convert_fusion.3.refs_1_
  257.9 16.7 %collective-permute-start.36 = (bf16[2,1,512,512]{3,2,1,0:T(8,128)(2,1)}, bf16[2,1,512,512]{3,2,1,0:T(8,128)(2,1)}, u32[]{:S(2)}, u32[]{:S(2)}) collective-permute-start(bf16[2,1,512,512]{3,2,1,0:T(8,128)(2,1)} %pad_maximum_fusion.6), channel_id=1, source_target_pairs={{0,1},{1,0},{2,3},{3,2},{4,5},{5,4},{6,7},{7,6},{8,9},{9,8},{10,11... | collective-permute-start | bytes 3145736 | tf_op jit(solution)/shard_map/ppermute | solution.py:61
  279.2 4.3 convolution_convert_fusion.4.refs_0_
  290.5 17.8 %collective-permute-start.37 = (bf16[1,512,512]{2,1,0:T(8,128)(2,1)}, bf16[1,512,512]{2,1,0:T(8,128)(2,1)S(1)}, u32[]{:S(2)}, u32[]{:S(2)}) collective-permute-start(bf16[1,512,512]{2,1,0:T(8,128)(2,1)} %fusion.51), channel_id=1, source_target_pairs={{0,2},{1,3},{2,0},{3,1},{4,6},{5,7},{6,4},{7,5},{8,10},{9,11},{10,... | collective-permute-start | bytes 1572872 | tf_op jit(solution)/shard_map/ppermute | solution.py:61
  308.3 4.3 convolution_convert_fusion.1.refs_1_
  317.4 3.5 shard_map.221
  325.5 3.4 shard_map.222
  336.8 5.7 %fusion.3 = (bf16[2048]{0:T(1024)(128)(2,1)S(1)}, f32[512]{0:T(512)S(1)}, f32[512,2048]{1,0:T(8,128)}) fusion(bf16[1,512,2048]{2,1,0:T(8,128)(2,1)S(1)} %copy-done.24, f32[512]{0:T(512)S(1)} %copy-done.55, f32[2048]{0:T(1024)S(1)} %copy-done.49, bf16[2048,1536]{1,0:T(8,128)(2,1)S(1)} %bitcast.242, bf16[256,512]{1,0:T(8,128)(2,1)S(1)} %fusion.55, ...), kind=kOutput, calls=%fused_computation.9 | convolution fusion | flops 3233281536 | bytes 14172160 | tf_op jit(solution)/shard_map/ret,de->rtd/dot_general | solution.py:498
  343.2 4.9 convolution_convert_fusion.refs_0_
  351.7 4.4 collective-permute-done.46
  356.2 5.0 collective-permute-start.47
  362.7 17.7 %collective-permute-start.48 = (f32[1,128]{1,0:T(1,128)S(1)}, f32[1,128]{1,0:T(1,128)S(1)}, u32[]{:S(2)}, u32[]{:S(2)}) collective-permute-start(f32[1,128]{1,0:T(1,128)S(1)} %add.337), channel_id=1, source_target_pairs={{0,4},{1,5},{2,6},{3,7},{4,0},{5,1},{6,2},{7,3},{8,12},{9,13},{10,... | collective-permute-start | bytes 1544 | tf_op jit(solution)/shard_map/ppermute | solution.py:61
  380.4 7.6 %fusion.12 = bf16[1,512,2048]{2,1,0:T(8,128)(2,1)} fusion(f32[1,512,2048]{2,1,0:T(8,128)} %copy-done.11, bf16[512,1024]{1,0:T(8,128)(2,1)} %get-tuple-element.85, bf16[2048,1024]{1,0:T(8,128)(2,1)} %copy-done.8), kind=kOutput, calls=%fused_computation.22 | convolution fusion | flops 2149580800 | bytes 11534336 | tf_op jit(solution)/shard_map/rtf,df->rtd/dot_general | solution.py:445
  388.1 3.5 collective-permute-done.49
  402.5 20.8 %collective-permute-done.55 = bf16[256,2048]{1,0:T(8,128)(2,1)S(1)} collective-permute-done((bf16[256,2048]{1,0:T(8,128)(2,1)S(1)}, bf16[256,2048]{1,0:T(8,128)(2,1)S(1)}, u32[]{:S(2)}, u32[]{:S(2)}) %collective-permute-start.55) | collective-permute-done | bytes 1048608 | tf_op jit(solution)/shard_map/ppermute | solution.py:61
  427.9 17.8 %collective-permute-done.63 = bf16[256,2048]{1,0:T(8,128)(2,1)S(1)} collective-permute-done((bf16[256,2048]{1,0:T(8,128)(2,1)S(1)}, bf16[256,2048]{1,0:T(8,128)(2,1)S(1)}, u32[]{:S(2)}, u32[]{:S(2)}) %collective-permute-start.63) | collective-permute-done | bytes 1048608 | tf_op jit(solution)/shard_map/ppermute | solution.py:61
  450.4 12.7 %collective-permute-done.56 = bf16[128,2048]{1,0:T(8,128)(2,1)S(1)} collective-permute-done((bf16[128,2048]{1,0:T(8,128)(2,1)S(1)}, bf16[128,2048]{1,0:T(8,128)(2,1)S(1)}, u32[]{:S(2)}, u32[]{:S(2)}) %collective-permute-start.56) | collective-permute-done | bytes 524320 | tf_op jit(solution)/shard_map/ppermute | solution.py:61
  464.7 30.3 %collective-permute-done.64 = bf16[128,2048]{1,0:T(8,128)(2,1)S(1)} collective-permute-done((bf16[128,2048]{1,0:T(8,128)(2,1)S(1)}, bf16[128,2048]{1,0:T(8,128)(2,1)S(1)}, u32[]{:S(2)}, u32[]{:S(2)}) %collective-permute-start.64) | collective-permute-done | bytes 524320 | tf_op jit(solution)/shard_map/ppermute | solution.py:61
  497.5 9.8 %collective-permute-done.43 = bf16[128,1664]{1,0:T(8,128)(2,1)S(1)} collective-permute-done((bf16[128,1664]{1,0:T(8,128)(2,1)S(1)}, bf16[128,1664]{1,0:T(8,128)(2,1)S(1)}, u32[]{:S(2)}, u32[]{:S(2)}) %collective-permute-start.43) | collective-permute-done | bytes 426016 | tf_op jit(solution)/shard_map/ppermute | solution.py:61
  507.3 4.1 collective-permute-start.66
  516.7 12.6 %collective-permute-done.39 = bf16[256,1664]{1,0:T(8,128)(2,1)S(1)} collective-permute-done((bf16[256,1664]{1,0:T(8,128)(2,1)S(1)}, bf16[256,1664]{1,0:T(8,128)(2,1)S(1)}, u32[]{:S(2)}, u32[]{:S(2)}) %collective-permute-start.39) | collective-permute-done | bytes 852000 | tf_op jit(solution)/shard_map/ppermute | solution.py:61
  532.3 6.9 %collective-permute-done.61 = bf16[128,2048]{1,0:T(8,128)(2,1)S(1)} collective-permute-done((bf16[128,2048]{1,0:T(8,128)(2,1)S(1)}, bf16[128,2048]{1,0:T(8,128)(2,1)S(1)}, u32[]{:S(2)}, u32[]{:S(2)}) %collective-permute-start.61) | collective-permute-done | bytes 524320 | tf_op jit(solution)/shard_map/ppermute | solution.py:61
  542.8 6.0 %collective-permute-done.54 = bf16[64,2048]{1,0:T(8,128)(2,1)S(1)} collective-permute-done((bf16[64,2048]{1,0:T(8,128)(2,1)S(1)}, bf16[64,2048]{1,0:T(8,128)(2,1)S(1)}, u32[]{:S(2)}, u32[]{:S(2)}) %collective-permute-start.54) | collective-permute-done | bytes 262176 | tf_op jit(solution)/shard_map/ppermute | solution.py:61
  551.3 9.7 %collective-permute-done.62 = bf16[64,2048]{1,0:T(8,128)(2,1)S(1)} collective-permute-done((bf16[64,2048]{1,0:T(8,128)(2,1)S(1)}, bf16[64,2048]{1,0:T(8,128)(2,1)S(1)}, u32[]{:S(2)}, u32[]{:S(2)}) %collective-permute-start.62) | collective-permute-done | bytes 262176 | tf_op jit(solution)/shard_map/ppermute | solution.py:61
  562.2 5.0 collective-permute-done.41
  (407 shorter events, 150.1 us)
Async XLA Ops:
  3.5 50.6 %collective-permute-start.14 = (bf16[64,2048]{1,0:T(8,128)(2,1)}, bf16[64,2048]{1,0:T(8,128)(2,1)}, u32[]{:S(2)}, u32[]{:S(2)}) collective-permute-start(bf16[64,2048]{1,0:T(8,128)(2,1)} %pad_maximum_fusion.19), channel_id=1, source_target_pairs={{0,8},{1,9},{2,10},{3,11},{4,12},{5,13},{6,14},{7,15},{8,0},{9,1},... | collective-permute-start | bytes 786440 | tf_op jit(solution)/shard_map/ppermute | solution.py:61
  6.5 50.0 %collective-permute-start.16 = (bf16[64,2048]{1,0:T(8,128)(2,1)}, bf16[64,2048]{1,0:T(8,128)(2,1)}, u32[]{:S(2)}, u32[]{:S(2)}) collective-permute-start(bf16[64,2048]{1,0:T(8,128)(2,1)} %pad_maximum_fusion.19), channel_id=1, source_target_pairs={{0,16},{1,17},{2,18},{3,19},{4,20},{5,21},{6,22},{7,23},{8,24},{9,... | collective-permute-start | bytes 786440 | tf_op jit(solution)/shard_map/ppermute | solution.py:61
  9.1 49.0 %collective-permute-start.17 = (bf16[64,2048]{1,0:T(8,128)(2,1)}, bf16[64,2048]{1,0:T(8,128)(2,1)S(1)}, u32[]{:S(2)}, u32[]{:S(2)}) collective-permute-start(bf16[64,2048]{1,0:T(8,128)(2,1)} %pad_maximum_fusion.19), channel_id=1, source_target_pairs={{0,24},{1,25},{2,26},{3,27},{4,28},{5,29},{6,30},{7,31},{8,16},{9,... | collective-permute-start | bytes 786440 | tf_op jit(solution)/shard_map/ppermute | solution.py:61
  11.8 17.5 %collective-permute-start = (bf16[64,1664]{1,0:T(8,128)(2,1)S(1)}, bf16[64,1664]{1,0:T(8,128)(2,1)S(1)}, u32[]{:S(2)}, u32[]{:S(2)}) collective-permute-start(bf16[64,1664]{1,0:T(8,128)(2,1)S(1)} %concatenate.160), channel_id=1, source_target_pairs={{0,8},{1,9},{2,10},{3,11},{4,12},{5,13},{6,14},{7,15},{8,0},{9,1},... | collective-permute-start | bytes 638984 | tf_op jit(solution)/shard_map/ppermute | solution.py:61
  12.8 34.8 %collective-permute-start.2 = (bf16[64,1664]{1,0:T(8,128)(2,1)S(1)}, bf16[64,1664]{1,0:T(8,128)(2,1)}, u32[]{:S(2)}, u32[]{:S(2)}) collective-permute-start(bf16[64,1664]{1,0:T(8,128)(2,1)S(1)} %concatenate.160), channel_id=1, source_target_pairs={{0,16},{1,17},{2,18},{3,19},{4,20},{5,21},{6,22},{7,23},{8,24},{9,... | collective-permute-start | bytes 638984 | tf_op jit(solution)/shard_map/ppermute | solution.py:61
  29.3 18.2 %collective-permute-start.3 = (bf16[64,1664]{1,0:T(8,128)(2,1)S(1)}, bf16[64,1664]{1,0:T(8,128)(2,1)S(1)}, u32[]{:S(2)}, u32[]{:S(2)}) collective-permute-start(bf16[64,1664]{1,0:T(8,128)(2,1)S(1)} %concatenate.160), channel_id=1, source_target_pairs={{0,24},{1,25},{2,26},{3,27},{4,28},{5,29},{6,30},{7,31},{8,16},{9,... | collective-permute-start | bytes 638984 | tf_op jit(solution)/shard_map/ppermute | solution.py:61
  47.5 28.0 %collective-permute-start.25 = (bf16[64,2048]{1,0:T(8,128)(2,1)S(1)}, bf16[64,2048]{1,0:T(8,128)(2,1)S(1)}, u32[]{:S(2)}, u32[]{:S(2)}) collective-permute-start(bf16[64,2048]{1,0:T(8,128)(2,1)S(1)} %pad_maximum_fusion.20), channel_id=1, source_target_pairs={{0,8},{1,9},{2,10},{3,11},{4,12},{5,13},{6,14},{7,15},{8,0},{9,1},... | collective-permute-start | bytes 786440 | tf_op jit(solution)/shard_map/ppermute | solution.py:61
  47.6 22.6 %collective-permute-start.27 = (bf16[64,2048]{1,0:T(8,128)(2,1)S(1)}, bf16[64,2048]{1,0:T(8,128)(2,1)S(1)}, u32[]{:S(2)}, u32[]{:S(2)}) collective-permute-start(bf16[64,2048]{1,0:T(8,128)(2,1)S(1)} %pad_maximum_fusion.20), channel_id=1, source_target_pairs={{0,16},{1,17},{2,18},{3,19},{4,20},{5,21},{6,22},{7,23},{8,24},{9,... | collective-permute-start | bytes 786440 | tf_op jit(solution)/shard_map/ppermute | solution.py:61
  54.1 17.6 %collective-permute-start.28 = (bf16[64,2048]{1,0:T(8,128)(2,1)S(1)}, bf16[64,2048]{1,0:T(8,128)(2,1)S(1)}, u32[]{:S(2)}, u32[]{:S(2)}) collective-permute-start(bf16[64,2048]{1,0:T(8,128)(2,1)S(1)} %pad_maximum_fusion.20), channel_id=1, source_target_pairs={{0,24},{1,25},{2,26},{3,27},{4,28},{5,29},{6,30},{7,31},{8,16},{9,... | collective-permute-start | bytes 786440 | tf_op jit(solution)/shard_map/ppermute | solution.py:61
  56.6 17.7 %collective-permute-start.1 = (bf16[128,1664]{1,0:T(8,128)(2,1)S(1)}, bf16[128,1664]{1,0:T(8,128)(2,1)S(1)}, u32[]{:S(2)}, u32[]{:S(2)}) collective-permute-start(bf16[128,1664]{1,0:T(8,128)(2,1)S(1)} %pad_maximum_fusion.17), channel_id=1, source_target_pairs={{0,4},{1,5},{2,6},{3,7},{4,0},{5,1},{6,2},{7,3},{8,12},{9,13},{10,... | collective-permute-start | bytes 1277960 | tf_op jit(solution)/shard_map/ppermute | solution.py:61
  58.1 16.8 %collective-permute-start.4 = (bf16[128,1664]{1,0:T(8,128)(2,1)S(1)}, bf16[128,1664]{1,0:T(8,128)(2,1)S(1)}, u32[]{:S(2)}, u32[]{:S(2)}) collective-permute-start(bf16[128,1664]{1,0:T(8,128)(2,1)S(1)} %pad_maximum_fusion.18), channel_id=1, source_target_pairs={{0,2},{1,3},{2,0},{3,1},{4,6},{5,7},{6,4},{7,5},{8,10},{9,11},{10,... | collective-permute-start | bytes 1277960 | tf_op jit(solution)/shard_map/ppermute | solution.py:61
  74.3 37.4 %collective-permute-start.5 = (bf16[256,1664]{1,0:T(8,128)(2,1)S(1)}, bf16[256,1664]{1,0:T(8,128)(2,1)S(1)}, u32[]{:S(2)}, u32[]{:S(2)}) collective-permute-start(bf16[256,1664]{1,0:T(8,128)(2,1)S(1)} %pad_maximum_fusion.7.refs_0_), channel_id=1, source_target_pairs={{0,2},{1,3},{2,0},{3,1},{4,6},{5,7},{6,4},{7,5},{8,10},{9,11},{10,... | collective-permute-start | bytes 2555912 | tf_op jit(solution)/shard_map/ppermute | solution.py:61
  74.9 37.3 %collective-permute-start.6 = (bf16[256,1664]{1,0:T(8,128)(2,1)S(1)}, bf16[256,1664]{1,0:T(8,128)(2,1)S(1)}, u32[]{:S(2)}, u32[]{:S(2)}) collective-permute-start(bf16[256,1664]{1,0:T(8,128)(2,1)S(1)} %constant_dynamic-update-slice_fusion.refs_1_), channel_id=1, source_target_pairs={{0,4},{1,5},{2,6},{3,7},{4,0},{5,1},{6,2},{7,3},{8,12},{9,13},{10,... | collective-permute-start | bytes 2555912 | tf_op jit(solution)/shard_map/ppermute | solution.py:61
  75.6 36.1 %collective-permute-start.29 = (bf16[128,2048]{1,0:T(8,128)(2,1)S(1)}, bf16[128,2048]{1,0:T(8,128)(2,1)S(1)}, u32[]{:S(2)}, u32[]{:S(2)}) collective-permute-start(bf16[128,2048]{1,0:T(8,128)(2,1)S(1)} %pad_maximum_fusion.15), channel_id=1, source_target_pairs={{0,2},{1,3},{2,0},{3,1},{4,6},{5,7},{6,4},{7,5},{8,10},{9,11},{10,... | collective-permute-start | bytes 1572872 | tf_op jit(solution)/shard_map/ppermute | solution.py:61
  85.0 28.4 %collective-permute-start.26 = (bf16[128,2048]{1,0:T(8,128)(2,1)S(1)}, bf16[128,2048]{1,0:T(8,128)(2,1)S(1)}, u32[]{:S(2)}, u32[]{:S(2)}) collective-permute-start(bf16[128,2048]{1,0:T(8,128)(2,1)S(1)} %pad_maximum_fusion.14), channel_id=1, source_target_pairs={{0,4},{1,5},{2,6},{3,7},{4,0},{5,1},{6,2},{7,3},{8,12},{9,13},{10,... | collective-permute-start | bytes 1572872 | tf_op jit(solution)/shard_map/ppermute | solution.py:61
  86.5 28.6 %collective-permute-start.7 = (bf16[256,1664]{1,0:T(8,128)(2,1)S(1)}, bf16[256,1664]{1,0:T(8,128)(2,1)S(1)}, u32[]{:S(2)}, u32[]{:S(2)}) collective-permute-start(bf16[256,1664]{1,0:T(8,128)(2,1)S(1)} %pad_maximum_fusion.7.refs_0_), channel_id=1, source_target_pairs={{0,1},{1,0},{2,3},{3,2},{4,5},{5,4},{6,7},{7,6},{8,9},{9,8},{10,11... | collective-permute-start | bytes 2555912 | tf_op jit(solution)/shard_map/ppermute | solution.py:61
  113.4 26.0 %collective-permute-start.19 = (bf16[256,2048]{1,0:T(8,128)(2,1)S(1)}, bf16[256,2048]{1,0:T(8,128)(2,1)S(1)}, u32[]{:S(2)}, u32[]{:S(2)}) collective-permute-start(bf16[256,2048]{1,0:T(8,128)(2,1)S(1)} %pad_maximum_fusion.4.refs_0_), channel_id=1, source_target_pairs={{0,2},{1,3},{2,0},{3,1},{4,6},{5,7},{6,4},{7,5},{8,10},{9,11},{10,... | collective-permute-start | bytes 3145736 | tf_op jit(solution)/shard_map/ppermute | solution.py:61
  115.1 26.3 %collective-permute-start.21 = (bf16[256,2048]{1,0:T(8,128)(2,1)S(1)}, bf16[256,2048]{1,0:T(8,128)(2,1)S(1)}, u32[]{:S(2)}, u32[]{:S(2)}) collective-permute-start(bf16[256,2048]{1,0:T(8,128)(2,1)S(1)} %pad_maximum_fusion.4.refs_0_), channel_id=1, source_target_pairs={{0,1},{1,0},{2,3},{3,2},{4,5},{5,4},{6,7},{7,6},{8,9},{9,8},{10,11... | collective-permute-start | bytes 3145736 | tf_op jit(solution)/shard_map/ppermute | solution.py:61
  115.4 25.4 %collective-permute-start.20 = (bf16[256,2048]{1,0:T(8,128)(2,1)S(1)}, bf16[256,2048]{1,0:T(8,128)(2,1)S(1)}, u32[]{:S(2)}, u32[]{:S(2)}) collective-permute-start(bf16[256,2048]{1,0:T(8,128)(2,1)S(1)} %constant_dynamic-update-slice_fusion.3.refs_1_), channel_id=1, source_target_pairs={{0,4},{1,5},{2,6},{3,7},{4,0},{5,1},{6,2},{7,3},{8,12},{9,13},{10,... | collective-permute-start | bytes 3145736 | tf_op jit(solution)/shard_map/ppermute | solution.py:61
  115.9 27.2 %collective-permute-start.22 = (bf16[256,2048]{1,0:T(8,128)(2,1)S(1)}, bf16[256,2048]{1,0:T(8,128)(2,1)S(1)}, u32[]{:S(2)}, u32[]{:S(2)}) collective-permute-start(bf16[256,2048]{1,0:T(8,128)(2,1)S(1)} %constant_dynamic-update-slice_fusion.3.refs_1_), channel_id=1, source_target_pairs={{0,1},{1,0},{2,3},{3,2},{4,5},{5,4},{6,7},{7,6},{8,9},{9,8},{10,11... | collective-permute-start | bytes 3145736 | tf_op jit(solution)/shard_map/ppermute | solution.py:61
  116.5 45.0 %collective-permute-start.30 = (bf16[256,2048]{1,0:T(8,128)(2,1)S(1)}, bf16[256,2048]{1,0:T(8,128)(2,1)S(1)}, u32[]{:S(2)}, u32[]{:S(2)}) collective-permute-start(bf16[256,2048]{1,0:T(8,128)(2,1)S(1)} %pad_maximum_fusion.5.refs_0_), channel_id=1, source_target_pairs={{0,2},{1,3},{2,0},{3,1},{4,6},{5,7},{6,4},{7,5},{8,10},{9,11},{10,... | collective-permute-start | bytes 3145736 | tf_op jit(solution)/shard_map/ppermute | solution.py:61
  139.5 24.3 %collective-permute-start.31 = (bf16[256,2048]{1,0:T(8,128)(2,1)S(1)}, bf16[256,2048]{1,0:T(8,128)(2,1)S(1)}, u32[]{:S(2)}, u32[]{:S(2)}) collective-permute-start(bf16[256,2048]{1,0:T(8,128)(2,1)S(1)} %constant_dynamic-update-slice_fusion.6.refs_1_), channel_id=1, source_target_pairs={{0,4},{1,5},{2,6},{3,7},{4,0},{5,1},{6,2},{7,3},{8,12},{9,13},{10,... | collective-permute-start | bytes 3145736 | tf_op jit(solution)/shard_map/ppermute | solution.py:61
  140.8 22.9 %collective-permute-start.23 = (bf16[256,2048]{1,0:T(8,128)(2,1)S(1)}, bf16[256,2048]{1,0:T(8,128)(2,1)S(1)}, u32[]{:S(2)}, u32[]{:S(2)}) collective-permute-start(bf16[256,2048]{1,0:T(8,128)(2,1)S(1)} %collective-permute-done.19.refs_2_), channel_id=1, source_target_pairs={{0,1},{1,0},{2,3},{3,2},{4,5},{5,4},{6,7},{7,6},{8,9},{9,8},{10,11... | collective-permute-start | bytes 3145736 | tf_op jit(solution)/shard_map/ppermute | solution.py:61
  141.4 24.0 %collective-permute-start.24 = (bf16[256,2048]{1,0:T(8,128)(2,1)S(1)}, bf16[256,2048]{1,0:T(8,128)(2,1)S(1)}, u32[]{:S(2)}, u32[]{:S(2)}) collective-permute-start(bf16[256,2048]{1,0:T(8,128)(2,1)S(1)} %collective-permute-done.20.refs_3_), channel_id=1, source_target_pairs={{0,1},{1,0},{2,3},{3,2},{4,5},{5,4},{6,7},{7,6},{8,9},{9,8},{10,11... | collective-permute-start | bytes 3145736 | tf_op jit(solution)/shard_map/ppermute | solution.py:61
  143.1 29.1 %collective-permute-start.32 = (bf16[256,2048]{1,0:T(8,128)(2,1)S(1)}, bf16[256,2048]{1,0:T(8,128)(2,1)S(1)}, u32[]{:S(2)}, u32[]{:S(2)}) collective-permute-start(bf16[256,2048]{1,0:T(8,128)(2,1)S(1)} %pad_maximum_fusion.5.refs_0_), channel_id=1, source_target_pairs={{0,1},{1,0},{2,3},{3,2},{4,5},{5,4},{6,7},{7,6},{8,9},{9,8},{10,11... | collective-permute-start | bytes 3145736 | tf_op jit(solution)/shard_map/ppermute | solution.py:61
  161.5 18.2 %collective-permute-start.33 = (bf16[256,2048]{1,0:T(8,128)(2,1)S(1)}, bf16[256,2048]{1,0:T(8,128)(2,1)S(1)}, u32[]{:S(2)}, u32[]{:S(2)}) collective-permute-start(bf16[256,2048]{1,0:T(8,128)(2,1)S(1)} %constant_dynamic-update-slice_fusion.6.refs_1_), channel_id=1, source_target_pairs={{0,1},{1,0},{2,3},{3,2},{4,5},{5,4},{6,7},{7,6},{8,9},{9,8},{10,11... | collective-permute-start | bytes 3145736 | tf_op jit(solution)/shard_map/ppermute | solution.py:61
  163.7 16.0 %collective-permute-start.34 = (bf16[256,2048]{1,0:T(8,128)(2,1)S(1)}, bf16[256,2048]{1,0:T(8,128)(2,1)S(1)}, u32[]{:S(2)}, u32[]{:S(2)}) collective-permute-start(bf16[256,2048]{1,0:T(8,128)(2,1)S(1)} %collective-permute-done.30.refs_2_), channel_id=1, source_target_pairs={{0,1},{1,0},{2,3},{3,2},{4,5},{5,4},{6,7},{7,6},{8,9},{9,8},{10,11... | collective-permute-start | bytes 3145736 | tf_op jit(solution)/shard_map/ppermute | solution.py:61
  257.9 29.4 %collective-permute-start.36 = (bf16[2,1,512,512]{3,2,1,0:T(8,128)(2,1)}, bf16[2,1,512,512]{3,2,1,0:T(8,128)(2,1)}, u32[]{:S(2)}, u32[]{:S(2)}) collective-permute-start(bf16[2,1,512,512]{3,2,1,0:T(8,128)(2,1)} %pad_maximum_fusion.6), channel_id=1, source_target_pairs={{0,1},{1,0},{2,3},{3,2},{4,5},{5,4},{6,7},{7,6},{8,9},{9,8},{10,11... | collective-permute-start | bytes 3145736 | tf_op jit(solution)/shard_map/ppermute | solution.py:61
  290.5 40.9 %collective-permute-start.37 = (bf16[1,512,512]{2,1,0:T(8,128)(2,1)}, bf16[1,512,512]{2,1,0:T(8,128)(2,1)S(1)}, u32[]{:S(2)}, u32[]{:S(2)}) collective-permute-start(bf16[1,512,512]{2,1,0:T(8,128)(2,1)} %fusion.51), channel_id=1, source_target_pairs={{0,2},{1,3},{2,0},{3,1},{4,6},{5,7},{6,4},{7,5},{8,10},{9,11},{10,... | collective-permute-start | bytes 1572872 | tf_op jit(solution)/shard_map/ppermute | solution.py:61
  322.9 72.5 %collective-permute-start.51 = (bf16[1024,2048]{1,0:T(8,128)(2,1)}, bf16[1024,2048]{1,0:T(8,128)(2,1)}, u32[]{:S(2)}, u32[]{:S(2)}) collective-permute-start(bf16[1024,2048]{1,0:T(8,128)(2,1)} %get-tuple-element.62), channel_id=1, source_target_pairs={{0,1},{1,0},{2,3},{3,2},{4,5},{5,4},{6,7},{7,6},{8,9},{9,8},{10,11... | collective-permute-start | bytes 12582920 | tf_op jit(solution)/shard_map/ppermute | solution.py:61
  330.8 66.5 %collective-permute-start.59 = (bf16[1024,2048]{1,0:T(8,128)(2,1)}, bf16[1024,2048]{1,0:T(8,128)(2,1)}, u32[]{:S(2)}, u32[]{:S(2)}) collective-permute-start(bf16[1024,2048]{1,0:T(8,128)(2,1)} %get-tuple-element.64), channel_id=1, source_target_pairs={{0,1},{1,0},{2,3},{3,2},{4,5},{5,4},{6,7},{7,6},{8,9},{9,8},{10,11... | collective-permute-start | bytes 12582920 | tf_op jit(solution)/shard_map/ppermute | solution.py:61
  351.4 49.6 %collective-permute-start.38 = (bf16[1024,1664]{1,0:T(8,128)(2,1)}, bf16[1024,1664]{1,0:T(8,128)(2,1)}, u32[]{:S(2)}, u32[]{:S(2)}) collective-permute-start(bf16[1024,1664]{1,0:T(8,128)(2,1)} %get-tuple-element.60), channel_id=1, source_target_pairs={{0,1},{1,0},{2,3},{3,2},{4,5},{5,4},{6,7},{7,6},{8,9},{9,8},{10,11... | collective-permute-start | bytes 10223624 | tf_op jit(solution)/shard_map/ppermute | solution.py:61
  362.7 25.3 %collective-permute-start.48 = (f32[1,128]{1,0:T(1,128)S(1)}, f32[1,128]{1,0:T(1,128)S(1)}, u32[]{:S(2)}, u32[]{:S(2)}) collective-permute-start(f32[1,128]{1,0:T(1,128)S(1)} %add.337), channel_id=1, source_target_pairs={{0,4},{1,5},{2,6},{3,7},{4,0},{5,1},{6,2},{7,3},{8,12},{9,13},{10,... | collective-permute-start | bytes 1544 | tf_op jit(solution)/shard_map/ppermute | solution.py:61
  397.2 26.0 %collective-permute-start.55 = (bf16[256,2048]{1,0:T(8,128)(2,1)S(1)}, bf16[256,2048]{1,0:T(8,128)(2,1)S(1)}, u32[]{:S(2)}, u32[]{:S(2)}) collective-permute-start(bf16[256,2048]{1,0:T(8,128)(2,1)S(1)} %add_convert_fusion.2), channel_id=1, source_target_pairs={{0,4},{1,5},{2,6},{3,7},{4,0},{5,1},{6,2},{7,3},{8,12},{9,13},{10,... | collective-permute-start | bytes 3145736 | tf_op jit(solution)/shard_map/ppermute | solution.py:61
  398.9 46.8 %collective-permute-start.63 = (bf16[256,2048]{1,0:T(8,128)(2,1)S(1)}, bf16[256,2048]{1,0:T(8,128)(2,1)S(1)}, u32[]{:S(2)}, u32[]{:S(2)}) collective-permute-start(bf16[256,2048]{1,0:T(8,128)(2,1)S(1)} %add_convert_fusion), channel_id=1, source_target_pairs={{0,4},{1,5},{2,6},{3,7},{4,0},{5,1},{6,2},{7,3},{8,12},{9,13},{10,... | collective-permute-start | bytes 3145736 | tf_op jit(solution)/shard_map/ppermute | solution.py:61
  402.4 92.8 %collective-permute-start.42 = (bf16[256,1664]{1,0:T(8,128)(2,1)S(1)}, bf16[256,1664]{1,0:T(8,128)(2,1)S(1)}, u32[]{:S(2)}, u32[]{:S(2)}) collective-permute-start(bf16[256,1664]{1,0:T(8,128)(2,1)S(1)} %add_convert_fusion.4), channel_id=1, source_target_pairs={{0,4},{1,5},{2,6},{3,7},{4,0},{5,1},{6,2},{7,3},{8,12},{9,13},{10,... | collective-permute-start | bytes 2555912 | tf_op jit(solution)/shard_map/ppermute | solution.py:61
  425.7 85.8 %collective-permute-start.52 = (bf16[256,2048]{1,0:T(8,128)(2,1)S(1)}, bf16[256,2048]{1,0:T(8,128)(2,1)S(1)}, u32[]{:S(2)}, u32[]{:S(2)}) collective-permute-start(bf16[256,2048]{1,0:T(8,128)(2,1)S(1)} %get-tuple-element.78), channel_id=1, source_target_pairs={{0,2},{1,3},{2,0},{3,1},{4,6},{5,7},{6,4},{7,5},{8,10},{9,11},{10,... | collective-permute-start | bytes 3145736 | tf_op jit(solution)/shard_map/ppermute | solution.py:61
  425.8 37.2 %collective-permute-start.56 = (bf16[128,2048]{1,0:T(8,128)(2,1)S(1)}, bf16[128,2048]{1,0:T(8,128)(2,1)S(1)}, u32[]{:S(2)}, u32[]{:S(2)}) collective-permute-start(bf16[128,2048]{1,0:T(8,128)(2,1)S(1)} %slice.490), channel_id=1, source_target_pairs={{0,2},{1,3},{2,0},{3,1},{4,6},{5,7},{6,4},{7,5},{8,10},{9,11},{10,... | collective-permute-start | bytes 1572872 | tf_op jit(solution)/shard_map/ppermute | solution.py:61
  448.1 65.8 %collective-permute-start.60 = (bf16[256,2048]{1,0:T(8,128)(2,1)S(1)}, bf16[256,2048]{1,0:T(8,128)(2,1)S(1)}, u32[]{:S(2)}, u32[]{:S(2)}) collective-permute-start(bf16[256,2048]{1,0:T(8,128)(2,1)S(1)} %get-tuple-element.76), channel_id=1, source_target_pairs={{0,2},{1,3},{2,0},{3,1},{4,6},{5,7},{6,4},{7,5},{8,10},{9,11},{10,... | collective-permute-start | bytes 3145736 | tf_op jit(solution)/shard_map/ppermute | solution.py:61
  448.3 46.7 %collective-permute-start.64 = (bf16[128,2048]{1,0:T(8,128)(2,1)S(1)}, bf16[128,2048]{1,0:T(8,128)(2,1)S(1)}, u32[]{:S(2)}, u32[]{:S(2)}) collective-permute-start(bf16[128,2048]{1,0:T(8,128)(2,1)S(1)} %slice.488), channel_id=1, source_target_pairs={{0,2},{1,3},{2,0},{3,1},{4,6},{5,7},{6,4},{7,5},{8,10},{9,11},{10,... | collective-permute-start | bytes 1572872 | tf_op jit(solution)/shard_map/ppermute | solution.py:61
  463.2 76.0 %collective-permute-start.58 = (bf16[64,2048]{1,0:T(8,128)(2,1)S(1)}, bf16[64,2048]{1,0:T(8,128)(2,1)S(1)}, u32[]{:S(2)}, u32[]{:S(2)}) collective-permute-start(bf16[64,2048]{1,0:T(8,128)(2,1)S(1)} %get-tuple-element.101), channel_id=1, source_target_pairs={{0,24},{1,25},{2,26},{3,27},{4,28},{5,29},{6,30},{7,31},{8,16},{9,... | collective-permute-start | bytes 786440 | tf_op jit(solution)/shard_map/ppermute | solution.py:61
  495.0 45.7 %collective-permute-start.57 = (bf16[64,2048]{1,0:T(8,128)(2,1)S(1)}, bf16[64,2048]{1,0:T(8,128)(2,1)S(1)}, u32[]{:S(2)}, u32[]{:S(2)}) collective-permute-start(bf16[64,2048]{1,0:T(8,128)(2,1)S(1)} %get-tuple-element.100), channel_id=1, source_target_pairs={{0,16},{1,17},{2,18},{3,19},{4,20},{5,21},{6,22},{7,23},{8,24},{9,... | collective-permute-start | bytes 786440 | tf_op jit(solution)/shard_map/ppermute | solution.py:61
  507.3 42.5 %collective-permute-start.66 = (bf16[64,2048]{1,0:T(8,128)(2,1)S(1)}, bf16[64,2048]{1,0:T(8,128)(2,1)S(1)}, u32[]{:S(2)}, u32[]{:S(2)}) collective-permute-start(bf16[64,2048]{1,0:T(8,128)(2,1)S(1)} %get-tuple-element.99), channel_id=1, source_target_pairs={{0,24},{1,25},{2,26},{3,27},{4,28},{5,29},{6,30},{7,31},{8,16},{9,... | collective-permute-start | bytes 786440 | tf_op jit(solution)/shard_map/ppermute | solution.py:61
  511.5 17.8 %collective-permute-start.39 = (bf16[256,1664]{1,0:T(8,128)(2,1)S(1)}, bf16[256,1664]{1,0:T(8,128)(2,1)S(1)}, u32[]{:S(2)}, u32[]{:S(2)}) collective-permute-start(bf16[256,1664]{1,0:T(8,128)(2,1)S(1)} %get-tuple-element.80), channel_id=1, source_target_pairs={{0,2},{1,3},{2,0},{3,1},{4,6},{5,7},{6,4},{7,5},{8,10},{9,11},{10,... | collective-permute-start | bytes 2555912 | tf_op jit(solution)/shard_map/ppermute | solution.py:61
  513.9 18.1 %collective-permute-start.53 = (bf16[128,2048]{1,0:T(8,128)(2,1)S(1)}, bf16[128,2048]{1,0:T(8,128)(2,1)S(1)}, u32[]{:S(2)}, u32[]{:S(2)}) collective-permute-start(bf16[128,2048]{1,0:T(8,128)(2,1)S(1)} %slice.491), channel_id=1, source_target_pairs={{0,4},{1,5},{2,6},{3,7},{4,0},{5,1},{6,2},{7,3},{8,12},{9,13},{10,... | collective-permute-start | bytes 1572872 | tf_op jit(solution)/shard_map/ppermute | solution.py:61
  532.0 19.3 %collective-permute-start.65 = (bf16[64,2048]{1,0:T(8,128)(2,1)S(1)}, bf16[64,2048]{1,0:T(8,128)(2,1)S(1)}, u32[]{:S(2)}, u32[]{:S(2)}) collective-permute-start(bf16[64,2048]{1,0:T(8,128)(2,1)S(1)} %get-tuple-element.98), channel_id=1, source_target_pairs={{0,16},{1,17},{2,18},{3,19},{4,20},{5,21},{6,22},{7,23},{8,24},{9,... | collective-permute-start | bytes 786440 | tf_op jit(solution)/shard_map/ppermute | solution.py:61
  539.3 22.9 %collective-permute-start.45 = (bf16[64,1664]{1,0:T(8,128)(2,1)S(1)}, bf16[64,1664]{1,0:T(8,128)(2,1)S(1)}, u32[]{:S(2)}, u32[]{:S(2)}) collective-permute-start(bf16[64,1664]{1,0:T(8,128)(2,1)S(1)} %get-tuple-element.111), channel_id=1, source_target_pairs={{0,24},{1,25},{2,26},{3,27},{4,28},{5,29},{6,30},{7,31},{8,16},{9,... | collective-permute-start | bytes 638984 | tf_op jit(solution)/shard_map/ppermute | solution.py:61
  540.8 21.4 %collective-permute-start.44 = (bf16[64,1664]{1,0:T(8,128)(2,1)S(1)}, bf16[64,1664]{1,0:T(8,128)(2,1)S(1)}, u32[]{:S(2)}, u32[]{:S(2)}) collective-permute-start(bf16[64,1664]{1,0:T(8,128)(2,1)S(1)} %get-tuple-element.110), channel_id=1, source_target_pairs={{0,16},{1,17},{2,18},{3,19},{4,20},{5,21},{6,22},{7,23},{8,24},{9,... | collective-permute-start | bytes 638984 | tf_op jit(solution)/shard_map/ppermute | solution.py:61
  (86 other events, 1250.8 us)

commit v4 on v3

--- a/solution.py
+++ b/solution.py
@@ -129,50 +129,102 @@
     )(me, *arrays)
 
 
-def gather_rows(parts, me, devices):
-    part = jnp.concatenate(parts, axis=1)
-    widths = [one.shape[1] for one in parts]
-    if devices != 32:
-        whole = lax.all_gather(part, ("dp", "shard"), axis=0, tiled=True)
-        return jnp.split(whole, [sum(widths[:i]) for i in range(1, len(widths))], axis=1)
-    near = jnp.concatenate([part, swap(part, 8, devices)])
-    far = jnp.concatenate([swap(part, 16, devices), swap(part, 24, devices)])
-    near = jnp.concatenate([near, swap(near, 4, devices)])
-    far = jnp.concatenate([far, swap(far, 2, devices)])
-    near_masks, far_masks = (0, 8, 4, 12), (16, 24, 18, 26)
-    blocks, masks = [near, far], [near_masks, far_masks]
-    blocks += [swap(near, 2, devices), swap(far, 4, devices)]
-    masks += [tuple(m | 2 for m in near_masks), tuple(m | 4 for m in far_masks)]
-    blocks += [swap(block, 1, devices) for block in blocks]
-    masks += [tuple(m | 1 for m in own) for own in masks]
-    return place(blocks, masks, widths, me, part.shape[0] * devices)
-
-
-def reduce_rows(grads, me, devices):
-    if devices != 32:
-        grad = jnp.concatenate([one.astype(jnp.float32) for one in grads], axis=1)
-        return lax.psum_scatter(grad, ("dp", "shard"), scatter_dimension=0, tiled=True)
-    size = grads[0].shape[0] // devices
-    order = [2, 10, 6, 14, 20, 28, 22, 30, 0, 8, 4, 12, 16, 24, 18, 26]
-    keep, send = pick(grads, [order, [m | 1 for m in order]], me, size)
-    came = swap(send, 1, devices)
-
-    def both(low, high):
-        rows = slice(low * size, high * size)
-        return keep[rows].astype(jnp.float32) + came[rows].astype(jnp.float32)
-
-    from_y = swap(both(0, 4).astype(LOW), 2, devices)
-    from_x = swap(both(4, 8).astype(LOW), 4, devices)
-    near = both(8, 12) + from_y.astype(jnp.float32)
-    far = both(12, 16) + from_x.astype(jnp.float32)
-    from_x = swap(near[2 * size :].astype(LOW), 4, devices)
-    from_y = swap(far[2 * size :].astype(LOW), 2, devices)
-    near = near[: 2 * size] + from_x.astype(jnp.float32)
-    far = far[: 2 * size] + from_y.astype(jnp.float32)
-    one = swap(near[size:].astype(LOW), 8, devices)
-    two = swap(far[:size].astype(LOW), 16, devices)
-    three = swap(far[size:].astype(LOW), 24, devices)
-    return (near[:size] + one.astype(jnp.float32)) + (two.astype(jnp.float32) + three.astype(jnp.float32))
+def after(value, *others):
+    others = [one for one in others if one is not None]
+    return lax.optimization_barrier((value, *others))[0] if others else value
+
+
+class Gather:
+    def __init__(self, parts, me, devices):
+        self.part = jnp.concatenate(parts, axis=1)
+        self.widths = [one.shape[1] for one in parts]
+        self.me, self.devices, self.staged = me, devices, devices == 32
+
+    def along_z(self, *others):
+        if self.staged:
+            part = after(self.part, *others)
+            one, two, three = (swap(part, mask, self.devices) for mask in (8, 16, 24))
+            self.near, self.far = jnp.concatenate([part, one]), jnp.concatenate([two, three])
+            return self.near, self.far
+        return ()
+
+    def first_half(self, *others):
+        if self.staged:
+            near, far = after(self.near, *others), after(self.far, *others)
+            self.near = jnp.concatenate([near, swap(near, 4, self.devices)])
+            self.far = jnp.concatenate([far, swap(far, 2, self.devices)])
+            return self.near, self.far
+        return ()
+
+    def second_half(self, *others):
+        if self.staged:
+            near, far = after(self.near, *others), after(self.far, *others)
+            self.blocks = [near, far, swap(near, 2, self.devices), swap(far, 4, self.devices)]
+            return tuple(self.blocks[2:])
+        return ()
+
+    def whole(self, *others):
+        if not self.staged:
+            whole = lax.all_gather(self.part, ("dp", "shard"), axis=0, tiled=True)
+            ends = [sum(self.widths[:i]) for i in range(1, len(self.widths))]
+            return jnp.split(whole, ends, axis=1)
+        masks = [(0, 8, 4, 12), (16, 24, 18, 26), (2, 10, 6, 14), (20, 28, 22, 30)]
+        blocks = self.blocks + [swap(block, 1, self.devices) for block in self.blocks]
+        masks += [tuple(m | 1 for m in own) for own in masks]
+        return place(blocks, masks, self.widths, self.me, self.part.shape[0] * self.devices)
+
+
+class Reduce:
+    def __init__(self, grads, me, devices):
+        self.grads, self.me, self.devices, self.staged = grads, me, devices, devices == 32
+        self.size = grads[0].shape[0] // devices
+
+    def send(self, values, mask):
+        return swap(values, mask, self.devices).astype(jnp.float32)
+
+    def between_cores(self):
+        if not self.staged:
+            grad = jnp.concatenate([one.astype(jnp.float32) for one in self.grads], axis=1)
+            self.total = lax.psum_scatter(grad, ("dp", "shard"), scatter_dimension=0, tiled=True)
+            return ()
+        order = [2, 10, 6, 14, 20, 28, 22, 30, 0, 8, 4, 12, 16, 24, 18, 26]
+        self.keep, send = pick(self.grads, [order, [m | 1 for m in order]], self.me, self.size)
+        self.came = swap(send, 1, self.devices)
+        return (send,)
+
+    def both(self, low, high):
+        rows = slice(low * self.size, high * self.size)
+        return self.keep[rows].astype(jnp.float32) + self.came[rows].astype(jnp.float32)
+
+    def second_half(self):
+        if not self.staged:
+            return ()
+        sent = self.both(0, 4).astype(LOW), self.both(4, 8).astype(LOW)
+        self.from_y, self.from_x = self.send(sent[0], 2), self.send(sent[1], 4)
+        return sent
+
+    def first_half(self):
+        if not self.staged:
+            return ()
+        near, far, size = self.both(8, 12) + self.from_y, self.both(12, 16) + self.from_x, self.size
+        sent = near[2 * size :].astype(LOW), far[2 * size :].astype(LOW)
+        self.near, self.far = near[: 2 * size], far[: 2 * size]
+        self.from_x, self.from_y = self.send(sent[0], 4), self.send(sent[1], 2)
+        return sent
+
+    def along_z(self):
+        if not self.staged:
+            return ()
+        near, far, size = self.near + self.from_x, self.far + self.from_y, self.size
+        sent = near[size:].astype(LOW), far[:size].astype(LOW), far[size:].astype(LOW)
+        self.own = near[:size]
+        self.others = [self.send(one, mask) for one, mask in zip(sent, (8, 16, 24))]
+        return sent
+
+    def result(self):
+        if not self.staged:
+            return self.total
+        return (self.own + self.others[0]) + (self.others[1] + self.others[2])
 
 
 def gather_pieces(part, devices, shards):
@@ -410,19 +462,33 @@
     gain_columns = jnp.concatenate(
         [attn_gain[:, None], ffn_gain[:, None], jnp.zeros((part_len, 126), jnp.float32)], axis=1
     )
-    wqkv, gains = gather_rows([w_qkv.astype(LOW), gain_columns.astype(LOW)], me, devices)
-    wout, wgate = gather_rows([w_out.astype(LOW).T, w_gate.astype(LOW)], me, devices)
-    wup, wdown = gather_rows([w_up.astype(LOW), w_down.astype(LOW).T], me, devices)
+    w_kv = Gather([w_qkv[:, q_width:].astype(LOW), gain_columns.astype(LOW)], me, devices)
+    w_q = Gather([w_qkv[:, :q_width].astype(LOW)], me, devices)
+    w_og = Gather([w_out.astype(LOW).T, w_gate.astype(LOW)], me, devices)
+    w_ud = Gather([w_up.astype(LOW), w_down.astype(LOW).T], me, devices)
+    z_kv = w_kv.along_z()
+    one_kv = w_kv.first_half()
+    z_q = w_q.along_z(*z_kv)
+    two_kv = w_kv.second_half()
+    one_q = w_q.first_half(*two_kv)
+    z_og = w_og.along_z(*z_q)
+    wkv, gains = w_kv.whole()
+    two_q = w_q.second_half()
+    one_og = w_og.first_half(*two_q)
+    z_ud = w_ud.along_z(*z_og)
+    (wq,) = w_q.whole()
     gain_attn = gains[:, 0].astype(jnp.float32)
     gain_ffn = gains[:, 1].astype(jnp.float32)
 
     x_float = tokens.astype(jnp.float32)
     normed_one, inverse_one = normalize(x_float)
     normed_low = (normed_one * gain_attn).astype(LOW)
-    projected = jnp.einsum("rtd,de->ret", normed_low, wqkv, preferred_element_type=jnp.float32)
-    q_raw = projected[:, :q_width].reshape(row_count, HEADS, HD, piece_len)
-    k_raw = projected[:, q_width : q_width + kv_width].reshape(row_count, KV, HD, piece_len)
-    v_raw = projected[:, q_width + kv_width :]
+    kv_raw = jnp.einsum("rtd,de->ret", normed_low, wkv, preferred_element_type=jnp.float32)
+    k_raw = kv_raw[:, :kv_width].reshape(row_count, KV, HD, piece_len)
+    v_raw = kv_raw[:, kv_width:]
+    q_raw = jnp.einsum("rtd,de->ret", normed_low, wq, preferred_element_type=jnp.float32).reshape(
+        row_count, HEADS, HD, piece_len
+    )
     q_unit, q_inverse = normalize(q_raw, 2)
     k_unit, k_inverse = normalize(k_raw, 2)
     q_low = (
@@ -432,7 +498,13 @@
     own_kv = jnp.concatenate([k_low, v_raw.astype(LOW)], axis=1)
     pieces, piece_at = gather_pieces(own_kv, devices, shards)
     info = jnp.concatenate([start.reshape(1), piece_at * piece_len, row_valid]).astype(jnp.int32)
+    two_og = w_og.second_half()
+    q_low = after(q_low, *one_og)
     o_heads, att_low, sums = attention(info, q_low, pieces)
+    wout, wgate = w_og.whole()
+    one_ud = w_ud.first_half(att_low, *two_og)
+    two_ud = w_ud.second_half()
+    wup, wdown = w_ud.whole()
     x_mid = x_float + jnp.einsum("rct,dc->rtd", att_low, wout, preferred_element_type=jnp.float32)
     normed_two, inverse_two = normalize(x_mid)
     ffn_in = (normed_two * gain_ffn).astype(LOW)
@@ -453,9 +525,9 @@
     grad_up = (grad_act * silu_gate).astype(LOW)
     grad_wgate = jnp.einsum("rtd,rtf->df", ffn_in, grad_gate, preferred_element_type=jnp.float32)
     grad_wup = jnp.einsum("rtd,rtf->df", ffn_in, grad_up, preferred_element_type=jnp.float32)
-    one = reduce_rows([grad_down.astype(LOW), grad_wgate.astype(LOW)], me, devices)
-    width = grad_down.shape[1]
-    summed_down, summed_wgate = one[:, :width].T, one[:, width:]
+    red_one = Reduce([grad_down.astype(LOW), grad_wgate.astype(LOW)], me, devices)
+    sent = red_one.between_cores()
+    grad_gate, grad_up = after(grad_gate, *sent), after(grad_up, *sent)
     grad_ffn_in = jnp.einsum(
         "rtf,df->rtd", grad_gate, wgate, preferred_element_type=jnp.float32
     ) + jnp.einsum("rtf,df->rtd", grad_up, wup, preferred_element_type=jnp.float32)
@@ -463,15 +535,25 @@
     grad_mid = grad_out + norm_back(x_mid, inverse_two, grad_ffn_in * gain_ffn)
     mid_low = grad_mid.astype(LOW)
     grad_wout = jnp.einsum("rtd,rct->dc", mid_low, att_low, preferred_element_type=jnp.float32)
-    two = reduce_rows([grad_wup.astype(LOW), grad_wout.astype(LOW)], me, devices)
-    summed_wup, summed_wout = two[:, :width], two[:, width:].T
-    grad_att = jnp.einsum("rtd,dc->rct", mid_low, wout, preferred_element_type=jnp.float32)
+    red_two = Reduce([grad_wup.astype(LOW), grad_wout.astype(LOW)], me, devices)
+    sent_two = red_two.between_cores()
+    sent_one = red_one.second_half()
+    mid_after = after(mid_low, *sent_two, *sent_one)
+    grad_att = jnp.einsum("rtd,dc->rct", mid_after, wout, preferred_element_type=jnp.float32)
     dq_parts, dk_parts, dv_parts = [], [], []
     for group in range(KV):
+        if group == 1:
+            grad_att = after(grad_att, dq_parts[-1], *red_two.second_half())
+        if group == 2:
+            grad_att = after(grad_att, dq_parts[-1], *red_one.first_half())
+        if group == 3:
+            grad_att = after(grad_att, dq_parts[-1])
         dq, dk, dv = attention_back(info, q_low, pieces, o_heads, sums, grad_att, group, 1)
         dq_parts.append(dq)
         dk_parts.append(dk)
         dv_parts.append(dv)
+    sent = red_two.first_half() + red_one.along_z()
+    dq_parts[-1] = after(dq_parts[-1], *sent)
     grad_query = jnp.concatenate(dq_parts, axis=1)
     grad_pieces = jnp.concatenate(dk_parts + dv_parts, axis=2)
     grad_kv = reduce_pieces(grad_pieces, devices, shards)
@@ -486,33 +568,48 @@
     grad_kgain = jnp.sum(grad_k_scaled * k_unit, axis=(0, 1, 3))
     grad_k_raw = norm_back(k_raw, k_inverse, grad_k_scaled * k_gain_h, 2)
     shared = sum_over_devices(jnp.concatenate([grad_qgain, grad_kgain])[None], devices)
-    grad_projected = jnp.concatenate(
-        [
-            grad_q_raw.reshape(row_count, q_width, piece_len),
-            grad_k_raw.reshape(row_count, kv_width, piece_len),
-            grad_kv[:, kv_width:],
-        ],
-        axis=1,
+    grad_q_low = grad_q_raw.reshape(row_count, q_width, piece_len).astype(LOW)
+    grad_kv_low = jnp.concatenate(
+        [grad_k_raw.reshape(row_count, kv_width, piece_len), grad_kv[:, kv_width:]], axis=1
     ).astype(LOW)
-    grad_wqkv = jnp.einsum("rtd,ret->de", normed_low, grad_projected, preferred_element_type=jnp.float32)
-    grad_normed = jnp.einsum("ret,de->rtd", grad_projected, wqkv, preferred_element_type=jnp.float32)
+    grad_wq = jnp.einsum("rtd,ret->de", normed_low, grad_q_low, preferred_element_type=jnp.float32)
+    red_q = Reduce([grad_wq.astype(LOW)], me, devices)
+    sent = red_q.between_cores() + red_two.along_z()
+    grad_kv_low = after(grad_kv_low, *sent)
+    grad_wkv = jnp.einsum("rtd,ret->de", normed_low, grad_kv_low, preferred_element_type=jnp.float32)
+    grad_normed = jnp.einsum(
+        "ret,de->rtd", grad_q_low, wq, preferred_element_type=jnp.float32
+    ) + jnp.einsum("ret,de->rtd", grad_kv_low, wkv, preferred_element_type=jnp.float32)
     grad_gain_one = jnp.sum(grad_normed * normed_one, axis=(0, 1))
-    input_grad = grad_mid + norm_back(x_float, inverse_one, grad_normed * gain_attn)
     grad_gains = jnp.concatenate(
         [grad_gain_one[:, None], grad_gain_two[:, None], jnp.zeros((model_width, 126), jnp.float32)],
         axis=1,
     )
-    three = reduce_rows([grad_wqkv.astype(LOW), grad_gains.astype(LOW)], me, devices)
-    qkv_width = w_qkv.shape[1]
+    red_q.second_half()
+    red_kv = Reduce([grad_wkv.astype(LOW), grad_gains.astype(LOW)], me, devices)
+    sent = red_kv.between_cores()
+    input_grad = grad_mid + norm_back(
+        x_float, inverse_one, after(grad_normed, *sent) * gain_attn
+    )
+    red_q.first_half()
+    red_kv.second_half()
+    red_q.along_z()
+    red_kv.first_half()
+    red_kv.along_z()
+    one, two, three, four = red_one.result(), red_two.result(), red_q.result(), red_kv.result()
+    width = grad_down.shape[1]
+    summed_down, summed_wgate = one[:, :width].T, one[:, width:]
+    summed_wup, summed_wout = two[:, :width], two[:, width:].T
+    tail_width = 2 * kv_width
     return (
         output,
         input_grad,
-        three[:, qkv_width],
-        three[:, :qkv_width],
+        four[:, tail_width],
+        jnp.concatenate([three, four[:, :tail_width]], axis=1),
         shared[0, :HD],
         shared[0, HD:],
         summed_wout,
-        three[:, qkv_width + 1],
+        four[:, tail_width + 1],
         summed_wgate,
         summed_wup,
         summed_down,

time: 574 us -> 493 us (0.86)
  waiting for transfers between devices: 247 us -> 173 us
  matrix products: 66.2 us -> 55.5 us
  Pallas kernels: 48.2 us -> 58.2 us
    ppermute x67 -> x86, waiting for transfers between devices: 247 us -> 173 us  [swap(): lax.ppermute(values, ('dp', 'shard'), [(i, i ^ mask) for i in range(devic...]
    convert_element_type x6 -> x7, other arithmetic: 7.83 us -> 15.1 us  [the longest x4 9.1 us: second_half(): sent = (self.both(0, 4).astype(LOW), self.both(4, 8).astype(LOW))]
    pallas_call x3 -> x4, Pallas kernels: 6.72 us -> 12.3 us  [place(): pl.pallas_call(kernel, out_shape=[jax.ShapeDtypeStruct((total_rows, width...]
    unnamed x150 -> x164, local copies, waits for them, and re-layouts: 22 us -> 17.2 us
    pallas_call x3 -> x4, Pallas kernels: 10.2 us -> 14.7 us  [pick(): pl.pallas_call(kernel, out_shape=[jax.ShapeDtypeStruct((len(own) * size,...]
    ppermute x67 -> x86, starting transfers between devices: 116 us -> 113 us  [swap(): lax.ppermute(values, ('dp', 'shard'), [(i, i ^ mask) for i in range(devic...]
    add x14 -> x15, other arithmetic: 18.9 us -> 15.5 us  [the longest x4 8.16 us: first_half(): self.both(12, 16) + self.from_x]
    dot_general x4 -> x7, matrix products: 16.7 us -> 18.3 us  [the longest x1 4.92 us: local(): jnp.einsum('ret,de->rtd', grad_q_low, wq, preferred_element_type=jnp.floa...]
  transfers between devices with their start and end apart: 67 -> 86, of which waited for: 24 -> 31; matrix products, arithmetic and copies ran while one was open for 16% -> 23% of each run, Pallas kernels for 3% -> 11%
where the time goes in v4:
time: 493 us
  waiting for transfers between devices  173 us (35%)
  starting transfers between devices  113 us (23%)
  other arithmetic  60.1 us (12%)
  Pallas kernels  58.2 us (12%)
  matrix products  55.5 us (11%)
  local copies, waits for them, and re-layouts  30 us (6%)
    ppermute x86, waiting for transfers between devices, swap(): lax.ppermute(values, ('dp', 'shard'), [(i, i ^ mask) for i in range(devic...  173 us
    ppermute x86, starting transfers between devices, swap(): lax.ppermute(values, ('dp', 'shard'), [(i, i ^ mask) for i in range(devic...  113 us
    pallas_call x4, Pallas kernels, attention_back(): pl.pallas_call(kernel, out_shape=[jax.ShapeDtypeStruct((rows, groups * gr...  20.5 us
    unnamed x164, local copies, waits for them, and re-layouts  17.2 us
    pallas_call x4, Pallas kernels, pick(): pl.pallas_call(kernel, out_shape=[jax.ShapeDtypeStruct((len(own) * size,...  14.7 us
    pallas_call x4, Pallas kernels, place(): pl.pallas_call(kernel, out_shape=[jax.ShapeDtypeStruct((total_rows, width...  12.3 us
    pallas_call x1, Pallas kernels, attention(): pl.pallas_call(kernel, out_shape=[jax.ShapeDtypeStruct(queries.shape, jnp...  10.7 us
  transfers between devices with their start and end apart: 86, of which 31 were waited for; matrix products, arithmetic and copies ran while one was open for 23% of the time, Pallas kernels for 11%

profile of v4, /device:TPU:0, one launch (start us, length us, event | category | flops | bytes accessed | tf_op | source)
XLA Modules:
  0.0 493.2 jit_solution(3349706550742094293)
XLA Ops:
  3.4 3.1 collective-permute-start
  25.1 3.7 collective-permute-done.9
  28.8 3.4 collective-permute-start.24
  35.5 14.6 %collective-permute-done.24 = bf16[64,2048]{1,0:T(8,128)(2,1)S(1)} collective-permute-done((bf16[64,2048]{1,0:T(8,128)(2,1)S(1)}, bf16[64,2048]{1,0:T(8,128)(2,1)S(1)}, u32[]{:S(2)}, u32[]{:S(2)}) %collective-permute-start.24) | collective-permute-done | bytes 262176 | tf_op jit(solution)/shard_map/ppermute | solution.py:61
  51.8 7.7 %collective-permute-done.7.refs_3_ = bf16[256,640]{1,0:T(8,128)(2,1)S(1)} collective-permute-done((bf16[256,640]{1,0:T(8,128)(2,1)S(1)}, bf16[256,640]{1,0:T(8,128)(2,1)S(1)}, u32[]{:S(2)}, u32[]{:S(2)}) %collective-permute-start.7) | collective-permute-done | bytes 327712 | tf_op jit(solution)/shard_map/ppermute | solution.py:61
  76.3 5.9 %collective-permute-done.12.refs_2_ = bf16[256,1024]{1,0:T(8,128)(2,1)S(1)} collective-permute-done((bf16[256,1024]{1,0:T(8,128)(2,1)S(1)}, bf16[256,1024]{1,0:T(8,128)(2,1)S(1)}, u32[]{:S(2)}, u32[]{:S(2)}) %collective-permute-start.12) | collective-permute-done | bytes 524320 | tf_op jit(solution)/shard_map/ppermute | solution.py:61
  84.7 6.9 %collective-permute-done.28 = bf16[1,512,512]{2,1,0:T(8,128)(2,1)S(1)} collective-permute-done((bf16[1,512,512]{2,1,0:T(8,128)(2,1)S(1)}, bf16[1,512,512]{2,1,0:T(8,128)(2,1)S(1)}, u32[]{:S(2)}, u32[]{:S(2)}) %collective-permute-start.28) | collective-permute-done | bytes 524320 | tf_op jit(solution)/shard_map/ppermute | solution.py:61
  95.2 5.9 %shard_map.212 = bf16[2048,1024]{1,0:T(8,128)(2,1)S(1)} custom-call(s32[1]{0:T(128)} %bitcast.3.me_ref, bf16[256,1024]{1,0:T(8,128)(2,1)S(1)} %constant_dynamic-update-slice_fusion.7.refs_0_, bf16[256,1024]{1,0:T(8,128)(2,1)S(1)} %constant_dynamic-update-slice_fusion.11.refs_1_, bf16[256,1024]{1,0:T(8,128)(2,1)S(1)} %collective-permute-done.12.refs_2_, ...), custom_call_target="tpu_custom_call" | custom-call | tf_op jit(solution)/shard_map/pallas_call | solution.py:88
  109.3 10.7 %shard_map.214 = (f32[1,1024,512]{2,1,0:T(8,128)S(1)}, bf16[1,1024,512]{2,1,0:T(8,128)(2,1)S(1)}, f32[1,4,4,512]{3,2,1,0:T(4,128)S(1)}) custom-call(s32[6]{0:T(128)S(1)} %pad_add_fusion.info_ref, bf16[1,1024,512]{2,1,0:T(8,128)(2,1)S(1)} %bitcast.250, bf16[4,1,512,512]{3,2,1,0:T(8,128)(2,1)S(1)} %pad_maximum_fusion.1.k_ref.v_ref, ...), custom_call_target="tpu_custom_call" | custom-call | flops 16777216000 | bytes 10485760 | tf_op jit(solution)/shard_map/pallas_call | solution.py:317
  120.0 12.3 %collective-permute-done.30.refs_2_ = bf16[256,2048]{1,0:T(8,128)(2,1)S(1)} collective-permute-done((bf16[256,2048]{1,0:T(8,128)(2,1)S(1)}, bf16[256,2048]{1,0:T(8,128)(2,1)S(1)}, u32[]{:S(2)}, u32[]{:S(2)}) %collective-permute-start.30) | collective-permute-done | bytes 1048608 | tf_op jit(solution)/shard_map/ppermute | solution.py:61
  133.1 4.6 collective-permute-start.40
  137.9 7.8 %collective-permute-done.37 = bf16[128,2048]{1,0:T(8,128)(2,1)S(1)} collective-permute-done((bf16[128,2048]{1,0:T(8,128)(2,1)S(1)}, bf16[128,2048]{1,0:T(8,128)(2,1)S(1)}, u32[]{:S(2)}, u32[]{:S(2)}) %collective-permute-start.37) | collective-permute-done | bytes 524320 | tf_op jit(solution)/shard_map/ppermute | solution.py:61
  145.7 4.2 collective-permute-done.40
  155.6 18.9 %collective-permute-done.41.refs_2_ = bf16[256,2048]{1,0:T(8,128)(2,1)S(1)} collective-permute-done((bf16[256,2048]{1,0:T(8,128)(2,1)S(1)}, bf16[256,2048]{1,0:T(8,128)(2,1)S(1)}, u32[]{:S(2)}, u32[]{:S(2)}) %collective-permute-start.41) | collective-permute-done | bytes 1048608 | tf_op jit(solution)/shard_map/ppermute | solution.py:61
  188.6 3.2 multiply_convert_fusion.2
  199.4 3.5 shard_map.217
  203.4 5.8 %fusion.39 = f32[512,2048]{1,0:T(8,128)} fusion(bf16[2048,1024]{1,0:T(8,128)(2,1)S(1)} %get-tuple-element.74, bf16[1,512,1024]{2,1,0:T(8,128)(2,1)} %bitcast.272), kind=kOutput, calls=%fused_computation.97 | convolution fusion | flops 2147483648 | bytes 9437184 | tf_op jit(solution)/shard_map/rtf,df->rtd/dot_general | solution.py:533
  209.3 7.3 %fusion.9 = (bf16[2048]{0:T(1024)(128)(2,1)S(1)}, f32[512]{0:T(512)S(1)}, f32[512,2048]{1,0:T(8,128)}) fusion(f32[1,512,2048]{2,1,0:T(8,128)S(1)} %copy-done.12, f32[512]{0:T(512)S(1)} %get-tuple-element.177, f32[2048]{0:T(1024)S(1)} %get-tuple-element.109, f32[512,2048]{1,0:T(8,128)} %fusion.39, bf16[2048,1024]{1,0:T(8,128)(2,1)S(1)} %get-tuple-element.70, ...), kind=kOutput, calls=%fused_computation.15 | convolution fusion | flops 2154821120 | bytes 17842176 | tf_op jit(solution)/shard_map/rtf,df->rtd/dot_general | solution.py:531
  216.5 5.0 %fusion.74 = (bf16[1,512,2048]{2,1,0:T(8,128)(2,1)S(1)}, f32[1,512,2048]{2,1,0:T(8,128)}) fusion(f32[512]{0:T(512)S(1)} %broadcast_multiply_fusion.8, f32[1,512,2048]{2,1,0:T(8,128)S(1)} %copy-done.12, f32[512]{0:T(512)S(1)} %get-tuple-element.176, f32[512,2048]{1,0:T(8,128)} %get-tuple-element.182, f32[2048]{0:T(1024)S(1)} %get-tuple-element.109, ...), kind=kLoop, calls=%fused_computation.251 | loop fusion | flops 9437184 | bytes 16793600 | tf_op jit(solution)/shard_map/convert_element_type | solution.py:536
  225.3 3.7 shard_map.218
  230.4 3.7 fusion.12
  234.1 4.0 add_convert_fusion.2
  241.4 3.8 add_convert_fusion
  248.3 5.2 %shard_map.219 = (f32[1,256,512]{2,1,0:T(8,128)S(1)}, f32[4,1,64,512]{3,2,1,0:T(8,128)S(1)}, f32[4,1,64,512]{3,2,1,0:T(8,128)S(1)}) custom-call(s32[6]{0:T(128)S(1)} %pad_add_fusion.info_ref, bf16[1,1024,512]{2,1,0:T(8,128)(2,1)S(1)} %bitcast.251, bf16[4,1,512,512]{3,2,1,0:T(8,128)(2,1)S(1)} %pad_maximum_fusion.1.k_ref.v_ref, ...), custom_call_target="tpu_custom_call" | custom-call | flops 10485760000 | bytes 10485760 | tf_op jit(solution)/shard_map/pallas_call | solution.py:394
  254.4 5.4 %shard_map.220 = (f32[1,256,512]{2,1,0:T(8,128)S(1)}, f32[4,1,64,512]{3,2,1,0:T(8,128)S(1)}, f32[4,1,64,512]{3,2,1,0:T(8,128)S(1)}) custom-call(s32[6]{0:T(128)S(1)} %pad_add_fusion.info_ref, bf16[1,1024,512]{2,1,0:T(8,128)(2,1)S(1)} %bitcast.252, bf16[4,1,512,512]{3,2,1,0:T(8,128)(2,1)S(1)} %pad_maximum_fusion.1.k_ref.v_ref, ...), custom_call_target="tpu_custom_call" | custom-call | flops 10485760000 | bytes 10485760 | tf_op jit(solution)/shard_map/pallas_call | solution.py:394
  260.6 3.6 collective-permute-done.50
  265.2 3.3 convert_add_fusion.3
  271.5 7.3 %collective-permute-start.54 = (bf16[128,2048]{1,0:T(8,128)(2,1)}, bf16[128,2048]{1,0:T(8,128)(2,1)}, u32[]{:S(2)}, u32[]{:S(2)}) collective-permute-start(bf16[128,2048]{1,0:T(8,128)(2,1)} %slice.590), channel_id=1, source_target_pairs={{0,2},{1,3},{2,0},{3,1},{4,6},{5,7},{6,4},{7,5},{8,10},{9,11},{10,... | collective-permute-start | bytes 1572872 | tf_op jit(solution)/shard_map/ppermute | solution.py:61
  278.8 4.9 shard_map.221
  283.8 5.1 %shard_map.222 = (f32[1,256,512]{2,1,0:T(8,128)S(1)}, f32[4,1,64,512]{3,2,1,0:T(8,128)S(1)}, f32[4,1,64,512]{3,2,1,0:T(8,128)S(1)}) custom-call(s32[6]{0:T(128)S(1)} %pad_add_fusion.info_ref, bf16[1,1024,512]{2,1,0:T(8,128)(2,1)S(1)} %bitcast.254, bf16[4,1,512,512]{3,2,1,0:T(8,128)(2,1)S(1)} %pad_maximum_fusion.1.k_ref.v_ref, ...), custom_call_target="tpu_custom_call" | custom-call | flops 10485760000 | bytes 10485760 | tf_op jit(solution)/shard_map/pallas_call | solution.py:394
  297.4 9.8 %collective-permute-start.55 = (bf16[2,1,512,512]{3,2,1,0:T(8,128)(2,1)}, bf16[2,1,512,512]{3,2,1,0:T(8,128)(2,1)}, u32[]{:S(2)}, u32[]{:S(2)}) collective-permute-start(bf16[2,1,512,512]{3,2,1,0:T(8,128)(2,1)} %pad_maximum_fusion.3), channel_id=1, source_target_pairs={{0,1},{1,0},{2,3},{3,2},{4,5},{5,4},{6,7},{7,6},{8,9},{9,8},{10,11... | collective-permute-start | bytes 3145736 | tf_op jit(solution)/shard_map/ppermute | solution.py:61
  310.9 11.4 %collective-permute-start.58 = (bf16[128,2048]{1,0:T(8,128)(2,1)S(1)}, bf16[128,2048]{1,0:T(8,128)(2,1)S(1)}, u32[]{:S(2)}, u32[]{:S(2)}) collective-permute-start(bf16[128,2048]{1,0:T(8,128)(2,1)S(1)} %slice.588), channel_id=1, source_target_pairs={{0,2},{1,3},{2,0},{3,1},{4,6},{5,7},{6,4},{7,5},{8,10},{9,11},{10,... | collective-permute-start | bytes 1572872 | tf_op jit(solution)/shard_map/ppermute | solution.py:61
  325.1 3.9 collective-permute-start.85
  329.7 4.4 collective-permute-done.58
  337.0 3.9 collective-permute-start.82
  346.6 5.9 %shard_map.223 = (bf16[1024,1024]{1,0:T(8,128)(2,1)S(1)}, bf16[1024,1024]{1,0:T(8,128)(2,1)S(1)}) custom-call(s32[1]{0:T(128)} %bitcast.3.me_ref, bf16[2048,1024]{1,0:T(8,128)(2,1)S(1)} %convolution_convert_fusion.refs_0_), custom_call_target="tpu_custom_call" | custom-call | tf_op jit(solution)/shard_map/pallas_call | solution.py:122
  353.9 5.5 %collective-permute-start.84 = (bf16[64,2048]{1,0:T(8,128)(2,1)}, bf16[64,2048]{1,0:T(8,128)(2,1)S(1)}, u32[]{:S(2)}, u32[]{:S(2)}) collective-permute-start(bf16[64,2048]{1,0:T(8,128)(2,1)} %get-tuple-element.149), channel_id=1, source_target_pairs={{0,16},{1,17},{2,18},{3,19},{4,20},{5,21},{6,22},{7,23},{8,24},{9,... | collective-permute-start | bytes 786440 | tf_op jit(solution)/shard_map/ppermute | solution.py:61
  359.4 9.2 %collective-permute-done.81 = bf16[64,2048]{1,0:T(8,128)(2,1)} collective-permute-done((bf16[64,2048]{1,0:T(8,128)(2,1)}, bf16[64,2048]{1,0:T(8,128)(2,1)}, u32[]{:S(2)}, u32[]{:S(2)}) %collective-permute-start.81) | collective-permute-done | bytes 262176 | tf_op jit(solution)/shard_map/ppermute | solution.py:61
  374.9 3.6 collective-permute-done.83
  379.4 7.0 %collective-permute-done.56 = bf16[1,512,512]{2,1,0:T(8,128)(2,1)S(1)} collective-permute-done((bf16[1,512,512]{2,1,0:T(8,128)(2,1)S(1)}, bf16[1,512,512]{2,1,0:T(8,128)(2,1)S(1)}, u32[]{:S(2)}, u32[]{:S(2)}) %collective-permute-start.56) | collective-permute-done | bytes 524320 | tf_op jit(solution)/shard_map/ppermute | solution.py:61
  393.2 4.9 fusion.3
  399.4 3.4 collective-permute-start.75
  404.2 3.2 convolution_convert_fusion.5.refs_0_
  427.0 15.5 %collective-permute-done.63 = bf16[256,640]{1,0:T(8,128)(2,1)S(1)} collective-permute-done((bf16[256,640]{1,0:T(8,128)(2,1)S(1)}, bf16[256,640]{1,0:T(8,128)(2,1)S(1)}, u32[]{:S(2)}, u32[]{:S(2)}) %collective-permute-start.63) | collective-permute-done | bytes 327712 | tf_op jit(solution)/shard_map/ppermute | solution.py:61
  450.8 15.9 %collective-permute-done.72 = bf16[128,1024]{1,0:T(8,128)(2,1)S(1)} collective-permute-done((bf16[128,1024]{1,0:T(8,128)(2,1)S(1)}, bf16[128,1024]{1,0:T(8,128)(2,1)S(1)}, u32[]{:S(2)}, u32[]{:S(2)}) %collective-permute-start.72) | collective-permute-done | bytes 262176 | tf_op jit(solution)/shard_map/ppermute | solution.py:61
  466.8 5.7 %collective-permute-done.60 = bf16[256,640]{1,0:T(8,128)(2,1)S(1)} collective-permute-done((bf16[256,640]{1,0:T(8,128)(2,1)S(1)}, bf16[256,640]{1,0:T(8,128)(2,1)S(1)}, u32[]{:S(2)}, u32[]{:S(2)}) %collective-permute-start.60) | collective-permute-done | bytes 327712 | tf_op jit(solution)/shard_map/ppermute | solution.py:61
  479.3 4.4 collective-permute-done.69
  485.9 4.6 collective-permute-done.62
  (472 shorter events, 183.1 us)
Async XLA Ops:
  28.8 21.3 %collective-permute-start.24 = (bf16[64,2048]{1,0:T(8,128)(2,1)S(1)}, bf16[64,2048]{1,0:T(8,128)(2,1)S(1)}, u32[]{:S(2)}, u32[]{:S(2)}) collective-permute-start(bf16[64,2048]{1,0:T(8,128)(2,1)S(1)} %pad_maximum_fusion.12), channel_id=1, source_target_pairs={{0,16},{1,17},{2,18},{3,19},{4,20},{5,21},{6,22},{7,23},{8,24},{9,... | collective-permute-start | bytes 786440 | tf_op jit(solution)/shard_map/ppermute | solution.py:61
  32.2 19.4 %collective-permute-start.22 = (bf16[64,2048]{1,0:T(8,128)(2,1)S(1)}, bf16[64,2048]{1,0:T(8,128)(2,1)S(1)}, u32[]{:S(2)}, u32[]{:S(2)}) collective-permute-start(bf16[64,2048]{1,0:T(8,128)(2,1)S(1)} %pad_maximum_fusion.12), channel_id=1, source_target_pairs={{0,8},{1,9},{2,10},{3,11},{4,12},{5,13},{6,14},{7,15},{8,0},{9,1},... | collective-permute-start | bytes 786440 | tf_op jit(solution)/shard_map/ppermute | solution.py:61
  32.3 29.2 %collective-permute-start.25 = (bf16[64,2048]{1,0:T(8,128)(2,1)S(1)}, bf16[64,2048]{1,0:T(8,128)(2,1)S(1)}, u32[]{:S(2)}, u32[]{:S(2)}) collective-permute-start(bf16[64,2048]{1,0:T(8,128)(2,1)S(1)} %pad_maximum_fusion.12), channel_id=1, source_target_pairs={{0,24},{1,25},{2,26},{3,27},{4,28},{5,29},{6,30},{7,31},{8,16},{9,... | collective-permute-start | bytes 786440 | tf_op jit(solution)/shard_map/ppermute | solution.py:61
  33.9 17.9 %collective-permute-start.5 = (bf16[256,640]{1,0:T(8,128)(2,1)S(1)}, bf16[256,640]{1,0:T(8,128)(2,1)S(1)}, u32[]{:S(2)}, u32[]{:S(2)}) collective-permute-start(bf16[256,640]{1,0:T(8,128)(2,1)S(1)} %pad_maximum_fusion.11.refs_0_), channel_id=1, source_target_pairs={{0,2},{1,3},{2,0},{3,1},{4,6},{5,7},{6,4},{7,5},{8,10},{9,11},{10,... | collective-permute-start | bytes 983048 | tf_op jit(solution)/shard_map/ppermute | solution.py:61
  35.5 32.5 %collective-permute-start.18 = (bf16[256,640]{1,0:T(8,128)(2,1)S(1)}, bf16[256,640]{1,0:T(8,128)(2,1)S(1)}, u32[]{:S(2)}, u32[]{:S(2)}) collective-permute-start(bf16[256,640]{1,0:T(8,128)(2,1)S(1)} %pad_maximum_fusion.11.refs_0_), channel_id=1, source_target_pairs={{0,1},{1,0},{2,3},{3,2},{4,5},{5,4},{6,7},{7,6},{8,9},{9,8},{10,11... | collective-permute-start | bytes 983048 | tf_op jit(solution)/shard_map/ppermute | solution.py:61
  51.6 17.9 %collective-permute-start.19 = (bf16[256,640]{1,0:T(8,128)(2,1)S(1)}, bf16[256,640]{1,0:T(8,128)(2,1)S(1)}, u32[]{:S(2)}, u32[]{:S(2)}) collective-permute-start(bf16[256,640]{1,0:T(8,128)(2,1)S(1)} %constant_dynamic-update-slice_fusion.4.refs_1_), channel_id=1, source_target_pairs={{0,1},{1,0},{2,3},{3,2},{4,5},{5,4},{6,7},{7,6},{8,9},{9,8},{10,11... | collective-permute-start | bytes 983048 | tf_op jit(solution)/shard_map/ppermute | solution.py:61
  69.6 14.5 %collective-permute-start.14 = (bf16[256,1024]{1,0:T(8,128)(2,1)S(1)}, bf16[256,1024]{1,0:T(8,128)(2,1)S(1)}, u32[]{:S(2)}, u32[]{:S(2)}) collective-permute-start(bf16[256,1024]{1,0:T(8,128)(2,1)S(1)} %constant_dynamic-update-slice_fusion.7.refs_0_), channel_id=1, source_target_pairs={{0,1},{1,0},{2,3},{3,2},{4,5},{5,4},{6,7},{7,6},{8,9},{9,8},{10,11... | collective-permute-start | bytes 1572872 | tf_op jit(solution)/shard_map/ppermute | solution.py:61
  69.6 14.3 %collective-permute-start.13 = (bf16[256,1024]{1,0:T(8,128)(2,1)S(1)}, bf16[256,1024]{1,0:T(8,128)(2,1)S(1)}, u32[]{:S(2)}, u32[]{:S(2)}) collective-permute-start(bf16[256,1024]{1,0:T(8,128)(2,1)S(1)} %constant_dynamic-update-slice_fusion.11.refs_1_), channel_id=1, source_target_pairs={{0,4},{1,5},{2,6},{3,7},{4,0},{5,1},{6,2},{7,3},{8,12},{9,13},{10,... | collective-permute-start | bytes 1572872 | tf_op jit(solution)/shard_map/ppermute | solution.py:61
  69.9 14.3 %collective-permute-start.15 = (bf16[256,1024]{1,0:T(8,128)(2,1)S(1)}, bf16[256,1024]{1,0:T(8,128)(2,1)S(1)}, u32[]{:S(2)}, u32[]{:S(2)}) collective-permute-start(bf16[256,1024]{1,0:T(8,128)(2,1)S(1)} %constant_dynamic-update-slice_fusion.11.refs_1_), channel_id=1, source_target_pairs={{0,1},{1,0},{2,3},{3,2},{4,5},{5,4},{6,7},{7,6},{8,9},{9,8},{10,11... | collective-permute-start | bytes 1572872 | tf_op jit(solution)/shard_map/ppermute | solution.py:61
  75.8 15.9 %collective-permute-start.28 = (bf16[1,512,512]{2,1,0:T(8,128)(2,1)S(1)}, bf16[1,512,512]{2,1,0:T(8,128)(2,1)S(1)}, u32[]{:S(2)}, u32[]{:S(2)}) collective-permute-start(bf16[1,512,512]{2,1,0:T(8,128)(2,1)S(1)} %get-tuple-element.155), channel_id=1, source_target_pairs={{0,2},{1,3},{2,0},{3,1},{4,6},{5,7},{6,4},{7,5},{8,10},{9,11},{10,... | collective-permute-start | bytes 1572872 | tf_op jit(solution)/shard_map/ppermute | solution.py:61
  84.1 48.9 %collective-permute-start.39 = (bf16[64,2048]{1,0:T(8,128)(2,1)S(1)}, bf16[64,2048]{1,0:T(8,128)(2,1)S(1)}, u32[]{:S(2)}, u32[]{:S(2)}) collective-permute-start(bf16[64,2048]{1,0:T(8,128)(2,1)S(1)} %pad_maximum_fusion.13), channel_id=1, source_target_pairs={{0,24},{1,25},{2,26},{3,27},{4,28},{5,29},{6,30},{7,31},{8,16},{9,... | collective-permute-start | bytes 786440 | tf_op jit(solution)/shard_map/ppermute | solution.py:61
  84.2 24.4 %collective-permute-start.27 = (bf16[1,512,512]{2,1,0:T(8,128)(2,1)S(1)}, bf16[1,512,512]{2,1,0:T(8,128)(2,1)S(1)}, u32[]{:S(2)}, u32[]{:S(2)}) collective-permute-start(bf16[1,512,512]{2,1,0:T(8,128)(2,1)S(1)} %get-tuple-element.155), channel_id=1, source_target_pairs={{0,1},{1,0},{2,3},{3,2},{4,5},{5,4},{6,7},{7,6},{8,9},{9,8},{10,11... | collective-permute-start | bytes 1572872 | tf_op jit(solution)/shard_map/ppermute | solution.py:61
  91.7 14.9 %collective-permute-start.23 = (bf16[128,2048]{1,0:T(8,128)(2,1)S(1)}, bf16[128,2048]{1,0:T(8,128)(2,1)S(1)}, u32[]{:S(2)}, u32[]{:S(2)}) collective-permute-start(bf16[128,2048]{1,0:T(8,128)(2,1)S(1)} %constant_dynamic-update-slice_fusion.13), channel_id=1, source_target_pairs={{0,4},{1,5},{2,6},{3,7},{4,0},{5,1},{6,2},{7,3},{8,12},{9,13},{10,... | collective-permute-start | bytes 1572872 | tf_op jit(solution)/shard_map/ppermute | solution.py:61
  106.6 26.4 %collective-permute-start.38 = (bf16[64,2048]{1,0:T(8,128)(2,1)S(1)}, bf16[64,2048]{1,0:T(8,128)(2,1)S(1)}, u32[]{:S(2)}, u32[]{:S(2)}) collective-permute-start(bf16[64,2048]{1,0:T(8,128)(2,1)S(1)} %pad_maximum_fusion.13), channel_id=1, source_target_pairs={{0,16},{1,17},{2,18},{3,19},{4,20},{5,21},{6,22},{7,23},{8,24},{9,... | collective-permute-start | bytes 786440 | tf_op jit(solution)/shard_map/ppermute | solution.py:61
  107.0 25.4 %collective-permute-start.30 = (bf16[256,2048]{1,0:T(8,128)(2,1)S(1)}, bf16[256,2048]{1,0:T(8,128)(2,1)S(1)}, u32[]{:S(2)}, u32[]{:S(2)}) collective-permute-start(bf16[256,2048]{1,0:T(8,128)(2,1)S(1)} %constant_dynamic-update-slice_fusion.15.refs_0_), channel_id=1, source_target_pairs={{0,2},{1,3},{2,0},{3,1},{4,6},{5,7},{6,4},{7,5},{8,10},{9,11},{10,... | collective-permute-start | bytes 3145736 | tf_op jit(solution)/shard_map/ppermute | solution.py:61
  108.6 24.1 %collective-permute-start.31 = (bf16[256,2048]{1,0:T(8,128)(2,1)S(1)}, bf16[256,2048]{1,0:T(8,128)(2,1)S(1)}, u32[]{:S(2)}, u32[]{:S(2)}) collective-permute-start(bf16[256,2048]{1,0:T(8,128)(2,1)S(1)} %constant_dynamic-update-slice_fusion.19.refs_1_), channel_id=1, source_target_pairs={{0,4},{1,5},{2,6},{3,7},{4,0},{5,1},{6,2},{7,3},{8,12},{9,13},{10,... | collective-permute-start | bytes 3145736 | tf_op jit(solution)/shard_map/ppermute | solution.py:61
  109.0 42.7 %collective-permute-start.32 = (bf16[256,2048]{1,0:T(8,128)(2,1)S(1)}, bf16[256,2048]{1,0:T(8,128)(2,1)S(1)}, u32[]{:S(2)}, u32[]{:S(2)}) collective-permute-start(bf16[256,2048]{1,0:T(8,128)(2,1)S(1)} %constant_dynamic-update-slice_fusion.15.refs_0_), channel_id=1, source_target_pairs={{0,1},{1,0},{2,3},{3,2},{4,5},{5,4},{6,7},{7,6},{8,9},{9,8},{10,11... | collective-permute-start | bytes 3145736 | tf_op jit(solution)/shard_map/ppermute | solution.py:61
  133.0 19.7 %collective-permute-start.33 = (bf16[256,2048]{1,0:T(8,128)(2,1)S(1)}, bf16[256,2048]{1,0:T(8,128)(2,1)S(1)}, u32[]{:S(2)}, u32[]{:S(2)}) collective-permute-start(bf16[256,2048]{1,0:T(8,128)(2,1)S(1)} %constant_dynamic-update-slice_fusion.19.refs_1_), channel_id=1, source_target_pairs={{0,1},{1,0},{2,3},{3,2},{4,5},{5,4},{6,7},{7,6},{8,9},{9,8},{10,11... | collective-permute-start | bytes 3145736 | tf_op jit(solution)/shard_map/ppermute | solution.py:61
  133.1 16.8 %collective-permute-start.40 = (bf16[128,2048]{1,0:T(8,128)(2,1)S(1)}, bf16[128,2048]{1,0:T(8,128)(2,1)S(1)}, u32[]{:S(2)}, u32[]{:S(2)}) collective-permute-start(bf16[128,2048]{1,0:T(8,128)(2,1)S(1)} %pad_maximum_fusion.7), channel_id=1, source_target_pairs={{0,2},{1,3},{2,0},{3,1},{4,6},{5,7},{6,4},{7,5},{8,10},{9,11},{10,... | collective-permute-start | bytes 1572872 | tf_op jit(solution)/shard_map/ppermute | solution.py:61
  137.8 15.1 %collective-permute-start.34 = (bf16[256,2048]{1,0:T(8,128)(2,1)S(1)}, bf16[256,2048]{1,0:T(8,128)(2,1)S(1)}, u32[]{:S(2)}, u32[]{:S(2)}) collective-permute-start(bf16[256,2048]{1,0:T(8,128)(2,1)S(1)} %collective-permute-done.30.refs_2_), channel_id=1, source_target_pairs={{0,1},{1,0},{2,3},{3,2},{4,5},{5,4},{6,7},{7,6},{8,9},{9,8},{10,11... | collective-permute-start | bytes 3145736 | tf_op jit(solution)/shard_map/ppermute | solution.py:61
  149.9 24.6 %collective-permute-start.41 = (bf16[256,2048]{1,0:T(8,128)(2,1)S(1)}, bf16[256,2048]{1,0:T(8,128)(2,1)S(1)}, u32[]{:S(2)}, u32[]{:S(2)}) collective-permute-start(bf16[256,2048]{1,0:T(8,128)(2,1)S(1)} %constant_dynamic-update-slice_fusion.21.refs_0_), channel_id=1, source_target_pairs={{0,2},{1,3},{2,0},{3,1},{4,6},{5,7},{6,4},{7,5},{8,10},{9,11},{10,... | collective-permute-start | bytes 3145736 | tf_op jit(solution)/shard_map/ppermute | solution.py:61
  151.7 24.1 %collective-permute-start.42 = (bf16[256,2048]{1,0:T(8,128)(2,1)S(1)}, bf16[256,2048]{1,0:T(8,128)(2,1)S(1)}, u32[]{:S(2)}, u32[]{:S(2)}) collective-permute-start(bf16[256,2048]{1,0:T(8,128)(2,1)S(1)} %constant_dynamic-update-slice_fusion.23.refs_1_), channel_id=1, source_target_pairs={{0,4},{1,5},{2,6},{3,7},{4,0},{5,1},{6,2},{7,3},{8,12},{9,13},{10,... | collective-permute-start | bytes 3145736 | tf_op jit(solution)/shard_map/ppermute | solution.py:61
  152.7 27.7 %collective-permute-start.43 = (bf16[256,2048]{1,0:T(8,128)(2,1)S(1)}, bf16[256,2048]{1,0:T(8,128)(2,1)S(1)}, u32[]{:S(2)}, u32[]{:S(2)}) collective-permute-start(bf16[256,2048]{1,0:T(8,128)(2,1)S(1)} %constant_dynamic-update-slice_fusion.21.refs_0_), channel_id=1, source_target_pairs={{0,1},{1,0},{2,3},{3,2},{4,5},{5,4},{6,7},{7,6},{8,9},{9,8},{10,11... | collective-permute-start | bytes 3145736 | tf_op jit(solution)/shard_map/ppermute | solution.py:61
  152.8 27.6 %collective-permute-start.44 = (bf16[256,2048]{1,0:T(8,128)(2,1)S(1)}, bf16[256,2048]{1,0:T(8,128)(2,1)S(1)}, u32[]{:S(2)}, u32[]{:S(2)}) collective-permute-start(bf16[256,2048]{1,0:T(8,128)(2,1)S(1)} %constant_dynamic-update-slice_fusion.23.refs_1_), channel_id=1, source_target_pairs={{0,1},{1,0},{2,3},{3,2},{4,5},{5,4},{6,7},{7,6},{8,9},{9,8},{10,11... | collective-permute-start | bytes 3145736 | tf_op jit(solution)/shard_map/ppermute | solution.py:61
  202.9 31.2 %collective-permute-start.47 = (bf16[1024,2048]{1,0:T(8,128)(2,1)}, bf16[1024,2048]{1,0:T(8,128)(2,1)}, u32[]{:S(2)}, u32[]{:S(2)}) collective-permute-start(bf16[1024,2048]{1,0:T(8,128)(2,1)} %get-tuple-element.76), channel_id=1, source_target_pairs={{0,1},{1,0},{2,3},{3,2},{4,5},{5,4},{6,7},{7,6},{8,9},{9,8},{10,11... | collective-permute-start | bytes 12582920 | tf_op jit(solution)/shard_map/ppermute | solution.py:61
  238.0 26.2 %collective-permute-start.50 = (bf16[256,2048]{1,0:T(8,128)(2,1)}, bf16[256,2048]{1,0:T(8,128)(2,1)S(1)}, u32[]{:S(2)}, u32[]{:S(2)}) collective-permute-start(bf16[256,2048]{1,0:T(8,128)(2,1)} %get-tuple-element.121), channel_id=1, source_target_pairs={{0,4},{1,5},{2,6},{3,7},{4,0},{5,1},{6,2},{7,3},{8,12},{9,13},{10,... | collective-permute-start | bytes 3145736 | tf_op jit(solution)/shard_map/ppermute | solution.py:61
  238.4 26.8 %collective-permute-start.49 = (bf16[256,2048]{1,0:T(8,128)(2,1)}, bf16[256,2048]{1,0:T(8,128)(2,1)}, u32[]{:S(2)}, u32[]{:S(2)}) collective-permute-start(bf16[256,2048]{1,0:T(8,128)(2,1)} %get-tuple-element.122), channel_id=1, source_target_pairs={{0,2},{1,3},{2,0},{3,1},{4,6},{5,7},{6,4},{7,5},{8,10},{9,11},{10,... | collective-permute-start | bytes 3145736 | tf_op jit(solution)/shard_map/ppermute | solution.py:61
  245.2 62.1 %collective-permute-start.52 = (bf16[256,2048]{1,0:T(8,128)(2,1)}, bf16[256,2048]{1,0:T(8,128)(2,1)S(1)}, u32[]{:S(2)}, u32[]{:S(2)}) collective-permute-start(bf16[256,2048]{1,0:T(8,128)(2,1)} %get-tuple-element.119), channel_id=1, source_target_pairs={{0,4},{1,5},{2,6},{3,7},{4,0},{5,1},{6,2},{7,3},{8,12},{9,13},{10,... | collective-permute-start | bytes 3145736 | tf_op jit(solution)/shard_map/ppermute | solution.py:61
  246.9 60.4 %collective-permute-start.51 = (bf16[256,2048]{1,0:T(8,128)(2,1)}, bf16[256,2048]{1,0:T(8,128)(2,1)}, u32[]{:S(2)}, u32[]{:S(2)}) collective-permute-start(bf16[256,2048]{1,0:T(8,128)(2,1)} %get-tuple-element.120), channel_id=1, source_target_pairs={{0,2},{1,3},{2,0},{3,1},{4,6},{5,7},{6,4},{7,5},{8,10},{9,11},{10,... | collective-permute-start | bytes 3145736 | tf_op jit(solution)/shard_map/ppermute | solution.py:61
  270.3 51.9 %collective-permute-start.53 = (bf16[128,2048]{1,0:T(8,128)(2,1)}, bf16[128,2048]{1,0:T(8,128)(2,1)S(1)}, u32[]{:S(2)}, u32[]{:S(2)}) collective-permute-start(bf16[128,2048]{1,0:T(8,128)(2,1)} %slice.591), channel_id=1, source_target_pairs={{0,4},{1,5},{2,6},{3,7},{4,0},{5,1},{6,2},{7,3},{8,12},{9,13},{10,... | collective-permute-start | bytes 1572872 | tf_op jit(solution)/shard_map/ppermute | solution.py:61
  271.5 51.6 %collective-permute-start.54 = (bf16[128,2048]{1,0:T(8,128)(2,1)}, bf16[128,2048]{1,0:T(8,128)(2,1)}, u32[]{:S(2)}, u32[]{:S(2)}) collective-permute-start(bf16[128,2048]{1,0:T(8,128)(2,1)} %slice.590), channel_id=1, source_target_pairs={{0,2},{1,3},{2,0},{3,1},{4,6},{5,7},{6,4},{7,5},{8,10},{9,11},{10,... | collective-permute-start | bytes 1572872 | tf_op jit(solution)/shard_map/ppermute | solution.py:61
  297.4 72.9 %collective-permute-start.55 = (bf16[2,1,512,512]{3,2,1,0:T(8,128)(2,1)}, bf16[2,1,512,512]{3,2,1,0:T(8,128)(2,1)}, u32[]{:S(2)}, u32[]{:S(2)}) collective-permute-start(bf16[2,1,512,512]{3,2,1,0:T(8,128)(2,1)} %pad_maximum_fusion.3), channel_id=1, source_target_pairs={{0,1},{1,0},{2,3},{3,2},{4,5},{5,4},{6,7},{7,6},{8,9},{9,8},{10,11... | collective-permute-start | bytes 3145736 | tf_op jit(solution)/shard_map/ppermute | solution.py:61
  310.5 25.6 %collective-permute-start.57 = (bf16[128,2048]{1,0:T(8,128)(2,1)S(1)}, bf16[128,2048]{1,0:T(8,128)(2,1)S(1)}, u32[]{:S(2)}, u32[]{:S(2)}) collective-permute-start(bf16[128,2048]{1,0:T(8,128)(2,1)S(1)} %slice.589), channel_id=1, source_target_pairs={{0,4},{1,5},{2,6},{3,7},{4,0},{5,1},{6,2},{7,3},{8,12},{9,13},{10,... | collective-permute-start | bytes 1572872 | tf_op jit(solution)/shard_map/ppermute | solution.py:61
  310.9 23.2 %collective-permute-start.58 = (bf16[128,2048]{1,0:T(8,128)(2,1)S(1)}, bf16[128,2048]{1,0:T(8,128)(2,1)S(1)}, u32[]{:S(2)}, u32[]{:S(2)}) collective-permute-start(bf16[128,2048]{1,0:T(8,128)(2,1)S(1)} %slice.588), channel_id=1, source_target_pairs={{0,2},{1,3},{2,0},{3,1},{4,6},{5,7},{6,4},{7,5},{8,10},{9,11},{10,... | collective-permute-start | bytes 1572872 | tf_op jit(solution)/shard_map/ppermute | solution.py:61
  325.1 49.7 %collective-permute-start.85 = (bf16[64,2048]{1,0:T(8,128)(2,1)}, bf16[64,2048]{1,0:T(8,128)(2,1)S(1)}, u32[]{:S(2)}, u32[]{:S(2)}) collective-permute-start(bf16[64,2048]{1,0:T(8,128)(2,1)} %get-tuple-element.148), channel_id=1, source_target_pairs={{0,24},{1,25},{2,26},{3,27},{4,28},{5,29},{6,30},{7,31},{8,16},{9,... | collective-permute-start | bytes 786440 | tf_op jit(solution)/shard_map/ppermute | solution.py:61
  337.0 16.9 %collective-permute-start.82 = (bf16[64,2048]{1,0:T(8,128)(2,1)}, bf16[64,2048]{1,0:T(8,128)(2,1)}, u32[]{:S(2)}, u32[]{:S(2)}) collective-permute-start(bf16[64,2048]{1,0:T(8,128)(2,1)} %get-tuple-element.146), channel_id=1, source_target_pairs={{0,24},{1,25},{2,26},{3,27},{4,28},{5,29},{6,30},{7,31},{8,16},{9,... | collective-permute-start | bytes 786440 | tf_op jit(solution)/shard_map/ppermute | solution.py:61
  340.9 27.7 %collective-permute-start.81 = (bf16[64,2048]{1,0:T(8,128)(2,1)}, bf16[64,2048]{1,0:T(8,128)(2,1)}, u32[]{:S(2)}, u32[]{:S(2)}) collective-permute-start(bf16[64,2048]{1,0:T(8,128)(2,1)} %get-tuple-element.147), channel_id=1, source_target_pairs={{0,16},{1,17},{2,18},{3,19},{4,20},{5,21},{6,22},{7,23},{8,24},{9,... | collective-permute-start | bytes 786440 | tf_op jit(solution)/shard_map/ppermute | solution.py:61
  340.9 27.9 %collective-permute-start.80 = (bf16[64,2048]{1,0:T(8,128)(2,1)}, bf16[64,2048]{1,0:T(8,128)(2,1)}, u32[]{:S(2)}, u32[]{:S(2)}) collective-permute-start(bf16[64,2048]{1,0:T(8,128)(2,1)} %slice.594), channel_id=1, source_target_pairs={{0,8},{1,9},{2,10},{3,11},{4,12},{5,13},{6,14},{7,15},{8,0},{9,1},... | collective-permute-start | bytes 786440 | tf_op jit(solution)/shard_map/ppermute | solution.py:61
  353.9 21.0 %collective-permute-start.84 = (bf16[64,2048]{1,0:T(8,128)(2,1)}, bf16[64,2048]{1,0:T(8,128)(2,1)S(1)}, u32[]{:S(2)}, u32[]{:S(2)}) collective-permute-start(bf16[64,2048]{1,0:T(8,128)(2,1)} %get-tuple-element.149), channel_id=1, source_target_pairs={{0,16},{1,17},{2,18},{3,19},{4,20},{5,21},{6,22},{7,23},{8,24},{9,... | collective-permute-start | bytes 786440 | tf_op jit(solution)/shard_map/ppermute | solution.py:61
  368.8 51.1 %collective-permute-start.67 = (bf16[1024,1024]{1,0:T(8,128)(2,1)}, bf16[1024,1024]{1,0:T(8,128)(2,1)}, u32[]{:S(2)}, u32[]{:S(2)}) collective-permute-start(bf16[1024,1024]{1,0:T(8,128)(2,1)} %copy-done.8), channel_id=1, source_target_pairs={{0,1},{1,0},{2,3},{3,2},{4,5},{5,4},{6,7},{7,6},{8,9},{9,8},{10,11... | collective-permute-start | bytes 6291464 | tf_op jit(solution)/shard_map/ppermute | solution.py:61
  421.1 23.4 %collective-permute-start.71 = (bf16[256,1024]{1,0:T(8,128)(2,1)S(1)}, bf16[256,1024]{1,0:T(8,128)(2,1)S(1)}, u32[]{:S(2)}, u32[]{:S(2)}) collective-permute-start(bf16[256,1024]{1,0:T(8,128)(2,1)S(1)} %add_convert_fusion.4), channel_id=1, source_target_pairs={{0,4},{1,5},{2,6},{3,7},{4,0},{5,1},{6,2},{7,3},{8,12},{9,13},{10,... | collective-permute-start | bytes 1572872 | tf_op jit(solution)/shard_map/ppermute | solution.py:61
  422.9 19.6 %collective-permute-start.63 = (bf16[256,640]{1,0:T(8,128)(2,1)S(1)}, bf16[256,640]{1,0:T(8,128)(2,1)S(1)}, u32[]{:S(2)}, u32[]{:S(2)}) collective-permute-start(bf16[256,640]{1,0:T(8,128)(2,1)S(1)} %add_convert_fusion.6), channel_id=1, source_target_pairs={{0,4},{1,5},{2,6},{3,7},{4,0},{5,1},{6,2},{7,3},{8,12},{9,13},{10,... | collective-permute-start | bytes 983048 | tf_op jit(solution)/shard_map/ppermute | solution.py:61
  446.2 28.2 %collective-permute-start.68 = (bf16[256,1024]{1,0:T(8,128)(2,1)S(1)}, bf16[256,1024]{1,0:T(8,128)(2,1)S(1)}, u32[]{:S(2)}, u32[]{:S(2)}) collective-permute-start(bf16[256,1024]{1,0:T(8,128)(2,1)S(1)} %get-tuple-element.126), channel_id=1, source_target_pairs={{0,2},{1,3},{2,0},{3,1},{4,6},{5,7},{6,4},{7,5},{8,10},{9,11},{10,... | collective-permute-start | bytes 1572872 | tf_op jit(solution)/shard_map/ppermute | solution.py:61
  446.6 20.2 %collective-permute-start.72 = (bf16[128,1024]{1,0:T(8,128)(2,1)S(1)}, bf16[128,1024]{1,0:T(8,128)(2,1)S(1)}, u32[]{:S(2)}, u32[]{:S(2)}) collective-permute-start(bf16[128,1024]{1,0:T(8,128)(2,1)S(1)} %slice.592), channel_id=1, source_target_pairs={{0,2},{1,3},{2,0},{3,1},{4,6},{5,7},{6,4},{7,5},{8,10},{9,11},{10,... | collective-permute-start | bytes 786440 | tf_op jit(solution)/shard_map/ppermute | solution.py:61
  448.4 24.1 %collective-permute-start.60 = (bf16[256,640]{1,0:T(8,128)(2,1)S(1)}, bf16[256,640]{1,0:T(8,128)(2,1)S(1)}, u32[]{:S(2)}, u32[]{:S(2)}) collective-permute-start(bf16[256,640]{1,0:T(8,128)(2,1)S(1)} %get-tuple-element.133), channel_id=1, source_target_pairs={{0,2},{1,3},{2,0},{3,1},{4,6},{5,7},{6,4},{7,5},{8,10},{9,11},{10,... | collective-permute-start | bytes 983048 | tf_op jit(solution)/shard_map/ppermute | solution.py:61
  449.2 34.6 %collective-permute-start.66 = (bf16[64,640]{1,0:T(8,128)(2,1)S(1)}, bf16[64,640]{1,0:T(8,128)(2,1)S(1)}, u32[]{:S(2)}, u32[]{:S(2)}) collective-permute-start(bf16[64,640]{1,0:T(8,128)(2,1)S(1)} %get-tuple-element.161), channel_id=1, source_target_pairs={{0,24},{1,25},{2,26},{3,27},{4,28},{5,29},{6,30},{7,31},{8,16},{9,... | collective-permute-start | bytes 245768 | tf_op jit(solution)/shard_map/ppermute | solution.py:61
  450.1 35.8 %collective-permute-start.65 = (bf16[64,640]{1,0:T(8,128)(2,1)S(1)}, bf16[64,640]{1,0:T(8,128)(2,1)S(1)}, u32[]{:S(2)}, u32[]{:S(2)}) collective-permute-start(bf16[64,640]{1,0:T(8,128)(2,1)S(1)} %get-tuple-element.160), channel_id=1, source_target_pairs={{0,16},{1,17},{2,18},{3,19},{4,20},{5,21},{6,22},{7,23},{8,24},{9,... | collective-permute-start | bytes 245768 | tf_op jit(solution)/shard_map/ppermute | solution.py:61
  476.2 15.1 %collective-permute-start.74 = (bf16[64,1024]{1,0:T(8,128)(2,1)S(1)}, bf16[64,1024]{1,0:T(8,128)(2,1)S(1)}, u32[]{:S(2)}, u32[]{:S(2)}) collective-permute-start(bf16[64,1024]{1,0:T(8,128)(2,1)S(1)} %get-tuple-element.159), channel_id=1, source_target_pairs={{0,24},{1,25},{2,26},{3,27},{4,28},{5,29},{6,30},{7,31},{8,16},{9,... | collective-permute-start | bytes 393224 | tf_op jit(solution)/shard_map/ppermute | solution.py:61
  (109 other events, 1086.2 us)

commit v5 on v3

--- a/solution.py
+++ b/solution.py
@@ -129,75 +129,191 @@
     )(me, *arrays)
 
 
-def gather_rows(parts, me, devices):
-    part = jnp.concatenate(parts, axis=1)
-    widths = [one.shape[1] for one in parts]
-    if devices != 32:
-        whole = lax.all_gather(part, ("dp", "shard"), axis=0, tiled=True)
-        return jnp.split(whole, [sum(widths[:i]) for i in range(1, len(widths))], axis=1)
-    near = jnp.concatenate([part, swap(part, 8, devices)])
-    far = jnp.concatenate([swap(part, 16, devices), swap(part, 24, devices)])
-    near = jnp.concatenate([near, swap(near, 4, devices)])
-    far = jnp.concatenate([far, swap(far, 2, devices)])
-    near_masks, far_masks = (0, 8, 4, 12), (16, 24, 18, 26)
-    blocks, masks = [near, far], [near_masks, far_masks]
-    blocks += [swap(near, 2, devices), swap(far, 4, devices)]
-    masks += [tuple(m | 2 for m in near_masks), tuple(m | 4 for m in far_masks)]
-    blocks += [swap(block, 1, devices) for block in blocks]
-    masks += [tuple(m | 1 for m in own) for own in masks]
-    return place(blocks, masks, widths, me, part.shape[0] * devices)
-
-
-def reduce_rows(grads, me, devices):
-    if devices != 32:
-        grad = jnp.concatenate([one.astype(jnp.float32) for one in grads], axis=1)
-        return lax.psum_scatter(grad, ("dp", "shard"), scatter_dimension=0, tiled=True)
-    size = grads[0].shape[0] // devices
-    order = [2, 10, 6, 14, 20, 28, 22, 30, 0, 8, 4, 12, 16, 24, 18, 26]
-    keep, send = pick(grads, [order, [m | 1 for m in order]], me, size)
-    came = swap(send, 1, devices)
-
-    def both(low, high):
-        rows = slice(low * size, high * size)
-        return keep[rows].astype(jnp.float32) + came[rows].astype(jnp.float32)
-
-    from_y = swap(both(0, 4).astype(LOW), 2, devices)
-    from_x = swap(both(4, 8).astype(LOW), 4, devices)
-    near = both(8, 12) + from_y.astype(jnp.float32)
-    far = both(12, 16) + from_x.astype(jnp.float32)
-    from_x = swap(near[2 * size :].astype(LOW), 4, devices)
-    from_y = swap(far[2 * size :].astype(LOW), 2, devices)
-    near = near[: 2 * size] + from_x.astype(jnp.float32)
-    far = far[: 2 * size] + from_y.astype(jnp.float32)
-    one = swap(near[size:].astype(LOW), 8, devices)
-    two = swap(far[:size].astype(LOW), 16, devices)
-    three = swap(far[size:].astype(LOW), 24, devices)
-    return (near[:size] + one.astype(jnp.float32)) + (two.astype(jnp.float32) + three.astype(jnp.float32))
-
-
-def gather_pieces(part, devices, shards):
-    at = lax.axis_index("shard")
-    if shards != 4 or devices != 32:
-        return lax.all_gather(part, "shard", axis=0), jnp.arange(shards, dtype=jnp.int32)
-    over = swap(part, 2, devices)
-    pieces = jnp.stack([part, swap(part, 1, devices), over, swap(over, 1, devices)])
-    return pieces, jnp.arange(4, dtype=jnp.int32) ^ at
-
-
-def reduce_pieces(grad, devices, shards):
-    if shards != 4 or devices != 32:
-        return lax.psum_scatter(grad, "shard", scatter_dimension=0)
-    came = swap(jnp.stack([grad[1], grad[3]]).astype(LOW), 1, devices).astype(jnp.float32)
-    over = swap((grad[2] + came[1]).astype(LOW), 2, devices)
-    return grad[0] + came[0] + over.astype(jnp.float32)
-
-
-def sum_over_devices(values, devices):
-    if devices != 32:
-        return lax.psum(values, ("dp", "shard"))
-    for mask in (16, 8, 4, 2, 1):
-        values = values + swap(values, mask, devices)
+class Gather:
+    def __init__(self, parts, me, devices):
+        self.part = jnp.concatenate(parts, axis=1)
+        self.widths = [one.shape[1] for one in parts]
+        self.me, self.devices, self.staged = me, devices, devices == 32
+        self.stage, self.outgoing, self.incoming = 0, (), ()
+
+    def prepare(self):
+        stage = self.stage
+        self.stage += 1
+        if not self.staged:
+            return
+        if stage == 0:
+            self.outgoing, self.masks = (self.part,), ((8, 16, 24),)
+        elif stage == 1:
+            one, two, three = self.incoming
+            self.outgoing = jnp.concatenate([self.part, one]), jnp.concatenate([two, three])
+            self.masks = (4,), (2,)
+        elif stage == 2:
+            self.outgoing = tuple(
+                jnp.concatenate([own, came]) for own, came in zip(self.outgoing, self.incoming)
+            )
+            self.masks = (2,), (4,)
+        else:
+            self.outgoing, self.masks = (jnp.concatenate([*self.outgoing, *self.incoming]),), ((1,),)
+
+    def launch(self):
+        if self.staged:
+            self.incoming = tuple(
+                swap(one, mask, self.devices) for one, own in zip(self.outgoing, self.masks) for mask in own
+            )
+
+    def whole(self):
+        if not self.staged:
+            whole = lax.all_gather(self.part, ("dp", "shard"), axis=0, tiled=True)
+            ends = [sum(self.widths[:i]) for i in range(1, len(self.widths))]
+            return jnp.split(whole, ends, axis=1)
+        near, far = (0, 8, 4, 12), (16, 24, 18, 26)
+        masks = [*near, *far, *(m | 2 for m in near), *(m | 4 for m in far)]
+        masks = masks, [m | 1 for m in masks]
+        blocks = self.outgoing + self.incoming
+        return place(blocks, masks, self.widths, self.me, self.part.shape[0] * self.devices)
+
+
+class Reduce:
+    def __init__(self, grads, me, devices):
+        self.grads, self.me, self.devices, self.staged = grads, me, devices, devices == 32
+        self.size = grads[0].shape[0] // devices
+        self.stage, self.outgoing, self.incoming = 0, (), ()
+
+    def both(self, low, high):
+        rows = slice(low * self.size, high * self.size)
+        return self.keep[rows].astype(jnp.float32) + self.came[rows].astype(jnp.float32)
+
+    def prepare(self):
+        stage, size = self.stage, self.size
+        self.stage += 1
+        if not self.staged:
+            if stage == 0:
+                grad = jnp.concatenate([one.astype(jnp.float32) for one in self.grads], axis=1)
+                self.total = lax.psum_scatter(grad, ("dp", "shard"), scatter_dimension=0, tiled=True)
+            return
+        incoming = [one.astype(jnp.float32) for one in self.incoming]
+        if stage == 0:
+            order = [2, 10, 6, 14, 20, 28, 22, 30, 0, 8, 4, 12, 16, 24, 18, 26]
+            self.keep, send = pick(self.grads, [order, [m | 1 for m in order]], self.me, size)
+            self.outgoing, self.masks = (send,), (1,)
+        elif stage == 1:
+            (self.came,) = self.incoming
+            self.outgoing = self.both(0, 4).astype(LOW), self.both(4, 8).astype(LOW)
+            self.masks = 2, 4
+        elif stage == 2:
+            near, far = self.both(8, 12) + incoming[0], self.both(12, 16) + incoming[1]
+            self.outgoing = near[2 * size :].astype(LOW), far[2 * size :].astype(LOW)
+            self.near, self.far = near[: 2 * size], far[: 2 * size]
+            self.masks = 4, 2
+        elif stage == 3:
+            near, far = self.near + incoming[0], self.far + incoming[1]
+            self.outgoing = near[size:].astype(LOW), far[:size].astype(LOW), far[size:].astype(LOW)
+            self.own, self.masks = near[:size], (8, 16, 24)
+        else:
+            self.total = (self.own + incoming[0]) + (incoming[1] + incoming[2])
+
+    def launch(self):
+        if self.staged:
+            self.incoming = tuple(
+                swap(one, mask, self.devices) for one, mask in zip(self.outgoing, self.masks)
+            )
+
+
+class Sum:
+    def __init__(self, values, devices):
+        self.values, self.devices, self.staged = values, devices, devices == 32
+        self.stage, self.outgoing, self.incoming = 0, (), ()
+
+    def prepare(self):
+        stage = self.stage
+        self.stage += 1
+        if not self.staged:
+            if stage == 0:
+                self.values = lax.psum(self.values, ("dp", "shard"))
+            return
+        if stage in (1, 2, 3):
+            self.values = self.values + self.incoming[0]
+        if stage == 4:
+            one, two, three = self.incoming
+            self.values = (self.values + one) + (two + three)
+            return
+        self.outgoing, self.masks = (self.values,), ((1,), (2,), (4,), (8, 16, 24))[stage]
+
+    def launch(self):
+        if self.staged:
+            self.incoming = tuple(swap(self.outgoing[0], mask, self.devices) for mask in self.masks)
+
+
+def open_slot(travellers, *values):
+    for one in travellers:
+        one.prepare()
+    travellers = [one for one in travellers if one.staged]
+    if not travellers:
+        return values
+    outgoing, values = lax.optimization_barrier((tuple(one.outgoing for one in travellers), values))
+    for one, sent in zip(travellers, outgoing):
+        one.outgoing = sent
+        one.launch()
     return values
+
+
+def close_slot(travellers, *values):
+    travellers = [one for one in travellers if one.staged]
+    if not travellers:
+        return values
+    incoming, values = lax.optimization_barrier((tuple(one.incoming for one in travellers), values))
+    for one, came in zip(travellers, incoming):
+        one.incoming = came
+    return values
+
+
+class Pieces:
+    def __init__(self, part, devices, shards):
+        self.part, self.devices, self.shards = part, devices, shards
+        self.staged = devices == 32 and shards == 4
+        self.stage, self.outgoing, self.incoming = 0, (), ()
+
+    def prepare(self):
+        stage = self.stage
+        self.stage += 1
+        if stage == 0:
+            self.outgoing, self.mask = (self.part,), 2
+        elif self.staged:
+            self.outgoing, self.mask = (jnp.stack([self.part, *self.incoming]),), 1
+
+    def launch(self):
+        if self.staged:
+            self.incoming = (swap(self.outgoing[0], self.mask, self.devices),)
+
+    def whole(self):
+        if not self.staged:
+            return lax.all_gather(self.part, "shard", axis=0), jnp.arange(self.shards, dtype=jnp.int32)
+        at = jnp.array([0, 2, 1, 3], jnp.int32) ^ lax.axis_index("shard")
+        return jnp.concatenate([self.outgoing[0], self.incoming[0]]), at
+
+
+class PiecesBack:
+    def __init__(self, grad, devices, shards):
+        self.grad, self.devices, self.staged = grad, devices, devices == 32 and shards == 4
+        self.stage, self.outgoing, self.incoming = 0, (), ()
+
+    def prepare(self):
+        stage, grad = self.stage, self.grad
+        self.stage += 1
+        if not self.staged:
+            if stage == 0:
+                self.total = lax.psum_scatter(grad, "shard", scatter_dimension=0)
+        elif stage == 0:
+            self.outgoing, self.mask = (grad[2:].astype(LOW),), 1
+        elif stage == 1:
+            self.came = self.incoming[0].astype(jnp.float32)
+            self.outgoing, self.mask = ((grad[1] + self.came[1]).astype(LOW),), 2
+        else:
+            self.total = grad[0] + self.came[0] + self.incoming[0].astype(jnp.float32)
+
+    def launch(self):
+        if self.staged:
+            self.incoming = (swap(self.outgoing[0], self.mask, self.devices),)
 
 
 def allowed(base, start, valid, key_axis, shape):
@@ -224,7 +340,7 @@
     lax.fori_loop(0, pieces, one, 0)
 
 
-def attention(info, queries, keys_values):
+def attention(info, queries, keys_values, first, groups):
     rows, _, length = queries.shape
     pieces = keys_values.shape[0]
     group_width = GROUP * HD
@@ -257,34 +373,37 @@
             out_ref[0, own, :] = out
             low_ref[0, own, :] = out.astype(LOW)
 
-    q_spec = pl.BlockSpec((1, group_width, length), lambda row, group, *_: (row, group, 0))
-    k_spec = pl.BlockSpec((pieces, 1, HD, length), lambda row, group, *_: (0, row, group, 0))
-    v_spec = pl.BlockSpec((pieces, 1, HD, length), lambda row, group, *_: (0, row, group + KV, 0))
+    q_spec = pl.BlockSpec((1, group_width, length), lambda row, group, *_: (row, group + first, 0))
+    o_spec = pl.BlockSpec((1, group_width, length), lambda row, group, *_: (row, group, 0))
+    k_spec = pl.BlockSpec((pieces, 1, HD, length), lambda row, group, *_: (0, row, group + first, 0))
+    v_spec = pl.BlockSpec(
+        (pieces, 1, HD, length), lambda row, group, *_: (0, row, group + first + KV, 0)
+    )
     s_spec = pl.BlockSpec((1, 1, GROUP, length), lambda row, group, *_: (row, group, 0, 0))
-    work = rows * HEADS * length * length * pieces
+    work = rows * groups * GROUP * length * length * pieces
     return pl.pallas_call(
         kernel,
         out_shape=[
-            jax.ShapeDtypeStruct(queries.shape, jnp.float32),
-            jax.ShapeDtypeStruct(queries.shape, LOW),
-            jax.ShapeDtypeStruct((rows, KV, GROUP, length), jnp.float32),
+            jax.ShapeDtypeStruct((rows, groups * group_width, length), jnp.float32),
+            jax.ShapeDtypeStruct((rows, groups * group_width, length), LOW),
+            jax.ShapeDtypeStruct((rows, groups, GROUP, length), jnp.float32),
         ],
         grid_spec=pltpu.PrefetchScalarGridSpec(
             num_scalar_prefetch=1,
-            grid=(rows, KV),
+            grid=(rows, groups),
             in_specs=[q_spec, k_spec, v_spec],
-            out_specs=[q_spec, q_spec, s_spec],
+            out_specs=[o_spec, o_spec, s_spec],
             scratch_shapes=[
                 pltpu.VMEM((GROUP, length, HD), jnp.float32),
                 pltpu.VMEM((GROUP, length, min(128, length)), jnp.float32),
             ],
         ),
         compiler_params=pltpu.CompilerParams(vmem_limit_bytes=40 << 20),
-        cost_estimate=pl.CostEstimate(flops=work * 1000, transcendentals=work, bytes_accessed=10 << 20),
+        cost_estimate=pl.CostEstimate(flops=work, transcendentals=0, bytes_accessed=1 << 20),
     )(info, queries, keys_values, keys_values)
 
 
-def attention_back(info, queries, keys_values, out, sums, grad_out, first, groups):
+def attention_back(info, queries, keys_values, out, sums, grad_out, first, groups, part_first):
     rows, _, length = queries.shape
     pieces = keys_values.shape[0]
     group_width = GROUP * HD
@@ -334,7 +453,10 @@
     v_spec = pl.BlockSpec(
         (pieces, 1, HD, length), lambda row, group, *_: (0, row, group + first + KV, 0)
     )
-    s_spec = pl.BlockSpec((1, 1, GROUP, length), lambda row, group, *_: (row, group + first, 0, 0))
+    o_spec = pl.BlockSpec((1, group_width, length), lambda row, group, *_: (row, group + part_first, 0))
+    s_spec = pl.BlockSpec(
+        (1, 1, GROUP, length), lambda row, group, *_: (row, group + part_first, 0, 0)
+    )
     dq_spec = pl.BlockSpec((1, group_width, length), lambda row, group, *_: (row, group, 0))
     dk_spec = pl.BlockSpec((pieces, 1, HD, length), lambda row, group, *_: (0, row, group, 0))
     work = rows * groups * GROUP * length * length * pieces
@@ -349,7 +471,7 @@
         grid_spec=pltpu.PrefetchScalarGridSpec(
             num_scalar_prefetch=1,
             grid=(rows, groups),
-            in_specs=[q_spec, k_spec, v_spec, q_spec, s_spec, q_spec],
+            in_specs=[q_spec, k_spec, v_spec, o_spec, s_spec, q_spec],
             out_specs=[dq_spec, dk_spec, dk_spec],
             scratch_shapes=[
                 pltpu.VMEM((group_width, length), LOW),
@@ -361,7 +483,7 @@
             ],
         ),
         compiler_params=pltpu.CompilerParams(vmem_limit_bytes=40 << 20),
-        cost_estimate=pl.CostEstimate(flops=work * 2500, transcendentals=work, bytes_accessed=10 << 20),
+        cost_estimate=pl.CostEstimate(flops=work, transcendentals=0, bytes_accessed=1 << 20),
     )(info, queries, keys_values, keys_values, out, sums, grad_out)
 
 
@@ -409,110 +531,200 @@
 
     gain_columns = jnp.concatenate(
         [attn_gain[:, None], ffn_gain[:, None], jnp.zeros((part_len, 126), jnp.float32)], axis=1
-    )
-    wqkv, gains = gather_rows([w_qkv.astype(LOW), gain_columns.astype(LOW)], me, devices)
-    wout, wgate = gather_rows([w_out.astype(LOW).T, w_gate.astype(LOW)], me, devices)
-    wup, wdown = gather_rows([w_up.astype(LOW), w_down.astype(LOW).T], me, devices)
+    ).astype(LOW)
+    w_qkv_low, w_gate_low, w_up_low = w_qkv.astype(LOW), w_gate.astype(LOW), w_up.astype(LOW)
+    gather_a = Gather([w_qkv_low, gain_columns], me, devices)
+    gather_b = Gather([w_out.astype(LOW).T], me, devices)
+    w_down_low = w_down.astype(LOW).T
+    units = w_down_low.shape[1] // 2
+    halves = slice(0, units), slice(units, 2 * units)
+    gather_c = [
+        Gather([w_gate_low[:, own], w_up_low[:, own], w_down_low[:, own]], me, devices) for own in halves
+    ]
+    (tokens,) = open_slot([gather_a], tokens)
+    x_float = tokens.astype(jnp.float32)
+    normed_one, inverse_one = normalize(x_float)
+    (normed_one,) = close_slot([gather_a], normed_one)
+    (normed_one,) = open_slot([gather_a, gather_b], normed_one)
+    (normed_one,) = close_slot([gather_a, gather_b], normed_one)
+    (normed_one,) = open_slot([gather_a, gather_b], normed_one)
+    (normed_one,) = close_slot([gather_a, gather_b], normed_one)
+    (normed_one,) = open_slot([gather_a, gather_b, gather_c[0]], normed_one)
+    (normed_one,) = close_slot([gather_a], normed_one)
+    wqkv, gains = gather_a.whole()
     gain_attn = gains[:, 0].astype(jnp.float32)
     gain_ffn = gains[:, 1].astype(jnp.float32)
-
-    x_float = tokens.astype(jnp.float32)
-    normed_one, inverse_one = normalize(x_float)
     normed_low = (normed_one * gain_attn).astype(LOW)
     projected = jnp.einsum("rtd,de->ret", normed_low, wqkv, preferred_element_type=jnp.float32)
     q_raw = projected[:, :q_width].reshape(row_count, HEADS, HD, piece_len)
     k_raw = projected[:, q_width : q_width + kv_width].reshape(row_count, KV, HD, piece_len)
     v_raw = projected[:, q_width + kv_width :]
+    k_unit, k_inverse = normalize(k_raw, 2)
+    k_low = rotate(k_unit * k_gain_h, cos_h, sin_h).astype(LOW).reshape(row_count, kv_width, piece_len)
+    own_kv = jnp.concatenate([k_low, v_raw.astype(LOW)], axis=1)
+    own_kv, q_raw = close_slot([gather_b, gather_c[0]], own_kv, q_raw)
+    row_pieces = Pieces(own_kv, devices, shards)
+    (q_raw,) = open_slot([row_pieces, gather_b, gather_c[0]], q_raw)
     q_unit, q_inverse = normalize(q_raw, 2)
-    k_unit, k_inverse = normalize(k_raw, 2)
     q_low = (
         rotate(q_unit * q_gain_h, cos_h, sin_h).astype(LOW) * jnp.array(scale_factor, LOW)
     ).reshape(row_count, q_width, piece_len)
-    k_low = rotate(k_unit * k_gain_h, cos_h, sin_h).astype(LOW).reshape(row_count, kv_width, piece_len)
-    own_kv = jnp.concatenate([k_low, v_raw.astype(LOW)], axis=1)
-    pieces, piece_at = gather_pieces(own_kv, devices, shards)
+    (q_low,) = close_slot([row_pieces, gather_b, gather_c[0]], q_low)
+    (q_low,) = open_slot([row_pieces, *gather_c], q_low)
+    (q_low,) = close_slot([row_pieces], q_low)
+    pieces, piece_at = row_pieces.whole()
     info = jnp.concatenate([start.reshape(1), piece_at * piece_len, row_valid]).astype(jnp.int32)
-    o_heads, att_low, sums = attention(info, q_low, pieces)
+    o_heads, att_low, sums = attention(info, q_low, pieces, 0, KV)
+    o_heads, att_low, sums = close_slot(gather_c, o_heads, att_low, sums)
+    (att_low,) = open_slot(gather_c, att_low)
+    (wout,) = gather_b.whole()
     x_mid = x_float + jnp.einsum("rct,dc->rtd", att_low, wout, preferred_element_type=jnp.float32)
     normed_two, inverse_two = normalize(x_mid)
     ffn_in = (normed_two * gain_ffn).astype(LOW)
-    gate_proj = jnp.einsum("rtd,df->rtf", ffn_in, wgate, preferred_element_type=jnp.float32)
-    up_proj = jnp.einsum("rtd,df->rtf", ffn_in, wup, preferred_element_type=jnp.float32)
-    gate_sig = jax.nn.sigmoid(gate_proj)
-    silu_gate = gate_proj * gate_sig
-    activated = (silu_gate * up_proj).astype(LOW)
-    output = (
-        x_mid + jnp.einsum("rtf,df->rtd", activated, wdown, preferred_element_type=jnp.float32)
-    ).astype(LOW)
-
     grad_out = cotangent.astype(jnp.float32) * live_mask[..., None]
     grad_low = grad_out.astype(LOW)
-    grad_down = jnp.einsum("rtd,rtf->df", grad_low, activated, preferred_element_type=jnp.float32)
-    grad_act = jnp.einsum("rtd,df->rtf", grad_low, wdown, preferred_element_type=jnp.float32)
-    grad_gate = (grad_act * up_proj * gate_sig * (1.0 + gate_proj * (1.0 - gate_sig))).astype(LOW)
-    grad_up = (grad_act * silu_gate).astype(LOW)
-    grad_wgate = jnp.einsum("rtd,rtf->df", ffn_in, grad_gate, preferred_element_type=jnp.float32)
-    grad_wup = jnp.einsum("rtd,rtf->df", ffn_in, grad_up, preferred_element_type=jnp.float32)
-    one = reduce_rows([grad_down.astype(LOW), grad_wgate.astype(LOW)], me, devices)
-    width = grad_down.shape[1]
-    summed_down, summed_wgate = one[:, :width].T, one[:, width:]
+
+    def feed_forward(ffn_in, grad_low, wgate, wup, wdown):
+        gate_proj = jnp.einsum("rtd,df->rtf", ffn_in, wgate, preferred_element_type=jnp.float32)
+        up_proj = jnp.einsum("rtd,df->rtf", ffn_in, wup, preferred_element_type=jnp.float32)
+        gate_sig = jax.nn.sigmoid(gate_proj)
+        silu_gate = gate_proj * gate_sig
+        activated = (silu_gate * up_proj).astype(LOW)
+        grad_down = jnp.einsum("rtd,rtf->df", grad_low, activated, preferred_element_type=jnp.float32)
+        grad_act = jnp.einsum("rtd,df->rtf", grad_low, wdown, preferred_element_type=jnp.float32)
+        grad_gate = (grad_act * up_proj * gate_sig * (1.0 + gate_proj * (1.0 - gate_sig))).astype(LOW)
+        grad_up = (grad_act * silu_gate).astype(LOW)
+        grad_wgate = jnp.einsum("rtd,rtf->df", ffn_in, grad_gate, preferred_element_type=jnp.float32)
+        grad_wup = jnp.einsum("rtd,rtf->df", ffn_in, grad_up, preferred_element_type=jnp.float32)
+        grads = [grad_down.astype(LOW), grad_wgate.astype(LOW), grad_wup.astype(LOW)]
+        return activated, grad_gate, grad_up, grads
+
+    ffn_in, x_mid = close_slot(gather_c, ffn_in, x_mid)
+    (ffn_in,) = open_slot([gather_c[1]], ffn_in)
+    one = gather_c[0].whole()
+    act_one, gate_one, up_one, grads = feed_forward(ffn_in, grad_low, *one)
+    ffn_in, grads, act_one, gate_one, up_one = close_slot(
+        [gather_c[1]], ffn_in, grads, act_one, gate_one, up_one
+    )
+    red_one = Reduce(grads, me, devices)
+    (ffn_in,) = open_slot([gather_c[1], red_one], ffn_in)
+    (ffn_in,) = close_slot([gather_c[1], red_one], ffn_in)
+    (ffn_in,) = open_slot([red_one], ffn_in)
+    two = gather_c[1].whole()
+    act_two, gate_two, up_two, grads = feed_forward(ffn_in, grad_low, *two)
+    ffn_in, grads, act_two, gate_two, up_two = close_slot(
+        [red_one], ffn_in, grads, act_two, gate_two, up_two
+    )
+    red_two = Reduce(grads, me, devices)
+    gate_two, up_two, act_two = open_slot([red_one, red_two], gate_two, up_two, act_two)
     grad_ffn_in = jnp.einsum(
-        "rtf,df->rtd", grad_gate, wgate, preferred_element_type=jnp.float32
-    ) + jnp.einsum("rtf,df->rtd", grad_up, wup, preferred_element_type=jnp.float32)
-    grad_gain_two = jnp.sum(grad_ffn_in * normed_two, axis=(0, 1))
+        "rtf,df->rtd",
+        jnp.concatenate([gate_one, up_one, gate_two, up_two], axis=2),
+        jnp.concatenate([*one[:2], *two[:2]], axis=1),
+        preferred_element_type=jnp.float32,
+    )
     grad_mid = grad_out + norm_back(x_mid, inverse_two, grad_ffn_in * gain_ffn)
     mid_low = grad_mid.astype(LOW)
     grad_wout = jnp.einsum("rtd,rct->dc", mid_low, att_low, preferred_element_type=jnp.float32)
-    two = reduce_rows([grad_wup.astype(LOW), grad_wout.astype(LOW)], me, devices)
-    summed_wup, summed_wout = two[:, :width], two[:, width:].T
     grad_att = jnp.einsum("rtd,dc->rct", mid_low, wout, preferred_element_type=jnp.float32)
-    dq_parts, dk_parts, dv_parts = [], [], []
-    for group in range(KV):
-        dq, dk, dv = attention_back(info, q_low, pieces, o_heads, sums, grad_att, group, 1)
-        dq_parts.append(dq)
-        dk_parts.append(dk)
-        dv_parts.append(dv)
-    grad_query = jnp.concatenate(dq_parts, axis=1)
-    grad_pieces = jnp.concatenate(dk_parts + dv_parts, axis=2)
-    grad_kv = reduce_pieces(grad_pieces, devices, shards)
+    red_out = Reduce([grad_wout.astype(LOW)], me, devices)
+    grad_att, red_out.grads = close_slot([red_one, red_two], grad_att, red_out.grads)
+    grad_att, act_two = open_slot([red_one, red_two], grad_att, act_two)
+
+    def back(group, grad_att):
+        return attention_back(info, q_low, pieces, o_heads, sums, grad_att, group, 1, group)
+
+    output = (
+        x_mid
+        + jnp.einsum(
+            "rtf,df->rtd",
+            jnp.concatenate([act_one, act_two], axis=2),
+            jnp.concatenate([one[2], two[2]], axis=1),
+            preferred_element_type=jnp.float32,
+        )
+    ).astype(LOW)
+    parts = [back(0, grad_att)]
+    parts[0], grad_att, output = close_slot([red_one, red_two], parts[0], grad_att, output)
+    red_one.prepare()
+    (grad_att,) = open_slot([red_two, red_out], grad_att)
+    parts.append(back(1, grad_att))
+    parts[1], grad_att = close_slot([red_two, red_out], parts[1], grad_att)
+    (grad_att,) = open_slot([red_two, red_out], grad_att)
+    parts.append(back(2, grad_att))
+    parts[2], grad_att = close_slot([red_two, red_out], parts[2], grad_att)
+    red_two.prepare()
+    (grad_att,) = open_slot([red_out], grad_att)
+    parts.append(back(3, grad_att))
+    (parts,) = close_slot([red_out], parts)
+    grad_query = jnp.concatenate([one_part[0] for one_part in parts], axis=1)
+    grad_pieces = jnp.concatenate(
+        [one_part[1] for one_part in parts] + [one_part[2] for one_part in parts], axis=2
+    )
+    kv_back = PiecesBack(grad_pieces, devices, shards)
+    (grad_query,) = open_slot([kv_back, red_out], grad_query)
+    (grad_query,) = close_slot([kv_back], grad_query)
+    (grad_query,) = open_slot([kv_back], grad_query)
     grad_q_scaled = rotate_back(
         scale_factor * grad_query.reshape(row_count, HEADS, HD, piece_len), cos_h, sin_h
     )
     grad_qgain = jnp.sum(grad_q_scaled * q_unit, axis=(0, 1, 3))
     grad_q_raw = norm_back(q_raw, q_inverse, grad_q_scaled * q_gain_h, 2)
+    grad_q_low = grad_q_raw.reshape(row_count, q_width, piece_len).astype(LOW)
+    grad_wq = jnp.einsum("rtd,ret->de", normed_low, grad_q_low, preferred_element_type=jnp.float32)
+    grad_wq, grad_q_low = close_slot([kv_back, red_out], grad_wq, grad_q_low)
+    red_out.prepare()
+    kv_back.prepare()
+    red_q = Reduce([grad_wq.astype(LOW)], me, devices)
+    grad_kv, grad_q_low = open_slot([red_q], kv_back.total, grad_q_low)
     grad_k_scaled = rotate_back(
         grad_kv[:, :kv_width].reshape(row_count, KV, HD, piece_len), cos_h, sin_h
     )
     grad_kgain = jnp.sum(grad_k_scaled * k_unit, axis=(0, 1, 3))
     grad_k_raw = norm_back(k_raw, k_inverse, grad_k_scaled * k_gain_h, 2)
-    shared = sum_over_devices(jnp.concatenate([grad_qgain, grad_kgain])[None], devices)
-    grad_projected = jnp.concatenate(
-        [
-            grad_q_raw.reshape(row_count, q_width, piece_len),
-            grad_k_raw.reshape(row_count, kv_width, piece_len),
-            grad_kv[:, kv_width:],
-        ],
-        axis=1,
+    grad_kv_low = jnp.concatenate(
+        [grad_k_raw.reshape(row_count, kv_width, piece_len), grad_kv[:, kv_width:]], axis=1
     ).astype(LOW)
-    grad_wqkv = jnp.einsum("rtd,ret->de", normed_low, grad_projected, preferred_element_type=jnp.float32)
-    grad_normed = jnp.einsum("ret,de->rtd", grad_projected, wqkv, preferred_element_type=jnp.float32)
-    grad_gain_one = jnp.sum(grad_normed * normed_one, axis=(0, 1))
+    grad_wkv = jnp.einsum("rtd,ret->de", normed_low, grad_kv_low, preferred_element_type=jnp.float32)
+    grad_wkv, grad_kv_low, grad_q_low = close_slot([red_q], grad_wkv, grad_kv_low, grad_q_low)
+    shared = Sum(jnp.concatenate([grad_qgain, grad_kgain])[None], devices)
+    red_kv = Reduce([grad_wkv.astype(LOW)], me, devices)
+    grad_kv_low, grad_q_low = open_slot([red_q, red_kv, shared], grad_kv_low, grad_q_low)
+    grad_normed = jnp.einsum(
+        "ret,de->rtd",
+        jnp.concatenate([grad_q_low, grad_kv_low], axis=1),
+        wqkv,
+        preferred_element_type=jnp.float32,
+    )
     input_grad = grad_mid + norm_back(x_float, inverse_one, grad_normed * gain_attn)
-    grad_gains = jnp.concatenate(
-        [grad_gain_one[:, None], grad_gain_two[:, None], jnp.zeros((model_width, 126), jnp.float32)],
-        axis=1,
-    )
-    three = reduce_rows([grad_wqkv.astype(LOW), grad_gains.astype(LOW)], me, devices)
-    qkv_width = w_qkv.shape[1]
+    (input_grad,) = close_slot([red_q, red_kv, shared], input_grad)
+    open_slot([red_q, red_kv, shared])
+    close_slot([red_q, red_kv, shared])
+    open_slot([red_q, red_kv, shared])
+    close_slot([red_q, red_kv, shared])
+    open_slot([red_kv, shared])
+    red_q.prepare()
+    close_slot([red_kv, shared])
+    red_kv.prepare()
+    shared.prepare()
+    shared = shared.values
+    three, four = red_q.total, red_kv.total
+    summed = [jnp.split(one_red.total, 3, axis=1) for one_red in (red_one, red_two)]
+    summed_down, summed_wgate, summed_wup = (
+        jnp.concatenate([summed[0][at], summed[1][at]], axis=1) for at in range(3)
+    )
+    summed_down, summed_wout = summed_down.T, red_out.total.T
+    summed_wqkv = jnp.concatenate([three, four], axis=1)
+    grad_gain_one = jnp.sum(summed_wqkv * w_qkv_low, axis=1) / attn_gain.astype(LOW)
+    grad_gain_two = jnp.sum(summed_wgate * w_gate_low + summed_wup * w_up_low, axis=1) / ffn_gain.astype(LOW)
     return (
         output,
         input_grad,
-        three[:, qkv_width],
-        three[:, :qkv_width],
+        grad_gain_one,
+        summed_wqkv,
         shared[0, :HD],
         shared[0, HD:],
         summed_wout,
-        three[:, qkv_width + 1],
+        grad_gain_two,
         summed_wgate,
         summed_wup,
         summed_down,

time: 574 us -> 451 us (0.79)
  waiting for transfers between devices: 247 us -> 122 us
  Pallas kernels: 48.2 us -> 64.9 us
  matrix products: 66.2 us -> 52.6 us
  local copies, waits for them, and re-layouts: 30.5 us -> 19.8 us
  starting transfers between devices: 116 us -> 123 us
    ppermute x67 -> x82, waiting for transfers between devices: 247 us -> 122 us  [swap(): lax.ppermute(values, ('dp', 'shard'), [(i, i ^ mask) for i in range(devic...]
    dot_general x11 -> x17, matrix products: 51.6 us -> 41.8 us  [the longest x1 10.2 us: local(): jnp.einsum('rtf,df->rtd', jnp.concatenate([gate_one, up_one, gate_two, up...]
    pallas_call x3 -> x5, Pallas kernels: 10.2 us -> 18.8 us  [pick(): pl.pallas_call(kernel, out_shape=[jax.ShapeDtypeStruct((len(own) * size,...]
    pallas_call x3 -> x4, Pallas kernels: 6.72 us -> 14.7 us  [place(): pl.pallas_call(kernel, out_shape=[jax.ShapeDtypeStruct((total_rows, width...]
    ppermute x67 -> x82, starting transfers between devices: 116 us -> 123 us  [swap(): lax.ppermute(values, ('dp', 'shard'), [(i, i ^ mask) for i in range(devic...]
    unnamed x150 -> x226, local copies, waits for them, and re-layouts: 22 us -> 15.9 us
    add x18 -> x19, other arithmetic: 14.3 us -> 8.77 us  [the longest x5 5.57 us: prepare(): self.both(12, 16) + incoming[1]]
  transfers between devices with their start and end apart: 67 -> 82, of which waited for: 24 -> 28; matrix products, arithmetic and copies ran while one was open for 16% -> 20% of each run, Pallas kernels for 3% -> 12%
where the time goes in v5:
time: 451 us; the launch traced here: 445 us
  starting transfers between devices  123 us (27%)
  waiting for transfers between devices  122 us (27%)
  Pallas kernels  64.9 us (14%)
  other arithmetic  59.4 us (13%)
  matrix products  52.6 us (12%)
  local copies, waits for them, and re-layouts  19.8 us (4%)
    ppermute x82, starting transfers between devices, swap(): lax.ppermute(values, ('dp', 'shard'), [(i, i ^ mask) for i in range(devic...  123 us
    ppermute x82, waiting for transfers between devices, swap(): lax.ppermute(values, ('dp', 'shard'), [(i, i ^ mask) for i in range(devic...  122 us
    pallas_call x4, Pallas kernels, attention_back(): pl.pallas_call(kernel, out_shape=[jax.ShapeDtypeStruct((rows, groups * gr...  20.7 us
    pallas_call x5, Pallas kernels, pick(): pl.pallas_call(kernel, out_shape=[jax.ShapeDtypeStruct((len(own) * size,...  18.8 us
    unnamed x226, local copies, waits for them, and re-layouts  15.9 us
    pallas_call x4, Pallas kernels, place(): pl.pallas_call(kernel, out_shape=[jax.ShapeDtypeStruct((total_rows, width...  14.7 us
    pallas_call x1, Pallas kernels, attention(): pl.pallas_call(kernel, out_shape=[jax.ShapeDtypeStruct((rows, groups * gr...  10.8 us
    dot_general x1, matrix products, local(): jnp.einsum('rtf,df->rtd', jnp.concatenate([gate_one, up_one, gate_two, up...  10.2 us
  transfers between devices with their start and end apart: 82, of which 28 were waited for; matrix products, arithmetic and copies ran while one was open for 20% of the time, Pallas kernels for 12%

profile of v5, /device:TPU:0, one launch (start us, length us, event | category | flops | bytes accessed | tf_op | source)
XLA Modules:
  0.0 445.3 jit_solution(9228012521374096836)
XLA Ops:
  3.5 3.1 collective-permute-start
  6.6 2.6 collective-permute-start.1
  15.6 9.2 %collective-permute-done.1 = bf16[64,1664]{1,0:T(8,128)(2,1)S(1)} collective-permute-done((bf16[64,1664]{1,0:T(8,128)(2,1)S(1)}, bf16[64,1664]{1,0:T(8,128)(2,1)S(1)}, u32[]{:S(2)}, u32[]{:S(2)}) %collective-permute-start.1) | collective-permute-done | bytes 213024 | tf_op jit(solution)/shard_map/ppermute | solution.py:61
  28.0 3.8 collective-permute-start.5
  35.8 7.1 %collective-permute-done.6 = bf16[64,1024]{1,0:T(8,128)(2,1)S(1)} collective-permute-done((bf16[64,1024]{1,0:T(8,128)(2,1)S(1)}, bf16[64,1024]{1,0:T(8,128)(2,1)S(1)}, u32[]{:S(2)}, u32[]{:S(2)}) %collective-permute-start.6) | collective-permute-done | bytes 131104 | tf_op jit(solution)/shard_map/ppermute | solution.py:61
  48.2 17.1 %collective-permute-done.10 = bf16[128,1024]{1,0:T(8,128)(2,1)S(1)} collective-permute-done((bf16[128,1024]{1,0:T(8,128)(2,1)S(1)}, bf16[128,1024]{1,0:T(8,128)(2,1)S(1)}, u32[]{:S(2)}, u32[]{:S(2)}) %collective-permute-start.10) | collective-permute-done | bytes 262176 | tf_op jit(solution)/shard_map/ppermute | solution.py:61
  67.1 5.3 %pad_maximum_fusion.refs_0_ = bf16[1024,1664]{1,0:T(8,128)(2,1)S(1)} fusion(bf16[256,1664]{1,0:T(8,128)(2,1)S(1)} %collective-permute-done.9, bf16[256,1664]{1,0:T(8,128)(2,1)S(1)} %collective-permute-done.8, bf16[256,1664]{1,0:T(8,128)(2,1)S(1)} %pad_maximum_fusion.7, bf16[256,1664]{1,0:T(8,128)(2,1)S(1)} %pad_maximum_fusion.6), kind=kLoop, calls=%fused_computation.34 | loop fusion | flops 13631488 | bytes 6815744 | tf_op jit(solution)/shard_map/concatenate | solution.py:156
  73.6 4.8 %collective-permute-start.14 = (bf16[64,1536]{1,0:T(8,128)(2,1)}, bf16[64,1536]{1,0:T(8,128)(2,1)S(1)}, u32[]{:S(2)}, u32[]{:S(2)}) collective-permute-start(bf16[64,1536]{1,0:T(8,128)(2,1)} %get-tuple-element.311), channel_id=1, source_target_pairs={{0,8},{1,9},{2,10},{3,11},{4,12},{5,13},{6,14},{7,15},{8,0},{9,1},... | collective-permute-start | bytes 589832 | tf_op jit(solution)/shard_map/ppermute | solution.py:61
  83.8 3.8 shard_map.221
  90.3 3.5 convolution_bitcast_fusion
  104.3 5.8 %collective-permute-done.20 = bf16[128,1536]{1,0:T(8,128)(2,1)S(1)} collective-permute-done((bf16[128,1536]{1,0:T(8,128)(2,1)S(1)}, bf16[128,1536]{1,0:T(8,128)(2,1)S(1)}, u32[]{:S(2)}, u32[]{:S(2)}) %collective-permute-start.20) | collective-permute-done | bytes 393248 | tf_op jit(solution)/shard_map/ppermute | solution.py:61
  110.1 11.0 %collective-permute-done.21 = bf16[128,1536]{1,0:T(8,128)(2,1)S(1)} collective-permute-done((bf16[128,1536]{1,0:T(8,128)(2,1)S(1)}, bf16[128,1536]{1,0:T(8,128)(2,1)S(1)}, u32[]{:S(2)}, u32[]{:S(2)}) %collective-permute-start.21) | collective-permute-done | bytes 393248 | tf_op jit(solution)/shard_map/ppermute | solution.py:61
  131.0 10.8 %shard_map.222 = (f32[1,1024,512]{2,1,0:T(8,128)S(1)}, bf16[1,1024,512]{2,1,0:T(8,128)(2,1)S(1)}, f32[1,4,4,512]{3,2,1,0:T(4,128)S(1)}) custom-call(s32[6]{0:T(128)S(1)} %pad_add_fusion.info_ref, bf16[1,1024,512]{2,1,0:T(8,128)(2,1)S(1)} %bitcast.200, bf16[4,1,512,512]{3,2,1,0:T(8,128)(2,1)S(1)} %constant_dynamic-update-slice_fusion.k_ref.v_ref, ...), custom_call_target="tpu_custom_call" | custom-call | flops 16777216 | bytes 1048576 | tf_op jit(solution)/shard_map/pallas_call | solution.py:384
  141.8 2.9 collective-permute-done.25
  147.3 5.9 %shard_map.223 = bf16[2048,1024]{1,0:T(8,128)(2,1)S(1)} custom-call(s32[1]{0:T(128)} %bitcast.me_ref, bf16[1024,1024]{1,0:T(8,128)(2,1)S(1)} %pad_maximum_fusion.3.refs_0_, bf16[1024,1024]{1,0:T(8,128)(2,1)S(1)} %collective-permute-done.19.refs_1_), custom_call_target="tpu_custom_call" | custom-call | tf_op jit(solution)/shard_map/pallas_call | solution.py:88
  154.8 9.2 %collective-permute-start.30 = (bf16[128,1536]{1,0:T(8,128)(2,1)S(1)}, bf16[128,1536]{1,0:T(8,128)(2,1)S(1)}, u32[]{:S(2)}, u32[]{:S(2)}) collective-permute-start(bf16[128,1536]{1,0:T(8,128)(2,1)S(1)} %pad_maximum_fusion.23), channel_id=1, source_target_pairs={{0,2},{1,3},{2,0},{3,1},{4,6},{5,7},{6,4},{7,5},{8,10},{9,11},{10,... | collective-permute-start | bytes 1179656 | tf_op jit(solution)/shard_map/ppermute | solution.py:61
  164.0 2.6 multiply_reduce_fusion
  168.7 4.6 %collective-permute-done.30 = bf16[128,1536]{1,0:T(8,128)(2,1)S(1)} collective-permute-done((bf16[128,1536]{1,0:T(8,128)(2,1)S(1)}, bf16[128,1536]{1,0:T(8,128)(2,1)S(1)}, u32[]{:S(2)}, u32[]{:S(2)}) %collective-permute-start.30) | collective-permute-done | bytes 393248 | tf_op jit(solution)/shard_map/ppermute | solution.py:61
  176.9 2.6 shard_map.224
  189.0 3.4 collective-permute-done.31
  196.6 5.1 %collective-permute-done.33.refs_1_ = bf16[1024,1536]{1,0:T(8,128)(2,1)S(1)} collective-permute-done((bf16[1024,1536]{1,0:T(8,128)(2,1)S(1)}, bf16[1024,1536]{1,0:T(8,128)(2,1)S(1)}, u32[]{:S(2)}, u32[]{:S(2)}) %collective-permute-start.33) | collective-permute-done | bytes 3145760 | tf_op jit(solution)/shard_map/ppermute | solution.py:61
  201.7 4.5 %collective-permute-done.34 = bf16[1024,1536]{1,0:T(8,128)(2,1)S(1)} collective-permute-done((bf16[1024,1536]{1,0:T(8,128)(2,1)S(1)}, bf16[1024,1536]{1,0:T(8,128)(2,1)S(1)}, u32[]{:S(2)}, u32[]{:S(2)}) %collective-permute-start.34) | collective-permute-done | bytes 3145760 | tf_op jit(solution)/shard_map/ppermute | solution.py:61
  220.2 6.2 %collective-permute-done.35 = bf16[256,1536]{1,0:T(8,128)(2,1)S(1)} collective-permute-done((bf16[256,1536]{1,0:T(8,128)(2,1)S(1)}, bf16[256,1536]{1,0:T(8,128)(2,1)S(1)}, u32[]{:S(2)}, u32[]{:S(2)}) %collective-permute-start.35) | collective-permute-done | bytes 786464 | tf_op jit(solution)/shard_map/ppermute | solution.py:61
  229.0 3.2 shard_map.227
  236.6 10.2 %fusion.18 = (f32[512]{0:T(512)}, f32[512,2048]{1,0:T(8,128)}) fusion(f32[1,512,2048]{2,1,0:T(8,128)} %copy-done.17, f32[2048]{0:T(1024)S(1)} %get-tuple-element.557, bf16[2048,512]{1,0:T(8,128)(2,1)} %copy-done.10, bf16[2048,512]{1,0:T(8,128)(2,1)} %copy-done.9, bf16[2048,512]{1,0:T(8,128)(2,1)} %copy-done.8, bf16[2048,512]{1,0:T(8,128)(2,1)} %copy-done.7, ...), kind=kOutput, calls=%fused_computation.25 | convolution fusion | flops 4340055552 | bytes 18884608 | tf_op jit(solution)/shard_map/rtf,df->rtd/dot_general | solution.py:620
  247.5 5.2 %fusion.19 = f32[1,512,2048]{2,1,0:T(8,128)S(1)} fusion(f32[1,512,2048]{2,1,0:T(8,128)} %copy-done.17, bf16[1,512,2048]{2,1,0:T(8,128)(2,1)} %param.15, f32[512,2048]{1,0:T(8,128)} %get-tuple-element.642, f32[512]{0:T(512)S(1)} %broadcast_multiply_fusion.8, f32[512]{0:T(512)} %get-tuple-element.635, f32[2048]{0:T(1024)S(1)} %get-tuple-element.557, ...), kind=kLoop, calls=%fused_computation.27 | loop fusion | flops 8388608 | bytes 14696448 | tf_op jit(solution)/shard_map/add | solution.py:626
  267.6 3.6 fusion.17
  271.3 5.9 %shard_map.229 = (bf16[1024,1024]{1,0:T(8,128)(2,1)S(1)}, bf16[1024,1024]{1,0:T(8,128)(2,1)S(1)}) custom-call(s32[1]{0:T(128)} %bitcast.me_ref, bf16[2048,1024]{1,0:T(8,128)(2,1)S(1)} %convolution_convert_fusion.refs_0_), custom_call_target="tpu_custom_call" | custom-call | tf_op jit(solution)/shard_map/pallas_call | solution.py:122
  277.1 5.2 %shard_map.228 = (f32[1,256,512]{2,1,0:T(8,128)S(1)}, f32[4,1,64,512]{3,2,1,0:T(8,128)S(1)}, f32[4,1,64,512]{3,2,1,0:T(8,128)S(1)}) custom-call(s32[6]{0:T(128)S(1)} %pad_add_fusion.info_ref, bf16[1,1024,512]{2,1,0:T(8,128)(2,1)S(1)} %bitcast.201, bf16[4,1,512,512]{3,2,1,0:T(8,128)(2,1)S(1)} %constant_dynamic-update-slice_fusion.k_ref.v_ref, ...), custom_call_target="tpu_custom_call" | custom-call | flops 4194304 | bytes 1048576 | tf_op jit(solution)/shard_map/pallas_call | solution.py:464
  289.1 5.7 %collective-permute-start.46 = (bf16[128,1536]{1,0:T(8,128)(2,1)S(1)}, bf16[128,1536]{1,0:T(8,128)(2,1)S(1)}, u32[]{:S(2)}, u32[]{:S(2)}) collective-permute-start(bf16[128,1536]{1,0:T(8,128)(2,1)S(1)} %slice.646), channel_id=1, source_target_pairs={{0,2},{1,3},{2,0},{3,1},{4,6},{5,7},{6,4},{7,5},{8,10},{9,11},{10,... | collective-permute-start | bytes 1179656 | tf_op jit(solution)/shard_map/ppermute | solution.py:61
  294.7 5.4 %shard_map.230 = (f32[1,256,512]{2,1,0:T(8,128)S(1)}, f32[4,1,64,512]{3,2,1,0:T(8,128)S(1)}, f32[4,1,64,512]{3,2,1,0:T(8,128)S(1)}) custom-call(s32[6]{0:T(128)S(1)} %pad_add_fusion.info_ref, bf16[1,1024,512]{2,1,0:T(8,128)(2,1)S(1)} %bitcast.202, bf16[4,1,512,512]{3,2,1,0:T(8,128)(2,1)S(1)} %constant_dynamic-update-slice_fusion.k_ref.v_ref, ...), custom_call_target="tpu_custom_call" | custom-call | flops 4194304 | bytes 1048576 | tf_op jit(solution)/shard_map/pallas_call | solution.py:464
  300.1 4.1 collective-permute-done.46
  308.7 3.0 collective-permute-start.49
  313.1 5.1 %shard_map.231 = (f32[1,256,512]{2,1,0:T(8,128)S(1)}, f32[4,1,64,512]{3,2,1,0:T(8,128)S(1)}, f32[4,1,64,512]{3,2,1,0:T(8,128)S(1)}) custom-call(s32[6]{0:T(128)S(1)} %pad_add_fusion.info_ref, bf16[1,1024,512]{2,1,0:T(8,128)(2,1)S(1)} %bitcast.203, bf16[4,1,512,512]{3,2,1,0:T(8,128)(2,1)S(1)} %constant_dynamic-update-slice_fusion.k_ref.v_ref, ...), custom_call_target="tpu_custom_call" | custom-call | flops 4194304 | bytes 1048576 | tf_op jit(solution)/shard_map/pallas_call | solution.py:464
  319.8 5.9 %collective-permute-done.49 = bf16[64,1536]{1,0:T(8,128)(2,1)S(1)} collective-permute-done((bf16[64,1536]{1,0:T(8,128)(2,1)S(1)}, bf16[64,1536]{1,0:T(8,128)(2,1)S(1)}, u32[]{:S(2)}, u32[]{:S(2)}) %collective-permute-start.49) | collective-permute-done | bytes 196640 | tf_op jit(solution)/shard_map/ppermute | solution.py:61
  328.2 5.1 %shard_map.232 = (f32[1,256,512]{2,1,0:T(8,128)S(1)}, f32[4,1,64,512]{3,2,1,0:T(8,128)S(1)}, f32[4,1,64,512]{3,2,1,0:T(8,128)S(1)}) custom-call(s32[6]{0:T(128)S(1)} %pad_add_fusion.info_ref, bf16[1,1024,512]{2,1,0:T(8,128)(2,1)S(1)} %bitcast.204, bf16[4,1,512,512]{3,2,1,0:T(8,128)(2,1)S(1)} %constant_dynamic-update-slice_fusion.k_ref.v_ref, ...), custom_call_target="tpu_custom_call" | custom-call | flops 4194304 | bytes 1048576 | tf_op jit(solution)/shard_map/pallas_call | solution.py:464
  339.8 4.5 %collective-permute-start.57 = (bf16[64,1024]{1,0:T(8,128)(2,1)S(1)}, bf16[64,1024]{1,0:T(8,128)(2,1)S(1)}, u32[]{:S(2)}, u32[]{:S(2)}) collective-permute-start(bf16[64,1024]{1,0:T(8,128)(2,1)S(1)} %slice.661), channel_id=1, source_target_pairs={{0,8},{1,9},{2,10},{3,11},{4,12},{5,13},{6,14},{7,15},{8,0},{9,1},... | collective-permute-start | bytes 393224 | tf_op jit(solution)/shard_map/ppermute | solution.py:61
  347.2 4.8 %collective-permute-start.56 = (bf16[1,512,512]{2,1,0:T(8,128)(2,1)S(1)}, bf16[1,512,512]{2,1,0:T(8,128)(2,1)S(1)}, u32[]{:S(2)}, u32[]{:S(2)}) collective-permute-start(bf16[1,512,512]{2,1,0:T(8,128)(2,1)S(1)} %fusion.73), channel_id=1, source_target_pairs={{0,2},{1,3},{2,0},{3,1},{4,6},{5,7},{6,4},{7,5},{8,10},{9,11},{10,... | collective-permute-start | bytes 1572872 | tf_op jit(solution)/shard_map/ppermute | solution.py:61
  359.3 4.7 %collective-permute-done.56 = bf16[1,512,512]{2,1,0:T(8,128)(2,1)S(1)} collective-permute-done((bf16[1,512,512]{2,1,0:T(8,128)(2,1)S(1)}, bf16[1,512,512]{2,1,0:T(8,128)(2,1)S(1)}, u32[]{:S(2)}, u32[]{:S(2)}) %collective-permute-start.56) | collective-permute-done | bytes 524320 | tf_op jit(solution)/shard_map/ppermute | solution.py:61
  364.0 4.3 shard_map.233
  373.4 2.9 fusion.76.refs_0_
  376.3 3.2 shard_map.234
  383.1 2.8 collective-permute-start.62
  386.5 6.2 %fusion.12 = (f32[512]{0:T(512)S(1)}, f32[512,2048]{1,0:T(8,128)S(1)}) fusion(bf16[1,512,2048]{2,1,0:T(8,128)(2,1)S(1)} %copy-done.15, f32[2048]{0:T(1024)S(1)} %copy-done.87, bf16[2048,1536]{1,0:T(8,128)(2,1)} %copy-done.2, bf16[1,512,512]{2,1,0:T(8,128)(2,1)S(1)} %pad_maximum_fusion.17, bf16[1,1024,512]{2,1,0:T(8,128)(2,1)S(1)} %bitcast.224), kind=kOutput, calls=%fused_computation.17 | convolution fusion | flops 3228564992 | bytes 14166016 | tf_op jit(solution)/shard_map/ret,de->rtd/dot_general | solution.py:692
  392.7 3.1 fusion.11
  395.8 2.5 collective-permute-done.62
  405.0 10.1 %collective-permute-done.69 = f32[1,128]{1,0:T(1,128)S(1)} collective-permute-done((f32[1,128]{1,0:T(1,128)S(1)}, f32[1,128]{1,0:T(1,128)S(1)}, u32[]{:S(2)}, u32[]{:S(2)}) %collective-permute-start.69) | collective-permute-done | bytes 544 | tf_op jit(solution)/shard_map/ppermute | solution.py:61
  425.1 4.4 collective-permute-done.71
  (534 shorter events, 185.7 us)
Async XLA Ops:
  6.6 18.2 %collective-permute-start.1 = (bf16[64,1664]{1,0:T(8,128)(2,1)S(1)}, bf16[64,1664]{1,0:T(8,128)(2,1)S(1)}, u32[]{:S(2)}, u32[]{:S(2)}) collective-permute-start(bf16[64,1664]{1,0:T(8,128)(2,1)S(1)} %concatenate.199), channel_id=1, source_target_pairs={{0,16},{1,17},{2,18},{3,19},{4,20},{5,21},{6,22},{7,23},{8,24},{9,... | collective-permute-start | bytes 638984 | tf_op jit(solution)/shard_map/ppermute | solution.py:61
  9.2 15.6 %collective-permute-start.2 = (bf16[64,1664]{1,0:T(8,128)(2,1)S(1)}, bf16[64,1664]{1,0:T(8,128)(2,1)S(1)}, u32[]{:S(2)}, u32[]{:S(2)}) collective-permute-start(bf16[64,1664]{1,0:T(8,128)(2,1)S(1)} %concatenate.199), channel_id=1, source_target_pairs={{0,24},{1,25},{2,26},{3,27},{4,28},{5,29},{6,30},{7,31},{8,16},{9,... | collective-permute-start | bytes 638984 | tf_op jit(solution)/shard_map/ppermute | solution.py:61
  24.9 18.1 %collective-permute-start.3 = (bf16[128,1664]{1,0:T(8,128)(2,1)S(1)}, bf16[128,1664]{1,0:T(8,128)(2,1)S(1)}, u32[]{:S(2)}, u32[]{:S(2)}) collective-permute-start(bf16[128,1664]{1,0:T(8,128)(2,1)S(1)} %get-tuple-element.289), channel_id=1, source_target_pairs={{0,4},{1,5},{2,6},{3,7},{4,0},{5,1},{6,2},{7,3},{8,12},{9,13},{10,... | collective-permute-start | bytes 1277960 | tf_op jit(solution)/shard_map/ppermute | solution.py:61
  26.4 16.5 %collective-permute-start.4 = (bf16[128,1664]{1,0:T(8,128)(2,1)S(1)}, bf16[128,1664]{1,0:T(8,128)(2,1)S(1)}, u32[]{:S(2)}, u32[]{:S(2)}) collective-permute-start(bf16[128,1664]{1,0:T(8,128)(2,1)S(1)} %get-tuple-element.290), channel_id=1, source_target_pairs={{0,2},{1,3},{2,0},{3,1},{4,6},{5,7},{6,4},{7,5},{8,10},{9,11},{10,... | collective-permute-start | bytes 1277960 | tf_op jit(solution)/shard_map/ppermute | solution.py:61
  43.1 22.2 %collective-permute-start.8 = (bf16[256,1664]{1,0:T(8,128)(2,1)S(1)}, bf16[256,1664]{1,0:T(8,128)(2,1)S(1)}, u32[]{:S(2)}, u32[]{:S(2)}) collective-permute-start(bf16[256,1664]{1,0:T(8,128)(2,1)S(1)} %pad_maximum_fusion.6), channel_id=1, source_target_pairs={{0,2},{1,3},{2,0},{3,1},{4,6},{5,7},{6,4},{7,5},{8,10},{9,11},{10,... | collective-permute-start | bytes 2555912 | tf_op jit(solution)/shard_map/ppermute | solution.py:61
  43.7 21.7 %collective-permute-start.9 = (bf16[256,1664]{1,0:T(8,128)(2,1)S(1)}, bf16[256,1664]{1,0:T(8,128)(2,1)S(1)}, u32[]{:S(2)}, u32[]{:S(2)}) collective-permute-start(bf16[256,1664]{1,0:T(8,128)(2,1)S(1)} %pad_maximum_fusion.7), channel_id=1, source_target_pairs={{0,4},{1,5},{2,6},{3,7},{4,0},{5,1},{6,2},{7,3},{8,12},{9,13},{10,... | collective-permute-start | bytes 2555912 | tf_op jit(solution)/shard_map/ppermute | solution.py:61
  44.3 21.0 %collective-permute-start.10 = (bf16[128,1024]{1,0:T(8,128)(2,1)S(1)}, bf16[128,1024]{1,0:T(8,128)(2,1)S(1)}, u32[]{:S(2)}, u32[]{:S(2)}) collective-permute-start(bf16[128,1024]{1,0:T(8,128)(2,1)S(1)} %pad_maximum_fusion.25), channel_id=1, source_target_pairs={{0,4},{1,5},{2,6},{3,7},{4,0},{5,1},{6,2},{7,3},{8,12},{9,13},{10,... | collective-permute-start | bytes 786440 | tf_op jit(solution)/shard_map/ppermute | solution.py:61
  45.9 19.4 %collective-permute-start.11 = (bf16[128,1024]{1,0:T(8,128)(2,1)S(1)}, bf16[128,1024]{1,0:T(8,128)(2,1)S(1)}, u32[]{:S(2)}, u32[]{:S(2)}) collective-permute-start(bf16[128,1024]{1,0:T(8,128)(2,1)S(1)} %pad_maximum_fusion.26), channel_id=1, source_target_pairs={{0,2},{1,3},{2,0},{3,1},{4,6},{5,7},{6,4},{7,5},{8,10},{9,11},{10,... | collective-permute-start | bytes 786440 | tf_op jit(solution)/shard_map/ppermute | solution.py:61
  73.6 23.0 %collective-permute-start.14 = (bf16[64,1536]{1,0:T(8,128)(2,1)}, bf16[64,1536]{1,0:T(8,128)(2,1)S(1)}, u32[]{:S(2)}, u32[]{:S(2)}) collective-permute-start(bf16[64,1536]{1,0:T(8,128)(2,1)} %get-tuple-element.311), channel_id=1, source_target_pairs={{0,8},{1,9},{2,10},{3,11},{4,12},{5,13},{6,14},{7,15},{8,0},{9,1},... | collective-permute-start | bytes 589832 | tf_op jit(solution)/shard_map/ppermute | solution.py:61
  78.4 18.2 %collective-permute-start.15 = (bf16[64,1536]{1,0:T(8,128)(2,1)}, bf16[64,1536]{1,0:T(8,128)(2,1)S(1)}, u32[]{:S(2)}, u32[]{:S(2)}) collective-permute-start(bf16[64,1536]{1,0:T(8,128)(2,1)} %get-tuple-element.311), channel_id=1, source_target_pairs={{0,16},{1,17},{2,18},{3,19},{4,20},{5,21},{6,22},{7,23},{8,24},{9,... | collective-permute-start | bytes 589832 | tf_op jit(solution)/shard_map/ppermute | solution.py:61
  80.3 16.4 %collective-permute-start.16 = (bf16[64,1536]{1,0:T(8,128)(2,1)}, bf16[64,1536]{1,0:T(8,128)(2,1)S(1)}, u32[]{:S(2)}, u32[]{:S(2)}) collective-permute-start(bf16[64,1536]{1,0:T(8,128)(2,1)} %get-tuple-element.311), channel_id=1, source_target_pairs={{0,24},{1,25},{2,26},{3,27},{4,28},{5,29},{6,30},{7,31},{8,16},{9,... | collective-permute-start | bytes 589832 | tf_op jit(solution)/shard_map/ppermute | solution.py:61
  81.7 14.9 %collective-permute-start.12 = (bf16[256,1024]{1,0:T(8,128)(2,1)}, bf16[256,1024]{1,0:T(8,128)(2,1)S(1)}, u32[]{:S(2)}, u32[]{:S(2)}) collective-permute-start(bf16[256,1024]{1,0:T(8,128)(2,1)} %pad_maximum_fusion.12), channel_id=1, source_target_pairs={{0,2},{1,3},{2,0},{3,1},{4,6},{5,7},{6,4},{7,5},{8,10},{9,11},{10,... | collective-permute-start | bytes 1572872 | tf_op jit(solution)/shard_map/ppermute | solution.py:61
  98.3 22.9 %collective-permute-start.19 = (bf16[1024,1024]{1,0:T(8,128)(2,1)S(1)}, bf16[1024,1024]{1,0:T(8,128)(2,1)S(1)}, u32[]{:S(2)}, u32[]{:S(2)}) collective-permute-start(bf16[1024,1024]{1,0:T(8,128)(2,1)S(1)} %pad_maximum_fusion.3.refs_0_), channel_id=1, source_target_pairs={{0,1},{1,0},{2,3},{3,2},{4,5},{5,4},{6,7},{7,6},{8,9},{9,8},{10,11... | collective-permute-start | bytes 6291464 | tf_op jit(solution)/shard_map/ppermute | solution.py:61
  98.4 22.8 %collective-permute-start.18 = (bf16[1,512,512]{2,1,0:T(8,128)(2,1)S(1)}, bf16[1,512,512]{2,1,0:T(8,128)(2,1)S(1)}, u32[]{:S(2)}, u32[]{:S(2)}) collective-permute-start(bf16[1,512,512]{2,1,0:T(8,128)(2,1)S(1)} %pad_maximum_fusion.15), channel_id=1, source_target_pairs={{0,2},{1,3},{2,0},{3,1},{4,6},{5,7},{6,4},{7,5},{8,10},{9,11},{10,... | collective-permute-start | bytes 1572872 | tf_op jit(solution)/shard_map/ppermute | solution.py:61
  100.4 20.7 %collective-permute-start.21 = (bf16[128,1536]{1,0:T(8,128)(2,1)S(1)}, bf16[128,1536]{1,0:T(8,128)(2,1)S(1)}, u32[]{:S(2)}, u32[]{:S(2)}) collective-permute-start(bf16[128,1536]{1,0:T(8,128)(2,1)S(1)} %pad_maximum_fusion.21), channel_id=1, source_target_pairs={{0,2},{1,3},{2,0},{3,1},{4,6},{5,7},{6,4},{7,5},{8,10},{9,11},{10,... | collective-permute-start | bytes 1179656 | tf_op jit(solution)/shard_map/ppermute | solution.py:61
  121.5 23.2 %collective-permute-start.22 = (bf16[256,1536]{1,0:T(8,128)(2,1)S(1)}, bf16[256,1536]{1,0:T(8,128)(2,1)S(1)}, u32[]{:S(2)}, u32[]{:S(2)}) collective-permute-start(bf16[256,1536]{1,0:T(8,128)(2,1)S(1)} %pad_maximum_fusion.8), channel_id=1, source_target_pairs={{0,2},{1,3},{2,0},{3,1},{4,6},{5,7},{6,4},{7,5},{8,10},{9,11},{10,... | collective-permute-start | bytes 2359304 | tf_op jit(solution)/shard_map/ppermute | solution.py:61
  122.1 22.6 %collective-permute-start.23 = (bf16[256,1536]{1,0:T(8,128)(2,1)S(1)}, bf16[256,1536]{1,0:T(8,128)(2,1)S(1)}, u32[]{:S(2)}, u32[]{:S(2)}) collective-permute-start(bf16[256,1536]{1,0:T(8,128)(2,1)S(1)} %pad_maximum_fusion.9), channel_id=1, source_target_pairs={{0,4},{1,5},{2,6},{3,7},{4,0},{5,1},{6,2},{7,3},{8,12},{9,13},{10,... | collective-permute-start | bytes 2359304 | tf_op jit(solution)/shard_map/ppermute | solution.py:61
  125.6 16.2 %collective-permute-start.24 = (bf16[64,1536]{1,0:T(8,128)(2,1)S(1)}, bf16[64,1536]{1,0:T(8,128)(2,1)S(1)}, u32[]{:S(2)}, u32[]{:S(2)}) collective-permute-start(bf16[64,1536]{1,0:T(8,128)(2,1)S(1)} %copy-done.72), channel_id=1, source_target_pairs={{0,8},{1,9},{2,10},{3,11},{4,12},{5,13},{6,14},{7,15},{8,0},{9,1},... | collective-permute-start | bytes 589832 | tf_op jit(solution)/shard_map/ppermute | solution.py:61
  127.5 17.1 %collective-permute-start.25 = (bf16[64,1536]{1,0:T(8,128)(2,1)S(1)}, bf16[64,1536]{1,0:T(8,128)(2,1)S(1)}, u32[]{:S(2)}, u32[]{:S(2)}) collective-permute-start(bf16[64,1536]{1,0:T(8,128)(2,1)S(1)} %copy-done.72), channel_id=1, source_target_pairs={{0,16},{1,17},{2,18},{3,19},{4,20},{5,21},{6,22},{7,23},{8,24},{9,... | collective-permute-start | bytes 589832 | tf_op jit(solution)/shard_map/ppermute | solution.py:61
  129.4 15.3 %collective-permute-start.26 = (bf16[64,1536]{1,0:T(8,128)(2,1)S(1)}, bf16[64,1536]{1,0:T(8,128)(2,1)S(1)}, u32[]{:S(2)}, u32[]{:S(2)}) collective-permute-start(bf16[64,1536]{1,0:T(8,128)(2,1)S(1)} %copy-done.72), channel_id=1, source_target_pairs={{0,24},{1,25},{2,26},{3,27},{4,28},{5,29},{6,30},{7,31},{8,16},{9,... | collective-permute-start | bytes 589832 | tf_op jit(solution)/shard_map/ppermute | solution.py:61
  145.0 28.3 %collective-permute-start.28 = (bf16[1024,1536]{1,0:T(8,128)(2,1)S(1)}, bf16[1024,1536]{1,0:T(8,128)(2,1)S(1)}, u32[]{:S(2)}, u32[]{:S(2)}) collective-permute-start(bf16[1024,1536]{1,0:T(8,128)(2,1)S(1)} %pad_maximum_fusion.1.refs_0_), channel_id=1, source_target_pairs={{0,1},{1,0},{2,3},{3,2},{4,5},{5,4},{6,7},{7,6},{8,9},{9,8},{10,11... | collective-permute-start | bytes 9437192 | tf_op jit(solution)/shard_map/ppermute | solution.py:61
  153.2 15.4 %collective-permute-start.29 = (bf16[128,1536]{1,0:T(8,128)(2,1)S(1)}, bf16[128,1536]{1,0:T(8,128)(2,1)S(1)}, u32[]{:S(2)}, u32[]{:S(2)}) collective-permute-start(bf16[128,1536]{1,0:T(8,128)(2,1)S(1)} %pad_maximum_fusion.22), channel_id=1, source_target_pairs={{0,4},{1,5},{2,6},{3,7},{4,0},{5,1},{6,2},{7,3},{8,12},{9,13},{10,... | collective-permute-start | bytes 1179656 | tf_op jit(solution)/shard_map/ppermute | solution.py:61
  154.8 18.5 %collective-permute-start.30 = (bf16[128,1536]{1,0:T(8,128)(2,1)S(1)}, bf16[128,1536]{1,0:T(8,128)(2,1)S(1)}, u32[]{:S(2)}, u32[]{:S(2)}) collective-permute-start(bf16[128,1536]{1,0:T(8,128)(2,1)S(1)} %pad_maximum_fusion.23), channel_id=1, source_target_pairs={{0,2},{1,3},{2,0},{3,1},{4,6},{5,7},{6,4},{7,5},{8,10},{9,11},{10,... | collective-permute-start | bytes 1179656 | tf_op jit(solution)/shard_map/ppermute | solution.py:61
  173.4 19.0 %collective-permute-start.31 = (bf16[256,1536]{1,0:T(8,128)(2,1)S(1)}, bf16[256,1536]{1,0:T(8,128)(2,1)S(1)}, u32[]{:S(2)}, u32[]{:S(2)}) collective-permute-start(bf16[256,1536]{1,0:T(8,128)(2,1)S(1)} %pad_maximum_fusion.10), channel_id=1, source_target_pairs={{0,2},{1,3},{2,0},{3,1},{4,6},{5,7},{6,4},{7,5},{8,10},{9,11},{10,... | collective-permute-start | bytes 2359304 | tf_op jit(solution)/shard_map/ppermute | solution.py:61
  175.2 18.3 %collective-permute-start.32 = (bf16[256,1536]{1,0:T(8,128)(2,1)S(1)}, bf16[256,1536]{1,0:T(8,128)(2,1)S(1)}, u32[]{:S(2)}, u32[]{:S(2)}) collective-permute-start(bf16[256,1536]{1,0:T(8,128)(2,1)S(1)} %pad_maximum_fusion.11), channel_id=1, source_target_pairs={{0,4},{1,5},{2,6},{3,7},{4,0},{5,1},{6,2},{7,3},{8,12},{9,13},{10,... | collective-permute-start | bytes 2359304 | tf_op jit(solution)/shard_map/ppermute | solution.py:61
  206.7 19.6 %collective-permute-start.35 = (bf16[256,1536]{1,0:T(8,128)(2,1)S(1)}, bf16[256,1536]{1,0:T(8,128)(2,1)S(1)}, u32[]{:S(2)}, u32[]{:S(2)}) collective-permute-start(bf16[256,1536]{1,0:T(8,128)(2,1)S(1)} %get-tuple-element.378), channel_id=1, source_target_pairs={{0,2},{1,3},{2,0},{3,1},{4,6},{5,7},{6,4},{7,5},{8,10},{9,11},{10,... | collective-permute-start | bytes 2359304 | tf_op jit(solution)/shard_map/ppermute | solution.py:61
  207.3 19.3 %collective-permute-start.36 = (bf16[256,1536]{1,0:T(8,128)(2,1)S(1)}, bf16[256,1536]{1,0:T(8,128)(2,1)S(1)}, u32[]{:S(2)}, u32[]{:S(2)}) collective-permute-start(bf16[256,1536]{1,0:T(8,128)(2,1)S(1)} %get-tuple-element.379), channel_id=1, source_target_pairs={{0,4},{1,5},{2,6},{3,7},{4,0},{5,1},{6,2},{7,3},{8,12},{9,13},{10,... | collective-permute-start | bytes 2359304 | tf_op jit(solution)/shard_map/ppermute | solution.py:61
  233.8 23.7 %collective-permute-start.37 = (bf16[128,1536]{1,0:T(8,128)(2,1)S(1)}, bf16[128,1536]{1,0:T(8,128)(2,1)}, u32[]{:S(2)}, u32[]{:S(2)}) collective-permute-start(bf16[128,1536]{1,0:T(8,128)(2,1)S(1)} %slice.649), channel_id=1, source_target_pairs={{0,4},{1,5},{2,6},{3,7},{4,0},{5,1},{6,2},{7,3},{8,12},{9,13},{10,... | collective-permute-start | bytes 1179656 | tf_op jit(solution)/shard_map/ppermute | solution.py:61
  235.2 22.3 %collective-permute-start.38 = (bf16[128,1536]{1,0:T(8,128)(2,1)S(1)}, bf16[128,1536]{1,0:T(8,128)(2,1)}, u32[]{:S(2)}, u32[]{:S(2)}) collective-permute-start(bf16[128,1536]{1,0:T(8,128)(2,1)S(1)} %slice.648), channel_id=1, source_target_pairs={{0,2},{1,3},{2,0},{3,1},{4,6},{5,7},{6,4},{7,5},{8,10},{9,11},{10,... | collective-permute-start | bytes 1179656 | tf_op jit(solution)/shard_map/ppermute | solution.py:61
  236.6 20.9 %collective-permute-start.39 = (bf16[1024,1536]{1,0:T(8,128)(2,1)}, bf16[1024,1536]{1,0:T(8,128)(2,1)}, u32[]{:S(2)}, u32[]{:S(2)}) collective-permute-start(bf16[1024,1536]{1,0:T(8,128)(2,1)} %get-tuple-element.396), channel_id=1, source_target_pairs={{0,1},{1,0},{2,3},{3,2},{4,5},{5,4},{6,7},{7,6},{8,9},{9,8},{10,11... | collective-permute-start | bytes 9437192 | tf_op jit(solution)/shard_map/ppermute | solution.py:61
  261.9 20.5 %collective-permute-start.43 = (bf16[256,1536]{1,0:T(8,128)(2,1)S(1)}, bf16[256,1536]{1,0:T(8,128)(2,1)S(1)}, u32[]{:S(2)}, u32[]{:S(2)}) collective-permute-start(bf16[256,1536]{1,0:T(8,128)(2,1)S(1)} %get-tuple-element.411), channel_id=1, source_target_pairs={{0,2},{1,3},{2,0},{3,1},{4,6},{5,7},{6,4},{7,5},{8,10},{9,11},{10,... | collective-permute-start | bytes 2359304 | tf_op jit(solution)/shard_map/ppermute | solution.py:61
  262.6 19.8 %collective-permute-start.44 = (bf16[256,1536]{1,0:T(8,128)(2,1)S(1)}, bf16[256,1536]{1,0:T(8,128)(2,1)}, u32[]{:S(2)}, u32[]{:S(2)}) collective-permute-start(bf16[256,1536]{1,0:T(8,128)(2,1)S(1)} %get-tuple-element.412), channel_id=1, source_target_pairs={{0,4},{1,5},{2,6},{3,7},{4,0},{5,1},{6,2},{7,3},{8,12},{9,13},{10,... | collective-permute-start | bytes 2359304 | tf_op jit(solution)/shard_map/ppermute | solution.py:61
  263.2 19.1 %collective-permute-start.40 = (bf16[64,1536]{1,0:T(8,128)(2,1)S(1)}, bf16[64,1536]{1,0:T(8,128)(2,1)}, u32[]{:S(2)}, u32[]{:S(2)}) collective-permute-start(bf16[64,1536]{1,0:T(8,128)(2,1)S(1)} %slice.657), channel_id=1, source_target_pairs={{0,8},{1,9},{2,10},{3,11},{4,12},{5,13},{6,14},{7,15},{8,0},{9,1},... | collective-permute-start | bytes 589832 | tf_op jit(solution)/shard_map/ppermute | solution.py:61
  264.6 17.7 %collective-permute-start.41 = (bf16[64,1536]{1,0:T(8,128)(2,1)S(1)}, bf16[64,1536]{1,0:T(8,128)(2,1)}, u32[]{:S(2)}, u32[]{:S(2)}) collective-permute-start(bf16[64,1536]{1,0:T(8,128)(2,1)S(1)} %get-tuple-element.409), channel_id=1, source_target_pairs={{0,16},{1,17},{2,18},{3,19},{4,20},{5,21},{6,22},{7,23},{8,24},{9,... | collective-permute-start | bytes 589832 | tf_op jit(solution)/shard_map/ppermute | solution.py:61
  266.2 16.1 %collective-permute-start.42 = (bf16[64,1536]{1,0:T(8,128)(2,1)S(1)}, bf16[64,1536]{1,0:T(8,128)(2,1)}, u32[]{:S(2)}, u32[]{:S(2)}) collective-permute-start(bf16[64,1536]{1,0:T(8,128)(2,1)S(1)} %get-tuple-element.410), channel_id=1, source_target_pairs={{0,24},{1,25},{2,26},{3,27},{4,28},{5,29},{6,30},{7,31},{8,16},{9,... | collective-permute-start | bytes 589832 | tf_op jit(solution)/shard_map/ppermute | solution.py:61
  285.8 18.4 %collective-permute-start.47 = (bf16[1024,1024]{1,0:T(8,128)(2,1)S(1)}, bf16[1024,1024]{1,0:T(8,128)(2,1)S(1)}, u32[]{:S(2)}, u32[]{:S(2)}) collective-permute-start(bf16[1024,1024]{1,0:T(8,128)(2,1)S(1)} %get-tuple-element.430), channel_id=1, source_target_pairs={{0,1},{1,0},{2,3},{3,2},{4,5},{5,4},{6,7},{7,6},{8,9},{9,8},{10,11... | collective-permute-start | bytes 6291464 | tf_op jit(solution)/shard_map/ppermute | solution.py:61
  289.1 15.1 %collective-permute-start.46 = (bf16[128,1536]{1,0:T(8,128)(2,1)S(1)}, bf16[128,1536]{1,0:T(8,128)(2,1)S(1)}, u32[]{:S(2)}, u32[]{:S(2)}) collective-permute-start(bf16[128,1536]{1,0:T(8,128)(2,1)S(1)} %slice.646), channel_id=1, source_target_pairs={{0,2},{1,3},{2,0},{3,1},{4,6},{5,7},{6,4},{7,5},{8,10},{9,11},{10,... | collective-permute-start | bytes 1179656 | tf_op jit(solution)/shard_map/ppermute | solution.py:61
  305.1 20.6 %collective-permute-start.51 = (bf16[256,1024]{1,0:T(8,128)(2,1)S(1)}, bf16[256,1024]{1,0:T(8,128)(2,1)S(1)}, u32[]{:S(2)}, u32[]{:S(2)}) collective-permute-start(bf16[256,1024]{1,0:T(8,128)(2,1)S(1)} %get-tuple-element.442), channel_id=1, source_target_pairs={{0,2},{1,3},{2,0},{3,1},{4,6},{5,7},{6,4},{7,5},{8,10},{9,11},{10,... | collective-permute-start | bytes 1572872 | tf_op jit(solution)/shard_map/ppermute | solution.py:61
  306.9 18.9 %collective-permute-start.52 = (bf16[256,1024]{1,0:T(8,128)(2,1)S(1)}, bf16[256,1024]{1,0:T(8,128)(2,1)S(1)}, u32[]{:S(2)}, u32[]{:S(2)}) collective-permute-start(bf16[256,1024]{1,0:T(8,128)(2,1)S(1)} %get-tuple-element.443), channel_id=1, source_target_pairs={{0,4},{1,5},{2,6},{3,7},{4,0},{5,1},{6,2},{7,3},{8,12},{9,13},{10,... | collective-permute-start | bytes 1572872 | tf_op jit(solution)/shard_map/ppermute | solution.py:61
  308.7 17.0 %collective-permute-start.49 = (bf16[64,1536]{1,0:T(8,128)(2,1)S(1)}, bf16[64,1536]{1,0:T(8,128)(2,1)S(1)}, u32[]{:S(2)}, u32[]{:S(2)}) collective-permute-start(bf16[64,1536]{1,0:T(8,128)(2,1)S(1)} %get-tuple-element.440), channel_id=1, source_target_pairs={{0,16},{1,17},{2,18},{3,19},{4,20},{5,21},{6,22},{7,23},{8,24},{9,... | collective-permute-start | bytes 589832 | tf_op jit(solution)/shard_map/ppermute | solution.py:61
  311.7 14.0 %collective-permute-start.50 = (bf16[64,1536]{1,0:T(8,128)(2,1)S(1)}, bf16[64,1536]{1,0:T(8,128)(2,1)S(1)}, u32[]{:S(2)}, u32[]{:S(2)}) collective-permute-start(bf16[64,1536]{1,0:T(8,128)(2,1)S(1)} %get-tuple-element.441), channel_id=1, source_target_pairs={{0,24},{1,25},{2,26},{3,27},{4,28},{5,29},{6,30},{7,31},{8,16},{9,... | collective-permute-start | bytes 589832 | tf_op jit(solution)/shard_map/ppermute | solution.py:61
  339.8 19.5 %collective-permute-start.57 = (bf16[64,1024]{1,0:T(8,128)(2,1)S(1)}, bf16[64,1024]{1,0:T(8,128)(2,1)S(1)}, u32[]{:S(2)}, u32[]{:S(2)}) collective-permute-start(bf16[64,1024]{1,0:T(8,128)(2,1)S(1)} %slice.661), channel_id=1, source_target_pairs={{0,8},{1,9},{2,10},{3,11},{4,12},{5,13},{6,14},{7,15},{8,0},{9,1},... | collective-permute-start | bytes 393224 | tf_op jit(solution)/shard_map/ppermute | solution.py:61
  344.3 15.0 %collective-permute-start.58 = (bf16[64,1024]{1,0:T(8,128)(2,1)S(1)}, bf16[64,1024]{1,0:T(8,128)(2,1)S(1)}, u32[]{:S(2)}, u32[]{:S(2)}) collective-permute-start(bf16[64,1024]{1,0:T(8,128)(2,1)S(1)} %get-tuple-element.486), channel_id=1, source_target_pairs={{0,16},{1,17},{2,18},{3,19},{4,20},{5,21},{6,22},{7,23},{8,24},{9,... | collective-permute-start | bytes 393224 | tf_op jit(solution)/shard_map/ppermute | solution.py:61
  344.3 15.1 %collective-permute-start.59 = (bf16[64,1024]{1,0:T(8,128)(2,1)S(1)}, bf16[64,1024]{1,0:T(8,128)(2,1)S(1)}, u32[]{:S(2)}, u32[]{:S(2)}) collective-permute-start(bf16[64,1024]{1,0:T(8,128)(2,1)S(1)} %get-tuple-element.487), channel_id=1, source_target_pairs={{0,24},{1,25},{2,26},{3,27},{4,28},{5,29},{6,30},{7,31},{8,16},{9,... | collective-permute-start | bytes 393224 | tf_op jit(solution)/shard_map/ppermute | solution.py:61
  347.2 16.8 %collective-permute-start.56 = (bf16[1,512,512]{2,1,0:T(8,128)(2,1)S(1)}, bf16[1,512,512]{2,1,0:T(8,128)(2,1)S(1)}, u32[]{:S(2)}, u32[]{:S(2)}) collective-permute-start(bf16[1,512,512]{2,1,0:T(8,128)(2,1)S(1)} %fusion.73), channel_id=1, source_target_pairs={{0,2},{1,3},{2,0},{3,1},{4,6},{5,7},{6,4},{7,5},{8,10},{9,11},{10,... | collective-permute-start | bytes 1572872 | tf_op jit(solution)/shard_map/ppermute | solution.py:61
  381.3 14.5 %collective-permute-start.61 = (bf16[256,1024]{1,0:T(8,128)(2,1)S(1)}, bf16[256,1024]{1,0:T(8,128)(2,1)S(1)}, u32[]{:S(2)}, u32[]{:S(2)}) collective-permute-start(bf16[256,1024]{1,0:T(8,128)(2,1)S(1)} %get-tuple-element.502), channel_id=1, source_target_pairs={{0,2},{1,3},{2,0},{3,1},{4,6},{5,7},{6,4},{7,5},{8,10},{9,11},{10,... | collective-permute-start | bytes 1572872 | tf_op jit(solution)/shard_map/ppermute | solution.py:61
  383.1 15.1 %collective-permute-start.62 = (bf16[256,1024]{1,0:T(8,128)(2,1)S(1)}, bf16[256,1024]{1,0:T(8,128)(2,1)S(1)}, u32[]{:S(2)}, u32[]{:S(2)}) collective-permute-start(bf16[256,1024]{1,0:T(8,128)(2,1)S(1)} %get-tuple-element.503), channel_id=1, source_target_pairs={{0,4},{1,5},{2,6},{3,7},{4,0},{5,1},{6,2},{7,3},{8,12},{9,13},{10,... | collective-permute-start | bytes 1572872 | tf_op jit(solution)/shard_map/ppermute | solution.py:61
  400.4 14.8 %collective-permute-start.65 = (bf16[128,1024]{1,0:T(8,128)(2,1)S(1)}, bf16[128,1024]{1,0:T(8,128)(2,1)S(1)}, u32[]{:S(2)}, u32[]{:S(2)}) collective-permute-start(bf16[128,1024]{1,0:T(8,128)(2,1)S(1)} %slice.651), channel_id=1, source_target_pairs={{0,4},{1,5},{2,6},{3,7},{4,0},{5,1},{6,2},{7,3},{8,12},{9,13},{10,... | collective-permute-start | bytes 786440 | tf_op jit(solution)/shard_map/ppermute | solution.py:61
  (143 other events, 1068.2 us)

commit v6 on v5

--- a/solution.py
+++ b/solution.py
@@ -92,6 +92,7 @@
         out_specs=[VMEM] * len(widths),
         scratch_shapes=[pltpu.SemaphoreType.DMA((copies,))],
         compiler_params=pltpu.CompilerParams(vmem_limit_bytes=24 << 20),
+        cost_estimate=pl.CostEstimate(flops=0, transcendentals=0, bytes_accessed=1 << 16),
     )(me, *blocks)
 
 
@@ -126,14 +127,15 @@
         out_specs=[ANY] * len(orders),
         scratch_shapes=[pltpu.SemaphoreType.DMA((copies,))],
         compiler_params=pltpu.CompilerParams(vmem_limit_bytes=24 << 20),
+        cost_estimate=pl.CostEstimate(flops=0, transcendentals=0, bytes_accessed=1 << 16),
     )(me, *arrays)
 
 
 class Gather:
-    def __init__(self, parts, me, devices):
+    def __init__(self, parts, me, devices, first=False):
         self.part = jnp.concatenate(parts, axis=1)
         self.widths = [one.shape[1] for one in parts]
-        self.me, self.devices, self.staged = me, devices, devices == 32
+        self.me, self.devices, self.staged, self.first = me, devices, devices == 32, first
         self.stage, self.outgoing, self.incoming = 0, (), ()
 
     def prepare(self):
@@ -152,6 +154,8 @@
                 jnp.concatenate([own, came]) for own, came in zip(self.outgoing, self.incoming)
             )
             self.masks = (2,), (4,)
+        elif self.first:
+            self.outgoing, self.masks = self.outgoing + self.incoming, ((1,),) * 4
         else:
             self.outgoing, self.masks = (jnp.concatenate([*self.outgoing, *self.incoming]),), ((1,),)
 
@@ -167,8 +171,10 @@
             ends = [sum(self.widths[:i]) for i in range(1, len(self.widths))]
             return jnp.split(whole, ends, axis=1)
         near, far = (0, 8, 4, 12), (16, 24, 18, 26)
-        masks = [*near, *far, *(m | 2 for m in near), *(m | 4 for m in far)]
-        masks = masks, [m | 1 for m in masks]
+        masks = [near, far, [m | 2 for m in near], [m | 4 for m in far]]
+        if not self.first:
+            masks = [[m for own in masks for m in own]]
+        masks += [[m | 1 for m in own] for own in masks]
         blocks = self.outgoing + self.incoming
         return place(blocks, masks, self.widths, self.me, self.part.shape[0] * self.devices)
 
@@ -231,22 +237,20 @@
             if stage == 0:
                 self.values = lax.psum(self.values, ("dp", "shard"))
             return
-        if stage in (1, 2, 3):
+        if stage:
             self.values = self.values + self.incoming[0]
-        if stage == 4:
-            one, two, three = self.incoming
-            self.values = (self.values + one) + (two + three)
-            return
-        self.outgoing, self.masks = (self.values,), ((1,), (2,), (4,), (8, 16, 24))[stage]
+        if stage < 5:
+            self.outgoing, self.masks = (self.values,), ((1,), (2,), (4,), (8,), (16,))[stage]
 
     def launch(self):
         if self.staged:
             self.incoming = tuple(swap(self.outgoing[0], mask, self.devices) for mask in self.masks)
 
 
-def open_slot(travellers, *values):
+def open_slot(travellers, *values, ready=()):
     for one in travellers:
-        one.prepare()
+        if one not in ready:
+            one.prepare()
     travellers = [one for one in travellers if one.staged]
     if not travellers:
         return values
@@ -302,14 +306,14 @@
         self.stage += 1
         if not self.staged:
             if stage == 0:
-                self.total = lax.psum_scatter(grad, "shard", scatter_dimension=0)
+                self.shares = lax.psum_scatter(grad, "shard", scatter_dimension=0)[None], ()
         elif stage == 0:
             self.outgoing, self.mask = (grad[2:].astype(LOW),), 1
         elif stage == 1:
-            self.came = self.incoming[0].astype(jnp.float32)
-            self.outgoing, self.mask = ((grad[1] + self.came[1]).astype(LOW),), 2
+            (self.came,) = self.incoming
+            self.outgoing, self.mask = ((grad[1:2] + self.came[1:].astype(jnp.float32)).astype(LOW),), 2
         else:
-            self.total = grad[0] + self.came[0] + self.incoming[0].astype(jnp.float32)
+            self.shares = grad, (self.came, *self.incoming)
 
     def launch(self):
         if self.staged:
@@ -403,16 +407,39 @@
     )(info, queries, keys_values, keys_values)
 
 
-def attention_back(info, queries, keys_values, out, sums, grad_out, first, groups, part_first):
+def head_back(grad, raw, gain, cos_t, sin_t):
+    half_len = HD // 2
+    along = grad * sin_t
+    grad = grad * cos_t + jnp.concatenate([along[half_len:], -along[:half_len]], axis=0)
+    inverse = lax.rsqrt(jnp.mean(raw * raw, axis=0, keepdims=True) + EPS)
+    products = grad * (raw * inverse)
+    grad = grad * gain
+    cubed = inverse * inverse * inverse
+    return inverse * grad - raw * cubed * jnp.mean(grad * raw, axis=0, keepdims=True), products
+
+
+def fold(values):
+    total = values[:, :128]
+    for at in range(128, values.shape[1], 128):
+        total = total + values[:, at : at + 128]
+    return total
+
+
+def attention_back(
+    info, queries, keys_values, out, sums, grad_out, q_raw, gain, cos_t, sin_t, group, carried
+):
     rows, _, length = queries.shape
     pieces = keys_values.shape[0]
     group_width = GROUP * HD
+    scale_factor = 1.0 / math.sqrt(HD)
 
     def kernel(
-        info_ref, q_ref, k_ref, v_ref, out_ref, sums_ref, grad_ref, dq_ref, dk_ref, dv_ref,
-        grad_low, grad_sums, q_rows, grad_rows, k_accum, v_accum,
+        info_ref, q_ref, k_ref, v_ref, out_ref, sums_ref, grad_ref, raw_ref, gain_ref, cos_ref, sin_ref, *refs
     ):
-        dq_ref[...] = jnp.zeros_like(dq_ref)
+        refs = refs[len(carried) :]
+        dq_ref, dkv_ref, gain_grad_ref = refs[:3]
+        grad_low, grad_sums, q_rows, grad_rows, k_accum, v_accum, q_accum = refs[3:]
+        q_accum[...] = jnp.zeros_like(q_accum)
         for head in range(GROUP):
             own = slice(head * HD, (head + 1) * HD)
             inverse = 1.0 / sums_ref[0, 0, head : head + 1, :]
@@ -436,43 +463,51 @@
                 grad_scores = (exps * grad_exps).astype(LOW)
                 v_accum[...] += dot(exps.astype(LOW), grad_rows[head], LAST_FIRST)
                 k_accum[...] += dot(grad_scores, q_rows[head], LAST_FIRST)
-                dq_ref[0, own, :] += dot(key_t, grad_scores, LAST_FIRST)
+                q_accum[own, :] += dot(key_t, grad_scores, LAST_FIRST)
 
         def before():
             k_accum[...] = jnp.zeros_like(k_accum)
             v_accum[...] = jnp.zeros_like(v_accum)
 
         def after(piece):
-            dk_ref[piece, 0] = k_accum[...].T
-            dv_ref[piece, 0] = v_accum[...].T
+            dkv_ref[piece, 0, 0] = k_accum[...].T
+            dkv_ref[piece, 0, 1] = v_accum[...].T
 
         over_pieces(info_ref, pieces, length, pl.program_id(0), tile, before, after)
-
-    q_spec = pl.BlockSpec((1, group_width, length), lambda row, group, *_: (row, group + first, 0))
-    k_spec = pl.BlockSpec((pieces, 1, HD, length), lambda row, group, *_: (0, row, group + first, 0))
-    v_spec = pl.BlockSpec(
-        (pieces, 1, HD, length), lambda row, group, *_: (0, row, group + first + KV, 0)
-    )
-    o_spec = pl.BlockSpec((1, group_width, length), lambda row, group, *_: (row, group + part_first, 0))
-    s_spec = pl.BlockSpec(
-        (1, 1, GROUP, length), lambda row, group, *_: (row, group + part_first, 0, 0)
-    )
-    dq_spec = pl.BlockSpec((1, group_width, length), lambda row, group, *_: (row, group, 0))
-    dk_spec = pl.BlockSpec((pieces, 1, HD, length), lambda row, group, *_: (0, row, group, 0))
-    work = rows * groups * GROUP * length * length * pieces
-    pieces_shape = jax.ShapeDtypeStruct((pieces, rows, groups * HD, length), jnp.float32)
+        total = jnp.zeros((HD, 128), jnp.float32)
+        for head in range(GROUP):
+            own = slice(head * HD, (head + 1) * HD)
+            grad, products = head_back(
+                scale_factor * q_accum[own, :], raw_ref[0, own, :], gain_ref[...], cos_ref[...], sin_ref[...]
+            )
+            dq_ref[0, own, :] = grad.astype(LOW)
+            total = total + fold(products)
+        gain_grad_ref[0] = total
+
+    q_spec = pl.BlockSpec((1, group_width, length), lambda row, *_: (row, group, 0))
+    k_spec = pl.BlockSpec((pieces, 1, HD, length), lambda row, *_: (0, row, group, 0))
+    v_spec = pl.BlockSpec((pieces, 1, HD, length), lambda row, *_: (0, row, group + KV, 0))
+    s_spec = pl.BlockSpec((1, 1, GROUP, length), lambda row, *_: (row, group, 0, 0))
+    table_spec = pl.BlockSpec((HD, length), lambda row, *_: (0, 0))
+    gain_spec = pl.BlockSpec((HD, 1), lambda row, *_: (0, 0))
+    dkv_spec = pl.BlockSpec((pieces, 1, 2, HD, length), lambda row, *_: (0, row, 0, group, 0))
+    work = rows * GROUP * length * length * pieces
+    inputs = [info, queries, keys_values, keys_values, out, sums, grad_out, q_raw, gain, cos_t, sin_t]
     return pl.pallas_call(
         kernel,
         out_shape=[
-            jax.ShapeDtypeStruct((rows, groups * group_width, length), jnp.float32),
-            pieces_shape,
-            pieces_shape,
+            jax.ShapeDtypeStruct(queries.shape, LOW),
+            jax.ShapeDtypeStruct((pieces, rows, 2, KV * HD, length), jnp.float32),
+            jax.ShapeDtypeStruct((rows, HD, 128), jnp.float32),
         ],
         grid_spec=pltpu.PrefetchScalarGridSpec(
             num_scalar_prefetch=1,
-            grid=(rows, groups),
-            in_specs=[q_spec, k_spec, v_spec, o_spec, s_spec, q_spec],
-            out_specs=[dq_spec, dk_spec, dk_spec],
+            grid=(rows,),
+            in_specs=[
+                q_spec, k_spec, v_spec, q_spec, s_spec, q_spec, q_spec, gain_spec, table_spec, table_spec,
+                *[ANY] * len(carried),
+            ],
+            out_specs=[q_spec, dkv_spec, pl.BlockSpec((1, HD, 128), lambda row, *_: (row, 0, 0))],
             scratch_shapes=[
                 pltpu.VMEM((group_width, length), LOW),
                 pltpu.VMEM((GROUP, 1, length), jnp.float32),
@@ -480,11 +515,60 @@
                 pltpu.VMEM((GROUP, length, HD), LOW),
                 pltpu.VMEM((length, HD), jnp.float32),
                 pltpu.VMEM((length, HD), jnp.float32),
+                pltpu.VMEM((group_width, length), jnp.float32),
             ],
         ),
+        input_output_aliases={len(inputs) + at: at for at in range(len(carried))},
         compiler_params=pltpu.CompilerParams(vmem_limit_bytes=40 << 20),
         cost_estimate=pl.CostEstimate(flops=work, transcendentals=0, bytes_accessed=1 << 20),
-    )(info, queries, keys_values, keys_values, out, sums, grad_out)
+    )(*inputs, *carried)
+
+
+def finish_keys(own, others, k_raw, gain, cos_t, sin_t):
+    _, rows, _, width, length = own.shape
+
+    def kernel(own_ref, *refs):
+        shares, (raw_ref, gain_ref, cos_ref, sin_ref, out_ref, gain_grad_ref) = refs[:-6], refs[-6:]
+
+        def share(which, rows_of):
+            total = own_ref[0, 0, which, rows_of, :]
+            for ref in shares:
+                total = total + ref[0, 0, which, rows_of, :].astype(jnp.float32)
+            return total
+
+        total = jnp.zeros((HD, 128), jnp.float32)
+        for head in range(KV):
+            rows_of = slice(head * HD, (head + 1) * HD)
+            grad, products = head_back(
+                share(0, rows_of), raw_ref[0, rows_of, :], gain_ref[...], cos_ref[...], sin_ref[...]
+            )
+            out_ref[0, rows_of, :] = grad.astype(LOW)
+            out_ref[0, slice(width + head * HD, width + (head + 1) * HD), :] = share(1, rows_of).astype(LOW)
+            total = total + fold(products)
+        gain_grad_ref[0] = total
+
+    piece_spec = pl.BlockSpec((1, 1, 2, width, length), lambda row: (0, row, 0, 0, 0))
+    table_spec = pl.BlockSpec((HD, length), lambda row: (0, 0))
+    return pl.pallas_call(
+        kernel,
+        out_shape=[
+            jax.ShapeDtypeStruct((rows, 2 * width, length), LOW),
+            jax.ShapeDtypeStruct((rows, HD, 128), jnp.float32),
+        ],
+        grid=(rows,),
+        in_specs=[
+            *[piece_spec] * (1 + len(others)),
+            pl.BlockSpec((1, width, length), lambda row: (row, 0, 0)),
+            pl.BlockSpec((HD, 1), lambda row: (0, 0)),
+            table_spec,
+            table_spec,
+        ],
+        out_specs=[
+            pl.BlockSpec((1, 2 * width, length), lambda row: (row, 0, 0)),
+            pl.BlockSpec((1, HD, 128), lambda row: (row, 0, 0)),
+        ],
+        compiler_params=pltpu.CompilerParams(vmem_limit_bytes=40 << 20),
+    )(own, *others, k_raw, gain, cos_t, sin_t)
 
 
 def local(
@@ -533,13 +617,18 @@
         [attn_gain[:, None], ffn_gain[:, None], jnp.zeros((part_len, 126), jnp.float32)], axis=1
     ).astype(LOW)
     w_qkv_low, w_gate_low, w_up_low = w_qkv.astype(LOW), w_gate.astype(LOW), w_up.astype(LOW)
-    gather_a = Gather([w_qkv_low, gain_columns], me, devices)
+    gather_a = Gather([w_qkv_low[:, :q_width], w_qkv_low[:, q_width:], gain_columns], me, devices, True)
     gather_b = Gather([w_out.astype(LOW).T], me, devices)
     w_down_low = w_down.astype(LOW).T
     units = w_down_low.shape[1] // 2
     halves = slice(0, units), slice(units, 2 * units)
     gather_c = [
-        Gather([w_gate_low[:, own], w_up_low[:, own], w_down_low[:, own]], me, devices) for own in halves
+        Gather(
+            [jnp.concatenate([w_gate_low[:, own], w_up_low[:, own]], axis=1), w_down_low[:, own]],
+            me,
+            devices,
+        )
+        for own in halves
     ]
     (tokens,) = open_slot([gather_a], tokens)
     x_float = tokens.astype(jnp.float32)
@@ -551,20 +640,22 @@
     (normed_one,) = close_slot([gather_a, gather_b], normed_one)
     (normed_one,) = open_slot([gather_a, gather_b, gather_c[0]], normed_one)
     (normed_one,) = close_slot([gather_a], normed_one)
-    wqkv, gains = gather_a.whole()
+    wq, wkv, gains = gather_a.whole()
     gain_attn = gains[:, 0].astype(jnp.float32)
     gain_ffn = gains[:, 1].astype(jnp.float32)
     normed_low = (normed_one * gain_attn).astype(LOW)
-    projected = jnp.einsum("rtd,de->ret", normed_low, wqkv, preferred_element_type=jnp.float32)
-    q_raw = projected[:, :q_width].reshape(row_count, HEADS, HD, piece_len)
-    k_raw = projected[:, q_width : q_width + kv_width].reshape(row_count, KV, HD, piece_len)
-    v_raw = projected[:, q_width + kv_width :]
+    kv_raw = jnp.einsum("rtd,de->ret", normed_low, wkv, preferred_element_type=jnp.float32)
+    k_raw = kv_raw[:, :kv_width].reshape(row_count, KV, HD, piece_len)
+    v_raw = kv_raw[:, kv_width:]
     k_unit, k_inverse = normalize(k_raw, 2)
     k_low = rotate(k_unit * k_gain_h, cos_h, sin_h).astype(LOW).reshape(row_count, kv_width, piece_len)
     own_kv = jnp.concatenate([k_low, v_raw.astype(LOW)], axis=1)
-    own_kv, q_raw = close_slot([gather_b, gather_c[0]], own_kv, q_raw)
+    own_kv, normed_low = close_slot([gather_b, gather_c[0]], own_kv, normed_low)
     row_pieces = Pieces(own_kv, devices, shards)
-    (q_raw,) = open_slot([row_pieces, gather_b, gather_c[0]], q_raw)
+    (normed_low,) = open_slot([row_pieces, gather_b, gather_c[0]], normed_low)
+    q_raw = jnp.einsum("rtd,de->ret", normed_low, wq, preferred_element_type=jnp.float32).reshape(
+        row_count, HEADS, HD, piece_len
+    )
     q_unit, q_inverse = normalize(q_raw, 2)
     q_low = (
         rotate(q_unit * q_gain_h, cos_h, sin_h).astype(LOW) * jnp.array(scale_factor, LOW)
@@ -584,9 +675,9 @@
     grad_out = cotangent.astype(jnp.float32) * live_mask[..., None]
     grad_low = grad_out.astype(LOW)
 
-    def feed_forward(ffn_in, grad_low, wgate, wup, wdown):
-        gate_proj = jnp.einsum("rtd,df->rtf", ffn_in, wgate, preferred_element_type=jnp.float32)
-        up_proj = jnp.einsum("rtd,df->rtf", ffn_in, wup, preferred_element_type=jnp.float32)
+    def feed_forward(ffn_in, grad_low, wgu, wdown):
+        both = jnp.einsum("rtd,df->rtf", ffn_in, wgu, preferred_element_type=jnp.float32)
+        gate_proj, up_proj = both[..., :units], both[..., units:]
         gate_sig = jax.nn.sigmoid(gate_proj)
         silu_gate = gate_proj * gate_sig
         activated = (silu_gate * up_proj).astype(LOW)
@@ -594,123 +685,119 @@
         grad_act = jnp.einsum("rtd,df->rtf", grad_low, wdown, preferred_element_type=jnp.float32)
         grad_gate = (grad_act * up_proj * gate_sig * (1.0 + gate_proj * (1.0 - gate_sig))).astype(LOW)
         grad_up = (grad_act * silu_gate).astype(LOW)
-        grad_wgate = jnp.einsum("rtd,rtf->df", ffn_in, grad_gate, preferred_element_type=jnp.float32)
-        grad_wup = jnp.einsum("rtd,rtf->df", ffn_in, grad_up, preferred_element_type=jnp.float32)
-        grads = [grad_down.astype(LOW), grad_wgate.astype(LOW), grad_wup.astype(LOW)]
-        return activated, grad_gate, grad_up, grads
+        grad_both = jnp.concatenate([grad_gate, grad_up], axis=2)
+        grad_wgu = jnp.einsum("rtd,rtf->df", ffn_in, grad_both, preferred_element_type=jnp.float32)
+        return activated, grad_both, [grad_wgu.astype(LOW), grad_down.astype(LOW)]
 
     ffn_in, x_mid = close_slot(gather_c, ffn_in, x_mid)
     (ffn_in,) = open_slot([gather_c[1]], ffn_in)
-    one = gather_c[0].whole()
-    act_one, gate_one, up_one, grads = feed_forward(ffn_in, grad_low, *one)
-    ffn_in, grads, act_one, gate_one, up_one = close_slot(
-        [gather_c[1]], ffn_in, grads, act_one, gate_one, up_one
-    )
+    wgu_one, wdown_one = gather_c[0].whole()
+    act_one, both_one, grads = feed_forward(ffn_in, grad_low, wgu_one, wdown_one)
     red_one = Reduce(grads, me, devices)
-    (ffn_in,) = open_slot([gather_c[1], red_one], ffn_in)
-    (ffn_in,) = close_slot([gather_c[1], red_one], ffn_in)
+    red_one.prepare()
+    ffn_in, red_one.outgoing, act_one, both_one = close_slot(
+        [gather_c[1]], ffn_in, red_one.outgoing, act_one, both_one
+    )
+    (ffn_in,) = open_slot([gather_c[1]], ffn_in)
+    (ffn_in,) = open_slot([red_one], ffn_in, ready=[red_one])
+    (ffn_in,) = close_slot([gather_c[1]], ffn_in)
+    wgu_two, wdown_two = gather_c[1].whole()
+    ffn_in, wgu_two, wdown_two = close_slot([red_one], ffn_in, wgu_two, wdown_two)
     (ffn_in,) = open_slot([red_one], ffn_in)
-    two = gather_c[1].whole()
-    act_two, gate_two, up_two, grads = feed_forward(ffn_in, grad_low, *two)
-    ffn_in, grads, act_two, gate_two, up_two = close_slot(
-        [red_one], ffn_in, grads, act_two, gate_two, up_two
-    )
+    act_two, both_two, grads = feed_forward(ffn_in, grad_low, wgu_two, wdown_two)
     red_two = Reduce(grads, me, devices)
-    gate_two, up_two, act_two = open_slot([red_one, red_two], gate_two, up_two, act_two)
+    red_two.prepare()
+    ffn_in, red_two.outgoing, act_two, both_two = close_slot(
+        [red_one], ffn_in, red_two.outgoing, act_two, both_two
+    )
+    both_two, act_two = open_slot([red_one, red_two], both_two, act_two, ready=[red_two])
     grad_ffn_in = jnp.einsum(
-        "rtf,df->rtd",
-        jnp.concatenate([gate_one, up_one, gate_two, up_two], axis=2),
-        jnp.concatenate([*one[:2], *two[:2]], axis=1),
-        preferred_element_type=jnp.float32,
-    )
+        "rtf,df->rtd", both_one, wgu_one, preferred_element_type=jnp.float32
+    ) + jnp.einsum("rtf,df->rtd", both_two, wgu_two, preferred_element_type=jnp.float32)
     grad_mid = grad_out + norm_back(x_mid, inverse_two, grad_ffn_in * gain_ffn)
     mid_low = grad_mid.astype(LOW)
     grad_wout = jnp.einsum("rtd,rct->dc", mid_low, att_low, preferred_element_type=jnp.float32)
     grad_att = jnp.einsum("rtd,dc->rct", mid_low, wout, preferred_element_type=jnp.float32)
     red_out = Reduce([grad_wout.astype(LOW)], me, devices)
-    grad_att, red_out.grads = close_slot([red_one, red_two], grad_att, red_out.grads)
+    red_out.prepare()
+    grad_att, red_out.outgoing = close_slot([red_one, red_two], grad_att, red_out.outgoing)
     grad_att, act_two = open_slot([red_one, red_two], grad_att, act_two)
 
-    def back(group, grad_att):
-        return attention_back(info, q_low, pieces, o_heads, sums, grad_att, group, 1, group)
+    q_gain_c, k_gain_c = q_gain[:, None], k_gain[:, None]
+    q_raw_flat = q_raw.reshape(row_count, q_width, piece_len)
+    k_raw_flat = k_raw.reshape(row_count, kv_width, piece_len)
+
+    def back(group, grad_att, carried=()):
+        return attention_back(
+            info, q_low, pieces, o_heads, sums, grad_att, q_raw_flat, q_gain_c, cos_t, sin_t, group, carried
+        )
 
     output = (
         x_mid
-        + jnp.einsum(
-            "rtf,df->rtd",
-            jnp.concatenate([act_one, act_two], axis=2),
-            jnp.concatenate([one[2], two[2]], axis=1),
-            preferred_element_type=jnp.float32,
-        )
+        + jnp.einsum("rtf,df->rtd", act_one, wdown_one, preferred_element_type=jnp.float32)
+        + jnp.einsum("rtf,df->rtd", act_two, wdown_two, preferred_element_type=jnp.float32)
     ).astype(LOW)
-    parts = [back(0, grad_att)]
-    parts[0], grad_att, output = close_slot([red_one, red_two], parts[0], grad_att, output)
+    gain_parts = []
+
+    def more(group, grad_att, carried=()):
+        *carried, gain_part = back(group, grad_att, carried)
+        gain_parts.append(gain_part)
+        return tuple(carried)
+
+    carried = more(0, grad_att)
+    carried, grad_att, output = close_slot([red_one, red_two], carried, grad_att, output)
     red_one.prepare()
+    (grad_att,) = open_slot([red_two, red_out], grad_att, ready=[red_out])
+    carried = more(1, grad_att, carried)
+    carried, grad_att = close_slot([red_two, red_out], carried, grad_att)
     (grad_att,) = open_slot([red_two, red_out], grad_att)
-    parts.append(back(1, grad_att))
-    parts[1], grad_att = close_slot([red_two, red_out], parts[1], grad_att)
-    (grad_att,) = open_slot([red_two, red_out], grad_att)
-    parts.append(back(2, grad_att))
-    parts[2], grad_att = close_slot([red_two, red_out], parts[2], grad_att)
+    carried = more(2, grad_att, carried)
+    carried, grad_att = close_slot([red_two, red_out], carried, grad_att)
     red_two.prepare()
     (grad_att,) = open_slot([red_out], grad_att)
-    parts.append(back(3, grad_att))
-    (parts,) = close_slot([red_out], parts)
-    grad_query = jnp.concatenate([one_part[0] for one_part in parts], axis=1)
-    grad_pieces = jnp.concatenate(
-        [one_part[1] for one_part in parts] + [one_part[2] for one_part in parts], axis=2
-    )
+    carried = more(3, grad_att, carried)
+    grad_q_low, grad_pieces = close_slot([red_out], carried)[0]
     kv_back = PiecesBack(grad_pieces, devices, shards)
-    (grad_query,) = open_slot([kv_back, red_out], grad_query)
-    (grad_query,) = close_slot([kv_back], grad_query)
-    (grad_query,) = open_slot([kv_back], grad_query)
-    grad_q_scaled = rotate_back(
-        scale_factor * grad_query.reshape(row_count, HEADS, HD, piece_len), cos_h, sin_h
-    )
-    grad_qgain = jnp.sum(grad_q_scaled * q_unit, axis=(0, 1, 3))
-    grad_q_raw = norm_back(q_raw, q_inverse, grad_q_scaled * q_gain_h, 2)
-    grad_q_low = grad_q_raw.reshape(row_count, q_width, piece_len).astype(LOW)
+    (grad_q_low,) = open_slot([kv_back], grad_q_low)
     grad_wq = jnp.einsum("rtd,ret->de", normed_low, grad_q_low, preferred_element_type=jnp.float32)
-    grad_wq, grad_q_low = close_slot([kv_back, red_out], grad_wq, grad_q_low)
+    red_q = Reduce([grad_wq.astype(LOW)], me, devices)
+    red_q.prepare()
+    red_q.outgoing, grad_q_low = close_slot([kv_back], red_q.outgoing, grad_q_low)
+    (grad_q_low,) = open_slot([kv_back, red_q], grad_q_low, ready=[red_q])
+    grad_normed_q = jnp.einsum("ret,de->rtd", grad_q_low, wq, preferred_element_type=jnp.float32)
+    (grad_normed_q,) = close_slot([kv_back, red_q], grad_normed_q)
+    kv_back.prepare()
+    grad_kv_low, k_gain_part = finish_keys(*kv_back.shares, k_raw_flat, k_gain_c, cos_t, sin_t)
+    shared = Sum(
+        jnp.concatenate([jnp.sum(sum(gain_parts), axis=(0, 2)), jnp.sum(k_gain_part, axis=(0, 2))])[None],
+        devices,
+    )
+    (grad_kv_low,) = open_slot([red_q, shared, red_out], grad_kv_low)
+    grad_wkv = jnp.einsum("rtd,ret->de", normed_low, grad_kv_low, preferred_element_type=jnp.float32)
+    red_kv = Reduce([grad_wkv.astype(LOW)], me, devices)
+    red_kv.prepare()
+    red_kv.outgoing, grad_kv_low = close_slot([red_q, red_out, shared], red_kv.outgoing, grad_kv_low)
     red_out.prepare()
-    kv_back.prepare()
-    red_q = Reduce([grad_wq.astype(LOW)], me, devices)
-    grad_kv, grad_q_low = open_slot([red_q], kv_back.total, grad_q_low)
-    grad_k_scaled = rotate_back(
-        grad_kv[:, :kv_width].reshape(row_count, KV, HD, piece_len), cos_h, sin_h
-    )
-    grad_kgain = jnp.sum(grad_k_scaled * k_unit, axis=(0, 1, 3))
-    grad_k_raw = norm_back(k_raw, k_inverse, grad_k_scaled * k_gain_h, 2)
-    grad_kv_low = jnp.concatenate(
-        [grad_k_raw.reshape(row_count, kv_width, piece_len), grad_kv[:, kv_width:]], axis=1
-    ).astype(LOW)
-    grad_wkv = jnp.einsum("rtd,ret->de", normed_low, grad_kv_low, preferred_element_type=jnp.float32)
-    grad_wkv, grad_kv_low, grad_q_low = close_slot([red_q], grad_wkv, grad_kv_low, grad_q_low)
-    shared = Sum(jnp.concatenate([grad_qgain, grad_kgain])[None], devices)
-    red_kv = Reduce([grad_wkv.astype(LOW)], me, devices)
-    grad_kv_low, grad_q_low = open_slot([red_q, red_kv, shared], grad_kv_low, grad_q_low)
-    grad_normed = jnp.einsum(
-        "ret,de->rtd",
-        jnp.concatenate([grad_q_low, grad_kv_low], axis=1),
-        wqkv,
-        preferred_element_type=jnp.float32,
+    (grad_kv_low,) = open_slot([red_q, red_kv, shared], grad_kv_low, ready=[red_kv])
+    grad_normed = grad_normed_q + jnp.einsum(
+        "ret,de->rtd", grad_kv_low, wkv, preferred_element_type=jnp.float32
     )
     input_grad = grad_mid + norm_back(x_float, inverse_one, grad_normed * gain_attn)
     (input_grad,) = close_slot([red_q, red_kv, shared], input_grad)
     open_slot([red_q, red_kv, shared])
     close_slot([red_q, red_kv, shared])
-    open_slot([red_q, red_kv, shared])
-    close_slot([red_q, red_kv, shared])
+    red_q.prepare()
     open_slot([red_kv, shared])
-    red_q.prepare()
+    close_slot([red_kv, shared])
+    open_slot([red_kv, shared])
     close_slot([red_kv, shared])
     red_kv.prepare()
     shared.prepare()
     shared = shared.values
     three, four = red_q.total, red_kv.total
-    summed = [jnp.split(one_red.total, 3, axis=1) for one_red in (red_one, red_two)]
-    summed_down, summed_wgate, summed_wup = (
-        jnp.concatenate([summed[0][at], summed[1][at]], axis=1) for at in range(3)
+    summed = red_one.total, red_two.total
+    summed_wgate, summed_wup, summed_down = (
+        jnp.concatenate([one[:, at * units : (at + 1) * units] for one in summed], axis=1) for at in range(3)
     )
     summed_down, summed_wout = summed_down.T, red_out.total.T
     summed_wqkv = jnp.concatenate([three, four], axis=1)

time: 451 us -> 441 us (0.978)
  other arithmetic: 59.4 us -> 51.9 us
  Pallas kernels: 64.9 us -> 72.1 us
  starting transfers between devices: 123 us -> 118 us
    pallas_call x4 -> x5, Pallas kernels: 20.7 us -> 26.3 us  [the longest x4 25.7 us: attention_back(): pl.pallas_call(kernel, out_shape=[jax.ShapeDtypeStruct(queries.shape, LOW...]
    unnamed x226 -> x217, local copies, waits for them, and re-layouts: 15.9 us -> 10.7 us
    ppermute x82 -> x84, starting transfers between devices: 123 us -> 118 us  [swap(): lax.ppermute(values, ('dp', 'shard'), [(i, i ^ mask) for i in range(devic...]
    ppermute x82 -> x84, waiting for transfers between devices: 122 us -> 118 us  [swap(): lax.ppermute(values, ('dp', 'shard'), [(i, i ^ mask) for i in range(devic...]
  transfers between devices with their start and end apart: 82 -> 84, of which waited for: 28 -> 27; matrix products, arithmetic and copies ran while one was open for 20% -> 19% of each run, Pallas kernels for 12% -> 16%
where the time goes in v6:
time: 441 us; the launch traced here: 436 us
  starting transfers between devices  118 us (27%)
  waiting for transfers between devices  118 us (27%)
  Pallas kernels  72.1 us (16%)
  matrix products  53 us (12%)
  other arithmetic  51.9 us (12%)
  local copies, waits for them, and re-layouts  19.3 us (4%)
    ppermute x84, waiting for transfers between devices, swap(): lax.ppermute(values, ('dp', 'shard'), [(i, i ^ mask) for i in range(devic...  118 us
    ppermute x84, starting transfers between devices, swap(): lax.ppermute(values, ('dp', 'shard'), [(i, i ^ mask) for i in range(devic...  118 us
    pallas_call x4, Pallas kernels, attention_back(): pl.pallas_call(kernel, out_shape=[jax.ShapeDtypeStruct(queries.shape, LOW...  25.7 us
    pallas_call x5, Pallas kernels, pick(): pl.pallas_call(kernel, out_shape=[jax.ShapeDtypeStruct((len(own) * size,...  20.6 us
    pallas_call x4, Pallas kernels, place(): pl.pallas_call(kernel, out_shape=[jax.ShapeDtypeStruct((total_rows, width...  14.5 us
    unnamed x217, local copies, waits for them, and re-layouts  10.7 us
    pallas_call x1, Pallas kernels, attention(): pl.pallas_call(kernel, out_shape=[jax.ShapeDtypeStruct((rows, groups * gr...  10.7 us
  transfers between devices with their start and end apart: 84, of which 27 were waited for; matrix products, arithmetic and copies ran while one was open for 19% of the time, Pallas kernels for 16%

profile of v6, /device:TPU:0, one launch (start us, length us, event | category | flops | bytes accessed | tf_op | source)
XLA Modules:
  0.0 436.4 jit_solution(1338384728574541498)
XLA Ops:
  3.5 3.1 collective-permute-start
  15.6 9.2 %collective-permute-done.1 = bf16[64,1664]{1,0:T(8,128)(2,1)S(1)} collective-permute-done((bf16[64,1664]{1,0:T(8,128)(2,1)S(1)}, bf16[64,1664]{1,0:T(8,128)(2,1)S(1)}, u32[]{:S(2)}, u32[]{:S(2)}) %collective-permute-start.1) | collective-permute-done | bytes 213024 | tf_op jit(solution)/shard_map/ppermute | solution.py:61
  28.0 3.8 collective-permute-start.5
  35.8 7.1 %collective-permute-done.6 = bf16[64,1024]{1,0:T(8,128)(2,1)S(1)} collective-permute-done((bf16[64,1024]{1,0:T(8,128)(2,1)S(1)}, bf16[64,1024]{1,0:T(8,128)(2,1)S(1)}, u32[]{:S(2)}, u32[]{:S(2)}) %collective-permute-start.6) | collective-permute-done | bytes 131104 | tf_op jit(solution)/shard_map/ppermute | solution.py:61
  48.2 17.1 %collective-permute-done.10 = bf16[128,1024]{1,0:T(8,128)(2,1)S(1)} collective-permute-done((bf16[128,1024]{1,0:T(8,128)(2,1)S(1)}, bf16[128,1024]{1,0:T(8,128)(2,1)S(1)}, u32[]{:S(2)}, u32[]{:S(2)}) %collective-permute-start.10) | collective-permute-done | bytes 262176 | tf_op jit(solution)/shard_map/ppermute | solution.py:61
  67.8 4.9 %collective-permute-start.14 = (bf16[64,1536]{1,0:T(8,128)(2,1)}, bf16[64,1536]{1,0:T(8,128)(2,1)S(1)}, u32[]{:S(2)}, u32[]{:S(2)}) collective-permute-start(bf16[64,1536]{1,0:T(8,128)(2,1)} %get-tuple-element.299), channel_id=1, source_target_pairs={{0,8},{1,9},{2,10},{3,11},{4,12},{5,13},{6,14},{7,15},{8,0},{9,1},... | collective-permute-start | bytes 589832 | tf_op jit(solution)/shard_map/ppermute | solution.py:61
  72.7 2.9 collective-permute-start.15
  78.2 4.4 shard_map.221
  95.7 5.2 %fusion.25 = f32[1024,512]{1,0:T(8,128)S(1)} fusion(bf16[2048,1024]{1,0:T(8,128)(2,1)} %copy-done.27, bf16[1,512,2048]{2,1,0:T(8,128)(2,1)} %copy-done.59), kind=kOutput, calls=%fused_computation.56 | convolution fusion | flops 2147483648 | bytes 8388608 | tf_op jit(solution)/shard_map/rtd,de->ret/dot_general | solution.py:656
  105.1 11.0 %collective-permute-done.24 = bf16[128,1536]{1,0:T(8,128)(2,1)S(1)} collective-permute-done((bf16[128,1536]{1,0:T(8,128)(2,1)}, bf16[128,1536]{1,0:T(8,128)(2,1)S(1)}, u32[]{:S(2)}, u32[]{:S(2)}) %collective-permute-start.24) | collective-permute-done | bytes 393248 | tf_op jit(solution)/shard_map/ppermute | solution.py:61
  122.6 4.0 collective-permute-start.27
  129.5 10.7 %shard_map.222 = (f32[1,1024,512]{2,1,0:T(8,128)S(1)}, bf16[1,1024,512]{2,1,0:T(8,128)(2,1)S(1)}, f32[1,4,4,512]{3,2,1,0:T(4,128)S(1)}) custom-call(s32[6]{0:T(128)S(1)} %pad_add_fusion.info_ref, bf16[1,1024,512]{2,1,0:T(8,128)(2,1)S(1)} %bitcast.231, bf16[4,1,512,512]{3,2,1,0:T(8,128)(2,1)S(1)} %constant_dynamic-update-slice_fusion.k_ref.v_ref, ...), custom_call_target="tpu_custom_call" | custom-call | flops 16777216 | bytes 1048576 | tf_op jit(solution)/shard_map/pallas_call | solution.py:388
  140.3 3.5 collective-permute-done.28
  146.7 4.7 %shard_map.223 = bf16[2048,1024]{1,0:T(8,128)(2,1)S(1)} custom-call(s32[1]{0:T(128)} %bitcast.me_ref, bf16[1024,1024]{1,0:T(8,128)(2,1)S(1)} %copy-done.8, bf16[1024,1024]{1,0:T(8,128)(2,1)} %collective-permute-done.22.refs_1_), custom_call_target="tpu_custom_call" | custom-call | bytes 65536 | tf_op jit(solution)/shard_map/pallas_call | solution.py:88
  152.9 10.6 %collective-permute-start.33 = (bf16[128,1536]{1,0:T(8,128)(2,1)S(1)}, bf16[128,1536]{1,0:T(8,128)(2,1)S(1)}, u32[]{:S(2)}, u32[]{:S(2)}) collective-permute-start(bf16[128,1536]{1,0:T(8,128)(2,1)S(1)} %pad_maximum_fusion.22), channel_id=1, source_target_pairs={{0,2},{1,3},{2,0},{3,1},{4,6},{5,7},{6,4},{7,5},{8,10},{9,11},{10,... | collective-permute-start | bytes 1179656 | tf_op jit(solution)/shard_map/ppermute | solution.py:61
  168.2 4.9 %collective-permute-done.33 = bf16[128,1536]{1,0:T(8,128)(2,1)S(1)} collective-permute-done((bf16[128,1536]{1,0:T(8,128)(2,1)S(1)}, bf16[128,1536]{1,0:T(8,128)(2,1)S(1)}, u32[]{:S(2)}, u32[]{:S(2)}) %collective-permute-start.33) | collective-permute-done | bytes 393248 | tf_op jit(solution)/shard_map/ppermute | solution.py:61
  186.5 2.9 shard_map.225
  196.5 5.4 %collective-permute-done.37.refs_1_ = bf16[1024,1536]{1,0:T(8,128)(2,1)} collective-permute-done((bf16[1024,1536]{1,0:T(8,128)(2,1)}, bf16[1024,1536]{1,0:T(8,128)(2,1)}, u32[]{:S(2)}, u32[]{:S(2)}) %collective-permute-start.37) | collective-permute-done | bytes 3145760 | tf_op jit(solution)/shard_map/ppermute | solution.py:61
  201.9 3.4 shard_map.226
  220.2 7.8 %collective-permute-done.38 = bf16[256,1536]{1,0:T(8,128)(2,1)S(1)} collective-permute-done((bf16[256,1536]{1,0:T(8,128)(2,1)S(1)}, bf16[256,1536]{1,0:T(8,128)(2,1)S(1)}, u32[]{:S(2)}, u32[]{:S(2)}) %collective-permute-start.38) | collective-permute-done | bytes 786464 | tf_op jit(solution)/shard_map/ppermute | solution.py:61
  236.1 2.9 fusion.7
  239.0 2.8 fusion.8
  244.3 6.1 %shard_map.228 = (bf16[1024,1024]{1,0:T(8,128)(2,1)S(1)}, bf16[1024,1024]{1,0:T(8,128)(2,1)S(1)}) custom-call(s32[1]{0:T(128)} %bitcast.me_ref, bf16[2048,1024]{1,0:T(8,128)(2,1)S(1)} %convolution_convert_fusion.1.refs_0_), custom_call_target="tpu_custom_call" | custom-call | bytes 65536 | tf_op jit(solution)/shard_map/pallas_call | solution.py:123
  261.6 4.3 collective-permute-start.45
  265.9 2.9 fusion.6
  268.7 6.5 %shard_map.229 = (bf16[1,1024,512]{2,1,0:T(8,128)(2,1)S(1)}, f32[4,1,2,256,512]{4,3,2,1,0:T(8,128)}, f32[1,64,128]{2,1,0:T(8,128)S(1)}) custom-call(s32[6]{0:T(128)S(1)} %pad_add_fusion.info_ref, bf16[1,1024,512]{2,1,0:T(8,128)(2,1)S(1)} %bitcast.232, bf16[4,1,512,512]{3,2,1,0:T(8,128)(2,1)S(1)} %constant_dynamic-update-slice_fusion.k_ref.v_ref, ...), custom_call_target="tpu_custom_call" | custom-call | flops 4194304 | bytes 1048576 | tf_op jit(solution)/shard_map/pallas_call | solution.py:496
  275.2 3.8 collective-permute-done.44
  282.3 4.8 %collective-permute-start.49 = (bf16[128,1536]{1,0:T(8,128)(2,1)S(1)}, bf16[128,1536]{1,0:T(8,128)(2,1)S(1)}, u32[]{:S(2)}, u32[]{:S(2)}) collective-permute-start(bf16[128,1536]{1,0:T(8,128)(2,1)S(1)} %slice.650), channel_id=1, source_target_pairs={{0,2},{1,3},{2,0},{3,1},{4,6},{5,7},{6,4},{7,5},{8,10},{9,11},{10,... | collective-permute-start | bytes 1179656 | tf_op jit(solution)/shard_map/ppermute | solution.py:61
  287.2 6.2 %shard_map.230 = (bf16[1,1024,512]{2,1,0:T(8,128)(2,1)S(1)}, f32[4,1,2,256,512]{4,3,2,1,0:T(8,128)}, f32[1,64,128]{2,1,0:T(8,128)S(1)}) custom-call(s32[6]{0:T(128)S(1)} %pad_add_fusion.info_ref, bf16[1,1024,512]{2,1,0:T(8,128)(2,1)S(1)} %bitcast.233, ...), custom_call_target="tpu_custom_call", output_to_operand_aliasing={{0}: (11, {}), {1}: (12, {})} | custom-call | flops 4194304 | bytes 1048576 | tf_op jit(solution)/shard_map/pallas_call | solution.py:496
  293.4 2.9 collective-permute-done.49
  304.5 6.6 %shard_map.231 = (bf16[1,1024,512]{2,1,0:T(8,128)(2,1)S(1)}, f32[4,1,2,256,512]{4,3,2,1,0:T(8,128)}, f32[1,64,128]{2,1,0:T(8,128)S(1)}) custom-call(s32[6]{0:T(128)S(1)} %pad_add_fusion.info_ref, bf16[1,1024,512]{2,1,0:T(8,128)(2,1)S(1)} %bitcast.234, ...), custom_call_target="tpu_custom_call", output_to_operand_aliasing={{0}: (11, {}), {1}: (12, {})} | custom-call | flops 4194304 | bytes 1048576 | tf_op jit(solution)/shard_map/pallas_call | solution.py:496
  311.1 8.1 %collective-permute-done.52 = bf16[64,1536]{1,0:T(8,128)(2,1)S(1)} collective-permute-done((bf16[64,1536]{1,0:T(8,128)(2,1)S(1)}, bf16[64,1536]{1,0:T(8,128)(2,1)S(1)}, u32[]{:S(2)}, u32[]{:S(2)}) %collective-permute-start.52) | collective-permute-done | bytes 196640 | tf_op jit(solution)/shard_map/ppermute | solution.py:61
  321.3 6.4 %shard_map.232 = (bf16[1,1024,512]{2,1,0:T(8,128)(2,1)S(1)}, f32[4,1,2,256,512]{4,3,2,1,0:T(8,128)}, f32[1,64,128]{2,1,0:T(8,128)S(1)}) custom-call(s32[6]{0:T(128)S(1)} %pad_add_fusion.info_ref, bf16[1,1024,512]{2,1,0:T(8,128)(2,1)S(1)} %bitcast.235, ...), custom_call_target="tpu_custom_call", output_to_operand_aliasing={{0}: (11, {}), {1}: (12, {})} | custom-call | flops 4194304 | bytes 1048576 | tf_op jit(solution)/shard_map/pallas_call | solution.py:496
  329.2 2.8 slice.649
  332.0 3.6 collective-permute-start.58
  337.0 4.1 convolution_convert_fusion.refs_0_
  341.1 6.1 %shard_map.233 = (bf16[1024,1024]{1,0:T(8,128)(2,1)S(1)}, bf16[1024,1024]{1,0:T(8,128)(2,1)S(1)}) custom-call(s32[1]{0:T(128)} %bitcast.me_ref, bf16[2048,1024]{1,0:T(8,128)(2,1)S(1)} %convolution_convert_fusion.refs_0_), custom_call_target="tpu_custom_call" | custom-call | bytes 65536 | tf_op jit(solution)/shard_map/pallas_call | solution.py:123
  351.4 3.7 collective-permute-start.59
  355.1 4.4 %convolution_bitcast_fusion = f32[1,512,2048]{2,1,0:T(8,128)} fusion(bf16[2048,1024]{1,0:T(8,128)(2,1)S(1)} %copy-done.28, bf16[1,1024,512]{2,1,0:T(8,128)(2,1)S(1)} %copy-done.6), kind=kOutput, calls=%fused_computation.29 | convolution fusion | flops 2147483648 | bytes 9437184 | tf_op jit(solution)/shard_map/ret,de->rtd/dot_general | solution.py:767
  359.5 8.2 %collective-permute-done.59.refs_1_ = bf16[1,1,2,256,512]{4,3,2,1,0:T(8,128)(2,1)S(1)} collective-permute-done((bf16[1,1,2,256,512]{4,3,2,1,0:T(8,128)(2,1)S(1)}, bf16[1,1,2,256,512]{4,3,2,1,0:T(8,128)(2,1)S(1)}, u32[]{:S(2)}, u32[]{:S(2)}) %collective-permute-start.59) | collective-permute-done | bytes 524320 | tf_op jit(solution)/shard_map/ppermute | solution.py:61
  375.0 3.5 collective-permute-start.63
  381.0 3.0 convolution_convert_fusion.4.refs_0_
  384.0 3.2 shard_map.235
  387.3 4.4 %collective-permute-done.64 = bf16[64,1024]{1,0:T(8,128)(2,1)S(1)} collective-permute-done((bf16[64,1024]{1,0:T(8,128)(2,1)}, bf16[64,1024]{1,0:T(8,128)(2,1)S(1)}, u32[]{:S(2)}, u32[]{:S(2)}) %collective-permute-start.64) | collective-permute-done | bytes 131104 | tf_op jit(solution)/shard_map/ppermute | solution.py:61
  397.0 2.9 fusion.3
  403.1 2.9 collective-permute-start.71
  410.4 8.0 %collective-permute-done.72 = bf16[64,1024]{1,0:T(8,128)(2,1)S(1)} collective-permute-done((bf16[64,1024]{1,0:T(8,128)(2,1)S(1)}, bf16[64,1024]{1,0:T(8,128)(2,1)S(1)}, u32[]{:S(2)}, u32[]{:S(2)}) %collective-permute-start.72) | collective-permute-done | bytes 131104 | tf_op jit(solution)/shard_map/ppermute | solution.py:61
  430.8 3.3 collective-permute-done.83
  (516 shorter events, 178.1 us)
Async XLA Ops:
  6.6 18.2 %collective-permute-start.1 = (bf16[64,1664]{1,0:T(8,128)(2,1)S(1)}, bf16[64,1664]{1,0:T(8,128)(2,1)S(1)}, u32[]{:S(2)}, u32[]{:S(2)}) collective-permute-start(bf16[64,1664]{1,0:T(8,128)(2,1)S(1)} %concatenate.125), channel_id=1, source_target_pairs={{0,16},{1,17},{2,18},{3,19},{4,20},{5,21},{6,22},{7,23},{8,24},{9,... | collective-permute-start | bytes 638984 | tf_op jit(solution)/shard_map/ppermute | solution.py:61
  9.2 15.6 %collective-permute-start.2 = (bf16[64,1664]{1,0:T(8,128)(2,1)S(1)}, bf16[64,1664]{1,0:T(8,128)(2,1)S(1)}, u32[]{:S(2)}, u32[]{:S(2)}) collective-permute-start(bf16[64,1664]{1,0:T(8,128)(2,1)S(1)} %concatenate.125), channel_id=1, source_target_pairs={{0,24},{1,25},{2,26},{3,27},{4,28},{5,29},{6,30},{7,31},{8,16},{9,... | collective-permute-start | bytes 638984 | tf_op jit(solution)/shard_map/ppermute | solution.py:61
  24.9 18.1 %collective-permute-start.3 = (bf16[128,1664]{1,0:T(8,128)(2,1)S(1)}, bf16[128,1664]{1,0:T(8,128)(2,1)S(1)}, u32[]{:S(2)}, u32[]{:S(2)}) collective-permute-start(bf16[128,1664]{1,0:T(8,128)(2,1)S(1)} %get-tuple-element.277), channel_id=1, source_target_pairs={{0,4},{1,5},{2,6},{3,7},{4,0},{5,1},{6,2},{7,3},{8,12},{9,13},{10,... | collective-permute-start | bytes 1277960 | tf_op jit(solution)/shard_map/ppermute | solution.py:61
  26.4 16.5 %collective-permute-start.4 = (bf16[128,1664]{1,0:T(8,128)(2,1)S(1)}, bf16[128,1664]{1,0:T(8,128)(2,1)S(1)}, u32[]{:S(2)}, u32[]{:S(2)}) collective-permute-start(bf16[128,1664]{1,0:T(8,128)(2,1)S(1)} %get-tuple-element.278), channel_id=1, source_target_pairs={{0,2},{1,3},{2,0},{3,1},{4,6},{5,7},{6,4},{7,5},{8,10},{9,11},{10,... | collective-permute-start | bytes 1277960 | tf_op jit(solution)/shard_map/ppermute | solution.py:61
  43.2 22.2 %collective-permute-start.8 = (bf16[256,1664]{1,0:T(8,128)(2,1)S(1)}, bf16[256,1664]{1,0:T(8,128)(2,1)S(1)}, u32[]{:S(2)}, u32[]{:S(2)}) collective-permute-start(bf16[256,1664]{1,0:T(8,128)(2,1)S(1)} %pad_maximum_fusion.7.refs_0_), channel_id=1, source_target_pairs={{0,2},{1,3},{2,0},{3,1},{4,6},{5,7},{6,4},{7,5},{8,10},{9,11},{10,... | collective-permute-start | bytes 2555912 | tf_op jit(solution)/shard_map/ppermute | solution.py:61
  43.7 21.6 %collective-permute-start.9 = (bf16[256,1664]{1,0:T(8,128)(2,1)S(1)}, bf16[256,1664]{1,0:T(8,128)(2,1)}, u32[]{:S(2)}, u32[]{:S(2)}) collective-permute-start(bf16[256,1664]{1,0:T(8,128)(2,1)S(1)} %pad_maximum_fusion.8.refs_1_), channel_id=1, source_target_pairs={{0,4},{1,5},{2,6},{3,7},{4,0},{5,1},{6,2},{7,3},{8,12},{9,13},{10,... | collective-permute-start | bytes 2555912 | tf_op jit(solution)/shard_map/ppermute | solution.py:61
  44.3 21.0 %collective-permute-start.10 = (bf16[128,1024]{1,0:T(8,128)(2,1)S(1)}, bf16[128,1024]{1,0:T(8,128)(2,1)S(1)}, u32[]{:S(2)}, u32[]{:S(2)}) collective-permute-start(bf16[128,1024]{1,0:T(8,128)(2,1)S(1)} %pad_maximum_fusion.24), channel_id=1, source_target_pairs={{0,4},{1,5},{2,6},{3,7},{4,0},{5,1},{6,2},{7,3},{8,12},{9,13},{10,... | collective-permute-start | bytes 786440 | tf_op jit(solution)/shard_map/ppermute | solution.py:61
  45.9 19.5 %collective-permute-start.11 = (bf16[128,1024]{1,0:T(8,128)(2,1)S(1)}, bf16[128,1024]{1,0:T(8,128)(2,1)S(1)}, u32[]{:S(2)}, u32[]{:S(2)}) collective-permute-start(bf16[128,1024]{1,0:T(8,128)(2,1)S(1)} %pad_maximum_fusion.25), channel_id=1, source_target_pairs={{0,2},{1,3},{2,0},{3,1},{4,6},{5,7},{6,4},{7,5},{8,10},{9,11},{10,... | collective-permute-start | bytes 786440 | tf_op jit(solution)/shard_map/ppermute | solution.py:61
  67.8 20.8 %collective-permute-start.14 = (bf16[64,1536]{1,0:T(8,128)(2,1)}, bf16[64,1536]{1,0:T(8,128)(2,1)S(1)}, u32[]{:S(2)}, u32[]{:S(2)}) collective-permute-start(bf16[64,1536]{1,0:T(8,128)(2,1)} %get-tuple-element.299), channel_id=1, source_target_pairs={{0,8},{1,9},{2,10},{3,11},{4,12},{5,13},{6,14},{7,15},{8,0},{9,1},... | collective-permute-start | bytes 589832 | tf_op jit(solution)/shard_map/ppermute | solution.py:61
  72.7 17.3 %collective-permute-start.15 = (bf16[64,1536]{1,0:T(8,128)(2,1)}, bf16[64,1536]{1,0:T(8,128)(2,1)S(1)}, u32[]{:S(2)}, u32[]{:S(2)}) collective-permute-start(bf16[64,1536]{1,0:T(8,128)(2,1)} %get-tuple-element.299), channel_id=1, source_target_pairs={{0,16},{1,17},{2,18},{3,19},{4,20},{5,21},{6,22},{7,23},{8,24},{9,... | collective-permute-start | bytes 589832 | tf_op jit(solution)/shard_map/ppermute | solution.py:61
  75.5 14.4 %collective-permute-start.16 = (bf16[64,1536]{1,0:T(8,128)(2,1)}, bf16[64,1536]{1,0:T(8,128)(2,1)S(1)}, u32[]{:S(2)}, u32[]{:S(2)}) collective-permute-start(bf16[64,1536]{1,0:T(8,128)(2,1)} %get-tuple-element.299), channel_id=1, source_target_pairs={{0,24},{1,25},{2,26},{3,27},{4,28},{5,29},{6,30},{7,31},{8,16},{9,... | collective-permute-start | bytes 589832 | tf_op jit(solution)/shard_map/ppermute | solution.py:61
  76.1 13.9 %collective-permute-start.12 = (bf16[256,1024]{1,0:T(8,128)(2,1)S(1)}, bf16[256,1024]{1,0:T(8,128)(2,1)S(1)}, u32[]{:S(2)}, u32[]{:S(2)}) collective-permute-start(bf16[256,1024]{1,0:T(8,128)(2,1)S(1)} %pad_maximum_fusion.13), channel_id=1, source_target_pairs={{0,2},{1,3},{2,0},{3,1},{4,6},{5,7},{6,4},{7,5},{8,10},{9,11},{10,... | collective-permute-start | bytes 1572872 | tf_op jit(solution)/shard_map/ppermute | solution.py:61
  77.6 13.6 %collective-permute-start.13 = (bf16[256,1024]{1,0:T(8,128)(2,1)}, bf16[256,1024]{1,0:T(8,128)(2,1)S(1)}, u32[]{:S(2)}, u32[]{:S(2)}) collective-permute-start(bf16[256,1024]{1,0:T(8,128)(2,1)} %pad_maximum_fusion.14), channel_id=1, source_target_pairs={{0,4},{1,5},{2,6},{3,7},{4,0},{5,1},{6,2},{7,3},{8,12},{9,13},{10,... | collective-permute-start | bytes 1572872 | tf_op jit(solution)/shard_map/ppermute | solution.py:61
  93.0 23.1 %collective-permute-start.22 = (bf16[1024,1024]{1,0:T(8,128)(2,1)S(1)}, bf16[1024,1024]{1,0:T(8,128)(2,1)}, u32[]{:S(2)}, u32[]{:S(2)}) collective-permute-start(bf16[1024,1024]{1,0:T(8,128)(2,1)S(1)} %pad_maximum_fusion.2.refs_0_), channel_id=1, source_target_pairs={{0,1},{1,0},{2,3},{3,2},{4,5},{5,4},{6,7},{7,6},{8,9},{9,8},{10,11... | collective-permute-start | bytes 6291464 | tf_op jit(solution)/shard_map/ppermute | solution.py:61
  93.1 23.0 %collective-permute-start.21 = (bf16[1,512,512]{2,1,0:T(8,128)(2,1)}, bf16[1,512,512]{2,1,0:T(8,128)(2,1)S(1)}, u32[]{:S(2)}, u32[]{:S(2)}) collective-permute-start(bf16[1,512,512]{2,1,0:T(8,128)(2,1)} %pad_maximum_fusion.16), channel_id=1, source_target_pairs={{0,2},{1,3},{2,0},{3,1},{4,6},{5,7},{6,4},{7,5},{8,10},{9,11},{10,... | collective-permute-start | bytes 1572872 | tf_op jit(solution)/shard_map/ppermute | solution.py:61
  94.2 21.9 %collective-permute-start.24 = (bf16[128,1536]{1,0:T(8,128)(2,1)}, bf16[128,1536]{1,0:T(8,128)(2,1)S(1)}, u32[]{:S(2)}, u32[]{:S(2)}) collective-permute-start(bf16[128,1536]{1,0:T(8,128)(2,1)} %pad_maximum_fusion.20), channel_id=1, source_target_pairs={{0,2},{1,3},{2,0},{3,1},{4,6},{5,7},{6,4},{7,5},{8,10},{9,11},{10,... | collective-permute-start | bytes 1179656 | tf_op jit(solution)/shard_map/ppermute | solution.py:61
  119.5 24.3 %collective-permute-start.25 = (bf16[256,1536]{1,0:T(8,128)(2,1)S(1)}, bf16[256,1536]{1,0:T(8,128)(2,1)S(1)}, u32[]{:S(2)}, u32[]{:S(2)}) collective-permute-start(bf16[256,1536]{1,0:T(8,128)(2,1)S(1)} %pad_maximum_fusion.9), channel_id=1, source_target_pairs={{0,2},{1,3},{2,0},{3,1},{4,6},{5,7},{6,4},{7,5},{8,10},{9,11},{10,... | collective-permute-start | bytes 2359304 | tf_op jit(solution)/shard_map/ppermute | solution.py:61
  120.1 23.7 %collective-permute-start.26 = (bf16[256,1536]{1,0:T(8,128)(2,1)S(1)}, bf16[256,1536]{1,0:T(8,128)(2,1)S(1)}, u32[]{:S(2)}, u32[]{:S(2)}) collective-permute-start(bf16[256,1536]{1,0:T(8,128)(2,1)S(1)} %pad_maximum_fusion.10), channel_id=1, source_target_pairs={{0,4},{1,5},{2,6},{3,7},{4,0},{5,1},{6,2},{7,3},{8,12},{9,13},{10,... | collective-permute-start | bytes 2359304 | tf_op jit(solution)/shard_map/ppermute | solution.py:61
  122.6 17.6 %collective-permute-start.27 = (bf16[64,1536]{1,0:T(8,128)(2,1)S(1)}, bf16[64,1536]{1,0:T(8,128)(2,1)S(1)}, u32[]{:S(2)}, u32[]{:S(2)}) collective-permute-start(bf16[64,1536]{1,0:T(8,128)(2,1)S(1)} %copy-done.90), channel_id=1, source_target_pairs={{0,8},{1,9},{2,10},{3,11},{4,12},{5,13},{6,14},{7,15},{8,0},{9,1},... | collective-permute-start | bytes 589832 | tf_op jit(solution)/shard_map/ppermute | solution.py:61
  126.6 17.1 %collective-permute-start.28 = (bf16[64,1536]{1,0:T(8,128)(2,1)S(1)}, bf16[64,1536]{1,0:T(8,128)(2,1)S(1)}, u32[]{:S(2)}, u32[]{:S(2)}) collective-permute-start(bf16[64,1536]{1,0:T(8,128)(2,1)S(1)} %copy-done.90), channel_id=1, source_target_pairs={{0,16},{1,17},{2,18},{3,19},{4,20},{5,21},{6,22},{7,23},{8,24},{9,... | collective-permute-start | bytes 589832 | tf_op jit(solution)/shard_map/ppermute | solution.py:61
  128.0 15.8 %collective-permute-start.29 = (bf16[64,1536]{1,0:T(8,128)(2,1)S(1)}, bf16[64,1536]{1,0:T(8,128)(2,1)S(1)}, u32[]{:S(2)}, u32[]{:S(2)}) collective-permute-start(bf16[64,1536]{1,0:T(8,128)(2,1)S(1)} %copy-done.90), channel_id=1, source_target_pairs={{0,24},{1,25},{2,26},{3,27},{4,28},{5,29},{6,30},{7,31},{8,16},{9,... | collective-permute-start | bytes 589832 | tf_op jit(solution)/shard_map/ppermute | solution.py:61
  144.2 28.9 %collective-permute-start.31 = (bf16[1024,1536]{1,0:T(8,128)(2,1)S(1)}, bf16[1024,1536]{1,0:T(8,128)(2,1)S(1)}, u32[]{:S(2)}, u32[]{:S(2)}) collective-permute-start(bf16[1024,1536]{1,0:T(8,128)(2,1)S(1)} %pad_maximum_fusion.refs_0_), channel_id=1, source_target_pairs={{0,1},{1,0},{2,3},{3,2},{4,5},{5,4},{6,7},{7,6},{8,9},{9,8},{10,11... | collective-permute-start | bytes 9437192 | tf_op jit(solution)/shard_map/ppermute | solution.py:61
  151.3 16.9 %collective-permute-start.32 = (bf16[128,1536]{1,0:T(8,128)(2,1)S(1)}, bf16[128,1536]{1,0:T(8,128)(2,1)S(1)}, u32[]{:S(2)}, u32[]{:S(2)}) collective-permute-start(bf16[128,1536]{1,0:T(8,128)(2,1)S(1)} %pad_maximum_fusion.21), channel_id=1, source_target_pairs={{0,4},{1,5},{2,6},{3,7},{4,0},{5,1},{6,2},{7,3},{8,12},{9,13},{10,... | collective-permute-start | bytes 1179656 | tf_op jit(solution)/shard_map/ppermute | solution.py:61
  152.9 20.2 %collective-permute-start.33 = (bf16[128,1536]{1,0:T(8,128)(2,1)S(1)}, bf16[128,1536]{1,0:T(8,128)(2,1)S(1)}, u32[]{:S(2)}, u32[]{:S(2)}) collective-permute-start(bf16[128,1536]{1,0:T(8,128)(2,1)S(1)} %pad_maximum_fusion.22), channel_id=1, source_target_pairs={{0,2},{1,3},{2,0},{3,1},{4,6},{5,7},{6,4},{7,5},{8,10},{9,11},{10,... | collective-permute-start | bytes 1179656 | tf_op jit(solution)/shard_map/ppermute | solution.py:61
  173.2 19.3 %collective-permute-start.34 = (bf16[256,1536]{1,0:T(8,128)(2,1)S(1)}, bf16[256,1536]{1,0:T(8,128)(2,1)S(1)}, u32[]{:S(2)}, u32[]{:S(2)}) collective-permute-start(bf16[256,1536]{1,0:T(8,128)(2,1)S(1)} %pad_maximum_fusion.11), channel_id=1, source_target_pairs={{0,2},{1,3},{2,0},{3,1},{4,6},{5,7},{6,4},{7,5},{8,10},{9,11},{10,... | collective-permute-start | bytes 2359304 | tf_op jit(solution)/shard_map/ppermute | solution.py:61
  175.1 18.7 %collective-permute-start.35 = (bf16[256,1536]{1,0:T(8,128)(2,1)S(1)}, bf16[256,1536]{1,0:T(8,128)(2,1)S(1)}, u32[]{:S(2)}, u32[]{:S(2)}) collective-permute-start(bf16[256,1536]{1,0:T(8,128)(2,1)S(1)} %pad_maximum_fusion.12), channel_id=1, source_target_pairs={{0,4},{1,5},{2,6},{3,7},{4,0},{5,1},{6,2},{7,3},{8,12},{9,13},{10,... | collective-permute-start | bytes 2359304 | tf_op jit(solution)/shard_map/ppermute | solution.py:61
  208.3 19.6 %collective-permute-start.38 = (bf16[256,1536]{1,0:T(8,128)(2,1)S(1)}, bf16[256,1536]{1,0:T(8,128)(2,1)S(1)}, u32[]{:S(2)}, u32[]{:S(2)}) collective-permute-start(bf16[256,1536]{1,0:T(8,128)(2,1)S(1)} %get-tuple-element.375), channel_id=1, source_target_pairs={{0,2},{1,3},{2,0},{3,1},{4,6},{5,7},{6,4},{7,5},{8,10},{9,11},{10,... | collective-permute-start | bytes 2359304 | tf_op jit(solution)/shard_map/ppermute | solution.py:61
  208.9 19.3 %collective-permute-start.39 = (bf16[256,1536]{1,0:T(8,128)(2,1)S(1)}, bf16[256,1536]{1,0:T(8,128)(2,1)S(1)}, u32[]{:S(2)}, u32[]{:S(2)}) collective-permute-start(bf16[256,1536]{1,0:T(8,128)(2,1)S(1)} %get-tuple-element.376), channel_id=1, source_target_pairs={{0,4},{1,5},{2,6},{3,7},{4,0},{5,1},{6,2},{7,3},{8,12},{9,13},{10,... | collective-permute-start | bytes 2359304 | tf_op jit(solution)/shard_map/ppermute | solution.py:61
  231.5 21.3 %collective-permute-start.40 = (bf16[128,1536]{1,0:T(8,128)(2,1)}, bf16[128,1536]{1,0:T(8,128)(2,1)}, u32[]{:S(2)}, u32[]{:S(2)}) collective-permute-start(bf16[128,1536]{1,0:T(8,128)(2,1)} %slice.653), channel_id=1, source_target_pairs={{0,4},{1,5},{2,6},{3,7},{4,0},{5,1},{6,2},{7,3},{8,12},{9,13},{10,... | collective-permute-start | bytes 1179656 | tf_op jit(solution)/shard_map/ppermute | solution.py:61
  232.2 20.6 %collective-permute-start.41 = (bf16[128,1536]{1,0:T(8,128)(2,1)S(1)}, bf16[128,1536]{1,0:T(8,128)(2,1)}, u32[]{:S(2)}, u32[]{:S(2)}) collective-permute-start(bf16[128,1536]{1,0:T(8,128)(2,1)S(1)} %slice.652), channel_id=1, source_target_pairs={{0,2},{1,3},{2,0},{3,1},{4,6},{5,7},{6,4},{7,5},{8,10},{9,11},{10,... | collective-permute-start | bytes 1179656 | tf_op jit(solution)/shard_map/ppermute | solution.py:61
  233.7 19.2 %collective-permute-start.42 = (bf16[1024,1536]{1,0:T(8,128)(2,1)S(1)}, bf16[1024,1536]{1,0:T(8,128)(2,1)}, u32[]{:S(2)}, u32[]{:S(2)}) collective-permute-start(bf16[1024,1536]{1,0:T(8,128)(2,1)S(1)} %get-tuple-element.388), channel_id=1, source_target_pairs={{0,1},{1,0},{2,3},{3,2},{4,5},{5,4},{6,7},{7,6},{8,9},{9,8},{10,11... | collective-permute-start | bytes 9437192 | tf_op jit(solution)/shard_map/ppermute | solution.py:61
  258.1 20.9 %collective-permute-start.46 = (bf16[256,1536]{1,0:T(8,128)(2,1)S(1)}, bf16[256,1536]{1,0:T(8,128)(2,1)S(1)}, u32[]{:S(2)}, u32[]{:S(2)}) collective-permute-start(bf16[256,1536]{1,0:T(8,128)(2,1)S(1)} %get-tuple-element.402), channel_id=1, source_target_pairs={{0,2},{1,3},{2,0},{3,1},{4,6},{5,7},{6,4},{7,5},{8,10},{9,11},{10,... | collective-permute-start | bytes 2359304 | tf_op jit(solution)/shard_map/ppermute | solution.py:61
  258.7 20.3 %collective-permute-start.47 = (bf16[256,1536]{1,0:T(8,128)(2,1)S(1)}, bf16[256,1536]{1,0:T(8,128)(2,1)}, u32[]{:S(2)}, u32[]{:S(2)}) collective-permute-start(bf16[256,1536]{1,0:T(8,128)(2,1)S(1)} %get-tuple-element.403), channel_id=1, source_target_pairs={{0,4},{1,5},{2,6},{3,7},{4,0},{5,1},{6,2},{7,3},{8,12},{9,13},{10,... | collective-permute-start | bytes 2359304 | tf_op jit(solution)/shard_map/ppermute | solution.py:61
  261.4 13.8 %collective-permute-start.43 = (bf16[64,1536]{1,0:T(8,128)(2,1)S(1)}, bf16[64,1536]{1,0:T(8,128)(2,1)}, u32[]{:S(2)}, u32[]{:S(2)}) collective-permute-start(bf16[64,1536]{1,0:T(8,128)(2,1)S(1)} %slice.660), channel_id=1, source_target_pairs={{0,8},{1,9},{2,10},{3,11},{4,12},{5,13},{6,14},{7,15},{8,0},{9,1},... | collective-permute-start | bytes 589832 | tf_op jit(solution)/shard_map/ppermute | solution.py:61
  261.5 17.5 %collective-permute-start.44 = (bf16[64,1536]{1,0:T(8,128)(2,1)}, bf16[64,1536]{1,0:T(8,128)(2,1)}, u32[]{:S(2)}, u32[]{:S(2)}) collective-permute-start(bf16[64,1536]{1,0:T(8,128)(2,1)} %get-tuple-element.400), channel_id=1, source_target_pairs={{0,16},{1,17},{2,18},{3,19},{4,20},{5,21},{6,22},{7,23},{8,24},{9,... | collective-permute-start | bytes 589832 | tf_op jit(solution)/shard_map/ppermute | solution.py:61
  261.6 17.4 %collective-permute-start.45 = (bf16[64,1536]{1,0:T(8,128)(2,1)}, bf16[64,1536]{1,0:T(8,128)(2,1)}, u32[]{:S(2)}, u32[]{:S(2)}) collective-permute-start(bf16[64,1536]{1,0:T(8,128)(2,1)} %get-tuple-element.401), channel_id=1, source_target_pairs={{0,24},{1,25},{2,26},{3,27},{4,28},{5,29},{6,30},{7,31},{8,16},{9,... | collective-permute-start | bytes 589832 | tf_op jit(solution)/shard_map/ppermute | solution.py:61
  281.3 14.9 %collective-permute-start.50 = (bf16[1024,1024]{1,0:T(8,128)(2,1)S(1)}, bf16[1024,1024]{1,0:T(8,128)(2,1)S(1)}, u32[]{:S(2)}, u32[]{:S(2)}) collective-permute-start(bf16[1024,1024]{1,0:T(8,128)(2,1)S(1)} %get-tuple-element.419), channel_id=1, source_target_pairs={{0,1},{1,0},{2,3},{3,2},{4,5},{5,4},{6,7},{7,6},{8,9},{9,8},{10,11... | collective-permute-start | bytes 6291464 | tf_op jit(solution)/shard_map/ppermute | solution.py:61
  282.3 13.9 %collective-permute-start.49 = (bf16[128,1536]{1,0:T(8,128)(2,1)S(1)}, bf16[128,1536]{1,0:T(8,128)(2,1)S(1)}, u32[]{:S(2)}, u32[]{:S(2)}) collective-permute-start(bf16[128,1536]{1,0:T(8,128)(2,1)S(1)} %slice.650), channel_id=1, source_target_pairs={{0,2},{1,3},{2,0},{3,1},{4,6},{5,7},{6,4},{7,5},{8,10},{9,11},{10,... | collective-permute-start | bytes 1179656 | tf_op jit(solution)/shard_map/ppermute | solution.py:61
  297.3 21.9 %collective-permute-start.54 = (bf16[256,1024]{1,0:T(8,128)(2,1)S(1)}, bf16[256,1024]{1,0:T(8,128)(2,1)S(1)}, u32[]{:S(2)}, u32[]{:S(2)}) collective-permute-start(bf16[256,1024]{1,0:T(8,128)(2,1)S(1)} %get-tuple-element.432), channel_id=1, source_target_pairs={{0,2},{1,3},{2,0},{3,1},{4,6},{5,7},{6,4},{7,5},{8,10},{9,11},{10,... | collective-permute-start | bytes 1572872 | tf_op jit(solution)/shard_map/ppermute | solution.py:61
  300.0 19.2 %collective-permute-start.55 = (bf16[256,1024]{1,0:T(8,128)(2,1)S(1)}, bf16[256,1024]{1,0:T(8,128)(2,1)S(1)}, u32[]{:S(2)}, u32[]{:S(2)}) collective-permute-start(bf16[256,1024]{1,0:T(8,128)(2,1)S(1)} %get-tuple-element.433), channel_id=1, source_target_pairs={{0,4},{1,5},{2,6},{3,7},{4,0},{5,1},{6,2},{7,3},{8,12},{9,13},{10,... | collective-permute-start | bytes 1572872 | tf_op jit(solution)/shard_map/ppermute | solution.py:61
  302.1 17.1 %collective-permute-start.52 = (bf16[64,1536]{1,0:T(8,128)(2,1)S(1)}, bf16[64,1536]{1,0:T(8,128)(2,1)S(1)}, u32[]{:S(2)}, u32[]{:S(2)}) collective-permute-start(bf16[64,1536]{1,0:T(8,128)(2,1)S(1)} %get-tuple-element.430), channel_id=1, source_target_pairs={{0,16},{1,17},{2,18},{3,19},{4,20},{5,21},{6,22},{7,23},{8,24},{9,... | collective-permute-start | bytes 589832 | tf_op jit(solution)/shard_map/ppermute | solution.py:61
  302.1 17.1 %collective-permute-start.53 = (bf16[64,1536]{1,0:T(8,128)(2,1)S(1)}, bf16[64,1536]{1,0:T(8,128)(2,1)S(1)}, u32[]{:S(2)}, u32[]{:S(2)}) collective-permute-start(bf16[64,1536]{1,0:T(8,128)(2,1)S(1)} %get-tuple-element.431), channel_id=1, source_target_pairs={{0,24},{1,25},{2,26},{3,27},{4,28},{5,29},{6,30},{7,31},{8,16},{9,... | collective-permute-start | bytes 589832 | tf_op jit(solution)/shard_map/ppermute | solution.py:61
  332.0 15.3 %collective-permute-start.58 = (bf16[2,1,2,256,512]{4,3,2,1,0:T(8,128)(2,1)}, bf16[2,1,2,256,512]{4,3,2,1,0:T(8,128)(2,1)S(1)}, u32[]{:S(2)}, u32[]{:S(2)}) collective-permute-start(bf16[2,1,2,256,512]{4,3,2,1,0:T(8,128)(2,1)} %slice.649), channel_id=1, source_target_pairs={{0,1},{1,0},{2,3},{3,2},{4,5},{5,4},{6,7},{7,6},{8,9},{9,8},{10,11... | collective-permute-start | bytes 3145736 | tf_op jit(solution)/shard_map/ppermute | solution.py:61
  347.5 20.2 %collective-permute-start.60 = (bf16[1024,1024]{1,0:T(8,128)(2,1)S(1)}, bf16[1024,1024]{1,0:T(8,128)(2,1)S(1)}, u32[]{:S(2)}, u32[]{:S(2)}) collective-permute-start(bf16[1024,1024]{1,0:T(8,128)(2,1)S(1)} %get-tuple-element.459), channel_id=1, source_target_pairs={{0,1},{1,0},{2,3},{3,2},{4,5},{5,4},{6,7},{7,6},{8,9},{9,8},{10,11... | collective-permute-start | bytes 6291464 | tf_op jit(solution)/shard_map/ppermute | solution.py:61
  351.4 16.3 %collective-permute-start.59 = (bf16[1,1,2,256,512]{4,3,2,1,0:T(8,128)(2,1)S(1)}, bf16[1,1,2,256,512]{4,3,2,1,0:T(8,128)(2,1)S(1)}, u32[]{:S(2)}, u32[]{:S(2)}) collective-permute-start(bf16[1,1,2,256,512]{4,3,2,1,0:T(8,128)(2,1)S(1)} %add_convert_fusion.6), channel_id=1, source_target_pairs={{0,2},{1,3},{2,0},{3,1},{4,6},{5,7},{6,4},{7,5},{8,10},{9,11},{10,... | collective-permute-start | bytes 1572872 | tf_op jit(solution)/shard_map/ppermute | solution.py:61
  371.2 20.4 %collective-permute-start.61 = (bf16[256,1024]{1,0:T(8,128)(2,1)}, bf16[256,1024]{1,0:T(8,128)(2,1)S(1)}, u32[]{:S(2)}, u32[]{:S(2)}) collective-permute-start(bf16[256,1024]{1,0:T(8,128)(2,1)} %get-tuple-element.471), channel_id=1, source_target_pairs={{0,2},{1,3},{2,0},{3,1},{4,6},{5,7},{6,4},{7,5},{8,10},{9,11},{10,... | collective-permute-start | bytes 1572872 | tf_op jit(solution)/shard_map/ppermute | solution.py:61
  373.0 18.7 %collective-permute-start.62 = (bf16[256,1024]{1,0:T(8,128)(2,1)}, bf16[256,1024]{1,0:T(8,128)(2,1)S(1)}, u32[]{:S(2)}, u32[]{:S(2)}) collective-permute-start(bf16[256,1024]{1,0:T(8,128)(2,1)} %get-tuple-element.472), channel_id=1, source_target_pairs={{0,4},{1,5},{2,6},{3,7},{4,0},{5,1},{6,2},{7,3},{8,12},{9,13},{10,... | collective-permute-start | bytes 1572872 | tf_op jit(solution)/shard_map/ppermute | solution.py:61
  378.5 13.1 %collective-permute-start.64 = (bf16[64,1024]{1,0:T(8,128)(2,1)}, bf16[64,1024]{1,0:T(8,128)(2,1)S(1)}, u32[]{:S(2)}, u32[]{:S(2)}) collective-permute-start(bf16[64,1024]{1,0:T(8,128)(2,1)} %get-tuple-element.474), channel_id=1, source_target_pairs={{0,16},{1,17},{2,18},{3,19},{4,20},{5,21},{6,22},{7,23},{8,24},{9,... | collective-permute-start | bytes 393224 | tf_op jit(solution)/shard_map/ppermute | solution.py:61
  (144 other events, 1050.1 us)

commit v7 on v6

--- a/solution.py
+++ b/solution.py
@@ -132,22 +132,30 @@
 
 
 class Gather:
-    def __init__(self, parts, me, devices, first=False):
+    def __init__(self, parts, me, devices, first=False, spread=False):
         self.part = jnp.concatenate(parts, axis=1)
         self.widths = [one.shape[1] for one in parts]
         self.me, self.devices, self.staged, self.first = me, devices, devices == 32, first
-        self.stage, self.outgoing, self.incoming = 0, (), ()
+        self.stage, self.outgoing, self.incoming = -1 if spread else 0, (), ()
+        self.spread = spread
 
     def prepare(self):
         stage = self.stage
         self.stage += 1
         if not self.staged:
             return
-        if stage == 0:
+        if stage == -1:
+            self.outgoing, self.masks = (self.part,), ((8,),)
+        elif stage == 0 and self.spread:
+            self.outgoing, self.masks = (jnp.concatenate([self.part, *self.incoming]),), ((16,),)
+        elif stage == 0:
             self.outgoing, self.masks = (self.part,), ((8, 16, 24),)
         elif stage == 1:
-            one, two, three = self.incoming
-            self.outgoing = jnp.concatenate([self.part, one]), jnp.concatenate([two, three])
+            if self.spread:
+                self.outgoing += self.incoming
+            else:
+                one, two, three = self.incoming
+                self.outgoing = jnp.concatenate([self.part, one]), jnp.concatenate([two, three])
             self.masks = (4,), (2,)
         elif stage == 2:
             self.outgoing = tuple(
@@ -180,8 +188,9 @@
 
 
 class Reduce:
-    def __init__(self, grads, me, devices):
+    def __init__(self, grads, me, devices, spread=False):
         self.grads, self.me, self.devices, self.staged = grads, me, devices, devices == 32
+        self.spread = spread
         self.size = grads[0].shape[0] // devices
         self.stage, self.outgoing, self.incoming = 0, (), ()
 
@@ -211,6 +220,15 @@
             self.outgoing = near[2 * size :].astype(LOW), far[2 * size :].astype(LOW)
             self.near, self.far = near[: 2 * size], far[: 2 * size]
             self.masks = 4, 2
+        elif stage == 3 and self.spread:
+            self.near = self.near + incoming[0]
+            self.outgoing, self.masks = ((self.far + incoming[1]).astype(LOW),), (16,)
+        elif stage == 4 and self.spread:
+            near = self.near + incoming[0]
+            self.own = near[:size]
+            self.outgoing, self.masks = (near[size:].astype(LOW),), (8,)
+        elif self.spread and stage > 4:
+            self.total = self.own + incoming[0]
         elif stage == 3:
             near, far = self.near + incoming[0], self.far + incoming[1]
             self.outgoing = near[size:].astype(LOW), far[:size].astype(LOW), far[size:].astype(LOW)
@@ -311,9 +329,13 @@
             self.outgoing, self.mask = (grad[2:].astype(LOW),), 1
         elif stage == 1:
             (self.came,) = self.incoming
-            self.outgoing, self.mask = ((grad[1:2] + self.came[1:].astype(jnp.float32)).astype(LOW),), 2
+            self.over = (grad[1:2] + self.came[1:].astype(jnp.float32)).astype(LOW)
+            self.outgoing, self.mask = (self.over[:, :, :1],), 2
+        elif stage == 2:
+            (self.keys,) = self.incoming
+            self.outgoing = (self.over[:, :, 1:],)
         else:
-            self.shares = grad, (self.came, *self.incoming)
+            self.shares = grad, (self.came, jnp.concatenate([self.keys, *self.incoming], axis=2))
 
     def launch(self):
         if self.staged:
@@ -402,7 +424,7 @@
                 pltpu.VMEM((GROUP, length, min(128, length)), jnp.float32),
             ],
         ),
-        compiler_params=pltpu.CompilerParams(vmem_limit_bytes=40 << 20),
+        compiler_params=pltpu.CompilerParams(vmem_limit_bytes=16 << 20),
         cost_estimate=pl.CostEstimate(flops=work, transcendentals=0, bytes_accessed=1 << 20),
     )(info, queries, keys_values, keys_values)
 
@@ -519,7 +541,7 @@
             ],
         ),
         input_output_aliases={len(inputs) + at: at for at in range(len(carried))},
-        compiler_params=pltpu.CompilerParams(vmem_limit_bytes=40 << 20),
+        compiler_params=pltpu.CompilerParams(vmem_limit_bytes=16 << 20),
         cost_estimate=pl.CostEstimate(flops=work, transcendentals=0, bytes_accessed=1 << 20),
     )(*inputs, *carried)
 
@@ -567,7 +589,7 @@
             pl.BlockSpec((1, 2 * width, length), lambda row: (row, 0, 0)),
             pl.BlockSpec((1, HD, 128), lambda row: (row, 0, 0)),
         ],
-        compiler_params=pltpu.CompilerParams(vmem_limit_bytes=40 << 20),
+        compiler_params=pltpu.CompilerParams(vmem_limit_bytes=16 << 20),
     )(own, *others, k_raw, gain, cos_t, sin_t)
 
 
@@ -627,6 +649,7 @@
             [jnp.concatenate([w_gate_low[:, own], w_up_low[:, own]], axis=1), w_down_low[:, own]],
             me,
             devices,
+            spread=own is halves[1],
         )
         for own in halves
     ]
@@ -634,11 +657,11 @@
     x_float = tokens.astype(jnp.float32)
     normed_one, inverse_one = normalize(x_float)
     (normed_one,) = close_slot([gather_a], normed_one)
+    (normed_one,) = open_slot([gather_a, gather_c[0]], normed_one)
+    (normed_one,) = close_slot([gather_a, gather_c[0]], normed_one)
     (normed_one,) = open_slot([gather_a, gather_b], normed_one)
     (normed_one,) = close_slot([gather_a, gather_b], normed_one)
-    (normed_one,) = open_slot([gather_a, gather_b], normed_one)
-    (normed_one,) = close_slot([gather_a, gather_b], normed_one)
-    (normed_one,) = open_slot([gather_a, gather_b, gather_c[0]], normed_one)
+    (normed_one,) = open_slot([gather_a, gather_c[0]], normed_one)
     (normed_one,) = close_slot([gather_a], normed_one)
     wq, wkv, gains = gather_a.whole()
     gain_attn = gains[:, 0].astype(jnp.float32)
@@ -650,9 +673,9 @@
     k_unit, k_inverse = normalize(k_raw, 2)
     k_low = rotate(k_unit * k_gain_h, cos_h, sin_h).astype(LOW).reshape(row_count, kv_width, piece_len)
     own_kv = jnp.concatenate([k_low, v_raw.astype(LOW)], axis=1)
-    own_kv, normed_low = close_slot([gather_b, gather_c[0]], own_kv, normed_low)
+    own_kv, normed_low = close_slot([gather_c[0]], own_kv, normed_low)
     row_pieces = Pieces(own_kv, devices, shards)
-    (normed_low,) = open_slot([row_pieces, gather_b, gather_c[0]], normed_low)
+    (normed_low,) = open_slot([row_pieces, gather_b, gather_c[1]], normed_low)
     q_raw = jnp.einsum("rtd,de->ret", normed_low, wq, preferred_element_type=jnp.float32).reshape(
         row_count, HEADS, HD, piece_len
     )
@@ -660,14 +683,15 @@
     q_low = (
         rotate(q_unit * q_gain_h, cos_h, sin_h).astype(LOW) * jnp.array(scale_factor, LOW)
     ).reshape(row_count, q_width, piece_len)
-    (q_low,) = close_slot([row_pieces, gather_b, gather_c[0]], q_low)
-    (q_low,) = open_slot([row_pieces, *gather_c], q_low)
+    (q_low,) = close_slot([row_pieces, gather_b, gather_c[1]], q_low)
+    (q_low,) = open_slot([row_pieces, gather_b, *gather_c], q_low)
     (q_low,) = close_slot([row_pieces], q_low)
     pieces, piece_at = row_pieces.whole()
     info = jnp.concatenate([start.reshape(1), piece_at * piece_len, row_valid]).astype(jnp.int32)
     o_heads, att_low, sums = attention(info, q_low, pieces, 0, KV)
-    o_heads, att_low, sums = close_slot(gather_c, o_heads, att_low, sums)
-    (att_low,) = open_slot(gather_c, att_low)
+    o_heads, att_low, sums = close_slot([gather_b, *gather_c], o_heads, att_low, sums)
+    (att_low,) = open_slot([gather_b, *gather_c], att_low)
+    (att_low,) = close_slot([gather_b], att_low)
     (wout,) = gather_b.whole()
     x_mid = x_float + jnp.einsum("rct,dc->rtd", att_low, wout, preferred_element_type=jnp.float32)
     normed_two, inverse_two = normalize(x_mid)
@@ -699,18 +723,16 @@
         [gather_c[1]], ffn_in, red_one.outgoing, act_one, both_one
     )
     (ffn_in,) = open_slot([gather_c[1]], ffn_in)
+    (ffn_in,) = close_slot([gather_c[1]], ffn_in)
     (ffn_in,) = open_slot([red_one], ffn_in, ready=[red_one])
-    (ffn_in,) = close_slot([gather_c[1]], ffn_in)
     wgu_two, wdown_two = gather_c[1].whole()
-    ffn_in, wgu_two, wdown_two = close_slot([red_one], ffn_in, wgu_two, wdown_two)
-    (ffn_in,) = open_slot([red_one], ffn_in)
     act_two, both_two, grads = feed_forward(ffn_in, grad_low, wgu_two, wdown_two)
     red_two = Reduce(grads, me, devices)
     red_two.prepare()
     ffn_in, red_two.outgoing, act_two, both_two = close_slot(
         [red_one], ffn_in, red_two.outgoing, act_two, both_two
     )
-    both_two, act_two = open_slot([red_one, red_two], both_two, act_two, ready=[red_two])
+    both_two, act_two = open_slot([red_one], both_two, act_two)
     grad_ffn_in = jnp.einsum(
         "rtf,df->rtd", both_one, wgu_one, preferred_element_type=jnp.float32
     ) + jnp.einsum("rtf,df->rtd", both_two, wgu_two, preferred_element_type=jnp.float32)
@@ -718,10 +740,10 @@
     mid_low = grad_mid.astype(LOW)
     grad_wout = jnp.einsum("rtd,rct->dc", mid_low, att_low, preferred_element_type=jnp.float32)
     grad_att = jnp.einsum("rtd,dc->rct", mid_low, wout, preferred_element_type=jnp.float32)
-    red_out = Reduce([grad_wout.astype(LOW)], me, devices)
+    red_out = Reduce([grad_wout.astype(LOW)], me, devices, True)
     red_out.prepare()
-    grad_att, red_out.outgoing = close_slot([red_one, red_two], grad_att, red_out.outgoing)
-    grad_att, act_two = open_slot([red_one, red_two], grad_att, act_two)
+    grad_att, red_out.outgoing = close_slot([red_one], grad_att, red_out.outgoing)
+    grad_att, act_two = open_slot([red_one, red_two], grad_att, act_two, ready=[red_two])
 
     q_gain_c, k_gain_c = q_gain[:, None], k_gain[:, None]
     q_raw_flat = q_raw.reshape(row_count, q_width, piece_len)
@@ -746,26 +768,28 @@
 
     carried = more(0, grad_att)
     carried, grad_att, output = close_slot([red_one, red_two], carried, grad_att, output)
+    (grad_att,) = open_slot([red_one, red_two], grad_att)
+    carried = more(1, grad_att, carried)
+    carried, grad_att = close_slot([red_one, red_two], carried, grad_att)
     red_one.prepare()
     (grad_att,) = open_slot([red_two, red_out], grad_att, ready=[red_out])
-    carried = more(1, grad_att, carried)
+    carried = more(2, grad_att, carried)
     carried, grad_att = close_slot([red_two, red_out], carried, grad_att)
     (grad_att,) = open_slot([red_two, red_out], grad_att)
-    carried = more(2, grad_att, carried)
-    carried, grad_att = close_slot([red_two, red_out], carried, grad_att)
+    carried = more(3, grad_att, carried)
+    grad_q_low, grad_pieces = close_slot([red_two, red_out], carried)[0]
     red_two.prepare()
-    (grad_att,) = open_slot([red_out], grad_att)
-    carried = more(3, grad_att, carried)
-    grad_q_low, grad_pieces = close_slot([red_out], carried)[0]
     kv_back = PiecesBack(grad_pieces, devices, shards)
+    (grad_q_low,) = open_slot([kv_back, red_out], grad_q_low)
+    (grad_q_low,) = close_slot([kv_back], grad_q_low)
     (grad_q_low,) = open_slot([kv_back], grad_q_low)
     grad_wq = jnp.einsum("rtd,ret->de", normed_low, grad_q_low, preferred_element_type=jnp.float32)
     red_q = Reduce([grad_wq.astype(LOW)], me, devices)
     red_q.prepare()
-    red_q.outgoing, grad_q_low = close_slot([kv_back], red_q.outgoing, grad_q_low)
-    (grad_q_low,) = open_slot([kv_back, red_q], grad_q_low, ready=[red_q])
+    red_q.outgoing, grad_q_low = close_slot([kv_back, red_out], red_q.outgoing, grad_q_low)
+    (grad_q_low,) = open_slot([kv_back, red_q, red_out], grad_q_low, ready=[red_q])
     grad_normed_q = jnp.einsum("ret,de->rtd", grad_q_low, wq, preferred_element_type=jnp.float32)
-    (grad_normed_q,) = close_slot([kv_back, red_q], grad_normed_q)
+    (grad_normed_q,) = close_slot([kv_back, red_q, red_out], grad_normed_q)
     kv_back.prepare()
     grad_kv_low, k_gain_part = finish_keys(*kv_back.shares, k_raw_flat, k_gain_c, cos_t, sin_t)
     shared = Sum(

time: 441 us -> 422 us (0.957)
  waiting for transfers between devices: 118 us -> 103 us
  Pallas kernels: 72.1 us -> 66.8 us
  local copies, waits for them, and re-layouts: 19.3 us -> 24.4 us
    ppermute x84 -> x83, waiting for transfers between devices: 118 us -> 103 us  [swap(): lax.ppermute(values, ('dp', 'shard'), [(i, i ^ mask) for i in range(devic...]
    unnamed x217 -> x193, local copies, waits for them, and re-layouts: 10.7 us -> 18.2 us
    ppermute x84 -> x83, starting transfers between devices: 118 us -> 118 us  [swap(): lax.ppermute(values, ('dp', 'shard'), [(i, i ^ mask) for i in range(devic...]
  transfers between devices with their start and end apart: 84 -> 83, of which waited for: 27 -> 30; matrix products, arithmetic and copies ran while one was open for 19% -> 20% of each run, Pallas kernels for 16% -> 16%
where the time goes in v7:
time: 422 us; the launch traced here: 420 us
  starting transfers between devices  118 us (28%)
  waiting for transfers between devices  103 us (24%)
  Pallas kernels  66.8 us (16%)
  matrix products  54.6 us (13%)
  other arithmetic  49.7 us (12%)
  local copies, waits for them, and re-layouts  24.4 us (6%)
    ppermute x83, starting transfers between devices, swap(): lax.ppermute(values, ('dp', 'shard'), [(i, i ^ mask) for i in range(devic...  118 us
    ppermute x83, waiting for transfers between devices, swap(): lax.ppermute(values, ('dp', 'shard'), [(i, i ^ mask) for i in range(devic...  103 us
    pallas_call x4, Pallas kernels, attention_back(): pl.pallas_call(kernel, out_shape=[jax.ShapeDtypeStruct(queries.shape, LOW...  22 us
    pallas_call x5, Pallas kernels, pick(): pl.pallas_call(kernel, out_shape=[jax.ShapeDtypeStruct((len(own) * size,...  19.2 us
    unnamed x193, local copies, waits for them, and re-layouts  18.2 us
    pallas_call x4, Pallas kernels, place(): pl.pallas_call(kernel, out_shape=[jax.ShapeDtypeStruct((total_rows, width...  14.4 us
    pallas_call x1, Pallas kernels, attention(): pl.pallas_call(kernel, out_shape=[jax.ShapeDtypeStruct((rows, groups * gr...  10.7 us
    convert_element_type x5, other arithmetic, prepare(): self.outgoing = (self.both(0, 4).astype(LOW), self.both(4, 8).astype(LOW))  9.16 us
  transfers between devices with their start and end apart: 83, of which 30 were waited for; matrix products, arithmetic and copies ran while one was open for 20% of the time, Pallas kernels for 16%

profile of v7, /device:TPU:0, one launch (start us, length us, event | category | flops | bytes accessed | tf_op | source)
XLA Modules:
  0.0 419.5 jit_solution(18068883801076936505)
XLA Ops:
  3.5 3.1 collective-permute-start
  15.6 9.2 %collective-permute-done.1 = bf16[64,1664]{1,0:T(8,128)(2,1)S(1)} collective-permute-done((bf16[64,1664]{1,0:T(8,128)(2,1)S(1)}, bf16[64,1664]{1,0:T(8,128)(2,1)S(1)}, u32[]{:S(2)}, u32[]{:S(2)}) %collective-permute-start.1) | collective-permute-done | bytes 213024 | tf_op jit(solution)/shard_map/ppermute | solution.py:61
  27.9 3.7 collective-permute-start.5
  34.2 3.4 collective-permute-done.5
  37.5 10.2 %collective-permute-done.6 = bf16[64,1536]{1,0:T(8,128)(2,1)S(1)} collective-permute-done((bf16[64,1536]{1,0:T(8,128)(2,1)S(1)}, bf16[64,1536]{1,0:T(8,128)(2,1)S(1)}, u32[]{:S(2)}, u32[]{:S(2)}) %collective-permute-start.6) | collective-permute-done | bytes 196640 | tf_op jit(solution)/shard_map/ppermute | solution.py:61
  49.0 2.7 collective-permute-start.10
  55.0 7.5 %collective-permute-done.11 = bf16[64,1024]{1,0:T(8,128)(2,1)S(1)} collective-permute-done((bf16[64,1024]{1,0:T(8,128)(2,1)S(1)}, bf16[64,1024]{1,0:T(8,128)(2,1)S(1)}, u32[]{:S(2)}, u32[]{:S(2)}) %collective-permute-start.11) | collective-permute-done | bytes 131104 | tf_op jit(solution)/shard_map/ppermute | solution.py:61
  69.9 4.4 %shard_map.221 = (bf16[2048,1024]{1,0:T(8,128)(2,1)S(1)}, bf16[2048,512]{1,0:T(8,128)(2,1)S(1)}, bf16[2048,128]{1,0:T(8,128)(2,1)S(1)}) custom-call(s32[1]{0:T(128)} %bitcast.me_ref, bf16[256,1664]{1,0:T(8,128)(2,1)S(1)} %pad_maximum_fusion.7.refs_0_, bf16[256,1664]{1,0:T(8,128)(2,1)S(1)} %pad_maximum_fusion.8.refs_1_, ...), custom_call_target="tpu_custom_call" | custom-call | bytes 65536 | tf_op jit(solution)/shard_map/pallas_call | solution.py:88
  82.2 5.7 %collective-permute-start.22 = (bf16[64,1536]{1,0:T(8,128)(2,1)S(1)}, bf16[64,1536]{1,0:T(8,128)(2,1)S(1)}, u32[]{:S(2)}, u32[]{:S(2)}) collective-permute-start(bf16[64,1536]{1,0:T(8,128)(2,1)S(1)} %copy-done.74), channel_id=1, source_target_pairs={{0,8},{1,9},{2,10},{3,11},{4,12},{5,13},{6,14},{7,15},{8,0},{9,1},... | collective-permute-start | bytes 589832 | tf_op jit(solution)/shard_map/ppermute | solution.py:61
  93.1 5.1 %collective-permute-done.21 = bf16[128,1024]{1,0:T(8,128)(2,1)S(1)} collective-permute-done((bf16[128,1024]{1,0:T(8,128)(2,1)S(1)}, bf16[128,1024]{1,0:T(8,128)(2,1)S(1)}, u32[]{:S(2)}, u32[]{:S(2)}) %collective-permute-start.21) | collective-permute-done | bytes 262176 | tf_op jit(solution)/shard_map/ppermute | solution.py:61
  103.3 7.6 %collective-permute-start.27 = (bf16[128,1536]{1,0:T(8,128)(2,1)S(1)}, bf16[128,1536]{1,0:T(8,128)(2,1)S(1)}, u32[]{:S(2)}, u32[]{:S(2)}) collective-permute-start(bf16[128,1536]{1,0:T(8,128)(2,1)S(1)} %pad_maximum_fusion.22), channel_id=1, source_target_pairs={{0,16},{1,17},{2,18},{3,19},{4,20},{5,21},{6,22},{7,23},{8,24},{9,... | collective-permute-start | bytes 1179656 | tf_op jit(solution)/shard_map/ppermute | solution.py:61
  112.4 10.7 %shard_map.222 = (f32[1,1024,512]{2,1,0:T(8,128)S(1)}, bf16[1,1024,512]{2,1,0:T(8,128)(2,1)S(1)}, f32[1,4,4,512]{3,2,1,0:T(4,128)S(1)}) custom-call(s32[6]{0:T(128)S(1)} %pad_add_fusion.info_ref, bf16[1,1024,512]{2,1,0:T(8,128)(2,1)S(1)} %bitcast.231, bf16[4,1,512,512]{3,2,1,0:T(8,128)(2,1)S(1)} %constant_dynamic-update-slice_fusion.k_ref.v_ref, ...), custom_call_target="tpu_custom_call" | custom-call | flops 16777216 | bytes 1048576 | tf_op jit(solution)/shard_map/pallas_call | solution.py:410
  124.5 3.4 collective-permute-done.27
  133.3 8.8 %collective-permute-start.31 = (bf16[128,1536]{1,0:T(8,128)(2,1)S(1)}, bf16[128,1536]{1,0:T(8,128)(2,1)S(1)}, u32[]{:S(2)}, u32[]{:S(2)}) collective-permute-start(bf16[128,1536]{1,0:T(8,128)(2,1)S(1)} %collective-permute-done.27), channel_id=1, source_target_pairs={{0,2},{1,3},{2,0},{3,1},{4,6},{5,7},{6,4},{7,5},{8,10},{9,11},{10,... | collective-permute-start | bytes 1179656 | tf_op jit(solution)/shard_map/ppermute | solution.py:61
  142.1 5.9 %shard_map.223 = bf16[2048,1024]{1,0:T(8,128)(2,1)S(1)} custom-call(s32[1]{0:T(128)} %bitcast.me_ref, bf16[1024,1024]{1,0:T(8,128)(2,1)S(1)} %pad_maximum_fusion.3.refs_0_, bf16[1024,1024]{1,0:T(8,128)(2,1)S(1)} %collective-permute-done.32.refs_1_), custom_call_target="tpu_custom_call" | custom-call | bytes 65536 | tf_op jit(solution)/shard_map/pallas_call | solution.py:88
  168.1 5.2 %collective-permute-done.33 = bf16[256,1536]{1,0:T(8,128)(2,1)S(1)} collective-permute-done((bf16[256,1536]{1,0:T(8,128)(2,1)S(1)}, bf16[256,1536]{1,0:T(8,128)(2,1)S(1)}, u32[]{:S(2)}, u32[]{:S(2)}) %collective-permute-start.33) | collective-permute-done | bytes 786464 | tf_op jit(solution)/shard_map/ppermute | solution.py:61
  175.1 5.6 %collective-permute-done.35.refs_1_ = bf16[1024,1536]{1,0:T(8,128)(2,1)S(1)} collective-permute-done((bf16[1024,1536]{1,0:T(8,128)(2,1)S(1)}, bf16[1024,1536]{1,0:T(8,128)(2,1)S(1)}, u32[]{:S(2)}, u32[]{:S(2)}) %collective-permute-start.35) | collective-permute-done | bytes 3145760 | tf_op jit(solution)/shard_map/ppermute | solution.py:61
  183.1 3.7 fusion.32
  186.8 3.3 multiply_convert_fusion.4
  194.1 3.3 shard_map.227
  197.5 4.0 add_convert_fusion.2
  204.8 2.7 fusion.7
  207.5 2.7 fusion.8
  212.7 6.1 %shard_map.228 = (bf16[1024,1024]{1,0:T(8,128)(2,1)S(1)}, bf16[1024,1024]{1,0:T(8,128)(2,1)S(1)}) custom-call(s32[1]{0:T(128)} %bitcast.me_ref, bf16[2048,1024]{1,0:T(8,128)(2,1)S(1)} %convolution_convert_fusion.1.refs_0_), custom_call_target="tpu_custom_call" | custom-call | bytes 65536 | tf_op jit(solution)/shard_map/pallas_call | solution.py:123
  218.8 3.7 fusion.35.grad_ref
  234.9 5.5 %shard_map.229 = (bf16[1,1024,512]{2,1,0:T(8,128)(2,1)S(1)}, f32[4,1,2,256,512]{4,3,2,1,0:T(8,128)S(1)}, f32[1,64,128]{2,1,0:T(8,128)S(1)}) custom-call(s32[6]{0:T(128)S(1)} %pad_add_fusion.info_ref, bf16[1,1024,512]{2,1,0:T(8,128)(2,1)S(1)} %bitcast.232, bf16[4,1,512,512]{3,2,1,0:T(8,128)(2,1)S(1)} %constant_dynamic-update-slice_fusion.k_ref.v_ref, ...), custom_call_target="tpu_custom_call" | custom-call | flops 4194304 | bytes 1048576 | tf_op jit(solution)/shard_map/pallas_call | solution.py:518
  243.3 2.6 fusion.6
  250.1 6.0 %collective-permute-start.45 = (bf16[256,1536]{1,0:T(8,128)(2,1)S(1)}, bf16[256,1536]{1,0:T(8,128)(2,1)S(1)}, u32[]{:S(2)}, u32[]{:S(2)}) collective-permute-start(bf16[256,1536]{1,0:T(8,128)(2,1)S(1)} %get-tuple-element.407), channel_id=1, source_target_pairs={{0,2},{1,3},{2,0},{3,1},{4,6},{5,7},{6,4},{7,5},{8,10},{9,11},{10,... | collective-permute-start | bytes 2359304 | tf_op jit(solution)/shard_map/ppermute | solution.py:61
  257.5 3.5 collective-permute-start.44
  261.0 5.3 %shard_map.230 = (bf16[1,1024,512]{2,1,0:T(8,128)(2,1)S(1)}, f32[4,1,2,256,512]{4,3,2,1,0:T(8,128)S(1)}, f32[1,64,128]{2,1,0:T(8,128)S(1)}) custom-call(s32[6]{0:T(128)S(1)} %pad_add_fusion.info_ref, bf16[1,1024,512]{2,1,0:T(8,128)(2,1)S(1)} %bitcast.233, ...), custom_call_target="tpu_custom_call", output_to_operand_aliasing={{0}: (11, {}), {1}: (12, {})} | custom-call | flops 4194304 | bytes 1048576 | tf_op jit(solution)/shard_map/pallas_call | solution.py:518
  266.3 6.2 %collective-permute-done.43 = bf16[64,1536]{1,0:T(8,128)(2,1)S(1)} collective-permute-done((bf16[64,1536]{1,0:T(8,128)(2,1)S(1)}, bf16[64,1536]{1,0:T(8,128)(2,1)S(1)}, u32[]{:S(2)}, u32[]{:S(2)}) %collective-permute-start.43) | collective-permute-done | bytes 196640 | tf_op jit(solution)/shard_map/ppermute | solution.py:61
  280.9 5.7 %shard_map.231 = (bf16[1,1024,512]{2,1,0:T(8,128)(2,1)S(1)}, f32[4,1,2,256,512]{4,3,2,1,0:T(8,128)S(1)}, f32[1,64,128]{2,1,0:T(8,128)S(1)}) custom-call(s32[6]{0:T(128)S(1)} %pad_add_fusion.info_ref, bf16[1,1024,512]{2,1,0:T(8,128)(2,1)S(1)} %bitcast.234, ...), custom_call_target="tpu_custom_call", output_to_operand_aliasing={{0}: (11, {}), {1}: (12, {})} | custom-call | flops 4194304 | bytes 1048576 | tf_op jit(solution)/shard_map/pallas_call | solution.py:518
  286.6 3.0 collective-permute-done.47
  296.3 2.7 collective-permute-start.50
  301.4 5.5 %shard_map.232 = (bf16[1,1024,512]{2,1,0:T(8,128)(2,1)S(1)}, f32[4,1,2,256,512]{4,3,2,1,0:T(8,128)S(1)}, f32[1,64,128]{2,1,0:T(8,128)S(1)}) custom-call(s32[6]{0:T(128)S(1)} %pad_add_fusion.info_ref, bf16[1,1024,512]{2,1,0:T(8,128)(2,1)S(1)} %bitcast.235, ...), custom_call_target="tpu_custom_call", output_to_operand_aliasing={{0}: (11, {}), {1}: (12, {})} | custom-call | flops 4194304 | bytes 1048576 | tf_op jit(solution)/shard_map/pallas_call | solution.py:518
  306.9 9.1 %collective-permute-done.51 = bf16[64,1536]{1,0:T(8,128)(2,1)S(1)} collective-permute-done((bf16[64,1536]{1,0:T(8,128)(2,1)S(1)}, bf16[64,1536]{1,0:T(8,128)(2,1)S(1)}, u32[]{:S(2)}, u32[]{:S(2)}) %collective-permute-start.51) | collective-permute-done | bytes 196640 | tf_op jit(solution)/shard_map/ppermute | solution.py:61
  325.6 4.7 %shard_map.233 = (bf16[1024,1024]{1,0:T(8,128)(2,1)S(1)}, bf16[1024,1024]{1,0:T(8,128)(2,1)}) custom-call(s32[1]{0:T(128)} %bitcast.me_ref, bf16[2048,1024]{1,0:T(8,128)(2,1)S(1)} %convolution_convert_fusion.refs_0_), custom_call_target="tpu_custom_call" | custom-call | bytes 65536 | tf_op jit(solution)/shard_map/pallas_call | solution.py:123
  339.3 3.6 collective-permute-start.61
  342.9 6.7 %convolution_bitcast_fusion = f32[1,512,2048]{2,1,0:T(8,128)} fusion(bf16[2048,1024]{1,0:T(8,128)(2,1)} %copy-done.31, bf16[1,1024,512]{2,1,0:T(8,128)(2,1)S(1)} %copy-done.11), kind=kOutput, calls=%fused_computation.29 | convolution fusion | flops 2147483648 | bytes 9437184 | tf_op jit(solution)/shard_map/ret,de->rtd/dot_general | solution.py:791
  349.6 5.5 %collective-permute-done.61 = bf16[128,1024]{1,0:T(8,128)(2,1)S(1)} collective-permute-done((bf16[128,1024]{1,0:T(8,128)(2,1)S(1)}, bf16[128,1024]{1,0:T(8,128)(2,1)S(1)}, u32[]{:S(2)}, u32[]{:S(2)}) %collective-permute-start.61) | collective-permute-done | bytes 262176 | tf_op jit(solution)/shard_map/ppermute | solution.py:61
  355.9 2.7 add_convert_fusion.4
  362.2 3.0 convolution_convert_fusion.4.refs_0_
  365.3 3.2 shard_map.235
  368.5 4.8 %collective-permute-done.62 = bf16[256,1024]{1,0:T(8,128)(2,1)S(1)} collective-permute-done((bf16[256,1024]{1,0:T(8,128)(2,1)}, bf16[256,1024]{1,0:T(8,128)(2,1)S(1)}, u32[]{:S(2)}, u32[]{:S(2)}) %collective-permute-start.62) | collective-permute-done | bytes 524320 | tf_op jit(solution)/shard_map/ppermute | solution.py:61
  381.4 2.9 fusion.3
  387.7 3.4 collective-permute-start.71
  395.0 6.0 %collective-permute-done.71 = bf16[64,1024]{1,0:T(8,128)(2,1)S(1)} collective-permute-done((bf16[64,1024]{1,0:T(8,128)(2,1)S(1)}, bf16[64,1024]{1,0:T(8,128)(2,1)S(1)}, u32[]{:S(2)}, u32[]{:S(2)}) %collective-permute-start.71) | collective-permute-done | bytes 131104 | tf_op jit(solution)/shard_map/ppermute | solution.py:61
  414.4 2.9 collective-permute-done.82
  (490 shorter events, 179.8 us)
Async XLA Ops:
  3.5 12.1 %collective-permute-start = (bf16[64,1664]{1,0:T(8,128)(2,1)S(1)}, bf16[64,1664]{1,0:T(8,128)(2,1)S(1)}, u32[]{:S(2)}, u32[]{:S(2)}) collective-permute-start(bf16[64,1664]{1,0:T(8,128)(2,1)S(1)} %concatenate.125), channel_id=1, source_target_pairs={{0,8},{1,9},{2,10},{3,11},{4,12},{5,13},{6,14},{7,15},{8,0},{9,1},... | collective-permute-start | bytes 638984 | tf_op jit(solution)/shard_map/ppermute | solution.py:61
  6.6 18.2 %collective-permute-start.1 = (bf16[64,1664]{1,0:T(8,128)(2,1)S(1)}, bf16[64,1664]{1,0:T(8,128)(2,1)S(1)}, u32[]{:S(2)}, u32[]{:S(2)}) collective-permute-start(bf16[64,1664]{1,0:T(8,128)(2,1)S(1)} %concatenate.125), channel_id=1, source_target_pairs={{0,16},{1,17},{2,18},{3,19},{4,20},{5,21},{6,22},{7,23},{8,24},{9,... | collective-permute-start | bytes 638984 | tf_op jit(solution)/shard_map/ppermute | solution.py:61
  9.2 15.6 %collective-permute-start.2 = (bf16[64,1664]{1,0:T(8,128)(2,1)S(1)}, bf16[64,1664]{1,0:T(8,128)(2,1)S(1)}, u32[]{:S(2)}, u32[]{:S(2)}) collective-permute-start(bf16[64,1664]{1,0:T(8,128)(2,1)S(1)} %concatenate.125), channel_id=1, source_target_pairs={{0,24},{1,25},{2,26},{3,27},{4,28},{5,29},{6,30},{7,31},{8,16},{9,... | collective-permute-start | bytes 638984 | tf_op jit(solution)/shard_map/ppermute | solution.py:61
  24.9 22.9 %collective-permute-start.3 = (bf16[128,1664]{1,0:T(8,128)(2,1)S(1)}, bf16[128,1664]{1,0:T(8,128)(2,1)S(1)}, u32[]{:S(2)}, u32[]{:S(2)}) collective-permute-start(bf16[128,1664]{1,0:T(8,128)(2,1)S(1)} %get-tuple-element.276), channel_id=1, source_target_pairs={{0,4},{1,5},{2,6},{3,7},{4,0},{5,1},{6,2},{7,3},{8,12},{9,13},{10,... | collective-permute-start | bytes 1277960 | tf_op jit(solution)/shard_map/ppermute | solution.py:61
  26.4 21.3 %collective-permute-start.4 = (bf16[128,1664]{1,0:T(8,128)(2,1)S(1)}, bf16[128,1664]{1,0:T(8,128)(2,1)S(1)}, u32[]{:S(2)}, u32[]{:S(2)}) collective-permute-start(bf16[128,1664]{1,0:T(8,128)(2,1)S(1)} %get-tuple-element.277), channel_id=1, source_target_pairs={{0,2},{1,3},{2,0},{3,1},{4,6},{5,7},{6,4},{7,5},{8,10},{9,11},{10,... | collective-permute-start | bytes 1277960 | tf_op jit(solution)/shard_map/ppermute | solution.py:61
  31.6 16.1 %collective-permute-start.6 = (bf16[64,1536]{1,0:T(8,128)(2,1)S(1)}, bf16[64,1536]{1,0:T(8,128)(2,1)S(1)}, u32[]{:S(2)}, u32[]{:S(2)}) collective-permute-start(bf16[64,1536]{1,0:T(8,128)(2,1)S(1)} %get-tuple-element.278), channel_id=1, source_target_pairs={{0,16},{1,17},{2,18},{3,19},{4,20},{5,21},{6,22},{7,23},{8,24},{9,... | collective-permute-start | bytes 589832 | tf_op jit(solution)/shard_map/ppermute | solution.py:61
  32.7 15.1 %collective-permute-start.7 = (bf16[64,1536]{1,0:T(8,128)(2,1)S(1)}, bf16[64,1536]{1,0:T(8,128)(2,1)S(1)}, u32[]{:S(2)}, u32[]{:S(2)}) collective-permute-start(bf16[64,1536]{1,0:T(8,128)(2,1)S(1)} %get-tuple-element.278), channel_id=1, source_target_pairs={{0,24},{1,25},{2,26},{3,27},{4,28},{5,29},{6,30},{7,31},{8,16},{9,... | collective-permute-start | bytes 589832 | tf_op jit(solution)/shard_map/ppermute | solution.py:61
  47.9 15.5 %collective-permute-start.8 = (bf16[256,1664]{1,0:T(8,128)(2,1)S(1)}, bf16[256,1664]{1,0:T(8,128)(2,1)S(1)}, u32[]{:S(2)}, u32[]{:S(2)}) collective-permute-start(bf16[256,1664]{1,0:T(8,128)(2,1)S(1)} %pad_maximum_fusion.7.refs_0_), channel_id=1, source_target_pairs={{0,2},{1,3},{2,0},{3,1},{4,6},{5,7},{6,4},{7,5},{8,10},{9,11},{10,... | collective-permute-start | bytes 2555912 | tf_op jit(solution)/shard_map/ppermute | solution.py:61
  48.5 15.3 %collective-permute-start.9 = (bf16[256,1664]{1,0:T(8,128)(2,1)S(1)}, bf16[256,1664]{1,0:T(8,128)(2,1)}, u32[]{:S(2)}, u32[]{:S(2)}) collective-permute-start(bf16[256,1664]{1,0:T(8,128)(2,1)S(1)} %pad_maximum_fusion.8.refs_1_), channel_id=1, source_target_pairs={{0,4},{1,5},{2,6},{3,7},{4,0},{5,1},{6,2},{7,3},{8,12},{9,13},{10,... | collective-permute-start | bytes 2555912 | tf_op jit(solution)/shard_map/ppermute | solution.py:61
  65.3 13.2 %collective-permute-start.13 = (bf16[128,1536]{1,0:T(8,128)(2,1)}, bf16[128,1536]{1,0:T(8,128)(2,1)S(1)}, u32[]{:S(2)}, u32[]{:S(2)}) collective-permute-start(bf16[128,1536]{1,0:T(8,128)(2,1)} %pad_maximum_fusion.20), channel_id=1, source_target_pairs={{0,4},{1,5},{2,6},{3,7},{4,0},{5,1},{6,2},{7,3},{8,12},{9,13},{10,... | collective-permute-start | bytes 1179656 | tf_op jit(solution)/shard_map/ppermute | solution.py:61
  78.7 19.4 %collective-permute-start.19 = (bf16[1,512,512]{2,1,0:T(8,128)(2,1)S(1)}, bf16[1,512,512]{2,1,0:T(8,128)(2,1)S(1)}, u32[]{:S(2)}, u32[]{:S(2)}) collective-permute-start(bf16[1,512,512]{2,1,0:T(8,128)(2,1)S(1)} %pad_maximum_fusion.14), channel_id=1, source_target_pairs={{0,2},{1,3},{2,0},{3,1},{4,6},{5,7},{6,4},{7,5},{8,10},{9,11},{10,... | collective-permute-start | bytes 1572872 | tf_op jit(solution)/shard_map/ppermute | solution.py:61
  80.2 12.8 %collective-permute-start.20 = (bf16[128,1024]{1,0:T(8,128)(2,1)S(1)}, bf16[128,1024]{1,0:T(8,128)(2,1)S(1)}, u32[]{:S(2)}, u32[]{:S(2)}) collective-permute-start(bf16[128,1024]{1,0:T(8,128)(2,1)S(1)} %pad_maximum_fusion.24), channel_id=1, source_target_pairs={{0,4},{1,5},{2,6},{3,7},{4,0},{5,1},{6,2},{7,3},{8,12},{9,13},{10,... | collective-permute-start | bytes 786440 | tf_op jit(solution)/shard_map/ppermute | solution.py:61
  81.7 16.4 %collective-permute-start.21 = (bf16[128,1024]{1,0:T(8,128)(2,1)S(1)}, bf16[128,1024]{1,0:T(8,128)(2,1)S(1)}, u32[]{:S(2)}, u32[]{:S(2)}) collective-permute-start(bf16[128,1024]{1,0:T(8,128)(2,1)S(1)} %pad_maximum_fusion.25), channel_id=1, source_target_pairs={{0,2},{1,3},{2,0},{3,1},{4,6},{5,7},{6,4},{7,5},{8,10},{9,11},{10,... | collective-permute-start | bytes 786440 | tf_op jit(solution)/shard_map/ppermute | solution.py:61
  98.5 32.4 %collective-permute-start.25 = (bf16[256,1536]{1,0:T(8,128)(2,1)S(1)}, bf16[256,1536]{1,0:T(8,128)(2,1)S(1)}, u32[]{:S(2)}, u32[]{:S(2)}) collective-permute-start(bf16[256,1536]{1,0:T(8,128)(2,1)S(1)} %pad_maximum_fusion.9), channel_id=1, source_target_pairs={{0,2},{1,3},{2,0},{3,1},{4,6},{5,7},{6,4},{7,5},{8,10},{9,11},{10,... | collective-permute-start | bytes 2359304 | tf_op jit(solution)/shard_map/ppermute | solution.py:61
  100.1 30.9 %collective-permute-start.26 = (bf16[256,1536]{1,0:T(8,128)(2,1)S(1)}, bf16[256,1536]{1,0:T(8,128)(2,1)S(1)}, u32[]{:S(2)}, u32[]{:S(2)}) collective-permute-start(bf16[256,1536]{1,0:T(8,128)(2,1)S(1)} %pad_maximum_fusion.10), channel_id=1, source_target_pairs={{0,4},{1,5},{2,6},{3,7},{4,0},{5,1},{6,2},{7,3},{8,12},{9,13},{10,... | collective-permute-start | bytes 2359304 | tf_op jit(solution)/shard_map/ppermute | solution.py:61
  100.6 29.1 %collective-permute-start.23 = (bf16[256,1024]{1,0:T(8,128)(2,1)S(1)}, bf16[256,1024]{1,0:T(8,128)(2,1)S(1)}, u32[]{:S(2)}, u32[]{:S(2)}) collective-permute-start(bf16[256,1024]{1,0:T(8,128)(2,1)S(1)} %pad_maximum_fusion.15), channel_id=1, source_target_pairs={{0,2},{1,3},{2,0},{3,1},{4,6},{5,7},{6,4},{7,5},{8,10},{9,11},{10,... | collective-permute-start | bytes 1572872 | tf_op jit(solution)/shard_map/ppermute | solution.py:61
  101.1 29.8 %collective-permute-start.24 = (bf16[256,1024]{1,0:T(8,128)(2,1)S(1)}, bf16[256,1024]{1,0:T(8,128)(2,1)S(1)}, u32[]{:S(2)}, u32[]{:S(2)}) collective-permute-start(bf16[256,1024]{1,0:T(8,128)(2,1)S(1)} %pad_maximum_fusion.16), channel_id=1, source_target_pairs={{0,4},{1,5},{2,6},{3,7},{4,0},{5,1},{6,2},{7,3},{8,12},{9,13},{10,... | collective-permute-start | bytes 1572872 | tf_op jit(solution)/shard_map/ppermute | solution.py:61
  103.3 24.6 %collective-permute-start.27 = (bf16[128,1536]{1,0:T(8,128)(2,1)S(1)}, bf16[128,1536]{1,0:T(8,128)(2,1)S(1)}, u32[]{:S(2)}, u32[]{:S(2)}) collective-permute-start(bf16[128,1536]{1,0:T(8,128)(2,1)S(1)} %pad_maximum_fusion.22), channel_id=1, source_target_pairs={{0,16},{1,17},{2,18},{3,19},{4,20},{5,21},{6,22},{7,23},{8,24},{9,... | collective-permute-start | bytes 1179656 | tf_op jit(solution)/shard_map/ppermute | solution.py:61
  131.5 21.1 %collective-permute-start.29 = (bf16[1024,1536]{1,0:T(8,128)(2,1)S(1)}, bf16[1024,1536]{1,0:T(8,128)(2,1)S(1)}, u32[]{:S(2)}, u32[]{:S(2)}) collective-permute-start(bf16[1024,1536]{1,0:T(8,128)(2,1)S(1)} %pad_maximum_fusion.refs_0_), channel_id=1, source_target_pairs={{0,1},{1,0},{2,3},{3,2},{4,5},{5,4},{6,7},{7,6},{8,9},{9,8},{10,11... | collective-permute-start | bytes 9437192 | tf_op jit(solution)/shard_map/ppermute | solution.py:61
  132.7 20.0 %collective-permute-start.30 = (bf16[128,1536]{1,0:T(8,128)(2,1)S(1)}, bf16[128,1536]{1,0:T(8,128)(2,1)S(1)}, u32[]{:S(2)}, u32[]{:S(2)}) collective-permute-start(bf16[128,1536]{1,0:T(8,128)(2,1)S(1)} %pad_maximum_fusion.22), channel_id=1, source_target_pairs={{0,4},{1,5},{2,6},{3,7},{4,0},{5,1},{6,2},{7,3},{8,12},{9,13},{10,... | collective-permute-start | bytes 1179656 | tf_op jit(solution)/shard_map/ppermute | solution.py:61
  133.3 19.4 %collective-permute-start.31 = (bf16[128,1536]{1,0:T(8,128)(2,1)S(1)}, bf16[128,1536]{1,0:T(8,128)(2,1)S(1)}, u32[]{:S(2)}, u32[]{:S(2)}) collective-permute-start(bf16[128,1536]{1,0:T(8,128)(2,1)S(1)} %collective-permute-done.27), channel_id=1, source_target_pairs={{0,2},{1,3},{2,0},{3,1},{4,6},{5,7},{6,4},{7,5},{8,10},{9,11},{10,... | collective-permute-start | bytes 1179656 | tf_op jit(solution)/shard_map/ppermute | solution.py:61
  152.8 20.6 %collective-permute-start.33 = (bf16[256,1536]{1,0:T(8,128)(2,1)S(1)}, bf16[256,1536]{1,0:T(8,128)(2,1)S(1)}, u32[]{:S(2)}, u32[]{:S(2)}) collective-permute-start(bf16[256,1536]{1,0:T(8,128)(2,1)S(1)} %pad_maximum_fusion.11), channel_id=1, source_target_pairs={{0,2},{1,3},{2,0},{3,1},{4,6},{5,7},{6,4},{7,5},{8,10},{9,11},{10,... | collective-permute-start | bytes 2359304 | tf_op jit(solution)/shard_map/ppermute | solution.py:61
  155.3 19.5 %collective-permute-start.34 = (bf16[256,1536]{1,0:T(8,128)(2,1)S(1)}, bf16[256,1536]{1,0:T(8,128)(2,1)S(1)}, u32[]{:S(2)}, u32[]{:S(2)}) collective-permute-start(bf16[256,1536]{1,0:T(8,128)(2,1)S(1)} %pad_maximum_fusion.12), channel_id=1, source_target_pairs={{0,4},{1,5},{2,6},{3,7},{4,0},{5,1},{6,2},{7,3},{8,12},{9,13},{10,... | collective-permute-start | bytes 2359304 | tf_op jit(solution)/shard_map/ppermute | solution.py:61
  180.8 16.7 %collective-permute-start.36 = (bf16[1024,1536]{1,0:T(8,128)(2,1)S(1)}, bf16[1024,1536]{1,0:T(8,128)(2,1)}, u32[]{:S(2)}, u32[]{:S(2)}) collective-permute-start(bf16[1024,1536]{1,0:T(8,128)(2,1)S(1)} %get-tuple-element.368), channel_id=1, source_target_pairs={{0,1},{1,0},{2,3},{3,2},{4,5},{5,4},{6,7},{7,6},{8,9},{9,8},{10,11... | collective-permute-start | bytes 9437192 | tf_op jit(solution)/shard_map/ppermute | solution.py:61
  201.5 21.0 %collective-permute-start.37 = (bf16[256,1536]{1,0:T(8,128)(2,1)}, bf16[256,1536]{1,0:T(8,128)(2,1)}, u32[]{:S(2)}, u32[]{:S(2)}) collective-permute-start(bf16[256,1536]{1,0:T(8,128)(2,1)} %get-tuple-element.377), channel_id=1, source_target_pairs={{0,2},{1,3},{2,0},{3,1},{4,6},{5,7},{6,4},{7,5},{8,10},{9,11},{10,... | collective-permute-start | bytes 2359304 | tf_op jit(solution)/shard_map/ppermute | solution.py:61
  201.9 20.7 %collective-permute-start.38 = (bf16[256,1536]{1,0:T(8,128)(2,1)}, bf16[256,1536]{1,0:T(8,128)(2,1)}, u32[]{:S(2)}, u32[]{:S(2)}) collective-permute-start(bf16[256,1536]{1,0:T(8,128)(2,1)} %get-tuple-element.378), channel_id=1, source_target_pairs={{0,4},{1,5},{2,6},{3,7},{4,0},{5,1},{6,2},{7,3},{8,12},{9,13},{10,... | collective-permute-start | bytes 2359304 | tf_op jit(solution)/shard_map/ppermute | solution.py:61
  226.9 19.1 %collective-permute-start.41 = (bf16[1024,1536]{1,0:T(8,128)(2,1)}, bf16[1024,1536]{1,0:T(8,128)(2,1)}, u32[]{:S(2)}, u32[]{:S(2)}) collective-permute-start(bf16[1024,1536]{1,0:T(8,128)(2,1)} %get-tuple-element.390), channel_id=1, source_target_pairs={{0,1},{1,0},{2,3},{3,2},{4,5},{5,4},{6,7},{7,6},{8,9},{9,8},{10,11... | collective-permute-start | bytes 9437192 | tf_op jit(solution)/shard_map/ppermute | solution.py:61
  227.0 19.0 %collective-permute-start.39 = (bf16[128,1536]{1,0:T(8,128)(2,1)}, bf16[128,1536]{1,0:T(8,128)(2,1)S(1)}, u32[]{:S(2)}, u32[]{:S(2)}) collective-permute-start(bf16[128,1536]{1,0:T(8,128)(2,1)} %slice.651), channel_id=1, source_target_pairs={{0,4},{1,5},{2,6},{3,7},{4,0},{5,1},{6,2},{7,3},{8,12},{9,13},{10,... | collective-permute-start | bytes 1179656 | tf_op jit(solution)/shard_map/ppermute | solution.py:61
  228.5 17.5 %collective-permute-start.40 = (bf16[128,1536]{1,0:T(8,128)(2,1)}, bf16[128,1536]{1,0:T(8,128)(2,1)S(1)}, u32[]{:S(2)}, u32[]{:S(2)}) collective-permute-start(bf16[128,1536]{1,0:T(8,128)(2,1)} %slice.650), channel_id=1, source_target_pairs={{0,2},{1,3},{2,0},{3,1},{4,6},{5,7},{6,4},{7,5},{8,10},{9,11},{10,... | collective-permute-start | bytes 1179656 | tf_op jit(solution)/shard_map/ppermute | solution.py:61
  250.1 22.5 %collective-permute-start.45 = (bf16[256,1536]{1,0:T(8,128)(2,1)S(1)}, bf16[256,1536]{1,0:T(8,128)(2,1)S(1)}, u32[]{:S(2)}, u32[]{:S(2)}) collective-permute-start(bf16[256,1536]{1,0:T(8,128)(2,1)S(1)} %get-tuple-element.407), channel_id=1, source_target_pairs={{0,2},{1,3},{2,0},{3,1},{4,6},{5,7},{6,4},{7,5},{8,10},{9,11},{10,... | collective-permute-start | bytes 2359304 | tf_op jit(solution)/shard_map/ppermute | solution.py:61
  256.1 18.9 %collective-permute-start.46 = (bf16[256,1536]{1,0:T(8,128)(2,1)S(1)}, bf16[256,1536]{1,0:T(8,128)(2,1)S(1)}, u32[]{:S(2)}, u32[]{:S(2)}) collective-permute-start(bf16[256,1536]{1,0:T(8,128)(2,1)S(1)} %get-tuple-element.408), channel_id=1, source_target_pairs={{0,4},{1,5},{2,6},{3,7},{4,0},{5,1},{6,2},{7,3},{8,12},{9,13},{10,... | collective-permute-start | bytes 2359304 | tf_op jit(solution)/shard_map/ppermute | solution.py:61
  256.6 16.0 %collective-permute-start.43 = (bf16[64,1536]{1,0:T(8,128)(2,1)S(1)}, bf16[64,1536]{1,0:T(8,128)(2,1)S(1)}, u32[]{:S(2)}, u32[]{:S(2)}) collective-permute-start(bf16[64,1536]{1,0:T(8,128)(2,1)S(1)} %get-tuple-element.405), channel_id=1, source_target_pairs={{0,16},{1,17},{2,18},{3,19},{4,20},{5,21},{6,22},{7,23},{8,24},{9,... | collective-permute-start | bytes 589832 | tf_op jit(solution)/shard_map/ppermute | solution.py:61
  257.5 15.1 %collective-permute-start.44 = (bf16[64,1536]{1,0:T(8,128)(2,1)S(1)}, bf16[64,1536]{1,0:T(8,128)(2,1)S(1)}, u32[]{:S(2)}, u32[]{:S(2)}) collective-permute-start(bf16[64,1536]{1,0:T(8,128)(2,1)S(1)} %get-tuple-element.406), channel_id=1, source_target_pairs={{0,24},{1,25},{2,26},{3,27},{4,28},{5,29},{6,30},{7,31},{8,16},{9,... | collective-permute-start | bytes 589832 | tf_op jit(solution)/shard_map/ppermute | solution.py:61
  277.1 12.9 %collective-permute-start.49 = (bf16[1024,1024]{1,0:T(8,128)(2,1)S(1)}, bf16[1024,1024]{1,0:T(8,128)(2,1)S(1)}, u32[]{:S(2)}, u32[]{:S(2)}) collective-permute-start(bf16[1024,1024]{1,0:T(8,128)(2,1)S(1)} %copy-done.33), channel_id=1, source_target_pairs={{0,1},{1,0},{2,3},{3,2},{4,5},{5,4},{6,7},{7,6},{8,9},{9,8},{10,11... | collective-permute-start | bytes 6291464 | tf_op jit(solution)/shard_map/ppermute | solution.py:61
  278.6 11.1 %collective-permute-start.47 = (bf16[128,1536]{1,0:T(8,128)(2,1)S(1)}, bf16[128,1536]{1,0:T(8,128)(2,1)S(1)}, u32[]{:S(2)}, u32[]{:S(2)}) collective-permute-start(bf16[128,1536]{1,0:T(8,128)(2,1)S(1)} %slice.649), channel_id=1, source_target_pairs={{0,4},{1,5},{2,6},{3,7},{4,0},{5,1},{6,2},{7,3},{8,12},{9,13},{10,... | collective-permute-start | bytes 1179656 | tf_op jit(solution)/shard_map/ppermute | solution.py:61
  292.3 23.7 %collective-permute-start.53 = (bf16[256,1024]{1,0:T(8,128)(2,1)S(1)}, bf16[256,1024]{1,0:T(8,128)(2,1)S(1)}, u32[]{:S(2)}, u32[]{:S(2)}) collective-permute-start(bf16[256,1024]{1,0:T(8,128)(2,1)S(1)} %get-tuple-element.434), channel_id=1, source_target_pairs={{0,2},{1,3},{2,0},{3,1},{4,6},{5,7},{6,4},{7,5},{8,10},{9,11},{10,... | collective-permute-start | bytes 1572872 | tf_op jit(solution)/shard_map/ppermute | solution.py:61
  294.9 21.1 %collective-permute-start.54 = (bf16[256,1024]{1,0:T(8,128)(2,1)S(1)}, bf16[256,1024]{1,0:T(8,128)(2,1)S(1)}, u32[]{:S(2)}, u32[]{:S(2)}) collective-permute-start(bf16[256,1024]{1,0:T(8,128)(2,1)S(1)} %get-tuple-element.435), channel_id=1, source_target_pairs={{0,4},{1,5},{2,6},{3,7},{4,0},{5,1},{6,2},{7,3},{8,12},{9,13},{10,... | collective-permute-start | bytes 1572872 | tf_op jit(solution)/shard_map/ppermute | solution.py:61
  299.0 17.0 %collective-permute-start.51 = (bf16[64,1536]{1,0:T(8,128)(2,1)S(1)}, bf16[64,1536]{1,0:T(8,128)(2,1)S(1)}, u32[]{:S(2)}, u32[]{:S(2)}) collective-permute-start(bf16[64,1536]{1,0:T(8,128)(2,1)S(1)} %get-tuple-element.432), channel_id=1, source_target_pairs={{0,16},{1,17},{2,18},{3,19},{4,20},{5,21},{6,22},{7,23},{8,24},{9,... | collective-permute-start | bytes 589832 | tf_op jit(solution)/shard_map/ppermute | solution.py:61
  299.0 17.0 %collective-permute-start.52 = (bf16[64,1536]{1,0:T(8,128)(2,1)S(1)}, bf16[64,1536]{1,0:T(8,128)(2,1)S(1)}, u32[]{:S(2)}, u32[]{:S(2)}) collective-permute-start(bf16[64,1536]{1,0:T(8,128)(2,1)S(1)} %get-tuple-element.433), channel_id=1, source_target_pairs={{0,24},{1,25},{2,26},{3,27},{4,28},{5,29},{6,30},{7,31},{8,16},{9,... | collective-permute-start | bytes 589832 | tf_op jit(solution)/shard_map/ppermute | solution.py:61
  318.7 13.1 %collective-permute-start.57 = (bf16[128,1024]{1,0:T(8,128)(2,1)S(1)}, bf16[128,1024]{1,0:T(8,128)(2,1)S(1)}, u32[]{:S(2)}, u32[]{:S(2)}) collective-permute-start(bf16[128,1024]{1,0:T(8,128)(2,1)S(1)} %slice.655), channel_id=1, source_target_pairs={{0,4},{1,5},{2,6},{3,7},{4,0},{5,1},{6,2},{7,3},{8,12},{9,13},{10,... | collective-permute-start | bytes 786440 | tf_op jit(solution)/shard_map/ppermute | solution.py:61
  320.2 11.5 %collective-permute-start.58 = (bf16[128,1024]{1,0:T(8,128)(2,1)S(1)}, bf16[128,1024]{1,0:T(8,128)(2,1)S(1)}, u32[]{:S(2)}, u32[]{:S(2)}) collective-permute-start(bf16[128,1024]{1,0:T(8,128)(2,1)S(1)} %slice.654), channel_id=1, source_target_pairs={{0,2},{1,3},{2,0},{3,1},{4,6},{5,7},{6,4},{7,5},{8,10},{9,11},{10,... | collective-permute-start | bytes 786440 | tf_op jit(solution)/shard_map/ppermute | solution.py:61
  322.1 11.8 %collective-permute-start.56 = (bf16[1,1,1,256,512]{4,3,2,1,0:T(8,128)(2,1)S(1)}, bf16[1,1,1,256,512]{4,3,2,1,0:T(8,128)(2,1)S(1)}, u32[]{:S(2)}, u32[]{:S(2)}) collective-permute-start(bf16[1,1,1,256,512]{4,3,2,1,0:T(8,128)(2,1)S(1)} %get-tuple-element.451), channel_id=1, source_target_pairs={{0,2},{1,3},{2,0},{3,1},{4,6},{5,7},{6,4},{7,5},{8,10},{9,11},{10,... | collective-permute-start | bytes 786440 | tf_op jit(solution)/shard_map/ppermute | solution.py:61
  334.7 20.4 %collective-permute-start.60 = (bf16[1024,1024]{1,0:T(8,128)(2,1)}, bf16[1024,1024]{1,0:T(8,128)(2,1)}, u32[]{:S(2)}, u32[]{:S(2)}) collective-permute-start(bf16[1024,1024]{1,0:T(8,128)(2,1)} %get-tuple-element.459), channel_id=1, source_target_pairs={{0,1},{1,0},{2,3},{3,2},{4,5},{5,4},{6,7},{7,6},{8,9},{9,8},{10,11... | collective-permute-start | bytes 6291464 | tf_op jit(solution)/shard_map/ppermute | solution.py:61
  338.4 11.2 %collective-permute-start.59 = (bf16[1,1,1,256,512]{4,3,2,1,0:T(8,128)(2,1)}, bf16[1,1,1,256,512]{4,3,2,1,0:T(8,128)(2,1)S(1)}, u32[]{:S(2)}, u32[]{:S(2)}) collective-permute-start(bf16[1,1,1,256,512]{4,3,2,1,0:T(8,128)(2,1)} %get-tuple-element.458), channel_id=1, source_target_pairs={{0,2},{1,3},{2,0},{3,1},{4,6},{5,7},{6,4},{7,5},{8,10},{9,11},{10,... | collective-permute-start | bytes 786440 | tf_op jit(solution)/shard_map/ppermute | solution.py:61
  339.3 15.8 %collective-permute-start.61 = (bf16[128,1024]{1,0:T(8,128)(2,1)S(1)}, bf16[128,1024]{1,0:T(8,128)(2,1)S(1)}, u32[]{:S(2)}, u32[]{:S(2)}) collective-permute-start(bf16[128,1024]{1,0:T(8,128)(2,1)S(1)} %copy-done.73), channel_id=1, source_target_pairs={{0,16},{1,17},{2,18},{3,19},{4,20},{5,21},{6,22},{7,23},{8,24},{9,... | collective-permute-start | bytes 786440 | tf_op jit(solution)/shard_map/ppermute | solution.py:61
  359.6 13.7 %collective-permute-start.62 = (bf16[256,1024]{1,0:T(8,128)(2,1)}, bf16[256,1024]{1,0:T(8,128)(2,1)S(1)}, u32[]{:S(2)}, u32[]{:S(2)}) collective-permute-start(bf16[256,1024]{1,0:T(8,128)(2,1)} %get-tuple-element.473), channel_id=1, source_target_pairs={{0,2},{1,3},{2,0},{3,1},{4,6},{5,7},{6,4},{7,5},{8,10},{9,11},{10,... | collective-permute-start | bytes 1572872 | tf_op jit(solution)/shard_map/ppermute | solution.py:61
  361.2 13.4 %collective-permute-start.63 = (bf16[256,1024]{1,0:T(8,128)(2,1)}, bf16[256,1024]{1,0:T(8,128)(2,1)S(1)}, u32[]{:S(2)}, u32[]{:S(2)}) collective-permute-start(bf16[256,1024]{1,0:T(8,128)(2,1)} %get-tuple-element.474), channel_id=1, source_target_pairs={{0,4},{1,5},{2,6},{3,7},{4,0},{5,1},{6,2},{7,3},{8,12},{9,13},{10,... | collective-permute-start | bytes 1572872 | tf_op jit(solution)/shard_map/ppermute | solution.py:61
  387.7 13.4 %collective-permute-start.71 = (bf16[64,1024]{1,0:T(8,128)(2,1)S(1)}, bf16[64,1024]{1,0:T(8,128)(2,1)S(1)}, u32[]{:S(2)}, u32[]{:S(2)}) collective-permute-start(bf16[64,1024]{1,0:T(8,128)(2,1)S(1)} %get-tuple-element.497), channel_id=1, source_target_pairs={{0,16},{1,17},{2,18},{3,19},{4,20},{5,21},{6,22},{7,23},{8,24},{9,... | collective-permute-start | bytes 393224 | tf_op jit(solution)/shard_map/ppermute | solution.py:61
  (131 other events, 869.3 us)

commit v8 on v7

--- a/solution.py
+++ b/solution.py
@@ -258,7 +258,7 @@
         if stage:
             self.values = self.values + self.incoming[0]
         if stage < 5:
-            self.outgoing, self.masks = (self.values,), ((1,), (2,), (4,), (8,), (16,))[stage]
+            self.outgoing, self.masks = (self.values,), ((16,), (8,), (4,), (2,), (1,))[stage]
 
     def launch(self):
         if self.staged:
@@ -350,6 +350,8 @@
 
 def over_pieces(info_ref, pieces, length, row, tile, before=None, after=None):
     start, valid = info_ref[0], info_ref[1 + pieces + row]
+    everything = slice(0, length)
+    early, late = slice(0, length // 2), slice(length // 2, length)
 
     def one(piece, carry):
         base = info_ref[1 + piece]
@@ -357,8 +359,17 @@
             before()
         used = (base < start + length) & (base < valid)
         full = (base + length <= start) & (base + length <= valid)
-        pl.when(used & full)(lambda: tile(piece, None))
-        pl.when(used & jnp.logical_not(full))(lambda: tile(piece, (base, start, valid)))
+        own = base == start
+
+        def diagonal():
+            tile(piece, early, everything, (base, start, valid))
+            tile(piece, late, late, (base + length // 2, start + length // 2, valid))
+
+        pl.when(used & full)(lambda: tile(piece, everything, everything, None))
+        pl.when(used & own)(diagonal)
+        pl.when(used & jnp.logical_not(full | own))(
+            lambda: tile(piece, everything, everything, (base, start, valid))
+        )
         if after is not None:
             after(piece)
         return carry
@@ -375,20 +386,21 @@
         accum_ref[...] = jnp.zeros_like(accum_ref)
         part_ref[...] = jnp.zeros_like(part_ref)
 
-        def tile(piece, bounds):
-            key_t, value_t = k_ref[piece, 0], v_ref[piece, 0]
+        def tile(piece, keys, rows_of, bounds):
+            key_t, value_t = k_ref[piece, 0, :, keys], v_ref[piece, 0, :, keys]
+            key_count, row_count = keys.stop - keys.start, rows_of.stop - rows_of.start
             if bounds is not None:
-                mask = allowed(*bounds, 1, (length, length))
+                mask = allowed(*bounds, 1, (row_count, key_count))
             for head in range(GROUP):
-                exps = jnp.exp(dot(q_ref[0, head * HD : (head + 1) * HD, :], key_t, FIRST_FIRST))
+                own = slice(head * HD, (head + 1) * HD)
+                exps = jnp.exp(dot(q_ref[0, own, rows_of], key_t, FIRST_FIRST))
                 if bounds is not None:
                     exps = jnp.where(mask, exps, 0.0)
-                width = min(128, length)
-                part = exps[:, :width]
-                for at in range(width, length, width):
-                    part = part + exps[:, at : at + width]
-                part_ref[head] += part
-                accum_ref[head] += dot(exps.astype(LOW), value_t, LAST_LAST)
+                part = exps[:, :128]
+                for at in range(128, key_count, 128):
+                    part = part + exps[:, at : at + 128]
+                part_ref[head, rows_of] += part
+                accum_ref[head, rows_of] += dot(exps.astype(LOW), value_t, LAST_LAST)
 
         over_pieces(info_ref, pieces, length, pl.program_id(0), tile)
         for head in range(GROUP):
@@ -421,7 +433,7 @@
             out_specs=[o_spec, o_spec, s_spec],
             scratch_shapes=[
                 pltpu.VMEM((GROUP, length, HD), jnp.float32),
-                pltpu.VMEM((GROUP, length, min(128, length)), jnp.float32),
+                pltpu.VMEM((GROUP, length, 128), jnp.float32),
             ],
         ),
         compiler_params=pltpu.CompilerParams(vmem_limit_bytes=16 << 20),
@@ -472,20 +484,21 @@
             grad_rows[head] = scaled.T.astype(LOW)
             q_rows[head] = q_ref[0, own, :].T
 
-        def tile(piece, bounds):
-            key_t, value_t = k_ref[piece, 0], v_ref[piece, 0]
+        def tile(piece, keys, queries_of, bounds):
+            key_t, value_t = k_ref[piece, 0, :, keys], v_ref[piece, 0, :, keys]
+            key_count, query_count = keys.stop - keys.start, queries_of.stop - queries_of.start
             if bounds is not None:
-                mask = allowed(*bounds, 0, (length, length))
+                mask = allowed(*bounds, 0, (key_count, query_count))
             for head in range(GROUP):
                 own = slice(head * HD, (head + 1) * HD)
-                exps = jnp.exp(dot(key_t, q_ref[0, own, :], FIRST_FIRST))
+                exps = jnp.exp(dot(key_t, q_ref[0, own, queries_of], FIRST_FIRST))
                 if bounds is not None:
                     exps = jnp.where(mask, exps, 0.0)
-                grad_exps = dot(value_t, grad_low[own, :], FIRST_FIRST) + grad_sums[head]
-                grad_scores = (exps * grad_exps).astype(LOW)
-                v_accum[...] += dot(exps.astype(LOW), grad_rows[head], LAST_FIRST)
-                k_accum[...] += dot(grad_scores, q_rows[head], LAST_FIRST)
-                q_accum[own, :] += dot(key_t, grad_scores, LAST_FIRST)
+                grad_exps = dot(value_t, grad_low[own, queries_of], FIRST_FIRST)
+                grad_scores = (exps * (grad_exps + grad_sums[head, :, queries_of])).astype(LOW)
+                v_accum[keys] += dot(exps.astype(LOW), grad_rows[head, queries_of], LAST_FIRST)
+                k_accum[keys] += dot(grad_scores, q_rows[head, queries_of], LAST_FIRST)
+                q_accum[own, queries_of] += dot(key_t, grad_scores, LAST_FIRST)
 
         def before():
             k_accum[...] = jnp.zeros_like(k_accum)
@@ -635,8 +648,9 @@
     q_gain_h = q_gain[None, None, :, None]
     k_gain_h = k_gain[None, None, :, None]
 
-    gain_columns = jnp.concatenate(
-        [attn_gain[:, None], ffn_gain[:, None], jnp.zeros((part_len, 126), jnp.float32)], axis=1
+    column = jnp.arange(128)[None, :]
+    gain_columns = jnp.where(
+        column == 0, attn_gain[:, None], jnp.where(column == 1, ffn_gain[:, None], 0.0)
     ).astype(LOW)
     w_qkv_low, w_gate_low, w_up_low = w_qkv.astype(LOW), w_gate.astype(LOW), w_up.astype(LOW)
     gather_a = Gather([w_qkv_low[:, :q_width], w_qkv_low[:, q_width:], gain_columns], me, devices, True)
@@ -771,14 +785,12 @@
     (grad_att,) = open_slot([red_one, red_two], grad_att)
     carried = more(1, grad_att, carried)
     carried, grad_att = close_slot([red_one, red_two], carried, grad_att)
-    red_one.prepare()
     (grad_att,) = open_slot([red_two, red_out], grad_att, ready=[red_out])
     carried = more(2, grad_att, carried)
     carried, grad_att = close_slot([red_two, red_out], carried, grad_att)
     (grad_att,) = open_slot([red_two, red_out], grad_att)
     carried = more(3, grad_att, carried)
     grad_q_low, grad_pieces = close_slot([red_two, red_out], carried)[0]
-    red_two.prepare()
     kv_back = PiecesBack(grad_pieces, devices, shards)
     (grad_q_low,) = open_slot([kv_back, red_out], grad_q_low)
     (grad_q_low,) = close_slot([kv_back], grad_q_low)
@@ -789,25 +801,26 @@
     red_q.outgoing, grad_q_low = close_slot([kv_back, red_out], red_q.outgoing, grad_q_low)
     (grad_q_low,) = open_slot([kv_back, red_q, red_out], grad_q_low, ready=[red_q])
     grad_normed_q = jnp.einsum("ret,de->rtd", grad_q_low, wq, preferred_element_type=jnp.float32)
-    (grad_normed_q,) = close_slot([kv_back, red_q, red_out], grad_normed_q)
+    (grad_normed_q,) = close_slot([kv_back, red_q], grad_normed_q)
     kv_back.prepare()
     grad_kv_low, k_gain_part = finish_keys(*kv_back.shares, k_raw_flat, k_gain_c, cos_t, sin_t)
     shared = Sum(
         jnp.concatenate([jnp.sum(sum(gain_parts), axis=(0, 2)), jnp.sum(k_gain_part, axis=(0, 2))])[None],
         devices,
     )
-    (grad_kv_low,) = open_slot([red_q, shared, red_out], grad_kv_low)
+    (grad_kv_low,) = open_slot([red_q, shared], grad_kv_low)
     grad_wkv = jnp.einsum("rtd,ret->de", normed_low, grad_kv_low, preferred_element_type=jnp.float32)
     red_kv = Reduce([grad_wkv.astype(LOW)], me, devices)
     red_kv.prepare()
     red_kv.outgoing, grad_kv_low = close_slot([red_q, red_out, shared], red_kv.outgoing, grad_kv_low)
-    red_out.prepare()
-    (grad_kv_low,) = open_slot([red_q, red_kv, shared], grad_kv_low, ready=[red_kv])
+    (grad_kv_low,) = open_slot([red_q, red_kv, shared, red_out], grad_kv_low, ready=[red_kv])
     grad_normed = grad_normed_q + jnp.einsum(
         "ret,de->rtd", grad_kv_low, wkv, preferred_element_type=jnp.float32
     )
     input_grad = grad_mid + norm_back(x_float, inverse_one, grad_normed * gain_attn)
-    (input_grad,) = close_slot([red_q, red_kv, shared], input_grad)
+    (input_grad,) = close_slot([red_q, red_kv, shared, red_out, red_one, red_two], input_grad)
+    for one in (red_out, red_one, red_two):
+        one.prepare()
     open_slot([red_q, red_kv, shared])
     close_slot([red_q, red_kv, shared])
     red_q.prepare()

time: 422 us -> 408 us (0.967)
  starting transfers between devices: 118 us -> 111 us
  Pallas kernels: 66.8 us -> 62.1 us
    ppermute x83, starting transfers between devices: 118 us -> 111 us  [swap(): lax.ppermute(values, ('dp', 'shard'), [(i, i ^ mask) for i in range(devic...]
    unnamed x193 -> x203, local copies, waits for them, and re-layouts: 18.2 us -> 18.7 us
  transfers between devices with their start and end apart: 83 -> 83, of which waited for: 30 -> 31; matrix products, arithmetic and copies ran while one was open for 20% -> 19% of each run, Pallas kernels for 16% -> 15%
where the time goes in v8:
time: 408 us; the launch traced here: 404 us
  starting transfers between devices  111 us (27%)
  waiting for transfers between devices  106 us (26%)
  Pallas kernels  62.1 us (15%)
  matrix products  51.8 us (13%)
  other arithmetic  45.8 us (11%)
  local copies, waits for them, and re-layouts  23.2 us (6%)
    ppermute x83, starting transfers between devices, swap(): lax.ppermute(values, ('dp', 'shard'), [(i, i ^ mask) for i in range(devic...  111 us
    ppermute x83, waiting for transfers between devices, swap(): lax.ppermute(values, ('dp', 'shard'), [(i, i ^ mask) for i in range(devic...  106 us
    pallas_call x4, Pallas kernels, attention_back(): pl.pallas_call(kernel, out_shape=[jax.ShapeDtypeStruct(queries.shape, LOW...  19.3 us
    pallas_call x5, Pallas kernels, pick(): pl.pallas_call(kernel, out_shape=[jax.ShapeDtypeStruct((len(own) * size,...  19 us
    unnamed x203, local copies, waits for them, and re-layouts  18.7 us
    pallas_call x4, Pallas kernels, place(): pl.pallas_call(kernel, out_shape=[jax.ShapeDtypeStruct((total_rows, width...  14.2 us
    pallas_call x1, Pallas kernels, attention(): pl.pallas_call(kernel, out_shape=[jax.ShapeDtypeStruct((rows, groups * gr...  8.91 us
    convert_element_type x5, other arithmetic, prepare(): self.outgoing = (self.both(0, 4).astype(LOW), self.both(4, 8).astype(LOW))  8.19 us
  transfers between devices with their start and end apart: 83, of which 31 were waited for; matrix products, arithmetic and copies ran while one was open for 19% of the time, Pallas kernels for 15%

profile of v8, /device:TPU:0, one launch (start us, length us, event | category | flops | bytes accessed | tf_op | source)
XLA Modules:
  0.0 404.2 jit_solution(9340942433160011855)
XLA Ops:
  2.6 3.1 collective-permute-start
  5.7 2.6 collective-permute-start.1
  14.8 9.2 %collective-permute-done.1 = bf16[64,1664]{1,0:T(8,128)(2,1)S(1)} collective-permute-done((bf16[64,1664]{1,0:T(8,128)(2,1)S(1)}, bf16[64,1664]{1,0:T(8,128)(2,1)S(1)}, u32[]{:S(2)}, u32[]{:S(2)}) %collective-permute-start.1) | collective-permute-done | bytes 213024 | tf_op jit(solution)/shard_map/ppermute | solution.py:61
  27.1 3.7 collective-permute-start.5
  33.3 3.4 collective-permute-done.5
  36.7 10.2 %collective-permute-done.6 = bf16[64,1536]{1,0:T(8,128)(2,1)S(1)} collective-permute-done((bf16[64,1536]{1,0:T(8,128)(2,1)S(1)}, bf16[64,1536]{1,0:T(8,128)(2,1)S(1)}, u32[]{:S(2)}, u32[]{:S(2)}) %collective-permute-start.6) | collective-permute-done | bytes 196640 | tf_op jit(solution)/shard_map/ppermute | solution.py:61
  48.2 2.7 collective-permute-start.10
  54.1 7.5 %collective-permute-done.11 = bf16[64,1024]{1,0:T(8,128)(2,1)S(1)} collective-permute-done((bf16[64,1024]{1,0:T(8,128)(2,1)S(1)}, bf16[64,1024]{1,0:T(8,128)(2,1)S(1)}, u32[]{:S(2)}, u32[]{:S(2)}) %collective-permute-start.11) | collective-permute-done | bytes 131104 | tf_op jit(solution)/shard_map/ppermute | solution.py:61
  69.1 4.1 %shard_map.221 = (bf16[2048,1024]{1,0:T(8,128)(2,1)S(1)}, bf16[2048,512]{1,0:T(8,128)(2,1)S(1)}, bf16[2048,128]{1,0:T(8,128)(2,1)S(1)}) custom-call(s32[1]{0:T(128)} %bitcast.me_ref, bf16[256,1664]{1,0:T(8,128)(2,1)S(1)} %pad_maximum_fusion.7.refs_0_, bf16[256,1664]{1,0:T(8,128)(2,1)S(1)} %pad_maximum_fusion.8.refs_1_, ...), custom_call_target="tpu_custom_call" | custom-call | bytes 65536 | tf_op jit(solution)/shard_map/pallas_call | solution.py:88
  81.4 5.7 %collective-permute-start.22 = (bf16[64,1536]{1,0:T(8,128)(2,1)S(1)}, bf16[64,1536]{1,0:T(8,128)(2,1)S(1)}, u32[]{:S(2)}, u32[]{:S(2)}) collective-permute-start(bf16[64,1536]{1,0:T(8,128)(2,1)S(1)} %copy-done.74), channel_id=1, source_target_pairs={{0,8},{1,9},{2,10},{3,11},{4,12},{5,13},{6,14},{7,15},{8,0},{9,1},... | collective-permute-start | bytes 589832 | tf_op jit(solution)/shard_map/ppermute | solution.py:61
  92.2 4.7 %collective-permute-done.21 = bf16[128,1024]{1,0:T(8,128)(2,1)S(1)} collective-permute-done((bf16[128,1024]{1,0:T(8,128)(2,1)S(1)}, bf16[128,1024]{1,0:T(8,128)(2,1)S(1)}, u32[]{:S(2)}, u32[]{:S(2)}) %collective-permute-start.21) | collective-permute-done | bytes 262176 | tf_op jit(solution)/shard_map/ppermute | solution.py:61
  102.1 7.6 %collective-permute-start.27 = (bf16[128,1536]{1,0:T(8,128)(2,1)S(1)}, bf16[128,1536]{1,0:T(8,128)(2,1)S(1)}, u32[]{:S(2)}, u32[]{:S(2)}) collective-permute-start(bf16[128,1536]{1,0:T(8,128)(2,1)S(1)} %pad_maximum_fusion.22), channel_id=1, source_target_pairs={{0,16},{1,17},{2,18},{3,19},{4,20},{5,21},{6,22},{7,23},{8,24},{9,... | collective-permute-start | bytes 1179656 | tf_op jit(solution)/shard_map/ppermute | solution.py:61
  111.2 8.9 %shard_map.222 = (f32[1,1024,512]{2,1,0:T(8,128)S(1)}, bf16[1,1024,512]{2,1,0:T(8,128)(2,1)S(1)}, f32[1,4,4,512]{3,2,1,0:T(4,128)S(1)}) custom-call(s32[6]{0:T(128)S(1)} %pad_add_fusion.info_ref, bf16[1,1024,512]{2,1,0:T(8,128)(2,1)S(1)} %bitcast.227, bf16[4,1,512,512]{3,2,1,0:T(8,128)(2,1)S(1)} %constant_dynamic-update-slice_fusion.k_ref.v_ref, ...), custom_call_target="tpu_custom_call" | custom-call | flops 16777216 | bytes 1048576 | tf_op jit(solution)/shard_map/pallas_call | solution.py:422
  121.5 5.2 %collective-permute-done.27 = bf16[128,1536]{1,0:T(8,128)(2,1)S(1)} collective-permute-done((bf16[128,1536]{1,0:T(8,128)(2,1)S(1)}, bf16[128,1536]{1,0:T(8,128)(2,1)S(1)}, u32[]{:S(2)}, u32[]{:S(2)}) %collective-permute-start.27) | collective-permute-done | bytes 393248 | tf_op jit(solution)/shard_map/ppermute | solution.py:61
  132.3 3.9 collective-permute-start.31
  136.2 5.9 %shard_map.223 = bf16[2048,1024]{1,0:T(8,128)(2,1)S(1)} custom-call(s32[1]{0:T(128)} %bitcast.me_ref, bf16[1024,1024]{1,0:T(8,128)(2,1)S(1)} %pad_maximum_fusion.3.refs_0_, bf16[1024,1024]{1,0:T(8,128)(2,1)S(1)} %collective-permute-done.32.refs_1_), custom_call_target="tpu_custom_call" | custom-call | bytes 65536 | tf_op jit(solution)/shard_map/pallas_call | solution.py:88
  142.1 2.6 multiply_reduce_fusion
  158.0 2.4 convolution_convert_fusion.3.refs_0_
  162.4 4.9 %collective-permute-done.33 = bf16[256,1536]{1,0:T(8,128)(2,1)S(1)} collective-permute-done((bf16[256,1536]{1,0:T(8,128)(2,1)S(1)}, bf16[256,1536]{1,0:T(8,128)(2,1)S(1)}, u32[]{:S(2)}, u32[]{:S(2)}) %collective-permute-start.33) | collective-permute-done | bytes 786464 | tf_op jit(solution)/shard_map/ppermute | solution.py:61
  169.1 5.6 %collective-permute-done.35.refs_1_ = bf16[1024,1536]{1,0:T(8,128)(2,1)S(1)} collective-permute-done((bf16[1024,1536]{1,0:T(8,128)(2,1)S(1)}, bf16[1024,1536]{1,0:T(8,128)(2,1)S(1)}, u32[]{:S(2)}, u32[]{:S(2)}) %collective-permute-start.35) | collective-permute-done | bytes 3145760 | tf_op jit(solution)/shard_map/ppermute | solution.py:61
  182.6 2.4 convolution_convert_fusion.2.refs_0_
  185.1 3.0 shard_map.227
  188.2 4.0 add_convert_fusion.2
  195.7 2.7 fusion.7
  198.4 2.7 fusion.8
  203.6 6.3 %shard_map.228 = (bf16[1024,1024]{1,0:T(8,128)(2,1)S(1)}, bf16[1024,1024]{1,0:T(8,128)(2,1)S(1)}) custom-call(s32[1]{0:T(128)} %bitcast.me_ref, bf16[2048,1024]{1,0:T(8,128)(2,1)S(1)} %convolution_convert_fusion.1.refs_0_), custom_call_target="tpu_custom_call" | custom-call | bytes 65536 | tf_op jit(solution)/shard_map/pallas_call | solution.py:123
  209.9 3.8 fusion.35.grad_ref
  225.9 4.8 %shard_map.229 = (bf16[1,1024,512]{2,1,0:T(8,128)(2,1)S(1)}, f32[4,1,2,256,512]{4,3,2,1,0:T(8,128)S(1)}, f32[1,64,128]{2,1,0:T(8,128)S(1)}) custom-call(s32[6]{0:T(128)S(1)} %pad_add_fusion.info_ref, bf16[1,1024,512]{2,1,0:T(8,128)(2,1)S(1)} %bitcast.228, bf16[4,1,512,512]{3,2,1,0:T(8,128)(2,1)S(1)} %constant_dynamic-update-slice_fusion.k_ref.v_ref, ...), custom_call_target="tpu_custom_call" | custom-call | flops 4194304 | bytes 1048576 | tf_op jit(solution)/shard_map/pallas_call | solution.py:531
  233.6 2.6 fusion.6
  240.4 6.0 %collective-permute-start.45 = (bf16[256,1536]{1,0:T(8,128)(2,1)S(1)}, bf16[256,1536]{1,0:T(8,128)(2,1)S(1)}, u32[]{:S(2)}, u32[]{:S(2)}) collective-permute-start(bf16[256,1536]{1,0:T(8,128)(2,1)S(1)} %get-tuple-element.413), channel_id=1, source_target_pairs={{0,2},{1,3},{2,0},{3,1},{4,6},{5,7},{6,4},{7,5},{8,10},{9,11},{10,... | collective-permute-start | bytes 2359304 | tf_op jit(solution)/shard_map/ppermute | solution.py:61
  247.1 3.2 collective-permute-start.42
  253.5 4.6 %shard_map.230 = (bf16[1,1024,512]{2,1,0:T(8,128)(2,1)S(1)}, f32[4,1,2,256,512]{4,3,2,1,0:T(8,128)S(1)}, f32[1,64,128]{2,1,0:T(8,128)S(1)}) custom-call(s32[6]{0:T(128)S(1)} %pad_add_fusion.info_ref, bf16[1,1024,512]{2,1,0:T(8,128)(2,1)S(1)} %bitcast.229, ...), custom_call_target="tpu_custom_call", output_to_operand_aliasing={{0}: (11, {}), {1}: (12, {})} | custom-call | flops 4194304 | bytes 1048576 | tf_op jit(solution)/shard_map/pallas_call | solution.py:531
  258.2 8.8 %collective-permute-done.43 = bf16[64,1536]{1,0:T(8,128)(2,1)S(1)} collective-permute-done((bf16[64,1536]{1,0:T(8,128)(2,1)S(1)}, bf16[64,1536]{1,0:T(8,128)(2,1)S(1)}, u32[]{:S(2)}, u32[]{:S(2)}) %collective-permute-start.43) | collective-permute-done | bytes 196640 | tf_op jit(solution)/shard_map/ppermute | solution.py:61
  272.8 4.8 %shard_map.231 = (bf16[1,1024,512]{2,1,0:T(8,128)(2,1)S(1)}, f32[4,1,2,256,512]{4,3,2,1,0:T(8,128)S(1)}, f32[1,64,128]{2,1,0:T(8,128)S(1)}) custom-call(s32[6]{0:T(128)S(1)} %pad_add_fusion.info_ref, bf16[1,1024,512]{2,1,0:T(8,128)(2,1)S(1)} %bitcast.230, ...), custom_call_target="tpu_custom_call", output_to_operand_aliasing={{0}: (11, {}), {1}: (12, {})} | custom-call | flops 4194304 | bytes 1048576 | tf_op jit(solution)/shard_map/pallas_call | solution.py:531
  277.6 4.1 %collective-permute-done.47 = bf16[128,1536]{1,0:T(8,128)(2,1)S(1)} collective-permute-done((bf16[128,1536]{1,0:T(8,128)(2,1)S(1)}, bf16[128,1536]{1,0:T(8,128)(2,1)S(1)}, u32[]{:S(2)}, u32[]{:S(2)}) %collective-permute-start.47) | collective-permute-done | bytes 393248 | tf_op jit(solution)/shard_map/ppermute | solution.py:61
  287.4 4.3 %collective-permute-start.50 = (bf16[64,1536]{1,0:T(8,128)(2,1)S(1)}, bf16[64,1536]{1,0:T(8,128)(2,1)S(1)}, u32[]{:S(2)}, u32[]{:S(2)}) collective-permute-start(bf16[64,1536]{1,0:T(8,128)(2,1)S(1)} %slice.657), channel_id=1, source_target_pairs={{0,8},{1,9},{2,10},{3,11},{4,12},{5,13},{6,14},{7,15},{8,0},{9,1},... | collective-permute-start | bytes 589832 | tf_op jit(solution)/shard_map/ppermute | solution.py:61
  294.1 5.0 %shard_map.232 = (bf16[1,1024,512]{2,1,0:T(8,128)(2,1)S(1)}, f32[4,1,2,256,512]{4,3,2,1,0:T(8,128)S(1)}, f32[1,64,128]{2,1,0:T(8,128)S(1)}) custom-call(s32[6]{0:T(128)S(1)} %pad_add_fusion.info_ref, bf16[1,1024,512]{2,1,0:T(8,128)(2,1)S(1)} %bitcast.231, ...), custom_call_target="tpu_custom_call", output_to_operand_aliasing={{0}: (11, {}), {1}: (12, {})} | custom-call | flops 4194304 | bytes 1048576 | tf_op jit(solution)/shard_map/pallas_call | solution.py:531
  299.4 9.4 %collective-permute-done.51 = bf16[64,1536]{1,0:T(8,128)(2,1)S(1)} collective-permute-done((bf16[64,1536]{1,0:T(8,128)(2,1)S(1)}, bf16[64,1536]{1,0:T(8,128)(2,1)S(1)}, u32[]{:S(2)}, u32[]{:S(2)}) %collective-permute-start.51) | collective-permute-done | bytes 196640 | tf_op jit(solution)/shard_map/ppermute | solution.py:61
  317.5 4.6 %shard_map.233 = (bf16[1024,1024]{1,0:T(8,128)(2,1)S(1)}, bf16[1024,1024]{1,0:T(8,128)(2,1)}) custom-call(s32[1]{0:T(128)} %bitcast.me_ref, bf16[2048,1024]{1,0:T(8,128)(2,1)S(1)} %convolution_convert_fusion.refs_0_), custom_call_target="tpu_custom_call" | custom-call | bytes 65536 | tf_op jit(solution)/shard_map/pallas_call | solution.py:123
  327.1 6.8 %convolution_bitcast_fusion = f32[1,512,2048]{2,1,0:T(8,128)} fusion(bf16[2048,1024]{1,0:T(8,128)(2,1)} %copy-done.31, bf16[1,1024,512]{2,1,0:T(8,128)(2,1)S(1)} %copy-done.11), kind=kOutput, calls=%fused_computation.29 | convolution fusion | flops 2147483648 | bytes 9437184 | tf_op jit(solution)/shard_map/ret,de->rtd/dot_general | solution.py:803
  340.6 4.2 %collective-permute-start.63 = (bf16[128,1024]{1,0:T(8,128)(2,1)S(1)}, bf16[128,1024]{1,0:T(8,128)(2,1)S(1)}, u32[]{:S(2)}, u32[]{:S(2)}) collective-permute-start(bf16[128,1024]{1,0:T(8,128)(2,1)S(1)} %copy-done.71), channel_id=1, source_target_pairs={{0,16},{1,17},{2,18},{3,19},{4,20},{5,21},{6,22},{7,23},{8,24},{9,... | collective-permute-start | bytes 786440 | tf_op jit(solution)/shard_map/ppermute | solution.py:61
  344.8 3.0 convolution_convert_fusion.4.refs_0_
  347.9 3.2 shard_map.235
  351.1 5.0 %collective-permute-done.63 = bf16[128,1024]{1,0:T(8,128)(2,1)S(1)} collective-permute-done((bf16[128,1024]{1,0:T(8,128)(2,1)S(1)}, bf16[128,1024]{1,0:T(8,128)(2,1)S(1)}, u32[]{:S(2)}, u32[]{:S(2)}) %collective-permute-start.63) | collective-permute-done | bytes 262176 | tf_op jit(solution)/shard_map/ppermute | solution.py:61
  365.7 3.1 fusion.3
  375.9 4.0 collective-permute-done.75
  382.2 4.5 %collective-permute-done.72 = bf16[64,1024]{1,0:T(8,128)(2,1)S(1)} collective-permute-done((bf16[64,1024]{1,0:T(8,128)(2,1)S(1)}, bf16[64,1024]{1,0:T(8,128)(2,1)S(1)}, u32[]{:S(2)}, u32[]{:S(2)}) %collective-permute-start.72) | collective-permute-done | bytes 131104 | tf_op jit(solution)/shard_map/ppermute | solution.py:61
  395.9 2.5 collective-permute-start.81
  (498 shorter events, 173.1 us)
Async XLA Ops:
  2.6 12.1 %collective-permute-start = (bf16[64,1664]{1,0:T(8,128)(2,1)S(1)}, bf16[64,1664]{1,0:T(8,128)(2,1)S(1)}, u32[]{:S(2)}, u32[]{:S(2)}) collective-permute-start(bf16[64,1664]{1,0:T(8,128)(2,1)S(1)} %pad_maximum_fusion.28), channel_id=1, source_target_pairs={{0,8},{1,9},{2,10},{3,11},{4,12},{5,13},{6,14},{7,15},{8,0},{9,1},... | collective-permute-start | bytes 638984 | tf_op jit(solution)/shard_map/ppermute | solution.py:61
  5.7 18.2 %collective-permute-start.1 = (bf16[64,1664]{1,0:T(8,128)(2,1)S(1)}, bf16[64,1664]{1,0:T(8,128)(2,1)S(1)}, u32[]{:S(2)}, u32[]{:S(2)}) collective-permute-start(bf16[64,1664]{1,0:T(8,128)(2,1)S(1)} %pad_maximum_fusion.28), channel_id=1, source_target_pairs={{0,16},{1,17},{2,18},{3,19},{4,20},{5,21},{6,22},{7,23},{8,24},{9,... | collective-permute-start | bytes 638984 | tf_op jit(solution)/shard_map/ppermute | solution.py:61
  8.3 15.6 %collective-permute-start.2 = (bf16[64,1664]{1,0:T(8,128)(2,1)S(1)}, bf16[64,1664]{1,0:T(8,128)(2,1)S(1)}, u32[]{:S(2)}, u32[]{:S(2)}) collective-permute-start(bf16[64,1664]{1,0:T(8,128)(2,1)S(1)} %pad_maximum_fusion.28), channel_id=1, source_target_pairs={{0,24},{1,25},{2,26},{3,27},{4,28},{5,29},{6,30},{7,31},{8,16},{9,... | collective-permute-start | bytes 638984 | tf_op jit(solution)/shard_map/ppermute | solution.py:61
  24.0 22.9 %collective-permute-start.3 = (bf16[128,1664]{1,0:T(8,128)(2,1)S(1)}, bf16[128,1664]{1,0:T(8,128)(2,1)S(1)}, u32[]{:S(2)}, u32[]{:S(2)}) collective-permute-start(bf16[128,1664]{1,0:T(8,128)(2,1)S(1)} %pad_maximum_fusion.18), channel_id=1, source_target_pairs={{0,4},{1,5},{2,6},{3,7},{4,0},{5,1},{6,2},{7,3},{8,12},{9,13},{10,... | collective-permute-start | bytes 1277960 | tf_op jit(solution)/shard_map/ppermute | solution.py:61
  25.6 21.3 %collective-permute-start.4 = (bf16[128,1664]{1,0:T(8,128)(2,1)S(1)}, bf16[128,1664]{1,0:T(8,128)(2,1)S(1)}, u32[]{:S(2)}, u32[]{:S(2)}) collective-permute-start(bf16[128,1664]{1,0:T(8,128)(2,1)S(1)} %pad_maximum_fusion.19), channel_id=1, source_target_pairs={{0,2},{1,3},{2,0},{3,1},{4,6},{5,7},{6,4},{7,5},{8,10},{9,11},{10,... | collective-permute-start | bytes 1277960 | tf_op jit(solution)/shard_map/ppermute | solution.py:61
  30.8 16.1 %collective-permute-start.6 = (bf16[64,1536]{1,0:T(8,128)(2,1)S(1)}, bf16[64,1536]{1,0:T(8,128)(2,1)S(1)}, u32[]{:S(2)}, u32[]{:S(2)}) collective-permute-start(bf16[64,1536]{1,0:T(8,128)(2,1)S(1)} %get-tuple-element.284), channel_id=1, source_target_pairs={{0,16},{1,17},{2,18},{3,19},{4,20},{5,21},{6,22},{7,23},{8,24},{9,... | collective-permute-start | bytes 589832 | tf_op jit(solution)/shard_map/ppermute | solution.py:61
  31.8 15.1 %collective-permute-start.7 = (bf16[64,1536]{1,0:T(8,128)(2,1)S(1)}, bf16[64,1536]{1,0:T(8,128)(2,1)S(1)}, u32[]{:S(2)}, u32[]{:S(2)}) collective-permute-start(bf16[64,1536]{1,0:T(8,128)(2,1)S(1)} %get-tuple-element.284), channel_id=1, source_target_pairs={{0,24},{1,25},{2,26},{3,27},{4,28},{5,29},{6,30},{7,31},{8,16},{9,... | collective-permute-start | bytes 589832 | tf_op jit(solution)/shard_map/ppermute | solution.py:61
  47.0 15.5 %collective-permute-start.8 = (bf16[256,1664]{1,0:T(8,128)(2,1)S(1)}, bf16[256,1664]{1,0:T(8,128)(2,1)S(1)}, u32[]{:S(2)}, u32[]{:S(2)}) collective-permute-start(bf16[256,1664]{1,0:T(8,128)(2,1)S(1)} %pad_maximum_fusion.7.refs_0_), channel_id=1, source_target_pairs={{0,2},{1,3},{2,0},{3,1},{4,6},{5,7},{6,4},{7,5},{8,10},{9,11},{10,... | collective-permute-start | bytes 2555912 | tf_op jit(solution)/shard_map/ppermute | solution.py:61
  47.6 15.3 %collective-permute-start.9 = (bf16[256,1664]{1,0:T(8,128)(2,1)S(1)}, bf16[256,1664]{1,0:T(8,128)(2,1)}, u32[]{:S(2)}, u32[]{:S(2)}) collective-permute-start(bf16[256,1664]{1,0:T(8,128)(2,1)S(1)} %pad_maximum_fusion.8.refs_1_), channel_id=1, source_target_pairs={{0,4},{1,5},{2,6},{3,7},{4,0},{5,1},{6,2},{7,3},{8,12},{9,13},{10,... | collective-permute-start | bytes 2555912 | tf_op jit(solution)/shard_map/ppermute | solution.py:61
  64.4 12.9 %collective-permute-start.13 = (bf16[128,1536]{1,0:T(8,128)(2,1)}, bf16[128,1536]{1,0:T(8,128)(2,1)S(1)}, u32[]{:S(2)}, u32[]{:S(2)}) collective-permute-start(bf16[128,1536]{1,0:T(8,128)(2,1)} %pad_maximum_fusion.20), channel_id=1, source_target_pairs={{0,4},{1,5},{2,6},{3,7},{4,0},{5,1},{6,2},{7,3},{8,12},{9,13},{10,... | collective-permute-start | bytes 1179656 | tf_op jit(solution)/shard_map/ppermute | solution.py:61
  77.8 19.1 %collective-permute-start.19 = (bf16[1,512,512]{2,1,0:T(8,128)(2,1)S(1)}, bf16[1,512,512]{2,1,0:T(8,128)(2,1)S(1)}, u32[]{:S(2)}, u32[]{:S(2)}) collective-permute-start(bf16[1,512,512]{2,1,0:T(8,128)(2,1)S(1)} %pad_maximum_fusion.14), channel_id=1, source_target_pairs={{0,2},{1,3},{2,0},{3,1},{4,6},{5,7},{6,4},{7,5},{8,10},{9,11},{10,... | collective-permute-start | bytes 1572872 | tf_op jit(solution)/shard_map/ppermute | solution.py:61
  79.4 12.9 %collective-permute-start.20 = (bf16[128,1024]{1,0:T(8,128)(2,1)S(1)}, bf16[128,1024]{1,0:T(8,128)(2,1)S(1)}, u32[]{:S(2)}, u32[]{:S(2)}) collective-permute-start(bf16[128,1024]{1,0:T(8,128)(2,1)S(1)} %pad_maximum_fusion.24), channel_id=1, source_target_pairs={{0,4},{1,5},{2,6},{3,7},{4,0},{5,1},{6,2},{7,3},{8,12},{9,13},{10,... | collective-permute-start | bytes 786440 | tf_op jit(solution)/shard_map/ppermute | solution.py:61
  80.9 16.1 %collective-permute-start.21 = (bf16[128,1024]{1,0:T(8,128)(2,1)S(1)}, bf16[128,1024]{1,0:T(8,128)(2,1)S(1)}, u32[]{:S(2)}, u32[]{:S(2)}) collective-permute-start(bf16[128,1024]{1,0:T(8,128)(2,1)S(1)} %pad_maximum_fusion.25), channel_id=1, source_target_pairs={{0,2},{1,3},{2,0},{3,1},{4,6},{5,7},{6,4},{7,5},{8,10},{9,11},{10,... | collective-permute-start | bytes 786440 | tf_op jit(solution)/shard_map/ppermute | solution.py:61
  97.3 32.4 %collective-permute-start.25 = (bf16[256,1536]{1,0:T(8,128)(2,1)S(1)}, bf16[256,1536]{1,0:T(8,128)(2,1)S(1)}, u32[]{:S(2)}, u32[]{:S(2)}) collective-permute-start(bf16[256,1536]{1,0:T(8,128)(2,1)S(1)} %pad_maximum_fusion.9), channel_id=1, source_target_pairs={{0,2},{1,3},{2,0},{3,1},{4,6},{5,7},{6,4},{7,5},{8,10},{9,11},{10,... | collective-permute-start | bytes 2359304 | tf_op jit(solution)/shard_map/ppermute | solution.py:61
  98.9 30.9 %collective-permute-start.26 = (bf16[256,1536]{1,0:T(8,128)(2,1)S(1)}, bf16[256,1536]{1,0:T(8,128)(2,1)S(1)}, u32[]{:S(2)}, u32[]{:S(2)}) collective-permute-start(bf16[256,1536]{1,0:T(8,128)(2,1)S(1)} %pad_maximum_fusion.10), channel_id=1, source_target_pairs={{0,4},{1,5},{2,6},{3,7},{4,0},{5,1},{6,2},{7,3},{8,12},{9,13},{10,... | collective-permute-start | bytes 2359304 | tf_op jit(solution)/shard_map/ppermute | solution.py:61
  99.6 28.9 %collective-permute-start.23 = (bf16[256,1024]{1,0:T(8,128)(2,1)S(1)}, bf16[256,1024]{1,0:T(8,128)(2,1)S(1)}, u32[]{:S(2)}, u32[]{:S(2)}) collective-permute-start(bf16[256,1024]{1,0:T(8,128)(2,1)S(1)} %pad_maximum_fusion.15), channel_id=1, source_target_pairs={{0,2},{1,3},{2,0},{3,1},{4,6},{5,7},{6,4},{7,5},{8,10},{9,11},{10,... | collective-permute-start | bytes 1572872 | tf_op jit(solution)/shard_map/ppermute | solution.py:61
  100.1 29.6 %collective-permute-start.24 = (bf16[256,1024]{1,0:T(8,128)(2,1)S(1)}, bf16[256,1024]{1,0:T(8,128)(2,1)S(1)}, u32[]{:S(2)}, u32[]{:S(2)}) collective-permute-start(bf16[256,1024]{1,0:T(8,128)(2,1)S(1)} %pad_maximum_fusion.16), channel_id=1, source_target_pairs={{0,4},{1,5},{2,6},{3,7},{4,0},{5,1},{6,2},{7,3},{8,12},{9,13},{10,... | collective-permute-start | bytes 1572872 | tf_op jit(solution)/shard_map/ppermute | solution.py:61
  102.1 24.6 %collective-permute-start.27 = (bf16[128,1536]{1,0:T(8,128)(2,1)S(1)}, bf16[128,1536]{1,0:T(8,128)(2,1)S(1)}, u32[]{:S(2)}, u32[]{:S(2)}) collective-permute-start(bf16[128,1536]{1,0:T(8,128)(2,1)S(1)} %pad_maximum_fusion.22), channel_id=1, source_target_pairs={{0,16},{1,17},{2,18},{3,19},{4,20},{5,21},{6,22},{7,23},{8,24},{9,... | collective-permute-start | bytes 1179656 | tf_op jit(solution)/shard_map/ppermute | solution.py:61
  130.4 16.4 %collective-permute-start.29 = (bf16[1024,1536]{1,0:T(8,128)(2,1)S(1)}, bf16[1024,1536]{1,0:T(8,128)(2,1)S(1)}, u32[]{:S(2)}, u32[]{:S(2)}) collective-permute-start(bf16[1024,1536]{1,0:T(8,128)(2,1)S(1)} %pad_maximum_fusion.refs_0_), channel_id=1, source_target_pairs={{0,1},{1,0},{2,3},{3,2},{4,5},{5,4},{6,7},{7,6},{8,9},{9,8},{10,11... | collective-permute-start | bytes 9437192 | tf_op jit(solution)/shard_map/ppermute | solution.py:61
  131.5 15.2 %collective-permute-start.30 = (bf16[128,1536]{1,0:T(8,128)(2,1)S(1)}, bf16[128,1536]{1,0:T(8,128)(2,1)S(1)}, u32[]{:S(2)}, u32[]{:S(2)}) collective-permute-start(bf16[128,1536]{1,0:T(8,128)(2,1)S(1)} %pad_maximum_fusion.22), channel_id=1, source_target_pairs={{0,4},{1,5},{2,6},{3,7},{4,0},{5,1},{6,2},{7,3},{8,12},{9,13},{10,... | collective-permute-start | bytes 1179656 | tf_op jit(solution)/shard_map/ppermute | solution.py:61
  132.3 14.4 %collective-permute-start.31 = (bf16[128,1536]{1,0:T(8,128)(2,1)S(1)}, bf16[128,1536]{1,0:T(8,128)(2,1)S(1)}, u32[]{:S(2)}, u32[]{:S(2)}) collective-permute-start(bf16[128,1536]{1,0:T(8,128)(2,1)S(1)} %collective-permute-done.27), channel_id=1, source_target_pairs={{0,2},{1,3},{2,0},{3,1},{4,6},{5,7},{6,4},{7,5},{8,10},{9,11},{10,... | collective-permute-start | bytes 1179656 | tf_op jit(solution)/shard_map/ppermute | solution.py:61
  146.9 20.4 %collective-permute-start.33 = (bf16[256,1536]{1,0:T(8,128)(2,1)S(1)}, bf16[256,1536]{1,0:T(8,128)(2,1)S(1)}, u32[]{:S(2)}, u32[]{:S(2)}) collective-permute-start(bf16[256,1536]{1,0:T(8,128)(2,1)S(1)} %pad_maximum_fusion.11), channel_id=1, source_target_pairs={{0,2},{1,3},{2,0},{3,1},{4,6},{5,7},{6,4},{7,5},{8,10},{9,11},{10,... | collective-permute-start | bytes 2359304 | tf_op jit(solution)/shard_map/ppermute | solution.py:61
  149.2 19.5 %collective-permute-start.34 = (bf16[256,1536]{1,0:T(8,128)(2,1)S(1)}, bf16[256,1536]{1,0:T(8,128)(2,1)S(1)}, u32[]{:S(2)}, u32[]{:S(2)}) collective-permute-start(bf16[256,1536]{1,0:T(8,128)(2,1)S(1)} %pad_maximum_fusion.12), channel_id=1, source_target_pairs={{0,4},{1,5},{2,6},{3,7},{4,0},{5,1},{6,2},{7,3},{8,12},{9,13},{10,... | collective-permute-start | bytes 2359304 | tf_op jit(solution)/shard_map/ppermute | solution.py:61
  174.7 13.5 %collective-permute-start.36 = (bf16[1024,1536]{1,0:T(8,128)(2,1)S(1)}, bf16[1024,1536]{1,0:T(8,128)(2,1)}, u32[]{:S(2)}, u32[]{:S(2)}) collective-permute-start(bf16[1024,1536]{1,0:T(8,128)(2,1)S(1)} %get-tuple-element.374), channel_id=1, source_target_pairs={{0,1},{1,0},{2,3},{3,2},{4,5},{5,4},{6,7},{7,6},{8,9},{9,8},{10,11... | collective-permute-start | bytes 9437192 | tf_op jit(solution)/shard_map/ppermute | solution.py:61
  192.2 21.5 %collective-permute-start.37 = (bf16[256,1536]{1,0:T(8,128)(2,1)}, bf16[256,1536]{1,0:T(8,128)(2,1)}, u32[]{:S(2)}, u32[]{:S(2)}) collective-permute-start(bf16[256,1536]{1,0:T(8,128)(2,1)} %get-tuple-element.383), channel_id=1, source_target_pairs={{0,2},{1,3},{2,0},{3,1},{4,6},{5,7},{6,4},{7,5},{8,10},{9,11},{10,... | collective-permute-start | bytes 2359304 | tf_op jit(solution)/shard_map/ppermute | solution.py:61
  192.6 21.1 %collective-permute-start.38 = (bf16[256,1536]{1,0:T(8,128)(2,1)}, bf16[256,1536]{1,0:T(8,128)(2,1)}, u32[]{:S(2)}, u32[]{:S(2)}) collective-permute-start(bf16[256,1536]{1,0:T(8,128)(2,1)} %get-tuple-element.384), channel_id=1, source_target_pairs={{0,4},{1,5},{2,6},{3,7},{4,0},{5,1},{6,2},{7,3},{8,12},{9,13},{10,... | collective-permute-start | bytes 2359304 | tf_op jit(solution)/shard_map/ppermute | solution.py:61
  218.0 18.2 %collective-permute-start.41 = (bf16[1024,1536]{1,0:T(8,128)(2,1)}, bf16[1024,1536]{1,0:T(8,128)(2,1)}, u32[]{:S(2)}, u32[]{:S(2)}) collective-permute-start(bf16[1024,1536]{1,0:T(8,128)(2,1)} %get-tuple-element.396), channel_id=1, source_target_pairs={{0,1},{1,0},{2,3},{3,2},{4,5},{5,4},{6,7},{7,6},{8,9},{9,8},{10,11... | collective-permute-start | bytes 9437192 | tf_op jit(solution)/shard_map/ppermute | solution.py:61
  218.1 18.1 %collective-permute-start.39 = (bf16[128,1536]{1,0:T(8,128)(2,1)}, bf16[128,1536]{1,0:T(8,128)(2,1)S(1)}, u32[]{:S(2)}, u32[]{:S(2)}) collective-permute-start(bf16[128,1536]{1,0:T(8,128)(2,1)} %slice.651), channel_id=1, source_target_pairs={{0,4},{1,5},{2,6},{3,7},{4,0},{5,1},{6,2},{7,3},{8,12},{9,13},{10,... | collective-permute-start | bytes 1179656 | tf_op jit(solution)/shard_map/ppermute | solution.py:61
  219.5 16.8 %collective-permute-start.40 = (bf16[128,1536]{1,0:T(8,128)(2,1)}, bf16[128,1536]{1,0:T(8,128)(2,1)S(1)}, u32[]{:S(2)}, u32[]{:S(2)}) collective-permute-start(bf16[128,1536]{1,0:T(8,128)(2,1)} %slice.650), channel_id=1, source_target_pairs={{0,2},{1,3},{2,0},{3,1},{4,6},{5,7},{6,4},{7,5},{8,10},{9,11},{10,... | collective-permute-start | bytes 1179656 | tf_op jit(solution)/shard_map/ppermute | solution.py:61
  240.4 26.6 %collective-permute-start.45 = (bf16[256,1536]{1,0:T(8,128)(2,1)S(1)}, bf16[256,1536]{1,0:T(8,128)(2,1)S(1)}, u32[]{:S(2)}, u32[]{:S(2)}) collective-permute-start(bf16[256,1536]{1,0:T(8,128)(2,1)S(1)} %get-tuple-element.413), channel_id=1, source_target_pairs={{0,2},{1,3},{2,0},{3,1},{4,6},{5,7},{6,4},{7,5},{8,10},{9,11},{10,... | collective-permute-start | bytes 2359304 | tf_op jit(solution)/shard_map/ppermute | solution.py:61
  246.4 20.6 %collective-permute-start.46 = (bf16[256,1536]{1,0:T(8,128)(2,1)S(1)}, bf16[256,1536]{1,0:T(8,128)(2,1)S(1)}, u32[]{:S(2)}, u32[]{:S(2)}) collective-permute-start(bf16[256,1536]{1,0:T(8,128)(2,1)S(1)} %get-tuple-element.414), channel_id=1, source_target_pairs={{0,4},{1,5},{2,6},{3,7},{4,0},{5,1},{6,2},{7,3},{8,12},{9,13},{10,... | collective-permute-start | bytes 2359304 | tf_op jit(solution)/shard_map/ppermute | solution.py:61
  250.3 16.8 %collective-permute-start.43 = (bf16[64,1536]{1,0:T(8,128)(2,1)S(1)}, bf16[64,1536]{1,0:T(8,128)(2,1)S(1)}, u32[]{:S(2)}, u32[]{:S(2)}) collective-permute-start(bf16[64,1536]{1,0:T(8,128)(2,1)S(1)} %get-tuple-element.411), channel_id=1, source_target_pairs={{0,16},{1,17},{2,18},{3,19},{4,20},{5,21},{6,22},{7,23},{8,24},{9,... | collective-permute-start | bytes 589832 | tf_op jit(solution)/shard_map/ppermute | solution.py:61
  252.1 14.9 %collective-permute-start.44 = (bf16[64,1536]{1,0:T(8,128)(2,1)S(1)}, bf16[64,1536]{1,0:T(8,128)(2,1)S(1)}, u32[]{:S(2)}, u32[]{:S(2)}) collective-permute-start(bf16[64,1536]{1,0:T(8,128)(2,1)S(1)} %get-tuple-element.412), channel_id=1, source_target_pairs={{0,24},{1,25},{2,26},{3,27},{4,28},{5,29},{6,30},{7,31},{8,16},{9,... | collective-permute-start | bytes 589832 | tf_op jit(solution)/shard_map/ppermute | solution.py:61
  269.9 13.3 %collective-permute-start.49 = (bf16[1024,1024]{1,0:T(8,128)(2,1)S(1)}, bf16[1024,1024]{1,0:T(8,128)(2,1)S(1)}, u32[]{:S(2)}, u32[]{:S(2)}) collective-permute-start(bf16[1024,1024]{1,0:T(8,128)(2,1)S(1)} %copy-done.33), channel_id=1, source_target_pairs={{0,1},{1,0},{2,3},{3,2},{4,5},{5,4},{6,7},{7,6},{8,9},{9,8},{10,11... | collective-permute-start | bytes 6291464 | tf_op jit(solution)/shard_map/ppermute | solution.py:61
  285.5 23.4 %collective-permute-start.53 = (bf16[256,1024]{1,0:T(8,128)(2,1)S(1)}, bf16[256,1024]{1,0:T(8,128)(2,1)S(1)}, u32[]{:S(2)}, u32[]{:S(2)}) collective-permute-start(bf16[256,1024]{1,0:T(8,128)(2,1)S(1)} %get-tuple-element.440), channel_id=1, source_target_pairs={{0,2},{1,3},{2,0},{3,1},{4,6},{5,7},{6,4},{7,5},{8,10},{9,11},{10,... | collective-permute-start | bytes 1572872 | tf_op jit(solution)/shard_map/ppermute | solution.py:61
  287.2 21.6 %collective-permute-start.54 = (bf16[256,1024]{1,0:T(8,128)(2,1)S(1)}, bf16[256,1024]{1,0:T(8,128)(2,1)S(1)}, u32[]{:S(2)}, u32[]{:S(2)}) collective-permute-start(bf16[256,1024]{1,0:T(8,128)(2,1)S(1)} %get-tuple-element.441), channel_id=1, source_target_pairs={{0,4},{1,5},{2,6},{3,7},{4,0},{5,1},{6,2},{7,3},{8,12},{9,13},{10,... | collective-permute-start | bytes 1572872 | tf_op jit(solution)/shard_map/ppermute | solution.py:61
  287.4 12.0 %collective-permute-start.50 = (bf16[64,1536]{1,0:T(8,128)(2,1)S(1)}, bf16[64,1536]{1,0:T(8,128)(2,1)S(1)}, u32[]{:S(2)}, u32[]{:S(2)}) collective-permute-start(bf16[64,1536]{1,0:T(8,128)(2,1)S(1)} %slice.657), channel_id=1, source_target_pairs={{0,8},{1,9},{2,10},{3,11},{4,12},{5,13},{6,14},{7,15},{8,0},{9,1},... | collective-permute-start | bytes 589832 | tf_op jit(solution)/shard_map/ppermute | solution.py:61
  291.7 17.1 %collective-permute-start.51 = (bf16[64,1536]{1,0:T(8,128)(2,1)S(1)}, bf16[64,1536]{1,0:T(8,128)(2,1)S(1)}, u32[]{:S(2)}, u32[]{:S(2)}) collective-permute-start(bf16[64,1536]{1,0:T(8,128)(2,1)S(1)} %get-tuple-element.438), channel_id=1, source_target_pairs={{0,16},{1,17},{2,18},{3,19},{4,20},{5,21},{6,22},{7,23},{8,24},{9,... | collective-permute-start | bytes 589832 | tf_op jit(solution)/shard_map/ppermute | solution.py:61
  292.7 16.2 %collective-permute-start.52 = (bf16[64,1536]{1,0:T(8,128)(2,1)S(1)}, bf16[64,1536]{1,0:T(8,128)(2,1)S(1)}, u32[]{:S(2)}, u32[]{:S(2)}) collective-permute-start(bf16[64,1536]{1,0:T(8,128)(2,1)S(1)} %get-tuple-element.439), channel_id=1, source_target_pairs={{0,24},{1,25},{2,26},{3,27},{4,28},{5,29},{6,30},{7,31},{8,16},{9,... | collective-permute-start | bytes 589832 | tf_op jit(solution)/shard_map/ppermute | solution.py:61
  310.6 12.8 %collective-permute-start.57 = (bf16[128,1024]{1,0:T(8,128)(2,1)S(1)}, bf16[128,1024]{1,0:T(8,128)(2,1)S(1)}, u32[]{:S(2)}, u32[]{:S(2)}) collective-permute-start(bf16[128,1024]{1,0:T(8,128)(2,1)S(1)} %slice.655), channel_id=1, source_target_pairs={{0,4},{1,5},{2,6},{3,7},{4,0},{5,1},{6,2},{7,3},{8,12},{9,13},{10,... | collective-permute-start | bytes 786440 | tf_op jit(solution)/shard_map/ppermute | solution.py:61
  314.1 11.6 %collective-permute-start.56 = (bf16[1,1,1,256,512]{4,3,2,1,0:T(8,128)(2,1)S(1)}, bf16[1,1,1,256,512]{4,3,2,1,0:T(8,128)(2,1)S(1)}, u32[]{:S(2)}, u32[]{:S(2)}) collective-permute-start(bf16[1,1,1,256,512]{4,3,2,1,0:T(8,128)(2,1)S(1)} %get-tuple-element.457), channel_id=1, source_target_pairs={{0,2},{1,3},{2,0},{3,1},{4,6},{5,7},{6,4},{7,5},{8,10},{9,11},{10,... | collective-permute-start | bytes 786440 | tf_op jit(solution)/shard_map/ppermute | solution.py:61
  339.0 17.1 %collective-permute-start.61 = (bf16[256,1024]{1,0:T(8,128)(2,1)S(1)}, bf16[256,1024]{1,0:T(8,128)(2,1)S(1)}, u32[]{:S(2)}, u32[]{:S(2)}) collective-permute-start(bf16[256,1024]{1,0:T(8,128)(2,1)S(1)} %get-tuple-element.476), channel_id=1, source_target_pairs={{0,2},{1,3},{2,0},{3,1},{4,6},{5,7},{6,4},{7,5},{8,10},{9,11},{10,... | collective-permute-start | bytes 1572872 | tf_op jit(solution)/shard_map/ppermute | solution.py:61
  339.4 16.7 %collective-permute-start.62 = (bf16[256,1024]{1,0:T(8,128)(2,1)S(1)}, bf16[256,1024]{1,0:T(8,128)(2,1)S(1)}, u32[]{:S(2)}, u32[]{:S(2)}) collective-permute-start(bf16[256,1024]{1,0:T(8,128)(2,1)S(1)} %get-tuple-element.477), channel_id=1, source_target_pairs={{0,4},{1,5},{2,6},{3,7},{4,0},{5,1},{6,2},{7,3},{8,12},{9,13},{10,... | collective-permute-start | bytes 1572872 | tf_op jit(solution)/shard_map/ppermute | solution.py:61
  340.6 15.5 %collective-permute-start.63 = (bf16[128,1024]{1,0:T(8,128)(2,1)S(1)}, bf16[128,1024]{1,0:T(8,128)(2,1)S(1)}, u32[]{:S(2)}, u32[]{:S(2)}) collective-permute-start(bf16[128,1024]{1,0:T(8,128)(2,1)S(1)} %copy-done.71), channel_id=1, source_target_pairs={{0,16},{1,17},{2,18},{3,19},{4,20},{5,21},{6,22},{7,23},{8,24},{9,... | collective-permute-start | bytes 786440 | tf_op jit(solution)/shard_map/ppermute | solution.py:61
  369.3 12.9 %collective-permute-start.70 = (bf16[64,1024]{1,0:T(8,128)(2,1)S(1)}, bf16[64,1024]{1,0:T(8,128)(2,1)S(1)}, u32[]{:S(2)}, u32[]{:S(2)}) collective-permute-start(bf16[64,1024]{1,0:T(8,128)(2,1)S(1)} %slice.661), channel_id=1, source_target_pairs={{0,8},{1,9},{2,10},{3,11},{4,12},{5,13},{6,14},{7,15},{8,0},{9,1},... | collective-permute-start | bytes 393224 | tf_op jit(solution)/shard_map/ppermute | solution.py:61
  370.2 12.0 %collective-permute-start.71 = (bf16[64,1024]{1,0:T(8,128)(2,1)S(1)}, bf16[64,1024]{1,0:T(8,128)(2,1)S(1)}, u32[]{:S(2)}, u32[]{:S(2)}) collective-permute-start(bf16[64,1024]{1,0:T(8,128)(2,1)S(1)} %get-tuple-element.509), channel_id=1, source_target_pairs={{0,16},{1,17},{2,18},{3,19},{4,20},{5,21},{6,22},{7,23},{8,24},{9,... | collective-permute-start | bytes 393224 | tf_op jit(solution)/shard_map/ppermute | solution.py:61
  372.1 14.6 %collective-permute-start.73 = (bf16[256,512]{1,0:T(8,128)(2,1)S(1)}, bf16[256,512]{1,0:T(8,128)(2,1)S(1)}, u32[]{:S(2)}, u32[]{:S(2)}) collective-permute-start(bf16[256,512]{1,0:T(8,128)(2,1)S(1)} %get-tuple-element.511), channel_id=1, source_target_pairs={{0,2},{1,3},{2,0},{3,1},{4,6},{5,7},{6,4},{7,5},{8,10},{9,11},{10,... | collective-permute-start | bytes 786440 | tf_op jit(solution)/shard_map/ppermute | solution.py:61
  372.5 14.2 %collective-permute-start.74 = (bf16[256,512]{1,0:T(8,128)(2,1)S(1)}, bf16[256,512]{1,0:T(8,128)(2,1)S(1)}, u32[]{:S(2)}, u32[]{:S(2)}) collective-permute-start(bf16[256,512]{1,0:T(8,128)(2,1)S(1)} %get-tuple-element.512), channel_id=1, source_target_pairs={{0,4},{1,5},{2,6},{3,7},{4,0},{5,1},{6,2},{7,3},{8,12},{9,13},{10,... | collective-permute-start | bytes 786440 | tf_op jit(solution)/shard_map/ppermute | solution.py:61
  (136 other events, 880.3 us)

commit v9 on v8

--- a/solution.py
+++ b/solution.py
@@ -255,10 +255,13 @@
             if stage == 0:
                 self.values = lax.psum(self.values, ("dp", "shard"))
             return
-        if stage:
+        if len(self.incoming) == 3:
+            one, two, three = self.incoming
+            self.values = (self.values + one) + (two + three)
+        elif stage:
             self.values = self.values + self.incoming[0]
-        if stage < 5:
-            self.outgoing, self.masks = (self.values,), ((16,), (8,), (4,), (2,), (1,))[stage]
+        if stage < 4:
+            self.outgoing, self.masks = (self.values,), ((16,), (8,), (4, 2, 6), (1,))[stage]
 
     def launch(self):
         if self.staged:
@@ -757,7 +760,7 @@
     red_out = Reduce([grad_wout.astype(LOW)], me, devices, True)
     red_out.prepare()
     grad_att, red_out.outgoing = close_slot([red_one], grad_att, red_out.outgoing)
-    grad_att, act_two = open_slot([red_one, red_two], grad_att, act_two, ready=[red_two])
+    (grad_att,) = open_slot([red_one, red_two], grad_att, ready=[red_two])
 
     q_gain_c, k_gain_c = q_gain[:, None], k_gain[:, None]
     q_raw_flat = q_raw.reshape(row_count, q_width, piece_len)
@@ -768,11 +771,6 @@
             info, q_low, pieces, o_heads, sums, grad_att, q_raw_flat, q_gain_c, cos_t, sin_t, group, carried
         )
 
-    output = (
-        x_mid
-        + jnp.einsum("rtf,df->rtd", act_one, wdown_one, preferred_element_type=jnp.float32)
-        + jnp.einsum("rtf,df->rtd", act_two, wdown_two, preferred_element_type=jnp.float32)
-    ).astype(LOW)
     gain_parts = []
 
     def more(group, grad_att, carried=()):
@@ -781,7 +779,7 @@
         return tuple(carried)
 
     carried = more(0, grad_att)
-    carried, grad_att, output = close_slot([red_one, red_two], carried, grad_att, output)
+    carried, grad_att = close_slot([red_one, red_two], carried, grad_att)
     (grad_att,) = open_slot([red_one, red_two], grad_att)
     carried = more(1, grad_att, carried)
     carried, grad_att = close_slot([red_one, red_two], carried, grad_att)
@@ -821,8 +819,13 @@
     (input_grad,) = close_slot([red_q, red_kv, shared, red_out, red_one, red_two], input_grad)
     for one in (red_out, red_one, red_two):
         one.prepare()
-    open_slot([red_q, red_kv, shared])
-    close_slot([red_q, red_kv, shared])
+    (act_one,) = open_slot([red_q, red_kv], act_one)
+    output = (
+        x_mid
+        + jnp.einsum("rtf,df->rtd", act_one, wdown_one, preferred_element_type=jnp.float32)
+        + jnp.einsum("rtf,df->rtd", act_two, wdown_two, preferred_element_type=jnp.float32)
+    ).astype(LOW)
+    (output,) = close_slot([red_q, red_kv], output)
     red_q.prepare()
     open_slot([red_kv, shared])
     close_slot([red_kv, shared])

time: 408 us -> 404 us (level)
  waiting for transfers between devices: 106 us -> 98.2 us
    ppermute x83 -> x84, waiting for transfers between devices: 106 us -> 98.2 us  [swap(): lax.ppermute(values, ('dp', 'shard'), [(i, i ^ mask) for i in range(devic...]
    ppermute x83 -> x84, starting transfers between devices: 111 us -> 115 us  [swap(): lax.ppermute(values, ('dp', 'shard'), [(i, i ^ mask) for i in range(devic...]
  transfers between devices with their start and end apart: 83 -> 84, of which waited for: 31 -> 35; matrix products, arithmetic and copies ran while one was open for 19% -> 19% of each run, Pallas kernels for 15% -> 15%
where the time goes in v9:
time: 404 us; the launch traced here: 401 us
  starting transfers between devices  115 us (28%)
  waiting for transfers between devices  98.2 us (24%)
  Pallas kernels  62.3 us (15%)
  matrix products  51.7 us (13%)
  other arithmetic  48.1 us (12%)
  local copies, waits for them, and re-layouts  21.6 us (5%)
    ppermute x84, starting transfers between devices, swap(): lax.ppermute(values, ('dp', 'shard'), [(i, i ^ mask) for i in range(devic...  115 us
    ppermute x84, waiting for transfers between devices, swap(): lax.ppermute(values, ('dp', 'shard'), [(i, i ^ mask) for i in range(devic...  98.2 us
    pallas_call x4, Pallas kernels, attention_back(): pl.pallas_call(kernel, out_shape=[jax.ShapeDtypeStruct(queries.shape, LOW...  19.3 us
    pallas_call x5, Pallas kernels, pick(): pl.pallas_call(kernel, out_shape=[jax.ShapeDtypeStruct((len(own) * size,...  19 us
    unnamed x203, local copies, waits for them, and re-layouts  17.2 us
    pallas_call x4, Pallas kernels, place(): pl.pallas_call(kernel, out_shape=[jax.ShapeDtypeStruct((total_rows, width...  14.2 us
    pallas_call x1, Pallas kernels, attention(): pl.pallas_call(kernel, out_shape=[jax.ShapeDtypeStruct((rows, groups * gr...  9.22 us
    convert_element_type x5, other arithmetic, prepare(): self.outgoing = (self.both(0, 4).astype(LOW), self.both(4, 8).astype(LOW))  8.18 us
  transfers between devices with their start and end apart: 84, of which 35 were waited for; matrix products, arithmetic and copies ran while one was open for 19% of the time, Pallas kernels for 15%

profile of v9, /device:TPU:0, one launch (start us, length us, event | category | flops | bytes accessed | tf_op | source)
XLA Modules:
  0.0 400.7 jit_solution(18090098131434259444)
XLA Ops:
  2.6 3.1 collective-permute-start
  5.7 2.6 collective-permute-start.1
  14.8 9.2 %collective-permute-done.1 = bf16[64,1664]{1,0:T(8,128)(2,1)S(1)} collective-permute-done((bf16[64,1664]{1,0:T(8,128)(2,1)S(1)}, bf16[64,1664]{1,0:T(8,128)(2,1)S(1)}, u32[]{:S(2)}, u32[]{:S(2)}) %collective-permute-start.1) | collective-permute-done | bytes 213024 | tf_op jit(solution)/shard_map/ppermute | solution.py:61
  27.1 3.7 collective-permute-start.5
  33.3 3.4 collective-permute-done.5
  36.7 10.2 %collective-permute-done.6 = bf16[64,1536]{1,0:T(8,128)(2,1)S(1)} collective-permute-done((bf16[64,1536]{1,0:T(8,128)(2,1)S(1)}, bf16[64,1536]{1,0:T(8,128)(2,1)S(1)}, u32[]{:S(2)}, u32[]{:S(2)}) %collective-permute-start.6) | collective-permute-done | bytes 196640 | tf_op jit(solution)/shard_map/ppermute | solution.py:61
  48.2 2.7 collective-permute-start.10
  54.1 7.5 %collective-permute-done.11 = bf16[64,1024]{1,0:T(8,128)(2,1)S(1)} collective-permute-done((bf16[64,1024]{1,0:T(8,128)(2,1)S(1)}, bf16[64,1024]{1,0:T(8,128)(2,1)S(1)}, u32[]{:S(2)}, u32[]{:S(2)}) %collective-permute-start.11) | collective-permute-done | bytes 131104 | tf_op jit(solution)/shard_map/ppermute | solution.py:61
  69.1 4.2 %shard_map.221 = (bf16[2048,1024]{1,0:T(8,128)(2,1)S(1)}, bf16[2048,512]{1,0:T(8,128)(2,1)S(1)}, bf16[2048,128]{1,0:T(8,128)(2,1)S(1)}) custom-call(s32[1]{0:T(128)} %bitcast.me_ref, bf16[256,1664]{1,0:T(8,128)(2,1)S(1)} %pad_maximum_fusion.7.refs_0_, bf16[256,1664]{1,0:T(8,128)(2,1)S(1)} %pad_maximum_fusion.8.refs_1_, ...), custom_call_target="tpu_custom_call" | custom-call | bytes 65536 | tf_op jit(solution)/shard_map/pallas_call | solution.py:88
  81.4 5.7 %collective-permute-start.22 = (bf16[64,1536]{1,0:T(8,128)(2,1)S(1)}, bf16[64,1536]{1,0:T(8,128)(2,1)S(1)}, u32[]{:S(2)}, u32[]{:S(2)}) collective-permute-start(bf16[64,1536]{1,0:T(8,128)(2,1)S(1)} %copy-done.74), channel_id=1, source_target_pairs={{0,8},{1,9},{2,10},{3,11},{4,12},{5,13},{6,14},{7,15},{8,0},{9,1},... | collective-permute-start | bytes 589832 | tf_op jit(solution)/shard_map/ppermute | solution.py:61
  92.2 4.9 %collective-permute-done.21 = bf16[128,1024]{1,0:T(8,128)(2,1)S(1)} collective-permute-done((bf16[128,1024]{1,0:T(8,128)(2,1)S(1)}, bf16[128,1024]{1,0:T(8,128)(2,1)S(1)}, u32[]{:S(2)}, u32[]{:S(2)}) %collective-permute-start.21) | collective-permute-done | bytes 262176 | tf_op jit(solution)/shard_map/ppermute | solution.py:61
  102.3 7.6 %collective-permute-start.27 = (bf16[128,1536]{1,0:T(8,128)(2,1)S(1)}, bf16[128,1536]{1,0:T(8,128)(2,1)S(1)}, u32[]{:S(2)}, u32[]{:S(2)}) collective-permute-start(bf16[128,1536]{1,0:T(8,128)(2,1)S(1)} %pad_maximum_fusion.22), channel_id=1, source_target_pairs={{0,16},{1,17},{2,18},{3,19},{4,20},{5,21},{6,22},{7,23},{8,24},{9,... | collective-permute-start | bytes 1179656 | tf_op jit(solution)/shard_map/ppermute | solution.py:61
  111.4 9.2 %shard_map.222 = (f32[1,1024,512]{2,1,0:T(8,128)S(1)}, bf16[1,1024,512]{2,1,0:T(8,128)(2,1)S(1)}, f32[1,4,4,512]{3,2,1,0:T(4,128)S(1)}) custom-call(s32[6]{0:T(128)S(1)} %pad_add_fusion.info_ref, bf16[1,1024,512]{2,1,0:T(8,128)(2,1)S(1)} %bitcast.227, bf16[4,1,512,512]{3,2,1,0:T(8,128)(2,1)S(1)} %constant_dynamic-update-slice_fusion.k_ref.v_ref, ...), custom_call_target="tpu_custom_call" | custom-call | flops 16777216 | bytes 1048576 | tf_op jit(solution)/shard_map/pallas_call | solution.py:425
  121.9 5.0 %collective-permute-done.27 = bf16[128,1536]{1,0:T(8,128)(2,1)S(1)} collective-permute-done((bf16[128,1536]{1,0:T(8,128)(2,1)S(1)}, bf16[128,1536]{1,0:T(8,128)(2,1)S(1)}, u32[]{:S(2)}, u32[]{:S(2)}) %collective-permute-start.27) | collective-permute-done | bytes 393248 | tf_op jit(solution)/shard_map/ppermute | solution.py:61
  132.3 6.8 %collective-permute-start.31 = (bf16[128,1536]{1,0:T(8,128)(2,1)S(1)}, bf16[128,1536]{1,0:T(8,128)(2,1)S(1)}, u32[]{:S(2)}, u32[]{:S(2)}) collective-permute-start(bf16[128,1536]{1,0:T(8,128)(2,1)S(1)} %collective-permute-done.27), channel_id=1, source_target_pairs={{0,2},{1,3},{2,0},{3,1},{4,6},{5,7},{6,4},{7,5},{8,10},{9,11},{10,... | collective-permute-start | bytes 1179656 | tf_op jit(solution)/shard_map/ppermute | solution.py:61
  139.1 5.9 %shard_map.223 = bf16[2048,1024]{1,0:T(8,128)(2,1)S(1)} custom-call(s32[1]{0:T(128)} %bitcast.me_ref, bf16[1024,1024]{1,0:T(8,128)(2,1)S(1)} %pad_maximum_fusion.3.refs_0_, bf16[1024,1024]{1,0:T(8,128)(2,1)S(1)} %collective-permute-done.32.refs_1_), custom_call_target="tpu_custom_call" | custom-call | bytes 65536 | tf_op jit(solution)/shard_map/pallas_call | solution.py:88
  145.0 2.6 multiply_reduce_fusion
  149.8 3.0 collective-permute-start.33
  160.6 2.4 convolution_convert_fusion.3.refs_0_
  165.0 5.8 %collective-permute-done.33 = bf16[256,1536]{1,0:T(8,128)(2,1)S(1)} collective-permute-done((bf16[256,1536]{1,0:T(8,128)(2,1)S(1)}, bf16[256,1536]{1,0:T(8,128)(2,1)S(1)}, u32[]{:S(2)}, u32[]{:S(2)}) %collective-permute-start.33) | collective-permute-done | bytes 786464 | tf_op jit(solution)/shard_map/ppermute | solution.py:61
  172.6 5.6 %collective-permute-done.35.refs_1_ = bf16[1024,1536]{1,0:T(8,128)(2,1)S(1)} collective-permute-done((bf16[1024,1536]{1,0:T(8,128)(2,1)S(1)}, bf16[1024,1536]{1,0:T(8,128)(2,1)S(1)}, u32[]{:S(2)}, u32[]{:S(2)}) %collective-permute-start.35) | collective-permute-done | bytes 3145760 | tf_op jit(solution)/shard_map/ppermute | solution.py:61
  186.2 2.4 convolution_convert_fusion.2.refs_0_
  188.6 3.2 shard_map.227
  192.0 4.0 add_convert_fusion.2
  199.0 2.7 fusion.7
  201.8 2.7 fusion.8
  206.9 6.1 %shard_map.228 = (bf16[1024,1024]{1,0:T(8,128)(2,1)S(1)}, bf16[1024,1024]{1,0:T(8,128)(2,1)S(1)}) custom-call(s32[1]{0:T(128)} %bitcast.me_ref, bf16[2048,1024]{1,0:T(8,128)(2,1)S(1)} %convolution_convert_fusion.1.refs_0_), custom_call_target="tpu_custom_call" | custom-call | bytes 65536 | tf_op jit(solution)/shard_map/pallas_call | solution.py:123
  213.0 3.8 fusion.35.grad_ref
  229.4 4.8 %shard_map.229 = (bf16[1,1024,512]{2,1,0:T(8,128)(2,1)S(1)}, f32[4,1,2,256,512]{4,3,2,1,0:T(8,128)S(1)}, f32[1,64,128]{2,1,0:T(8,128)S(1)}) custom-call(s32[6]{0:T(128)S(1)} %pad_add_fusion.info_ref, bf16[1,1024,512]{2,1,0:T(8,128)(2,1)S(1)} %bitcast.228, bf16[4,1,512,512]{3,2,1,0:T(8,128)(2,1)S(1)} %constant_dynamic-update-slice_fusion.k_ref.v_ref, ...), custom_call_target="tpu_custom_call" | custom-call | flops 4194304 | bytes 1048576 | tf_op jit(solution)/shard_map/pallas_call | solution.py:534
  239.8 5.8 %collective-permute-start.45 = (bf16[256,1536]{1,0:T(8,128)(2,1)S(1)}, bf16[256,1536]{1,0:T(8,128)(2,1)S(1)}, u32[]{:S(2)}, u32[]{:S(2)}) collective-permute-start(bf16[256,1536]{1,0:T(8,128)(2,1)S(1)} %get-tuple-element.409), channel_id=1, source_target_pairs={{0,2},{1,3},{2,0},{3,1},{4,6},{5,7},{6,4},{7,5},{8,10},{9,11},{10,... | collective-permute-start | bytes 2359304 | tf_op jit(solution)/shard_map/ppermute | solution.py:61
  247.8 2.5 collective-permute-start.44
  250.3 4.6 %shard_map.230 = (bf16[1,1024,512]{2,1,0:T(8,128)(2,1)S(1)}, f32[4,1,2,256,512]{4,3,2,1,0:T(8,128)S(1)}, f32[1,64,128]{2,1,0:T(8,128)S(1)}) custom-call(s32[6]{0:T(128)S(1)} %pad_add_fusion.info_ref, bf16[1,1024,512]{2,1,0:T(8,128)(2,1)S(1)} %bitcast.229, ...), custom_call_target="tpu_custom_call", output_to_operand_aliasing={{0}: (11, {}), {1}: (12, {})} | custom-call | flops 4194304 | bytes 1048576 | tf_op jit(solution)/shard_map/pallas_call | solution.py:534
  256.5 5.8 %collective-permute-done.44 = bf16[64,1536]{1,0:T(8,128)(2,1)S(1)} collective-permute-done((bf16[64,1536]{1,0:T(8,128)(2,1)S(1)}, bf16[64,1536]{1,0:T(8,128)(2,1)S(1)}, u32[]{:S(2)}, u32[]{:S(2)}) %collective-permute-start.44) | collective-permute-done | bytes 196640 | tf_op jit(solution)/shard_map/ppermute | solution.py:61
  269.3 5.0 %shard_map.231 = (bf16[1,1024,512]{2,1,0:T(8,128)(2,1)S(1)}, f32[4,1,2,256,512]{4,3,2,1,0:T(8,128)S(1)}, f32[1,64,128]{2,1,0:T(8,128)S(1)}) custom-call(s32[6]{0:T(128)S(1)} %pad_add_fusion.info_ref, bf16[1,1024,512]{2,1,0:T(8,128)(2,1)S(1)} %bitcast.230, ...), custom_call_target="tpu_custom_call", output_to_operand_aliasing={{0}: (11, {}), {1}: (12, {})} | custom-call | flops 4194304 | bytes 1048576 | tf_op jit(solution)/shard_map/pallas_call | solution.py:534
  274.3 5.0 %collective-permute-done.47 = bf16[128,1536]{1,0:T(8,128)(2,1)S(1)} collective-permute-done((bf16[128,1536]{1,0:T(8,128)(2,1)S(1)}, bf16[128,1536]{1,0:T(8,128)(2,1)S(1)}, u32[]{:S(2)}, u32[]{:S(2)}) %collective-permute-start.47) | collective-permute-done | bytes 393248 | tf_op jit(solution)/shard_map/ppermute | solution.py:61
  285.2 2.7 collective-permute-start.50
  291.0 4.8 %shard_map.232 = (bf16[1,1024,512]{2,1,0:T(8,128)(2,1)S(1)}, f32[4,1,2,256,512]{4,3,2,1,0:T(8,128)S(1)}, f32[1,64,128]{2,1,0:T(8,128)S(1)}) custom-call(s32[6]{0:T(128)S(1)} %pad_add_fusion.info_ref, bf16[1,1024,512]{2,1,0:T(8,128)(2,1)S(1)} %bitcast.231, ...), custom_call_target="tpu_custom_call", output_to_operand_aliasing={{0}: (11, {}), {1}: (12, {})} | custom-call | flops 4194304 | bytes 1048576 | tf_op jit(solution)/shard_map/pallas_call | solution.py:534
  297.3 7.1 %collective-permute-done.52 = bf16[64,1536]{1,0:T(8,128)(2,1)S(1)} collective-permute-done((bf16[64,1536]{1,0:T(8,128)(2,1)S(1)}, bf16[64,1536]{1,0:T(8,128)(2,1)S(1)}, u32[]{:S(2)}, u32[]{:S(2)}) %collective-permute-start.52) | collective-permute-done | bytes 196640 | tf_op jit(solution)/shard_map/ppermute | solution.py:61
  313.4 4.6 %shard_map.233 = (bf16[1024,1024]{1,0:T(8,128)(2,1)S(1)}, bf16[1024,1024]{1,0:T(8,128)(2,1)}) custom-call(s32[1]{0:T(128)} %bitcast.me_ref, bf16[2048,1024]{1,0:T(8,128)(2,1)S(1)} %convolution_convert_fusion.refs_0_), custom_call_target="tpu_custom_call" | custom-call | bytes 65536 | tf_op jit(solution)/shard_map/pallas_call | solution.py:123
  319.4 2.7 collective-permute-done.56
  323.6 6.7 %convolution_bitcast_fusion = f32[1,512,2048]{2,1,0:T(8,128)} fusion(bf16[2048,1024]{1,0:T(8,128)(2,1)} %copy-done.31, bf16[1,1024,512]{2,1,0:T(8,128)(2,1)S(1)} %copy-done.11), kind=kOutput, calls=%fused_computation.29 | convolution fusion | flops 2147483648 | bytes 9437184 | tf_op jit(solution)/shard_map/ret,de->rtd/dot_general | solution.py:801
  336.5 5.8 %collective-permute-start.63 = (bf16[128,1024]{1,0:T(8,128)(2,1)S(1)}, bf16[128,1024]{1,0:T(8,128)(2,1)S(1)}, u32[]{:S(2)}, u32[]{:S(2)}) collective-permute-start(bf16[128,1024]{1,0:T(8,128)(2,1)S(1)} %copy-done.71), channel_id=1, source_target_pairs={{0,16},{1,17},{2,18},{3,19},{4,20},{5,21},{6,22},{7,23},{8,24},{9,... | collective-permute-start | bytes 786440 | tf_op jit(solution)/shard_map/ppermute | solution.py:61
  342.3 3.0 convolution_convert_fusion.4.refs_0_
  345.4 3.2 shard_map.235
  348.6 5.0 %collective-permute-done.63 = bf16[128,1024]{1,0:T(8,128)(2,1)S(1)} collective-permute-done((bf16[128,1024]{1,0:T(8,128)(2,1)S(1)}, bf16[128,1024]{1,0:T(8,128)(2,1)S(1)}, u32[]{:S(2)}, u32[]{:S(2)}) %collective-permute-start.63) | collective-permute-done | bytes 262176 | tf_op jit(solution)/shard_map/ppermute | solution.py:61
  363.1 3.1 fusion.3
  367.8 3.4 collective-permute-start.72
  375.9 2.6 fusion.5
  (499 shorter events, 172.8 us)
Async XLA Ops:
  2.6 12.1 %collective-permute-start = (bf16[64,1664]{1,0:T(8,128)(2,1)S(1)}, bf16[64,1664]{1,0:T(8,128)(2,1)S(1)}, u32[]{:S(2)}, u32[]{:S(2)}) collective-permute-start(bf16[64,1664]{1,0:T(8,128)(2,1)S(1)} %pad_maximum_fusion.28), channel_id=1, source_target_pairs={{0,8},{1,9},{2,10},{3,11},{4,12},{5,13},{6,14},{7,15},{8,0},{9,1},... | collective-permute-start | bytes 638984 | tf_op jit(solution)/shard_map/ppermute | solution.py:61
  5.7 18.2 %collective-permute-start.1 = (bf16[64,1664]{1,0:T(8,128)(2,1)S(1)}, bf16[64,1664]{1,0:T(8,128)(2,1)S(1)}, u32[]{:S(2)}, u32[]{:S(2)}) collective-permute-start(bf16[64,1664]{1,0:T(8,128)(2,1)S(1)} %pad_maximum_fusion.28), channel_id=1, source_target_pairs={{0,16},{1,17},{2,18},{3,19},{4,20},{5,21},{6,22},{7,23},{8,24},{9,... | collective-permute-start | bytes 638984 | tf_op jit(solution)/shard_map/ppermute | solution.py:61
  8.3 15.6 %collective-permute-start.2 = (bf16[64,1664]{1,0:T(8,128)(2,1)S(1)}, bf16[64,1664]{1,0:T(8,128)(2,1)S(1)}, u32[]{:S(2)}, u32[]{:S(2)}) collective-permute-start(bf16[64,1664]{1,0:T(8,128)(2,1)S(1)} %pad_maximum_fusion.28), channel_id=1, source_target_pairs={{0,24},{1,25},{2,26},{3,27},{4,28},{5,29},{6,30},{7,31},{8,16},{9,... | collective-permute-start | bytes 638984 | tf_op jit(solution)/shard_map/ppermute | solution.py:61
  24.0 22.9 %collective-permute-start.3 = (bf16[128,1664]{1,0:T(8,128)(2,1)S(1)}, bf16[128,1664]{1,0:T(8,128)(2,1)S(1)}, u32[]{:S(2)}, u32[]{:S(2)}) collective-permute-start(bf16[128,1664]{1,0:T(8,128)(2,1)S(1)} %pad_maximum_fusion.18), channel_id=1, source_target_pairs={{0,4},{1,5},{2,6},{3,7},{4,0},{5,1},{6,2},{7,3},{8,12},{9,13},{10,... | collective-permute-start | bytes 1277960 | tf_op jit(solution)/shard_map/ppermute | solution.py:61
  25.6 21.3 %collective-permute-start.4 = (bf16[128,1664]{1,0:T(8,128)(2,1)S(1)}, bf16[128,1664]{1,0:T(8,128)(2,1)S(1)}, u32[]{:S(2)}, u32[]{:S(2)}) collective-permute-start(bf16[128,1664]{1,0:T(8,128)(2,1)S(1)} %pad_maximum_fusion.19), channel_id=1, source_target_pairs={{0,2},{1,3},{2,0},{3,1},{4,6},{5,7},{6,4},{7,5},{8,10},{9,11},{10,... | collective-permute-start | bytes 1277960 | tf_op jit(solution)/shard_map/ppermute | solution.py:61
  30.8 16.1 %collective-permute-start.6 = (bf16[64,1536]{1,0:T(8,128)(2,1)S(1)}, bf16[64,1536]{1,0:T(8,128)(2,1)S(1)}, u32[]{:S(2)}, u32[]{:S(2)}) collective-permute-start(bf16[64,1536]{1,0:T(8,128)(2,1)S(1)} %get-tuple-element.284), channel_id=1, source_target_pairs={{0,16},{1,17},{2,18},{3,19},{4,20},{5,21},{6,22},{7,23},{8,24},{9,... | collective-permute-start | bytes 589832 | tf_op jit(solution)/shard_map/ppermute | solution.py:61
  31.8 15.1 %collective-permute-start.7 = (bf16[64,1536]{1,0:T(8,128)(2,1)S(1)}, bf16[64,1536]{1,0:T(8,128)(2,1)S(1)}, u32[]{:S(2)}, u32[]{:S(2)}) collective-permute-start(bf16[64,1536]{1,0:T(8,128)(2,1)S(1)} %get-tuple-element.284), channel_id=1, source_target_pairs={{0,24},{1,25},{2,26},{3,27},{4,28},{5,29},{6,30},{7,31},{8,16},{9,... | collective-permute-start | bytes 589832 | tf_op jit(solution)/shard_map/ppermute | solution.py:61
  47.0 15.5 %collective-permute-start.8 = (bf16[256,1664]{1,0:T(8,128)(2,1)S(1)}, bf16[256,1664]{1,0:T(8,128)(2,1)S(1)}, u32[]{:S(2)}, u32[]{:S(2)}) collective-permute-start(bf16[256,1664]{1,0:T(8,128)(2,1)S(1)} %pad_maximum_fusion.7.refs_0_), channel_id=1, source_target_pairs={{0,2},{1,3},{2,0},{3,1},{4,6},{5,7},{6,4},{7,5},{8,10},{9,11},{10,... | collective-permute-start | bytes 2555912 | tf_op jit(solution)/shard_map/ppermute | solution.py:61
  47.6 15.3 %collective-permute-start.9 = (bf16[256,1664]{1,0:T(8,128)(2,1)S(1)}, bf16[256,1664]{1,0:T(8,128)(2,1)}, u32[]{:S(2)}, u32[]{:S(2)}) collective-permute-start(bf16[256,1664]{1,0:T(8,128)(2,1)S(1)} %pad_maximum_fusion.8.refs_1_), channel_id=1, source_target_pairs={{0,4},{1,5},{2,6},{3,7},{4,0},{5,1},{6,2},{7,3},{8,12},{9,13},{10,... | collective-permute-start | bytes 2555912 | tf_op jit(solution)/shard_map/ppermute | solution.py:61
  64.4 13.0 %collective-permute-start.13 = (bf16[128,1536]{1,0:T(8,128)(2,1)}, bf16[128,1536]{1,0:T(8,128)(2,1)S(1)}, u32[]{:S(2)}, u32[]{:S(2)}) collective-permute-start(bf16[128,1536]{1,0:T(8,128)(2,1)} %pad_maximum_fusion.20), channel_id=1, source_target_pairs={{0,4},{1,5},{2,6},{3,7},{4,0},{5,1},{6,2},{7,3},{8,12},{9,13},{10,... | collective-permute-start | bytes 1179656 | tf_op jit(solution)/shard_map/ppermute | solution.py:61
  77.8 19.3 %collective-permute-start.19 = (bf16[1,512,512]{2,1,0:T(8,128)(2,1)S(1)}, bf16[1,512,512]{2,1,0:T(8,128)(2,1)S(1)}, u32[]{:S(2)}, u32[]{:S(2)}) collective-permute-start(bf16[1,512,512]{2,1,0:T(8,128)(2,1)S(1)} %pad_maximum_fusion.14), channel_id=1, source_target_pairs={{0,2},{1,3},{2,0},{3,1},{4,6},{5,7},{6,4},{7,5},{8,10},{9,11},{10,... | collective-permute-start | bytes 1572872 | tf_op jit(solution)/shard_map/ppermute | solution.py:61
  79.4 12.9 %collective-permute-start.20 = (bf16[128,1024]{1,0:T(8,128)(2,1)S(1)}, bf16[128,1024]{1,0:T(8,128)(2,1)S(1)}, u32[]{:S(2)}, u32[]{:S(2)}) collective-permute-start(bf16[128,1024]{1,0:T(8,128)(2,1)S(1)} %pad_maximum_fusion.24), channel_id=1, source_target_pairs={{0,4},{1,5},{2,6},{3,7},{4,0},{5,1},{6,2},{7,3},{8,12},{9,13},{10,... | collective-permute-start | bytes 786440 | tf_op jit(solution)/shard_map/ppermute | solution.py:61
  80.9 16.3 %collective-permute-start.21 = (bf16[128,1024]{1,0:T(8,128)(2,1)S(1)}, bf16[128,1024]{1,0:T(8,128)(2,1)S(1)}, u32[]{:S(2)}, u32[]{:S(2)}) collective-permute-start(bf16[128,1024]{1,0:T(8,128)(2,1)S(1)} %pad_maximum_fusion.25), channel_id=1, source_target_pairs={{0,2},{1,3},{2,0},{3,1},{4,6},{5,7},{6,4},{7,5},{8,10},{9,11},{10,... | collective-permute-start | bytes 786440 | tf_op jit(solution)/shard_map/ppermute | solution.py:61
  97.5 32.4 %collective-permute-start.25 = (bf16[256,1536]{1,0:T(8,128)(2,1)S(1)}, bf16[256,1536]{1,0:T(8,128)(2,1)S(1)}, u32[]{:S(2)}, u32[]{:S(2)}) collective-permute-start(bf16[256,1536]{1,0:T(8,128)(2,1)S(1)} %pad_maximum_fusion.9), channel_id=1, source_target_pairs={{0,2},{1,3},{2,0},{3,1},{4,6},{5,7},{6,4},{7,5},{8,10},{9,11},{10,... | collective-permute-start | bytes 2359304 | tf_op jit(solution)/shard_map/ppermute | solution.py:61
  99.1 30.9 %collective-permute-start.26 = (bf16[256,1536]{1,0:T(8,128)(2,1)S(1)}, bf16[256,1536]{1,0:T(8,128)(2,1)S(1)}, u32[]{:S(2)}, u32[]{:S(2)}) collective-permute-start(bf16[256,1536]{1,0:T(8,128)(2,1)S(1)} %pad_maximum_fusion.10), channel_id=1, source_target_pairs={{0,4},{1,5},{2,6},{3,7},{4,0},{5,1},{6,2},{7,3},{8,12},{9,13},{10,... | collective-permute-start | bytes 2359304 | tf_op jit(solution)/shard_map/ppermute | solution.py:61
  99.6 29.1 %collective-permute-start.23 = (bf16[256,1024]{1,0:T(8,128)(2,1)S(1)}, bf16[256,1024]{1,0:T(8,128)(2,1)S(1)}, u32[]{:S(2)}, u32[]{:S(2)}) collective-permute-start(bf16[256,1024]{1,0:T(8,128)(2,1)S(1)} %pad_maximum_fusion.15), channel_id=1, source_target_pairs={{0,2},{1,3},{2,0},{3,1},{4,6},{5,7},{6,4},{7,5},{8,10},{9,11},{10,... | collective-permute-start | bytes 1572872 | tf_op jit(solution)/shard_map/ppermute | solution.py:61
  100.1 29.8 %collective-permute-start.24 = (bf16[256,1024]{1,0:T(8,128)(2,1)S(1)}, bf16[256,1024]{1,0:T(8,128)(2,1)S(1)}, u32[]{:S(2)}, u32[]{:S(2)}) collective-permute-start(bf16[256,1024]{1,0:T(8,128)(2,1)S(1)} %pad_maximum_fusion.16), channel_id=1, source_target_pairs={{0,4},{1,5},{2,6},{3,7},{4,0},{5,1},{6,2},{7,3},{8,12},{9,13},{10,... | collective-permute-start | bytes 1572872 | tf_op jit(solution)/shard_map/ppermute | solution.py:61
  102.3 24.6 %collective-permute-start.27 = (bf16[128,1536]{1,0:T(8,128)(2,1)S(1)}, bf16[128,1536]{1,0:T(8,128)(2,1)S(1)}, u32[]{:S(2)}, u32[]{:S(2)}) collective-permute-start(bf16[128,1536]{1,0:T(8,128)(2,1)S(1)} %pad_maximum_fusion.22), channel_id=1, source_target_pairs={{0,16},{1,17},{2,18},{3,19},{4,20},{5,21},{6,22},{7,23},{8,24},{9,... | collective-permute-start | bytes 1179656 | tf_op jit(solution)/shard_map/ppermute | solution.py:61
  130.5 19.1 %collective-permute-start.29 = (bf16[1024,1536]{1,0:T(8,128)(2,1)S(1)}, bf16[1024,1536]{1,0:T(8,128)(2,1)S(1)}, u32[]{:S(2)}, u32[]{:S(2)}) collective-permute-start(bf16[1024,1536]{1,0:T(8,128)(2,1)S(1)} %pad_maximum_fusion.refs_0_), channel_id=1, source_target_pairs={{0,1},{1,0},{2,3},{3,2},{4,5},{5,4},{6,7},{7,6},{8,9},{9,8},{10,11... | collective-permute-start | bytes 9437192 | tf_op jit(solution)/shard_map/ppermute | solution.py:61
  131.7 17.9 %collective-permute-start.30 = (bf16[128,1536]{1,0:T(8,128)(2,1)S(1)}, bf16[128,1536]{1,0:T(8,128)(2,1)S(1)}, u32[]{:S(2)}, u32[]{:S(2)}) collective-permute-start(bf16[128,1536]{1,0:T(8,128)(2,1)S(1)} %pad_maximum_fusion.22), channel_id=1, source_target_pairs={{0,4},{1,5},{2,6},{3,7},{4,0},{5,1},{6,2},{7,3},{8,12},{9,13},{10,... | collective-permute-start | bytes 1179656 | tf_op jit(solution)/shard_map/ppermute | solution.py:61
  132.3 17.3 %collective-permute-start.31 = (bf16[128,1536]{1,0:T(8,128)(2,1)S(1)}, bf16[128,1536]{1,0:T(8,128)(2,1)S(1)}, u32[]{:S(2)}, u32[]{:S(2)}) collective-permute-start(bf16[128,1536]{1,0:T(8,128)(2,1)S(1)} %collective-permute-done.27), channel_id=1, source_target_pairs={{0,2},{1,3},{2,0},{3,1},{4,6},{5,7},{6,4},{7,5},{8,10},{9,11},{10,... | collective-permute-start | bytes 1179656 | tf_op jit(solution)/shard_map/ppermute | solution.py:61
  149.8 21.0 %collective-permute-start.33 = (bf16[256,1536]{1,0:T(8,128)(2,1)S(1)}, bf16[256,1536]{1,0:T(8,128)(2,1)S(1)}, u32[]{:S(2)}, u32[]{:S(2)}) collective-permute-start(bf16[256,1536]{1,0:T(8,128)(2,1)S(1)} %pad_maximum_fusion.11), channel_id=1, source_target_pairs={{0,2},{1,3},{2,0},{3,1},{4,6},{5,7},{6,4},{7,5},{8,10},{9,11},{10,... | collective-permute-start | bytes 2359304 | tf_op jit(solution)/shard_map/ppermute | solution.py:61
  152.7 19.5 %collective-permute-start.34 = (bf16[256,1536]{1,0:T(8,128)(2,1)S(1)}, bf16[256,1536]{1,0:T(8,128)(2,1)S(1)}, u32[]{:S(2)}, u32[]{:S(2)}) collective-permute-start(bf16[256,1536]{1,0:T(8,128)(2,1)S(1)} %pad_maximum_fusion.12), channel_id=1, source_target_pairs={{0,4},{1,5},{2,6},{3,7},{4,0},{5,1},{6,2},{7,3},{8,12},{9,13},{10,... | collective-permute-start | bytes 2359304 | tf_op jit(solution)/shard_map/ppermute | solution.py:61
  178.2 13.7 %collective-permute-start.36 = (bf16[1024,1536]{1,0:T(8,128)(2,1)S(1)}, bf16[1024,1536]{1,0:T(8,128)(2,1)}, u32[]{:S(2)}, u32[]{:S(2)}) collective-permute-start(bf16[1024,1536]{1,0:T(8,128)(2,1)S(1)} %get-tuple-element.379), channel_id=1, source_target_pairs={{0,1},{1,0},{2,3},{3,2},{4,5},{5,4},{6,7},{7,6},{8,9},{9,8},{10,11... | collective-permute-start | bytes 9437192 | tf_op jit(solution)/shard_map/ppermute | solution.py:61
  196.0 20.9 %collective-permute-start.37 = (bf16[256,1536]{1,0:T(8,128)(2,1)}, bf16[256,1536]{1,0:T(8,128)(2,1)}, u32[]{:S(2)}, u32[]{:S(2)}) collective-permute-start(bf16[256,1536]{1,0:T(8,128)(2,1)} %get-tuple-element.384), channel_id=1, source_target_pairs={{0,2},{1,3},{2,0},{3,1},{4,6},{5,7},{6,4},{7,5},{8,10},{9,11},{10,... | collective-permute-start | bytes 2359304 | tf_op jit(solution)/shard_map/ppermute | solution.py:61
  196.3 20.5 %collective-permute-start.38 = (bf16[256,1536]{1,0:T(8,128)(2,1)}, bf16[256,1536]{1,0:T(8,128)(2,1)}, u32[]{:S(2)}, u32[]{:S(2)}) collective-permute-start(bf16[256,1536]{1,0:T(8,128)(2,1)} %get-tuple-element.385), channel_id=1, source_target_pairs={{0,4},{1,5},{2,6},{3,7},{4,0},{5,1},{6,2},{7,3},{8,12},{9,13},{10,... | collective-permute-start | bytes 2359304 | tf_op jit(solution)/shard_map/ppermute | solution.py:61
  221.1 13.3 %collective-permute-start.41 = (bf16[1024,1536]{1,0:T(8,128)(2,1)}, bf16[1024,1536]{1,0:T(8,128)(2,1)}, u32[]{:S(2)}, u32[]{:S(2)}) collective-permute-start(bf16[1024,1536]{1,0:T(8,128)(2,1)} %get-tuple-element.396), channel_id=1, source_target_pairs={{0,1},{1,0},{2,3},{3,2},{4,5},{5,4},{6,7},{7,6},{8,9},{9,8},{10,11... | collective-permute-start | bytes 9437192 | tf_op jit(solution)/shard_map/ppermute | solution.py:61
  221.1 13.1 %collective-permute-start.39 = (bf16[128,1536]{1,0:T(8,128)(2,1)}, bf16[128,1536]{1,0:T(8,128)(2,1)}, u32[]{:S(2)}, u32[]{:S(2)}) collective-permute-start(bf16[128,1536]{1,0:T(8,128)(2,1)} %slice.651), channel_id=1, source_target_pairs={{0,4},{1,5},{2,6},{3,7},{4,0},{5,1},{6,2},{7,3},{8,12},{9,13},{10,... | collective-permute-start | bytes 1179656 | tf_op jit(solution)/shard_map/ppermute | solution.py:61
  222.9 11.6 %collective-permute-start.40 = (bf16[128,1536]{1,0:T(8,128)(2,1)}, bf16[128,1536]{1,0:T(8,128)(2,1)}, u32[]{:S(2)}, u32[]{:S(2)}) collective-permute-start(bf16[128,1536]{1,0:T(8,128)(2,1)} %slice.650), channel_id=1, source_target_pairs={{0,2},{1,3},{2,0},{3,1},{4,6},{5,7},{6,4},{7,5},{8,10},{9,11},{10,... | collective-permute-start | bytes 1179656 | tf_op jit(solution)/shard_map/ppermute | solution.py:61
  239.8 22.5 %collective-permute-start.45 = (bf16[256,1536]{1,0:T(8,128)(2,1)S(1)}, bf16[256,1536]{1,0:T(8,128)(2,1)S(1)}, u32[]{:S(2)}, u32[]{:S(2)}) collective-permute-start(bf16[256,1536]{1,0:T(8,128)(2,1)S(1)} %get-tuple-element.409), channel_id=1, source_target_pairs={{0,2},{1,3},{2,0},{3,1},{4,6},{5,7},{6,4},{7,5},{8,10},{9,11},{10,... | collective-permute-start | bytes 2359304 | tf_op jit(solution)/shard_map/ppermute | solution.py:61
  245.6 18.9 %collective-permute-start.46 = (bf16[256,1536]{1,0:T(8,128)(2,1)S(1)}, bf16[256,1536]{1,0:T(8,128)(2,1)S(1)}, u32[]{:S(2)}, u32[]{:S(2)}) collective-permute-start(bf16[256,1536]{1,0:T(8,128)(2,1)S(1)} %get-tuple-element.410), channel_id=1, source_target_pairs={{0,4},{1,5},{2,6},{3,7},{4,0},{5,1},{6,2},{7,3},{8,12},{9,13},{10,... | collective-permute-start | bytes 2359304 | tf_op jit(solution)/shard_map/ppermute | solution.py:61
  247.8 14.5 %collective-permute-start.44 = (bf16[64,1536]{1,0:T(8,128)(2,1)S(1)}, bf16[64,1536]{1,0:T(8,128)(2,1)S(1)}, u32[]{:S(2)}, u32[]{:S(2)}) collective-permute-start(bf16[64,1536]{1,0:T(8,128)(2,1)S(1)} %get-tuple-element.408), channel_id=1, source_target_pairs={{0,24},{1,25},{2,26},{3,27},{4,28},{5,29},{6,30},{7,31},{8,16},{9,... | collective-permute-start | bytes 589832 | tf_op jit(solution)/shard_map/ppermute | solution.py:61
  266.8 12.9 %collective-permute-start.49 = (bf16[1024,1024]{1,0:T(8,128)(2,1)S(1)}, bf16[1024,1024]{1,0:T(8,128)(2,1)S(1)}, u32[]{:S(2)}, u32[]{:S(2)}) collective-permute-start(bf16[1024,1024]{1,0:T(8,128)(2,1)S(1)} %copy-done.33), channel_id=1, source_target_pairs={{0,1},{1,0},{2,3},{3,2},{4,5},{5,4},{6,7},{7,6},{8,9},{9,8},{10,11... | collective-permute-start | bytes 6291464 | tf_op jit(solution)/shard_map/ppermute | solution.py:61
  268.2 11.1 %collective-permute-start.47 = (bf16[128,1536]{1,0:T(8,128)(2,1)S(1)}, bf16[128,1536]{1,0:T(8,128)(2,1)S(1)}, u32[]{:S(2)}, u32[]{:S(2)}) collective-permute-start(bf16[128,1536]{1,0:T(8,128)(2,1)S(1)} %slice.649), channel_id=1, source_target_pairs={{0,4},{1,5},{2,6},{3,7},{4,0},{5,1},{6,2},{7,3},{8,12},{9,13},{10,... | collective-permute-start | bytes 1179656 | tf_op jit(solution)/shard_map/ppermute | solution.py:61
  282.0 22.5 %collective-permute-start.53 = (bf16[256,1024]{1,0:T(8,128)(2,1)S(1)}, bf16[256,1024]{1,0:T(8,128)(2,1)S(1)}, u32[]{:S(2)}, u32[]{:S(2)}) collective-permute-start(bf16[256,1024]{1,0:T(8,128)(2,1)S(1)} %get-tuple-element.436), channel_id=1, source_target_pairs={{0,2},{1,3},{2,0},{3,1},{4,6},{5,7},{6,4},{7,5},{8,10},{9,11},{10,... | collective-permute-start | bytes 1572872 | tf_op jit(solution)/shard_map/ppermute | solution.py:61
  283.9 20.6 %collective-permute-start.54 = (bf16[256,1024]{1,0:T(8,128)(2,1)S(1)}, bf16[256,1024]{1,0:T(8,128)(2,1)S(1)}, u32[]{:S(2)}, u32[]{:S(2)}) collective-permute-start(bf16[256,1024]{1,0:T(8,128)(2,1)S(1)} %get-tuple-element.437), channel_id=1, source_target_pairs={{0,4},{1,5},{2,6},{3,7},{4,0},{5,1},{6,2},{7,3},{8,12},{9,13},{10,... | collective-permute-start | bytes 1572872 | tf_op jit(solution)/shard_map/ppermute | solution.py:61
  285.2 11.6 %collective-permute-start.50 = (bf16[64,1536]{1,0:T(8,128)(2,1)S(1)}, bf16[64,1536]{1,0:T(8,128)(2,1)S(1)}, u32[]{:S(2)}, u32[]{:S(2)}) collective-permute-start(bf16[64,1536]{1,0:T(8,128)(2,1)S(1)} %slice.657), channel_id=1, source_target_pairs={{0,8},{1,9},{2,10},{3,11},{4,12},{5,13},{6,14},{7,15},{8,0},{9,1},... | collective-permute-start | bytes 589832 | tf_op jit(solution)/shard_map/ppermute | solution.py:61
  289.5 14.9 %collective-permute-start.52 = (bf16[64,1536]{1,0:T(8,128)(2,1)S(1)}, bf16[64,1536]{1,0:T(8,128)(2,1)S(1)}, u32[]{:S(2)}, u32[]{:S(2)}) collective-permute-start(bf16[64,1536]{1,0:T(8,128)(2,1)S(1)} %get-tuple-element.435), channel_id=1, source_target_pairs={{0,24},{1,25},{2,26},{3,27},{4,28},{5,29},{6,30},{7,31},{8,16},{9,... | collective-permute-start | bytes 589832 | tf_op jit(solution)/shard_map/ppermute | solution.py:61
  306.7 12.7 %collective-permute-start.57 = (bf16[128,1024]{1,0:T(8,128)(2,1)S(1)}, bf16[128,1024]{1,0:T(8,128)(2,1)S(1)}, u32[]{:S(2)}, u32[]{:S(2)}) collective-permute-start(bf16[128,1024]{1,0:T(8,128)(2,1)S(1)} %slice.655), channel_id=1, source_target_pairs={{0,4},{1,5},{2,6},{3,7},{4,0},{5,1},{6,2},{7,3},{8,12},{9,13},{10,... | collective-permute-start | bytes 786440 | tf_op jit(solution)/shard_map/ppermute | solution.py:61
  308.1 11.3 %collective-permute-start.58 = (bf16[128,1024]{1,0:T(8,128)(2,1)S(1)}, bf16[128,1024]{1,0:T(8,128)(2,1)S(1)}, u32[]{:S(2)}, u32[]{:S(2)}) collective-permute-start(bf16[128,1024]{1,0:T(8,128)(2,1)S(1)} %slice.654), channel_id=1, source_target_pairs={{0,2},{1,3},{2,0},{3,1},{4,6},{5,7},{6,4},{7,5},{8,10},{9,11},{10,... | collective-permute-start | bytes 786440 | tf_op jit(solution)/shard_map/ppermute | solution.py:61
  309.9 12.2 %collective-permute-start.56 = (bf16[1,1,1,256,512]{4,3,2,1,0:T(8,128)(2,1)S(1)}, bf16[1,1,1,256,512]{4,3,2,1,0:T(8,128)(2,1)S(1)}, u32[]{:S(2)}, u32[]{:S(2)}) collective-permute-start(bf16[1,1,1,256,512]{4,3,2,1,0:T(8,128)(2,1)S(1)} %get-tuple-element.453), channel_id=1, source_target_pairs={{0,2},{1,3},{2,0},{3,1},{4,6},{5,7},{6,4},{7,5},{8,10},{9,11},{10,... | collective-permute-start | bytes 786440 | tf_op jit(solution)/shard_map/ppermute | solution.py:61
  335.4 18.3 %collective-permute-start.61 = (bf16[256,1024]{1,0:T(8,128)(2,1)S(1)}, bf16[256,1024]{1,0:T(8,128)(2,1)S(1)}, u32[]{:S(2)}, u32[]{:S(2)}) collective-permute-start(bf16[256,1024]{1,0:T(8,128)(2,1)S(1)} %get-tuple-element.472), channel_id=1, source_target_pairs={{0,2},{1,3},{2,0},{3,1},{4,6},{5,7},{6,4},{7,5},{8,10},{9,11},{10,... | collective-permute-start | bytes 1572872 | tf_op jit(solution)/shard_map/ppermute | solution.py:61
  335.8 17.9 %collective-permute-start.62 = (bf16[256,1024]{1,0:T(8,128)(2,1)S(1)}, bf16[256,1024]{1,0:T(8,128)(2,1)S(1)}, u32[]{:S(2)}, u32[]{:S(2)}) collective-permute-start(bf16[256,1024]{1,0:T(8,128)(2,1)S(1)} %get-tuple-element.473), channel_id=1, source_target_pairs={{0,4},{1,5},{2,6},{3,7},{4,0},{5,1},{6,2},{7,3},{8,12},{9,13},{10,... | collective-permute-start | bytes 1572872 | tf_op jit(solution)/shard_map/ppermute | solution.py:61
  336.5 17.1 %collective-permute-start.63 = (bf16[128,1024]{1,0:T(8,128)(2,1)S(1)}, bf16[128,1024]{1,0:T(8,128)(2,1)S(1)}, u32[]{:S(2)}, u32[]{:S(2)}) collective-permute-start(bf16[128,1024]{1,0:T(8,128)(2,1)S(1)} %copy-done.71), channel_id=1, source_target_pairs={{0,16},{1,17},{2,18},{3,19},{4,20},{5,21},{6,22},{7,23},{8,24},{9,... | collective-permute-start | bytes 786440 | tf_op jit(solution)/shard_map/ppermute | solution.py:61
  342.3 11.4 %collective-permute-start.64 = (f32[1,128]{1,0:T(1,128)S(1)}, f32[1,128]{1,0:T(1,128)S(1)}, u32[]{:S(2)}, u32[]{:S(2)}) collective-permute-start(f32[1,128]{1,0:T(1,128)S(1)} %maximum_bitcast_fusion.1), channel_id=1, source_target_pairs={{0,16},{1,17},{2,18},{3,19},{4,20},{5,21},{6,22},{7,23},{8,24},{9,... | collective-permute-start | bytes 1544 | tf_op jit(solution)/shard_map/ppermute | solution.py:61
  366.7 13.6 %collective-permute-start.70 = (bf16[64,1024]{1,0:T(8,128)(2,1)S(1)}, bf16[64,1024]{1,0:T(8,128)(2,1)S(1)}, u32[]{:S(2)}, u32[]{:S(2)}) collective-permute-start(bf16[64,1024]{1,0:T(8,128)(2,1)S(1)} %slice.661), channel_id=1, source_target_pairs={{0,8},{1,9},{2,10},{3,11},{4,12},{5,13},{6,14},{7,15},{8,0},{9,1},... | collective-permute-start | bytes 393224 | tf_op jit(solution)/shard_map/ppermute | solution.py:61
  367.0 13.3 %collective-permute-start.71 = (bf16[64,1024]{1,0:T(8,128)(2,1)S(1)}, bf16[64,1024]{1,0:T(8,128)(2,1)S(1)}, u32[]{:S(2)}, u32[]{:S(2)}) collective-permute-start(bf16[64,1024]{1,0:T(8,128)(2,1)S(1)} %get-tuple-element.504), channel_id=1, source_target_pairs={{0,16},{1,17},{2,18},{3,19},{4,20},{5,21},{6,22},{7,23},{8,24},{9,... | collective-permute-start | bytes 393224 | tf_op jit(solution)/shard_map/ppermute | solution.py:61
  367.8 12.5 %collective-permute-start.72 = (bf16[64,1024]{1,0:T(8,128)(2,1)S(1)}, bf16[64,1024]{1,0:T(8,128)(2,1)S(1)}, u32[]{:S(2)}, u32[]{:S(2)}) collective-permute-start(bf16[64,1024]{1,0:T(8,128)(2,1)S(1)} %get-tuple-element.505), channel_id=1, source_target_pairs={{0,24},{1,25},{2,26},{3,27},{4,28},{5,29},{6,30},{7,31},{8,16},{9,... | collective-permute-start | bytes 393224 | tf_op jit(solution)/shard_map/ppermute | solution.py:61
  (137 other events, 880.1 us)

commit v10 on v9

--- a/solution.py
+++ b/solution.py
@@ -530,6 +530,9 @@
     gain_spec = pl.BlockSpec((HD, 1), lambda row, *_: (0, 0))
     dkv_spec = pl.BlockSpec((pieces, 1, 2, HD, length), lambda row, *_: (0, row, 0, group, 0))
     work = rows * GROUP * length * length * pieces
+    out, grad_out, q_raw = (
+        pltpu.with_memory_space_constraint(one, pltpu.HBM) for one in (out, grad_out, q_raw)
+    )
     inputs = [info, queries, keys_values, keys_values, out, sums, grad_out, q_raw, gain, cos_t, sin_t]
     return pl.pallas_call(
         kernel,

time: 404 us -> 400 us (0.990)
  local copies, waits for them, and re-layouts: 21.6 us -> 15.3 us
  Pallas kernels: 62.3 us -> 67.7 us
    unnamed x203 -> x191, local copies, waits for them, and re-layouts: 17.2 us -> 10.9 us
    pallas_call x4, Pallas kernels: 19.3 us -> 24.7 us  [attention_back(): pl.pallas_call(kernel, out_shape=[jax.ShapeDtypeStruct(queries.shape, LOW...]
  transfers between devices with their start and end apart: 84 -> 84, of which waited for: 35 -> 33; matrix products, arithmetic and copies ran while one was open for 19% -> 20% of each run, Pallas kernels for 15% -> 17%
where the time goes in v10:
time: 400 us; the launch traced here: 396 us
  starting transfers between devices  114 us (28%)
  waiting for transfers between devices  95.8 us (24%)
  Pallas kernels  67.7 us (17%)
  matrix products  51.7 us (13%)
  other arithmetic  48.1 us (12%)
  local copies, waits for them, and re-layouts  15.3 us (4%)
    ppermute x84, starting transfers between devices, swap(): lax.ppermute(values, ('dp', 'shard'), [(i, i ^ mask) for i in range(devic...  114 us
    ppermute x84, waiting for transfers between devices, swap(): lax.ppermute(values, ('dp', 'shard'), [(i, i ^ mask) for i in range(devic...  95.8 us
    pallas_call x4, Pallas kernels, attention_back(): pl.pallas_call(kernel, out_shape=[jax.ShapeDtypeStruct(queries.shape, LOW...  24.7 us
    pallas_call x5, Pallas kernels, pick(): pl.pallas_call(kernel, out_shape=[jax.ShapeDtypeStruct((len(own) * size,...  19 us
    pallas_call x4, Pallas kernels, place(): pl.pallas_call(kernel, out_shape=[jax.ShapeDtypeStruct((total_rows, width...  14.2 us
    unnamed x191, local copies, waits for them, and re-layouts  10.9 us
    pallas_call x1, Pallas kernels, attention(): pl.pallas_call(kernel, out_shape=[jax.ShapeDtypeStruct((rows, groups * gr...  9.22 us
    convert_element_type x5, other arithmetic, prepare(): self.outgoing = (self.both(0, 4).astype(LOW), self.both(4, 8).astype(LOW))  8.06 us
  transfers between devices with their start and end apart: 84, of which 33 were waited for; matrix products, arithmetic and copies ran while one was open for 20% of the time, Pallas kernels for 17%

profile of v10, /device:TPU:0, one launch (start us, length us, event | category | flops | bytes accessed | tf_op | source)
XLA Modules:
  0.0 396.3 jit_solution(13297438838102595198)
XLA Ops:
  2.6 3.1 collective-permute-start
  5.7 2.6 collective-permute-start.1
  14.8 9.2 %collective-permute-done.1 = bf16[64,1664]{1,0:T(8,128)(2,1)S(1)} collective-permute-done((bf16[64,1664]{1,0:T(8,128)(2,1)S(1)}, bf16[64,1664]{1,0:T(8,128)(2,1)S(1)}, u32[]{:S(2)}, u32[]{:S(2)}) %collective-permute-start.1) | collective-permute-done | bytes 213024 | tf_op jit(solution)/shard_map/ppermute | solution.py:61
  27.1 3.7 collective-permute-start.5
  33.3 3.4 collective-permute-done.5
  36.7 10.2 %collective-permute-done.6 = bf16[64,1536]{1,0:T(8,128)(2,1)S(1)} collective-permute-done((bf16[64,1536]{1,0:T(8,128)(2,1)S(1)}, bf16[64,1536]{1,0:T(8,128)(2,1)S(1)}, u32[]{:S(2)}, u32[]{:S(2)}) %collective-permute-start.6) | collective-permute-done | bytes 196640 | tf_op jit(solution)/shard_map/ppermute | solution.py:61
  48.2 2.7 collective-permute-start.10
  54.1 7.5 %collective-permute-done.11 = bf16[64,1024]{1,0:T(8,128)(2,1)S(1)} collective-permute-done((bf16[64,1024]{1,0:T(8,128)(2,1)S(1)}, bf16[64,1024]{1,0:T(8,128)(2,1)S(1)}, u32[]{:S(2)}, u32[]{:S(2)}) %collective-permute-start.11) | collective-permute-done | bytes 131104 | tf_op jit(solution)/shard_map/ppermute | solution.py:61
  69.1 4.2 %shard_map.221 = (bf16[2048,1024]{1,0:T(8,128)(2,1)S(1)}, bf16[2048,512]{1,0:T(8,128)(2,1)S(1)}, bf16[2048,128]{1,0:T(8,128)(2,1)S(1)}) custom-call(s32[1]{0:T(128)} %bitcast.me_ref, bf16[256,1664]{1,0:T(8,128)(2,1)S(1)} %pad_maximum_fusion.7.refs_0_, bf16[256,1664]{1,0:T(8,128)(2,1)S(1)} %pad_maximum_fusion.8.refs_1_, ...), custom_call_target="tpu_custom_call" | custom-call | bytes 65536 | tf_op jit(solution)/shard_map/pallas_call | solution.py:88
  81.4 5.7 %collective-permute-start.22 = (bf16[64,1536]{1,0:T(8,128)(2,1)S(1)}, bf16[64,1536]{1,0:T(8,128)(2,1)S(1)}, u32[]{:S(2)}, u32[]{:S(2)}) collective-permute-start(bf16[64,1536]{1,0:T(8,128)(2,1)S(1)} %copy-done.68), channel_id=1, source_target_pairs={{0,8},{1,9},{2,10},{3,11},{4,12},{5,13},{6,14},{7,15},{8,0},{9,1},... | collective-permute-start | bytes 589832 | tf_op jit(solution)/shard_map/ppermute | solution.py:61
  92.2 4.9 %collective-permute-done.21 = bf16[128,1024]{1,0:T(8,128)(2,1)S(1)} collective-permute-done((bf16[128,1024]{1,0:T(8,128)(2,1)S(1)}, bf16[128,1024]{1,0:T(8,128)(2,1)S(1)}, u32[]{:S(2)}, u32[]{:S(2)}) %collective-permute-start.21) | collective-permute-done | bytes 262176 | tf_op jit(solution)/shard_map/ppermute | solution.py:61
  102.2 7.6 %collective-permute-start.27 = (bf16[128,1536]{1,0:T(8,128)(2,1)S(1)}, bf16[128,1536]{1,0:T(8,128)(2,1)S(1)}, u32[]{:S(2)}, u32[]{:S(2)}) collective-permute-start(bf16[128,1536]{1,0:T(8,128)(2,1)S(1)} %pad_maximum_fusion.22), channel_id=1, source_target_pairs={{0,16},{1,17},{2,18},{3,19},{4,20},{5,21},{6,22},{7,23},{8,24},{9,... | collective-permute-start | bytes 1179656 | tf_op jit(solution)/shard_map/ppermute | solution.py:61
  111.3 9.2 %shard_map.222 = (f32[1,1024,512]{2,1,0:T(8,128)S(1)}, bf16[1,1024,512]{2,1,0:T(8,128)(2,1)S(1)}, f32[1,4,4,512]{3,2,1,0:T(4,128)S(1)}) custom-call(s32[6]{0:T(128)S(1)} %pad_add_fusion.info_ref, bf16[1,1024,512]{2,1,0:T(8,128)(2,1)S(1)} %bitcast.222, bf16[4,1,512,512]{3,2,1,0:T(8,128)(2,1)S(1)} %constant_dynamic-update-slice_fusion.k_ref.v_ref, ...), custom_call_target="tpu_custom_call" | custom-call | flops 16777216 | bytes 1048576 | tf_op jit(solution)/shard_map/pallas_call | solution.py:425
  121.9 5.0 %collective-permute-done.27 = bf16[128,1536]{1,0:T(8,128)(2,1)S(1)} collective-permute-done((bf16[128,1536]{1,0:T(8,128)(2,1)S(1)}, bf16[128,1536]{1,0:T(8,128)(2,1)S(1)}, u32[]{:S(2)}, u32[]{:S(2)}) %collective-permute-start.27) | collective-permute-done | bytes 393248 | tf_op jit(solution)/shard_map/ppermute | solution.py:61
  132.3 7.3 %collective-permute-start.31 = (bf16[128,1536]{1,0:T(8,128)(2,1)S(1)}, bf16[128,1536]{1,0:T(8,128)(2,1)S(1)}, u32[]{:S(2)}, u32[]{:S(2)}) collective-permute-start(bf16[128,1536]{1,0:T(8,128)(2,1)S(1)} %collective-permute-done.27), channel_id=1, source_target_pairs={{0,2},{1,3},{2,0},{3,1},{4,6},{5,7},{6,4},{7,5},{8,10},{9,11},{10,... | collective-permute-start | bytes 1179656 | tf_op jit(solution)/shard_map/ppermute | solution.py:61
  139.6 5.9 %shard_map.223 = bf16[2048,1024]{1,0:T(8,128)(2,1)S(1)} custom-call(s32[1]{0:T(128)} %bitcast.me_ref, bf16[1024,1024]{1,0:T(8,128)(2,1)S(1)} %pad_maximum_fusion.3.refs_0_, bf16[1024,1024]{1,0:T(8,128)(2,1)S(1)} %collective-permute-done.32.refs_1_), custom_call_target="tpu_custom_call" | custom-call | bytes 65536 | tf_op jit(solution)/shard_map/pallas_call | solution.py:88
  145.5 2.6 multiply_reduce_fusion
  150.3 2.5 collective-permute-start.33
  165.6 5.3 %collective-permute-done.33 = bf16[256,1536]{1,0:T(8,128)(2,1)S(1)} collective-permute-done((bf16[256,1536]{1,0:T(8,128)(2,1)S(1)}, bf16[256,1536]{1,0:T(8,128)(2,1)S(1)}, u32[]{:S(2)}, u32[]{:S(2)}) %collective-permute-start.33) | collective-permute-done | bytes 786464 | tf_op jit(solution)/shard_map/ppermute | solution.py:61
  172.6 5.6 %collective-permute-done.35.refs_1_ = bf16[1024,1536]{1,0:T(8,128)(2,1)S(1)} collective-permute-done((bf16[1024,1536]{1,0:T(8,128)(2,1)S(1)}, bf16[1024,1536]{1,0:T(8,128)(2,1)S(1)}, u32[]{:S(2)}, u32[]{:S(2)}) %collective-permute-start.35) | collective-permute-done | bytes 3145760 | tf_op jit(solution)/shard_map/ppermute | solution.py:61
  186.2 2.4 convolution_convert_fusion.2.refs_0_
  188.7 3.2 shard_map.227
  192.0 4.0 %add_convert_fusion.2 = (bf16[256,1536]{1,0:T(8,128)(2,1)}, bf16[256,1536]{1,0:T(8,128)(2,1)}) fusion(bf16[1024,1536]{1,0:T(8,128)(2,1)} %collective-permute-done.36, bf16[1024,1536]{1,0:T(8,128)(2,1)S(1)} %get-tuple-element.378), kind=kLoop, calls=%fused_computation.71 | loop fusion | flops 3145728 | bytes 4718592 | tf_op jit(solution)/shard_map/convert_element_type | solution.py:216
  199.3 2.7 fusion.7
  202.1 2.7 fusion.8
  207.2 6.1 %shard_map.228 = (bf16[1024,1024]{1,0:T(8,128)(2,1)S(1)}, bf16[1024,1024]{1,0:T(8,128)(2,1)S(1)}) custom-call(s32[1]{0:T(128)} %bitcast.me_ref, bf16[2048,1024]{1,0:T(8,128)(2,1)S(1)} %convolution_convert_fusion.1.refs_0_), custom_call_target="tpu_custom_call" | custom-call | bytes 65536 | tf_op jit(solution)/shard_map/pallas_call | solution.py:123
  213.3 3.7 fusion.35.grad_ref
  224.6 6.2 %shard_map.229 = (bf16[1,1024,512]{2,1,0:T(8,128)(2,1)S(1)}, f32[4,1,2,256,512]{4,3,2,1,0:T(8,128)S(1)}, f32[1,64,128]{2,1,0:T(8,128)S(1)}) custom-call(s32[6]{0:T(128)S(1)} %pad_add_fusion.info_ref, bf16[1,1024,512]{2,1,0:T(8,128)(2,1)S(1)} %bitcast.223, bf16[4,1,512,512]{3,2,1,0:T(8,128)(2,1)S(1)} %constant_dynamic-update-slice_fusion.k_ref.v_ref, ...), custom_call_target="tpu_custom_call" | custom-call | flops 4194304 | bytes 1048576 | tf_op jit(solution)/shard_map/pallas_call | solution.py:537
  238.8 2.7 collective-permute-start.45
  243.7 2.8 collective-permute-start.44
  246.4 6.0 %shard_map.230 = (bf16[1,1024,512]{2,1,0:T(8,128)(2,1)S(1)}, f32[4,1,2,256,512]{4,3,2,1,0:T(8,128)S(1)}, f32[1,64,128]{2,1,0:T(8,128)S(1)}) custom-call(s32[6]{0:T(128)S(1)} %pad_add_fusion.info_ref, bf16[1,1024,512]{2,1,0:T(8,128)(2,1)S(1)} %bitcast.224, ...), custom_call_target="tpu_custom_call", output_to_operand_aliasing={{0}: (11, {}), {1}: (12, {})} | custom-call | flops 4194304 | bytes 1048576 | tf_op jit(solution)/shard_map/pallas_call | solution.py:537
  252.5 6.1 %collective-permute-done.44 = bf16[64,1536]{1,0:T(8,128)(2,1)S(1)} collective-permute-done((bf16[64,1536]{1,0:T(8,128)(2,1)S(1)}, bf16[64,1536]{1,0:T(8,128)(2,1)S(1)}, u32[]{:S(2)}, u32[]{:S(2)}) %collective-permute-start.44) | collective-permute-done | bytes 196640 | tf_op jit(solution)/shard_map/ppermute | solution.py:61
  267.1 6.4 %shard_map.231 = (bf16[1,1024,512]{2,1,0:T(8,128)(2,1)S(1)}, f32[4,1,2,256,512]{4,3,2,1,0:T(8,128)S(1)}, f32[1,64,128]{2,1,0:T(8,128)S(1)}) custom-call(s32[6]{0:T(128)S(1)} %pad_add_fusion.info_ref, bf16[1,1024,512]{2,1,0:T(8,128)(2,1)S(1)} %bitcast.225, ...), custom_call_target="tpu_custom_call", output_to_operand_aliasing={{0}: (11, {}), {1}: (12, {})} | custom-call | flops 4194304 | bytes 1048576 | tf_op jit(solution)/shard_map/pallas_call | solution.py:537
  278.4 3.0 collective-permute-start.53
  282.4 2.8 collective-permute-start.50
  288.1 6.1 %shard_map.232 = (bf16[1,1024,512]{2,1,0:T(8,128)(2,1)S(1)}, f32[4,1,2,256,512]{4,3,2,1,0:T(8,128)S(1)}, f32[1,64,128]{2,1,0:T(8,128)S(1)}) custom-call(s32[6]{0:T(128)S(1)} %pad_add_fusion.info_ref, bf16[1,1024,512]{2,1,0:T(8,128)(2,1)S(1)} %bitcast.226, ...), custom_call_target="tpu_custom_call", output_to_operand_aliasing={{0}: (11, {}), {1}: (12, {})} | custom-call | flops 4194304 | bytes 1048576 | tf_op jit(solution)/shard_map/pallas_call | solution.py:537
  294.6 7.7 %collective-permute-done.51 = bf16[64,1536]{1,0:T(8,128)(2,1)S(1)} collective-permute-done((bf16[64,1536]{1,0:T(8,128)(2,1)S(1)}, bf16[64,1536]{1,0:T(8,128)(2,1)S(1)}, u32[]{:S(2)}, u32[]{:S(2)}) %collective-permute-start.51) | collective-permute-done | bytes 196640 | tf_op jit(solution)/shard_map/ppermute | solution.py:61
  310.2 4.6 %shard_map.233 = (bf16[1024,1024]{1,0:T(8,128)(2,1)S(1)}, bf16[1024,1024]{1,0:T(8,128)(2,1)}) custom-call(s32[1]{0:T(128)} %bitcast.me_ref, bf16[2048,1024]{1,0:T(8,128)(2,1)S(1)} %convolution_convert_fusion.refs_0_), custom_call_target="tpu_custom_call" | custom-call | bytes 65536 | tf_op jit(solution)/shard_map/pallas_call | solution.py:123
  316.2 2.6 collective-permute-done.56
  320.2 6.7 %convolution_bitcast_fusion = f32[1,512,2048]{2,1,0:T(8,128)} fusion(bf16[2048,1024]{1,0:T(8,128)(2,1)} %copy-done.24, bf16[1,1024,512]{2,1,0:T(8,128)(2,1)S(1)} %copy-done.4), kind=kOutput, calls=%fused_computation.29 | convolution fusion | flops 2147483648 | bytes 9437184 | tf_op jit(solution)/shard_map/ret,de->rtd/dot_general | solution.py:804
  333.0 5.0 %collective-permute-start.63 = (bf16[128,1024]{1,0:T(8,128)(2,1)S(1)}, bf16[128,1024]{1,0:T(8,128)(2,1)S(1)}, u32[]{:S(2)}, u32[]{:S(2)}) collective-permute-start(bf16[128,1024]{1,0:T(8,128)(2,1)S(1)} %copy-done.65), channel_id=1, source_target_pairs={{0,16},{1,17},{2,18},{3,19},{4,20},{5,21},{6,22},{7,23},{8,24},{9,... | collective-permute-start | bytes 786440 | tf_op jit(solution)/shard_map/ppermute | solution.py:61
  338.1 3.0 convolution_convert_fusion.4.refs_0_
  341.1 3.2 shard_map.235
  344.3 5.0 %collective-permute-done.63 = bf16[128,1024]{1,0:T(8,128)(2,1)S(1)} collective-permute-done((bf16[128,1024]{1,0:T(8,128)(2,1)S(1)}, bf16[128,1024]{1,0:T(8,128)(2,1)S(1)}, u32[]{:S(2)}, u32[]{:S(2)}) %collective-permute-start.63) | collective-permute-done | bytes 262176 | tf_op jit(solution)/shard_map/ppermute | solution.py:61
  359.1 3.1 fusion.3
  363.9 3.2 collective-permute-start.72
  371.6 2.6 fusion.5
  380.9 2.5 collective-permute-start.79
  (487 shorter events, 168.4 us)
Async XLA Ops:
  2.6 12.1 %collective-permute-start = (bf16[64,1664]{1,0:T(8,128)(2,1)S(1)}, bf16[64,1664]{1,0:T(8,128)(2,1)S(1)}, u32[]{:S(2)}, u32[]{:S(2)}) collective-permute-start(bf16[64,1664]{1,0:T(8,128)(2,1)S(1)} %pad_maximum_fusion.28), channel_id=1, source_target_pairs={{0,8},{1,9},{2,10},{3,11},{4,12},{5,13},{6,14},{7,15},{8,0},{9,1},... | collective-permute-start | bytes 638984 | tf_op jit(solution)/shard_map/ppermute | solution.py:61
  5.7 18.2 %collective-permute-start.1 = (bf16[64,1664]{1,0:T(8,128)(2,1)S(1)}, bf16[64,1664]{1,0:T(8,128)(2,1)S(1)}, u32[]{:S(2)}, u32[]{:S(2)}) collective-permute-start(bf16[64,1664]{1,0:T(8,128)(2,1)S(1)} %pad_maximum_fusion.28), channel_id=1, source_target_pairs={{0,16},{1,17},{2,18},{3,19},{4,20},{5,21},{6,22},{7,23},{8,24},{9,... | collective-permute-start | bytes 638984 | tf_op jit(solution)/shard_map/ppermute | solution.py:61
  8.3 15.6 %collective-permute-start.2 = (bf16[64,1664]{1,0:T(8,128)(2,1)S(1)}, bf16[64,1664]{1,0:T(8,128)(2,1)S(1)}, u32[]{:S(2)}, u32[]{:S(2)}) collective-permute-start(bf16[64,1664]{1,0:T(8,128)(2,1)S(1)} %pad_maximum_fusion.28), channel_id=1, source_target_pairs={{0,24},{1,25},{2,26},{3,27},{4,28},{5,29},{6,30},{7,31},{8,16},{9,... | collective-permute-start | bytes 638984 | tf_op jit(solution)/shard_map/ppermute | solution.py:61
  24.0 22.9 %collective-permute-start.3 = (bf16[128,1664]{1,0:T(8,128)(2,1)S(1)}, bf16[128,1664]{1,0:T(8,128)(2,1)S(1)}, u32[]{:S(2)}, u32[]{:S(2)}) collective-permute-start(bf16[128,1664]{1,0:T(8,128)(2,1)S(1)} %pad_maximum_fusion.18), channel_id=1, source_target_pairs={{0,4},{1,5},{2,6},{3,7},{4,0},{5,1},{6,2},{7,3},{8,12},{9,13},{10,... | collective-permute-start | bytes 1277960 | tf_op jit(solution)/shard_map/ppermute | solution.py:61
  25.6 21.3 %collective-permute-start.4 = (bf16[128,1664]{1,0:T(8,128)(2,1)S(1)}, bf16[128,1664]{1,0:T(8,128)(2,1)S(1)}, u32[]{:S(2)}, u32[]{:S(2)}) collective-permute-start(bf16[128,1664]{1,0:T(8,128)(2,1)S(1)} %pad_maximum_fusion.19), channel_id=1, source_target_pairs={{0,2},{1,3},{2,0},{3,1},{4,6},{5,7},{6,4},{7,5},{8,10},{9,11},{10,... | collective-permute-start | bytes 1277960 | tf_op jit(solution)/shard_map/ppermute | solution.py:61
  30.8 16.1 %collective-permute-start.6 = (bf16[64,1536]{1,0:T(8,128)(2,1)S(1)}, bf16[64,1536]{1,0:T(8,128)(2,1)S(1)}, u32[]{:S(2)}, u32[]{:S(2)}) collective-permute-start(bf16[64,1536]{1,0:T(8,128)(2,1)S(1)} %get-tuple-element.284), channel_id=1, source_target_pairs={{0,16},{1,17},{2,18},{3,19},{4,20},{5,21},{6,22},{7,23},{8,24},{9,... | collective-permute-start | bytes 589832 | tf_op jit(solution)/shard_map/ppermute | solution.py:61
  31.8 15.1 %collective-permute-start.7 = (bf16[64,1536]{1,0:T(8,128)(2,1)S(1)}, bf16[64,1536]{1,0:T(8,128)(2,1)S(1)}, u32[]{:S(2)}, u32[]{:S(2)}) collective-permute-start(bf16[64,1536]{1,0:T(8,128)(2,1)S(1)} %get-tuple-element.284), channel_id=1, source_target_pairs={{0,24},{1,25},{2,26},{3,27},{4,28},{5,29},{6,30},{7,31},{8,16},{9,... | collective-permute-start | bytes 589832 | tf_op jit(solution)/shard_map/ppermute | solution.py:61
  47.0 15.5 %collective-permute-start.8 = (bf16[256,1664]{1,0:T(8,128)(2,1)S(1)}, bf16[256,1664]{1,0:T(8,128)(2,1)S(1)}, u32[]{:S(2)}, u32[]{:S(2)}) collective-permute-start(bf16[256,1664]{1,0:T(8,128)(2,1)S(1)} %pad_maximum_fusion.7.refs_0_), channel_id=1, source_target_pairs={{0,2},{1,3},{2,0},{3,1},{4,6},{5,7},{6,4},{7,5},{8,10},{9,11},{10,... | collective-permute-start | bytes 2555912 | tf_op jit(solution)/shard_map/ppermute | solution.py:61
  47.6 15.3 %collective-permute-start.9 = (bf16[256,1664]{1,0:T(8,128)(2,1)S(1)}, bf16[256,1664]{1,0:T(8,128)(2,1)}, u32[]{:S(2)}, u32[]{:S(2)}) collective-permute-start(bf16[256,1664]{1,0:T(8,128)(2,1)S(1)} %pad_maximum_fusion.8.refs_1_), channel_id=1, source_target_pairs={{0,4},{1,5},{2,6},{3,7},{4,0},{5,1},{6,2},{7,3},{8,12},{9,13},{10,... | collective-permute-start | bytes 2555912 | tf_op jit(solution)/shard_map/ppermute | solution.py:61
  64.4 13.0 %collective-permute-start.13 = (bf16[128,1536]{1,0:T(8,128)(2,1)}, bf16[128,1536]{1,0:T(8,128)(2,1)S(1)}, u32[]{:S(2)}, u32[]{:S(2)}) collective-permute-start(bf16[128,1536]{1,0:T(8,128)(2,1)} %pad_maximum_fusion.20), channel_id=1, source_target_pairs={{0,4},{1,5},{2,6},{3,7},{4,0},{5,1},{6,2},{7,3},{8,12},{9,13},{10,... | collective-permute-start | bytes 1179656 | tf_op jit(solution)/shard_map/ppermute | solution.py:61
  77.8 19.3 %collective-permute-start.19 = (bf16[1,512,512]{2,1,0:T(8,128)(2,1)S(1)}, bf16[1,512,512]{2,1,0:T(8,128)(2,1)S(1)}, u32[]{:S(2)}, u32[]{:S(2)}) collective-permute-start(bf16[1,512,512]{2,1,0:T(8,128)(2,1)S(1)} %pad_maximum_fusion.14), channel_id=1, source_target_pairs={{0,2},{1,3},{2,0},{3,1},{4,6},{5,7},{6,4},{7,5},{8,10},{9,11},{10,... | collective-permute-start | bytes 1572872 | tf_op jit(solution)/shard_map/ppermute | solution.py:61
  79.4 12.9 %collective-permute-start.20 = (bf16[128,1024]{1,0:T(8,128)(2,1)S(1)}, bf16[128,1024]{1,0:T(8,128)(2,1)S(1)}, u32[]{:S(2)}, u32[]{:S(2)}) collective-permute-start(bf16[128,1024]{1,0:T(8,128)(2,1)S(1)} %pad_maximum_fusion.24), channel_id=1, source_target_pairs={{0,4},{1,5},{2,6},{3,7},{4,0},{5,1},{6,2},{7,3},{8,12},{9,13},{10,... | collective-permute-start | bytes 786440 | tf_op jit(solution)/shard_map/ppermute | solution.py:61
  80.9 16.3 %collective-permute-start.21 = (bf16[128,1024]{1,0:T(8,128)(2,1)S(1)}, bf16[128,1024]{1,0:T(8,128)(2,1)S(1)}, u32[]{:S(2)}, u32[]{:S(2)}) collective-permute-start(bf16[128,1024]{1,0:T(8,128)(2,1)S(1)} %pad_maximum_fusion.25), channel_id=1, source_target_pairs={{0,2},{1,3},{2,0},{3,1},{4,6},{5,7},{6,4},{7,5},{8,10},{9,11},{10,... | collective-permute-start | bytes 786440 | tf_op jit(solution)/shard_map/ppermute | solution.py:61
  97.5 32.4 %collective-permute-start.25 = (bf16[256,1536]{1,0:T(8,128)(2,1)S(1)}, bf16[256,1536]{1,0:T(8,128)(2,1)S(1)}, u32[]{:S(2)}, u32[]{:S(2)}) collective-permute-start(bf16[256,1536]{1,0:T(8,128)(2,1)S(1)} %pad_maximum_fusion.9), channel_id=1, source_target_pairs={{0,2},{1,3},{2,0},{3,1},{4,6},{5,7},{6,4},{7,5},{8,10},{9,11},{10,... | collective-permute-start | bytes 2359304 | tf_op jit(solution)/shard_map/ppermute | solution.py:61
  99.0 30.9 %collective-permute-start.26 = (bf16[256,1536]{1,0:T(8,128)(2,1)S(1)}, bf16[256,1536]{1,0:T(8,128)(2,1)S(1)}, u32[]{:S(2)}, u32[]{:S(2)}) collective-permute-start(bf16[256,1536]{1,0:T(8,128)(2,1)S(1)} %pad_maximum_fusion.10), channel_id=1, source_target_pairs={{0,4},{1,5},{2,6},{3,7},{4,0},{5,1},{6,2},{7,3},{8,12},{9,13},{10,... | collective-permute-start | bytes 2359304 | tf_op jit(solution)/shard_map/ppermute | solution.py:61
  99.6 29.0 %collective-permute-start.23 = (bf16[256,1024]{1,0:T(8,128)(2,1)S(1)}, bf16[256,1024]{1,0:T(8,128)(2,1)S(1)}, u32[]{:S(2)}, u32[]{:S(2)}) collective-permute-start(bf16[256,1024]{1,0:T(8,128)(2,1)S(1)} %pad_maximum_fusion.15), channel_id=1, source_target_pairs={{0,2},{1,3},{2,0},{3,1},{4,6},{5,7},{6,4},{7,5},{8,10},{9,11},{10,... | collective-permute-start | bytes 1572872 | tf_op jit(solution)/shard_map/ppermute | solution.py:61
  100.1 29.8 %collective-permute-start.24 = (bf16[256,1024]{1,0:T(8,128)(2,1)S(1)}, bf16[256,1024]{1,0:T(8,128)(2,1)S(1)}, u32[]{:S(2)}, u32[]{:S(2)}) collective-permute-start(bf16[256,1024]{1,0:T(8,128)(2,1)S(1)} %pad_maximum_fusion.16), channel_id=1, source_target_pairs={{0,4},{1,5},{2,6},{3,7},{4,0},{5,1},{6,2},{7,3},{8,12},{9,13},{10,... | collective-permute-start | bytes 1572872 | tf_op jit(solution)/shard_map/ppermute | solution.py:61
  102.2 24.6 %collective-permute-start.27 = (bf16[128,1536]{1,0:T(8,128)(2,1)S(1)}, bf16[128,1536]{1,0:T(8,128)(2,1)S(1)}, u32[]{:S(2)}, u32[]{:S(2)}) collective-permute-start(bf16[128,1536]{1,0:T(8,128)(2,1)S(1)} %pad_maximum_fusion.22), channel_id=1, source_target_pairs={{0,16},{1,17},{2,18},{3,19},{4,20},{5,21},{6,22},{7,23},{8,24},{9,... | collective-permute-start | bytes 1179656 | tf_op jit(solution)/shard_map/ppermute | solution.py:61
  130.5 19.6 %collective-permute-start.29 = (bf16[1024,1536]{1,0:T(8,128)(2,1)S(1)}, bf16[1024,1536]{1,0:T(8,128)(2,1)S(1)}, u32[]{:S(2)}, u32[]{:S(2)}) collective-permute-start(bf16[1024,1536]{1,0:T(8,128)(2,1)S(1)} %pad_maximum_fusion.refs_0_), channel_id=1, source_target_pairs={{0,1},{1,0},{2,3},{3,2},{4,5},{5,4},{6,7},{7,6},{8,9},{9,8},{10,11... | collective-permute-start | bytes 9437192 | tf_op jit(solution)/shard_map/ppermute | solution.py:61
  131.7 18.5 %collective-permute-start.30 = (bf16[128,1536]{1,0:T(8,128)(2,1)S(1)}, bf16[128,1536]{1,0:T(8,128)(2,1)S(1)}, u32[]{:S(2)}, u32[]{:S(2)}) collective-permute-start(bf16[128,1536]{1,0:T(8,128)(2,1)S(1)} %pad_maximum_fusion.22), channel_id=1, source_target_pairs={{0,4},{1,5},{2,6},{3,7},{4,0},{5,1},{6,2},{7,3},{8,12},{9,13},{10,... | collective-permute-start | bytes 1179656 | tf_op jit(solution)/shard_map/ppermute | solution.py:61
  132.3 17.8 %collective-permute-start.31 = (bf16[128,1536]{1,0:T(8,128)(2,1)S(1)}, bf16[128,1536]{1,0:T(8,128)(2,1)S(1)}, u32[]{:S(2)}, u32[]{:S(2)}) collective-permute-start(bf16[128,1536]{1,0:T(8,128)(2,1)S(1)} %collective-permute-done.27), channel_id=1, source_target_pairs={{0,2},{1,3},{2,0},{3,1},{4,6},{5,7},{6,4},{7,5},{8,10},{9,11},{10,... | collective-permute-start | bytes 1179656 | tf_op jit(solution)/shard_map/ppermute | solution.py:61
  150.3 20.5 %collective-permute-start.33 = (bf16[256,1536]{1,0:T(8,128)(2,1)S(1)}, bf16[256,1536]{1,0:T(8,128)(2,1)S(1)}, u32[]{:S(2)}, u32[]{:S(2)}) collective-permute-start(bf16[256,1536]{1,0:T(8,128)(2,1)S(1)} %pad_maximum_fusion.11), channel_id=1, source_target_pairs={{0,2},{1,3},{2,0},{3,1},{4,6},{5,7},{6,4},{7,5},{8,10},{9,11},{10,... | collective-permute-start | bytes 2359304 | tf_op jit(solution)/shard_map/ppermute | solution.py:61
  152.8 19.5 %collective-permute-start.34 = (bf16[256,1536]{1,0:T(8,128)(2,1)S(1)}, bf16[256,1536]{1,0:T(8,128)(2,1)S(1)}, u32[]{:S(2)}, u32[]{:S(2)}) collective-permute-start(bf16[256,1536]{1,0:T(8,128)(2,1)S(1)} %pad_maximum_fusion.12), channel_id=1, source_target_pairs={{0,4},{1,5},{2,6},{3,7},{4,0},{5,1},{6,2},{7,3},{8,12},{9,13},{10,... | collective-permute-start | bytes 2359304 | tf_op jit(solution)/shard_map/ppermute | solution.py:61
  178.2 13.7 %collective-permute-start.36 = (bf16[1024,1536]{1,0:T(8,128)(2,1)S(1)}, bf16[1024,1536]{1,0:T(8,128)(2,1)}, u32[]{:S(2)}, u32[]{:S(2)}) collective-permute-start(bf16[1024,1536]{1,0:T(8,128)(2,1)S(1)} %get-tuple-element.379), channel_id=1, source_target_pairs={{0,1},{1,0},{2,3},{3,2},{4,5},{5,4},{6,7},{7,6},{8,9},{9,8},{10,11... | collective-permute-start | bytes 9437192 | tf_op jit(solution)/shard_map/ppermute | solution.py:61
  196.0 21.1 %collective-permute-start.37 = (bf16[256,1536]{1,0:T(8,128)(2,1)}, bf16[256,1536]{1,0:T(8,128)(2,1)}, u32[]{:S(2)}, u32[]{:S(2)}) collective-permute-start(bf16[256,1536]{1,0:T(8,128)(2,1)} %get-tuple-element.384), channel_id=1, source_target_pairs={{0,2},{1,3},{2,0},{3,1},{4,6},{5,7},{6,4},{7,5},{8,10},{9,11},{10,... | collective-permute-start | bytes 2359304 | tf_op jit(solution)/shard_map/ppermute | solution.py:61
  196.4 20.7 %collective-permute-start.38 = (bf16[256,1536]{1,0:T(8,128)(2,1)}, bf16[256,1536]{1,0:T(8,128)(2,1)}, u32[]{:S(2)}, u32[]{:S(2)}) collective-permute-start(bf16[256,1536]{1,0:T(8,128)(2,1)} %get-tuple-element.385), channel_id=1, source_target_pairs={{0,4},{1,5},{2,6},{3,7},{4,0},{5,1},{6,2},{7,3},{8,12},{9,13},{10,... | collective-permute-start | bytes 2359304 | tf_op jit(solution)/shard_map/ppermute | solution.py:61
  221.3 13.0 %collective-permute-start.41 = (bf16[1024,1536]{1,0:T(8,128)(2,1)}, bf16[1024,1536]{1,0:T(8,128)(2,1)}, u32[]{:S(2)}, u32[]{:S(2)}) collective-permute-start(bf16[1024,1536]{1,0:T(8,128)(2,1)} %get-tuple-element.396), channel_id=1, source_target_pairs={{0,1},{1,0},{2,3},{3,2},{4,5},{5,4},{6,7},{7,6},{8,9},{9,8},{10,11... | collective-permute-start | bytes 9437192 | tf_op jit(solution)/shard_map/ppermute | solution.py:61
  221.3 11.8 %collective-permute-start.39 = (bf16[128,1536]{1,0:T(8,128)(2,1)}, bf16[128,1536]{1,0:T(8,128)(2,1)}, u32[]{:S(2)}, u32[]{:S(2)}) collective-permute-start(bf16[128,1536]{1,0:T(8,128)(2,1)} %slice.651), channel_id=1, source_target_pairs={{0,4},{1,5},{2,6},{3,7},{4,0},{5,1},{6,2},{7,3},{8,12},{9,13},{10,... | collective-permute-start | bytes 1179656 | tf_op jit(solution)/shard_map/ppermute | solution.py:61
  222.8 11.6 %collective-permute-start.40 = (bf16[128,1536]{1,0:T(8,128)(2,1)}, bf16[128,1536]{1,0:T(8,128)(2,1)}, u32[]{:S(2)}, u32[]{:S(2)}) collective-permute-start(bf16[128,1536]{1,0:T(8,128)(2,1)} %slice.650), channel_id=1, source_target_pairs={{0,2},{1,3},{2,0},{3,1},{4,6},{5,7},{6,4},{7,5},{8,10},{9,11},{10,... | collective-permute-start | bytes 1179656 | tf_op jit(solution)/shard_map/ppermute | solution.py:61
  238.8 19.7 %collective-permute-start.45 = (bf16[256,1536]{1,0:T(8,128)(2,1)S(1)}, bf16[256,1536]{1,0:T(8,128)(2,1)S(1)}, u32[]{:S(2)}, u32[]{:S(2)}) collective-permute-start(bf16[256,1536]{1,0:T(8,128)(2,1)S(1)} %get-tuple-element.409), channel_id=1, source_target_pairs={{0,2},{1,3},{2,0},{3,1},{4,6},{5,7},{6,4},{7,5},{8,10},{9,11},{10,... | collective-permute-start | bytes 2359304 | tf_op jit(solution)/shard_map/ppermute | solution.py:61
  241.5 18.9 %collective-permute-start.46 = (bf16[256,1536]{1,0:T(8,128)(2,1)S(1)}, bf16[256,1536]{1,0:T(8,128)(2,1)S(1)}, u32[]{:S(2)}, u32[]{:S(2)}) collective-permute-start(bf16[256,1536]{1,0:T(8,128)(2,1)S(1)} %get-tuple-element.410), channel_id=1, source_target_pairs={{0,4},{1,5},{2,6},{3,7},{4,0},{5,1},{6,2},{7,3},{8,12},{9,13},{10,... | collective-permute-start | bytes 2359304 | tf_op jit(solution)/shard_map/ppermute | solution.py:61
  243.7 14.8 %collective-permute-start.44 = (bf16[64,1536]{1,0:T(8,128)(2,1)S(1)}, bf16[64,1536]{1,0:T(8,128)(2,1)S(1)}, u32[]{:S(2)}, u32[]{:S(2)}) collective-permute-start(bf16[64,1536]{1,0:T(8,128)(2,1)S(1)} %get-tuple-element.408), channel_id=1, source_target_pairs={{0,24},{1,25},{2,26},{3,27},{4,28},{5,29},{6,30},{7,31},{8,16},{9,... | collective-permute-start | bytes 589832 | tf_op jit(solution)/shard_map/ppermute | solution.py:61
  262.6 13.6 %collective-permute-start.49 = (bf16[1024,1024]{1,0:T(8,128)(2,1)S(1)}, bf16[1024,1024]{1,0:T(8,128)(2,1)S(1)}, u32[]{:S(2)}, u32[]{:S(2)}) collective-permute-start(bf16[1024,1024]{1,0:T(8,128)(2,1)S(1)} %copy-done.26), channel_id=1, source_target_pairs={{0,1},{1,0},{2,3},{3,2},{4,5},{5,4},{6,7},{7,6},{8,9},{9,8},{10,11... | collective-permute-start | bytes 6291464 | tf_op jit(solution)/shard_map/ppermute | solution.py:61
  264.7 11.4 %collective-permute-start.48 = (bf16[128,1536]{1,0:T(8,128)(2,1)S(1)}, bf16[128,1536]{1,0:T(8,128)(2,1)S(1)}, u32[]{:S(2)}, u32[]{:S(2)}) collective-permute-start(bf16[128,1536]{1,0:T(8,128)(2,1)S(1)} %slice.648), channel_id=1, source_target_pairs={{0,2},{1,3},{2,0},{3,1},{4,6},{5,7},{6,4},{7,5},{8,10},{9,11},{10,... | collective-permute-start | bytes 1179656 | tf_op jit(solution)/shard_map/ppermute | solution.py:61
  278.4 23.9 %collective-permute-start.53 = (bf16[256,1024]{1,0:T(8,128)(2,1)S(1)}, bf16[256,1024]{1,0:T(8,128)(2,1)S(1)}, u32[]{:S(2)}, u32[]{:S(2)}) collective-permute-start(bf16[256,1024]{1,0:T(8,128)(2,1)S(1)} %get-tuple-element.436), channel_id=1, source_target_pairs={{0,2},{1,3},{2,0},{3,1},{4,6},{5,7},{6,4},{7,5},{8,10},{9,11},{10,... | collective-permute-start | bytes 1572872 | tf_op jit(solution)/shard_map/ppermute | solution.py:61
  281.4 20.9 %collective-permute-start.54 = (bf16[256,1024]{1,0:T(8,128)(2,1)S(1)}, bf16[256,1024]{1,0:T(8,128)(2,1)S(1)}, u32[]{:S(2)}, u32[]{:S(2)}) collective-permute-start(bf16[256,1024]{1,0:T(8,128)(2,1)S(1)} %get-tuple-element.437), channel_id=1, source_target_pairs={{0,4},{1,5},{2,6},{3,7},{4,0},{5,1},{6,2},{7,3},{8,12},{9,13},{10,... | collective-permute-start | bytes 1572872 | tf_op jit(solution)/shard_map/ppermute | solution.py:61
  282.4 12.2 %collective-permute-start.50 = (bf16[64,1536]{1,0:T(8,128)(2,1)S(1)}, bf16[64,1536]{1,0:T(8,128)(2,1)S(1)}, u32[]{:S(2)}, u32[]{:S(2)}) collective-permute-start(bf16[64,1536]{1,0:T(8,128)(2,1)S(1)} %slice.657), channel_id=1, source_target_pairs={{0,8},{1,9},{2,10},{3,11},{4,12},{5,13},{6,14},{7,15},{8,0},{9,1},... | collective-permute-start | bytes 589832 | tf_op jit(solution)/shard_map/ppermute | solution.py:61
  285.2 17.2 %collective-permute-start.51 = (bf16[64,1536]{1,0:T(8,128)(2,1)S(1)}, bf16[64,1536]{1,0:T(8,128)(2,1)S(1)}, u32[]{:S(2)}, u32[]{:S(2)}) collective-permute-start(bf16[64,1536]{1,0:T(8,128)(2,1)S(1)} %get-tuple-element.434), channel_id=1, source_target_pairs={{0,16},{1,17},{2,18},{3,19},{4,20},{5,21},{6,22},{7,23},{8,24},{9,... | collective-permute-start | bytes 589832 | tf_op jit(solution)/shard_map/ppermute | solution.py:61
  286.6 15.7 %collective-permute-start.52 = (bf16[64,1536]{1,0:T(8,128)(2,1)S(1)}, bf16[64,1536]{1,0:T(8,128)(2,1)S(1)}, u32[]{:S(2)}, u32[]{:S(2)}) collective-permute-start(bf16[64,1536]{1,0:T(8,128)(2,1)S(1)} %get-tuple-element.435), channel_id=1, source_target_pairs={{0,24},{1,25},{2,26},{3,27},{4,28},{5,29},{6,30},{7,31},{8,16},{9,... | collective-permute-start | bytes 589832 | tf_op jit(solution)/shard_map/ppermute | solution.py:61
  303.3 12.9 %collective-permute-start.57 = (bf16[128,1024]{1,0:T(8,128)(2,1)S(1)}, bf16[128,1024]{1,0:T(8,128)(2,1)S(1)}, u32[]{:S(2)}, u32[]{:S(2)}) collective-permute-start(bf16[128,1024]{1,0:T(8,128)(2,1)S(1)} %slice.655), channel_id=1, source_target_pairs={{0,4},{1,5},{2,6},{3,7},{4,0},{5,1},{6,2},{7,3},{8,12},{9,13},{10,... | collective-permute-start | bytes 786440 | tf_op jit(solution)/shard_map/ppermute | solution.py:61
  304.8 11.4 %collective-permute-start.58 = (bf16[128,1024]{1,0:T(8,128)(2,1)S(1)}, bf16[128,1024]{1,0:T(8,128)(2,1)S(1)}, u32[]{:S(2)}, u32[]{:S(2)}) collective-permute-start(bf16[128,1024]{1,0:T(8,128)(2,1)S(1)} %slice.654), channel_id=1, source_target_pairs={{0,2},{1,3},{2,0},{3,1},{4,6},{5,7},{6,4},{7,5},{8,10},{9,11},{10,... | collective-permute-start | bytes 786440 | tf_op jit(solution)/shard_map/ppermute | solution.py:61
  306.9 12.0 %collective-permute-start.56 = (bf16[1,1,1,256,512]{4,3,2,1,0:T(8,128)(2,1)S(1)}, bf16[1,1,1,256,512]{4,3,2,1,0:T(8,128)(2,1)S(1)}, u32[]{:S(2)}, u32[]{:S(2)}) collective-permute-start(bf16[1,1,1,256,512]{4,3,2,1,0:T(8,128)(2,1)S(1)} %get-tuple-element.453), channel_id=1, source_target_pairs={{0,2},{1,3},{2,0},{3,1},{4,6},{5,7},{6,4},{7,5},{8,10},{9,11},{10,... | collective-permute-start | bytes 786440 | tf_op jit(solution)/shard_map/ppermute | solution.py:61
  332.2 17.2 %collective-permute-start.61 = (bf16[256,1024]{1,0:T(8,128)(2,1)S(1)}, bf16[256,1024]{1,0:T(8,128)(2,1)S(1)}, u32[]{:S(2)}, u32[]{:S(2)}) collective-permute-start(bf16[256,1024]{1,0:T(8,128)(2,1)S(1)} %get-tuple-element.472), channel_id=1, source_target_pairs={{0,2},{1,3},{2,0},{3,1},{4,6},{5,7},{6,4},{7,5},{8,10},{9,11},{10,... | collective-permute-start | bytes 1572872 | tf_op jit(solution)/shard_map/ppermute | solution.py:61
  332.5 16.9 %collective-permute-start.62 = (bf16[256,1024]{1,0:T(8,128)(2,1)S(1)}, bf16[256,1024]{1,0:T(8,128)(2,1)S(1)}, u32[]{:S(2)}, u32[]{:S(2)}) collective-permute-start(bf16[256,1024]{1,0:T(8,128)(2,1)S(1)} %get-tuple-element.473), channel_id=1, source_target_pairs={{0,4},{1,5},{2,6},{3,7},{4,0},{5,1},{6,2},{7,3},{8,12},{9,13},{10,... | collective-permute-start | bytes 1572872 | tf_op jit(solution)/shard_map/ppermute | solution.py:61
  333.0 16.3 %collective-permute-start.63 = (bf16[128,1024]{1,0:T(8,128)(2,1)S(1)}, bf16[128,1024]{1,0:T(8,128)(2,1)S(1)}, u32[]{:S(2)}, u32[]{:S(2)}) collective-permute-start(bf16[128,1024]{1,0:T(8,128)(2,1)S(1)} %copy-done.65), channel_id=1, source_target_pairs={{0,16},{1,17},{2,18},{3,19},{4,20},{5,21},{6,22},{7,23},{8,24},{9,... | collective-permute-start | bytes 786440 | tf_op jit(solution)/shard_map/ppermute | solution.py:61
  362.7 13.3 %collective-permute-start.70 = (bf16[64,1024]{1,0:T(8,128)(2,1)S(1)}, bf16[64,1024]{1,0:T(8,128)(2,1)S(1)}, u32[]{:S(2)}, u32[]{:S(2)}) collective-permute-start(bf16[64,1024]{1,0:T(8,128)(2,1)S(1)} %slice.661), channel_id=1, source_target_pairs={{0,8},{1,9},{2,10},{3,11},{4,12},{5,13},{6,14},{7,15},{8,0},{9,1},... | collective-permute-start | bytes 393224 | tf_op jit(solution)/shard_map/ppermute | solution.py:61
  362.9 13.0 %collective-permute-start.71 = (bf16[64,1024]{1,0:T(8,128)(2,1)S(1)}, bf16[64,1024]{1,0:T(8,128)(2,1)S(1)}, u32[]{:S(2)}, u32[]{:S(2)}) collective-permute-start(bf16[64,1024]{1,0:T(8,128)(2,1)S(1)} %get-tuple-element.504), channel_id=1, source_target_pairs={{0,16},{1,17},{2,18},{3,19},{4,20},{5,21},{6,22},{7,23},{8,24},{9,... | collective-permute-start | bytes 393224 | tf_op jit(solution)/shard_map/ppermute | solution.py:61
  363.9 12.1 %collective-permute-start.72 = (bf16[64,1024]{1,0:T(8,128)(2,1)S(1)}, bf16[64,1024]{1,0:T(8,128)(2,1)S(1)}, u32[]{:S(2)}, u32[]{:S(2)}) collective-permute-start(bf16[64,1024]{1,0:T(8,128)(2,1)S(1)} %get-tuple-element.505), channel_id=1, source_target_pairs={{0,24},{1,25},{2,26},{3,27},{4,28},{5,29},{6,30},{7,31},{8,16},{9,... | collective-permute-start | bytes 393224 | tf_op jit(solution)/shard_map/ppermute | solution.py:61
  (131 other events, 825.3 us)

commit v11 on v10

--- a/solution.py
+++ b/solution.py
@@ -261,7 +261,7 @@
         elif stage:
             self.values = self.values + self.incoming[0]
         if stage < 4:
-            self.outgoing, self.masks = (self.values,), ((16,), (8,), (4, 2, 6), (1,))[stage]
+            self.outgoing, self.masks = (self.values,), ((1,), (16,), (4, 2, 6), (8,))[stage]
 
     def launch(self):
         if self.staged:
@@ -800,7 +800,7 @@
     red_q = Reduce([grad_wq.astype(LOW)], me, devices)
     red_q.prepare()
     red_q.outgoing, grad_q_low = close_slot([kv_back, red_out], red_q.outgoing, grad_q_low)
-    (grad_q_low,) = open_slot([kv_back, red_q, red_out], grad_q_low, ready=[red_q])
+    (grad_q_low,) = open_slot([kv_back, red_q], grad_q_low, ready=[red_q])
     grad_normed_q = jnp.einsum("ret,de->rtd", grad_q_low, wq, preferred_element_type=jnp.float32)
     (grad_normed_q,) = close_slot([kv_back, red_q], grad_normed_q)
     kv_back.prepare()
@@ -813,14 +813,15 @@
     grad_wkv = jnp.einsum("rtd,ret->de", normed_low, grad_kv_low, preferred_element_type=jnp.float32)
     red_kv = Reduce([grad_wkv.astype(LOW)], me, devices)
     red_kv.prepare()
-    red_kv.outgoing, grad_kv_low = close_slot([red_q, red_out, shared], red_kv.outgoing, grad_kv_low)
-    (grad_kv_low,) = open_slot([red_q, red_kv, shared, red_out], grad_kv_low, ready=[red_kv])
+    (red_kv.outgoing,) = open_slot([red_out], red_kv.outgoing)
+    red_kv.outgoing, grad_kv_low = close_slot([red_q, shared], red_kv.outgoing, grad_kv_low)
+    (grad_kv_low,) = open_slot([red_q, red_kv, shared], grad_kv_low, ready=[red_kv])
     grad_normed = grad_normed_q + jnp.einsum(
         "ret,de->rtd", grad_kv_low, wkv, preferred_element_type=jnp.float32
     )
     input_grad = grad_mid + norm_back(x_float, inverse_one, grad_normed * gain_attn)
     (input_grad,) = close_slot([red_q, red_kv, shared, red_out, red_one, red_two], input_grad)
-    for one in (red_out, red_one, red_two):
+    for one in (red_one, red_two):
         one.prepare()
     (act_one,) = open_slot([red_q, red_kv], act_one)
     output = (
@@ -832,8 +833,9 @@
     red_q.prepare()
     open_slot([red_kv, shared])
     close_slot([red_kv, shared])
-    open_slot([red_kv, shared])
-    close_slot([red_kv, shared])
+    open_slot([red_kv, shared, red_out])
+    close_slot([red_kv, shared, red_out])
+    red_out.prepare()
     red_kv.prepare()
     shared.prepare()
     shared = shared.values

time: 400 us -> 402 us (level)
  starting transfers between devices: 114 us -> 121 us
  waiting for transfers between devices: 95.8 us -> 89.7 us
    ppermute x84, starting transfers between devices: 114 us -> 121 us  [swap(): lax.ppermute(values, ('dp', 'shard'), [(i, i ^ mask) for i in range(devic...]
    ppermute x84, waiting for transfers between devices: 95.8 us -> 89.7 us  [swap(): lax.ppermute(values, ('dp', 'shard'), [(i, i ^ mask) for i in range(devic...]
    unnamed x191 -> x193, local copies, waits for them, and re-layouts: 10.9 us -> 10.9 us
  transfers between devices with their start and end apart: 84 -> 84, of which waited for: 33 -> 32; matrix products, arithmetic and copies ran while one was open for 20% -> 20% of each run, Pallas kernels for 17% -> 17%
where the time goes in v11:
time: 402 us; the launch traced here: 398 us
  starting transfers between devices  121 us (30%)
  waiting for transfers between devices  89.7 us (22%)
  Pallas kernels  67.7 us (17%)
  matrix products  51.6 us (13%)
  other arithmetic  49.2 us (12%)
  local copies, waits for them, and re-layouts  15.3 us (4%)
    ppermute x84, starting transfers between devices, swap(): lax.ppermute(values, ('dp', 'shard'), [(i, i ^ mask) for i in range(devic...  121 us
    ppermute x84, waiting for transfers between devices, swap(): lax.ppermute(values, ('dp', 'shard'), [(i, i ^ mask) for i in range(devic...  89.7 us
    pallas_call x4, Pallas kernels, attention_back(): pl.pallas_call(kernel, out_shape=[jax.ShapeDtypeStruct(queries.shape, LOW...  24.7 us
    pallas_call x5, Pallas kernels, pick(): pl.pallas_call(kernel, out_shape=[jax.ShapeDtypeStruct((len(own) * size,...  19 us
    pallas_call x4, Pallas kernels, place(): pl.pallas_call(kernel, out_shape=[jax.ShapeDtypeStruct((total_rows, width...  14.2 us
    unnamed x193, local copies, waits for them, and re-layouts  10.9 us
    pallas_call x1, Pallas kernels, attention(): pl.pallas_call(kernel, out_shape=[jax.ShapeDtypeStruct((rows, groups * gr...  9.23 us
    convert_element_type x5, other arithmetic, prepare(): self.outgoing = (self.both(0, 4).astype(LOW), self.both(4, 8).astype(LOW))  9.08 us
  transfers between devices with their start and end apart: 84, of which 32 were waited for; matrix products, arithmetic and copies ran while one was open for 20% of the time, Pallas kernels for 17%

profile of v11, /device:TPU:0, one launch (start us, length us, event | category | flops | bytes accessed | tf_op | source)
XLA Modules:
  0.0 398.0 jit_solution(11598698126424025235)
XLA Ops:
  2.6 3.1 collective-permute-start
  5.7 2.6 collective-permute-start.1
  14.8 9.2 %collective-permute-done.1 = bf16[64,1664]{1,0:T(8,128)(2,1)S(1)} collective-permute-done((bf16[64,1664]{1,0:T(8,128)(2,1)S(1)}, bf16[64,1664]{1,0:T(8,128)(2,1)S(1)}, u32[]{:S(2)}, u32[]{:S(2)}) %collective-permute-start.1) | collective-permute-done | bytes 213024 | tf_op jit(solution)/shard_map/ppermute | solution.py:61
  27.1 3.7 collective-permute-start.5
  33.3 3.4 collective-permute-done.5
  36.7 10.2 %collective-permute-done.6 = bf16[64,1536]{1,0:T(8,128)(2,1)S(1)} collective-permute-done((bf16[64,1536]{1,0:T(8,128)(2,1)S(1)}, bf16[64,1536]{1,0:T(8,128)(2,1)S(1)}, u32[]{:S(2)}, u32[]{:S(2)}) %collective-permute-start.6) | collective-permute-done | bytes 196640 | tf_op jit(solution)/shard_map/ppermute | solution.py:61
  48.2 2.7 collective-permute-start.10
  54.1 7.5 %collective-permute-done.11 = bf16[64,1024]{1,0:T(8,128)(2,1)S(1)} collective-permute-done((bf16[64,1024]{1,0:T(8,128)(2,1)S(1)}, bf16[64,1024]{1,0:T(8,128)(2,1)S(1)}, u32[]{:S(2)}, u32[]{:S(2)}) %collective-permute-start.11) | collective-permute-done | bytes 131104 | tf_op jit(solution)/shard_map/ppermute | solution.py:61
  69.1 4.2 %shard_map.221 = (bf16[2048,1024]{1,0:T(8,128)(2,1)S(1)}, bf16[2048,512]{1,0:T(8,128)(2,1)S(1)}, bf16[2048,128]{1,0:T(8,128)(2,1)S(1)}) custom-call(s32[1]{0:T(128)} %bitcast.me_ref, bf16[256,1664]{1,0:T(8,128)(2,1)S(1)} %pad_maximum_fusion.7.refs_0_, bf16[256,1664]{1,0:T(8,128)(2,1)S(1)} %pad_maximum_fusion.8.refs_1_, ...), custom_call_target="tpu_custom_call" | custom-call | bytes 65536 | tf_op jit(solution)/shard_map/pallas_call | solution.py:88
  81.4 5.7 %collective-permute-start.22 = (bf16[64,1536]{1,0:T(8,128)(2,1)S(1)}, bf16[64,1536]{1,0:T(8,128)(2,1)S(1)}, u32[]{:S(2)}, u32[]{:S(2)}) collective-permute-start(bf16[64,1536]{1,0:T(8,128)(2,1)S(1)} %copy-done.69), channel_id=1, source_target_pairs={{0,8},{1,9},{2,10},{3,11},{4,12},{5,13},{6,14},{7,15},{8,0},{9,1},... | collective-permute-start | bytes 589832 | tf_op jit(solution)/shard_map/ppermute | solution.py:61
  92.2 4.8 %collective-permute-done.21 = bf16[128,1024]{1,0:T(8,128)(2,1)S(1)} collective-permute-done((bf16[128,1024]{1,0:T(8,128)(2,1)S(1)}, bf16[128,1024]{1,0:T(8,128)(2,1)S(1)}, u32[]{:S(2)}, u32[]{:S(2)}) %collective-permute-start.21) | collective-permute-done | bytes 262176 | tf_op jit(solution)/shard_map/ppermute | solution.py:61
  102.2 7.6 %collective-permute-start.27 = (bf16[128,1536]{1,0:T(8,128)(2,1)S(1)}, bf16[128,1536]{1,0:T(8,128)(2,1)S(1)}, u32[]{:S(2)}, u32[]{:S(2)}) collective-permute-start(bf16[128,1536]{1,0:T(8,128)(2,1)S(1)} %pad_maximum_fusion.22), channel_id=1, source_target_pairs={{0,16},{1,17},{2,18},{3,19},{4,20},{5,21},{6,22},{7,23},{8,24},{9,... | collective-permute-start | bytes 1179656 | tf_op jit(solution)/shard_map/ppermute | solution.py:61
  111.3 9.2 %shard_map.222 = (f32[1,1024,512]{2,1,0:T(8,128)S(1)}, bf16[1,1024,512]{2,1,0:T(8,128)(2,1)S(1)}, f32[1,4,4,512]{3,2,1,0:T(4,128)S(1)}) custom-call(s32[6]{0:T(128)S(1)} %pad_add_fusion.info_ref, bf16[1,1024,512]{2,1,0:T(8,128)(2,1)S(1)} %bitcast.222, bf16[4,1,512,512]{3,2,1,0:T(8,128)(2,1)S(1)} %constant_dynamic-update-slice_fusion.k_ref.v_ref, ...), custom_call_target="tpu_custom_call" | custom-call | flops 16777216 | bytes 1048576 | tf_op jit(solution)/shard_map/pallas_call | solution.py:425
  121.8 5.0 %collective-permute-done.27 = bf16[128,1536]{1,0:T(8,128)(2,1)S(1)} collective-permute-done((bf16[128,1536]{1,0:T(8,128)(2,1)S(1)}, bf16[128,1536]{1,0:T(8,128)(2,1)S(1)}, u32[]{:S(2)}, u32[]{:S(2)}) %collective-permute-start.27) | collective-permute-done | bytes 393248 | tf_op jit(solution)/shard_map/ppermute | solution.py:61
  132.3 6.7 %collective-permute-start.31 = (bf16[128,1536]{1,0:T(8,128)(2,1)S(1)}, bf16[128,1536]{1,0:T(8,128)(2,1)S(1)}, u32[]{:S(2)}, u32[]{:S(2)}) collective-permute-start(bf16[128,1536]{1,0:T(8,128)(2,1)S(1)} %collective-permute-done.27), channel_id=1, source_target_pairs={{0,2},{1,3},{2,0},{3,1},{4,6},{5,7},{6,4},{7,5},{8,10},{9,11},{10,... | collective-permute-start | bytes 1179656 | tf_op jit(solution)/shard_map/ppermute | solution.py:61
  139.1 5.9 %shard_map.223 = bf16[2048,1024]{1,0:T(8,128)(2,1)S(1)} custom-call(s32[1]{0:T(128)} %bitcast.me_ref, bf16[1024,1024]{1,0:T(8,128)(2,1)S(1)} %pad_maximum_fusion.3.refs_0_, bf16[1024,1024]{1,0:T(8,128)(2,1)S(1)} %collective-permute-done.32.refs_1_), custom_call_target="tpu_custom_call" | custom-call | bytes 65536 | tf_op jit(solution)/shard_map/pallas_call | solution.py:88
  145.0 2.6 multiply_reduce_fusion
  149.7 3.0 collective-permute-start.33
  164.9 5.8 %collective-permute-done.33 = bf16[256,1536]{1,0:T(8,128)(2,1)S(1)} collective-permute-done((bf16[256,1536]{1,0:T(8,128)(2,1)S(1)}, bf16[256,1536]{1,0:T(8,128)(2,1)S(1)}, u32[]{:S(2)}, u32[]{:S(2)}) %collective-permute-start.33) | collective-permute-done | bytes 786464 | tf_op jit(solution)/shard_map/ppermute | solution.py:61
  172.5 5.6 %collective-permute-done.35.refs_1_ = bf16[1024,1536]{1,0:T(8,128)(2,1)S(1)} collective-permute-done((bf16[1024,1536]{1,0:T(8,128)(2,1)S(1)}, bf16[1024,1536]{1,0:T(8,128)(2,1)S(1)}, u32[]{:S(2)}, u32[]{:S(2)}) %collective-permute-start.35) | collective-permute-done | bytes 3145760 | tf_op jit(solution)/shard_map/ppermute | solution.py:61
  188.6 3.2 shard_map.227
  191.9 4.0 add_convert_fusion.2
  199.0 2.7 fusion.7
  201.7 2.7 fusion.8
  206.8 6.1 %shard_map.228 = (bf16[1024,1024]{1,0:T(8,128)(2,1)S(1)}, bf16[1024,1024]{1,0:T(8,128)(2,1)S(1)}) custom-call(s32[1]{0:T(128)} %bitcast.me_ref, bf16[2048,1024]{1,0:T(8,128)(2,1)S(1)} %convolution_convert_fusion.1.refs_0_), custom_call_target="tpu_custom_call" | custom-call | bytes 65536 | tf_op jit(solution)/shard_map/pallas_call | solution.py:123
  212.9 3.7 fusion.35.grad_ref
  224.5 6.2 %shard_map.229 = (bf16[1,1024,512]{2,1,0:T(8,128)(2,1)S(1)}, f32[4,1,2,256,512]{4,3,2,1,0:T(8,128)S(1)}, f32[1,64,128]{2,1,0:T(8,128)S(1)}) custom-call(s32[6]{0:T(128)S(1)} %pad_add_fusion.info_ref, bf16[1,1024,512]{2,1,0:T(8,128)(2,1)S(1)} %bitcast.223, bf16[4,1,512,512]{3,2,1,0:T(8,128)(2,1)S(1)} %constant_dynamic-update-slice_fusion.k_ref.v_ref, ...), custom_call_target="tpu_custom_call" | custom-call | flops 4194304 | bytes 1048576 | tf_op jit(solution)/shard_map/pallas_call | solution.py:537
  238.7 2.7 collective-permute-start.45
  243.6 2.4 collective-permute-start.44
  246.1 6.0 %shard_map.230 = (bf16[1,1024,512]{2,1,0:T(8,128)(2,1)S(1)}, f32[4,1,2,256,512]{4,3,2,1,0:T(8,128)S(1)}, f32[1,64,128]{2,1,0:T(8,128)S(1)}) custom-call(s32[6]{0:T(128)S(1)} %pad_add_fusion.info_ref, bf16[1,1024,512]{2,1,0:T(8,128)(2,1)S(1)} %bitcast.224, ...), custom_call_target="tpu_custom_call", output_to_operand_aliasing={{0}: (11, {}), {1}: (12, {})} | custom-call | flops 4194304 | bytes 1048576 | tf_op jit(solution)/shard_map/pallas_call | solution.py:537
  252.3 5.9 %collective-permute-done.44 = bf16[64,1536]{1,0:T(8,128)(2,1)S(1)} collective-permute-done((bf16[64,1536]{1,0:T(8,128)(2,1)S(1)}, bf16[64,1536]{1,0:T(8,128)(2,1)S(1)}, u32[]{:S(2)}, u32[]{:S(2)}) %collective-permute-start.44) | collective-permute-done | bytes 196640 | tf_op jit(solution)/shard_map/ppermute | solution.py:61
  265.3 6.4 %shard_map.231 = (bf16[1,1024,512]{2,1,0:T(8,128)(2,1)S(1)}, f32[4,1,2,256,512]{4,3,2,1,0:T(8,128)S(1)}, f32[1,64,128]{2,1,0:T(8,128)S(1)}) custom-call(s32[6]{0:T(128)S(1)} %pad_add_fusion.info_ref, bf16[1,1024,512]{2,1,0:T(8,128)(2,1)S(1)} %bitcast.225, ...), custom_call_target="tpu_custom_call", output_to_operand_aliasing={{0}: (11, {}), {1}: (12, {})} | custom-call | flops 4194304 | bytes 1048576 | tf_op jit(solution)/shard_map/pallas_call | solution.py:537
  271.7 3.3 collective-permute-done.47
  277.7 3.3 collective-permute-start.53
  282.3 2.7 collective-permute-start.50
  288.2 6.1 %shard_map.232 = (bf16[1,1024,512]{2,1,0:T(8,128)(2,1)S(1)}, f32[4,1,2,256,512]{4,3,2,1,0:T(8,128)S(1)}, f32[1,64,128]{2,1,0:T(8,128)S(1)}) custom-call(s32[6]{0:T(128)S(1)} %pad_add_fusion.info_ref, bf16[1,1024,512]{2,1,0:T(8,128)(2,1)S(1)} %bitcast.226, ...), custom_call_target="tpu_custom_call", output_to_operand_aliasing={{0}: (11, {}), {1}: (12, {})} | custom-call | flops 4194304 | bytes 1048576 | tf_op jit(solution)/shard_map/pallas_call | solution.py:537
  294.4 7.2 %collective-permute-done.52 = bf16[64,1536]{1,0:T(8,128)(2,1)S(1)} collective-permute-done((bf16[64,1536]{1,0:T(8,128)(2,1)S(1)}, bf16[64,1536]{1,0:T(8,128)(2,1)S(1)}, u32[]{:S(2)}, u32[]{:S(2)}) %collective-permute-start.52) | collective-permute-done | bytes 196640 | tf_op jit(solution)/shard_map/ppermute | solution.py:61
  311.4 4.6 %shard_map.233 = (bf16[1024,1024]{1,0:T(8,128)(2,1)S(1)}, bf16[1024,1024]{1,0:T(8,128)(2,1)}) custom-call(s32[1]{0:T(128)} %bitcast.me_ref, bf16[2048,1024]{1,0:T(8,128)(2,1)S(1)} %convolution_convert_fusion.refs_0_), custom_call_target="tpu_custom_call" | custom-call | bytes 65536 | tf_op jit(solution)/shard_map/pallas_call | solution.py:123
  320.0 6.6 %convolution_bitcast_fusion = f32[1,512,2048]{2,1,0:T(8,128)} fusion(bf16[2048,1024]{1,0:T(8,128)(2,1)} %copy-done.24, bf16[1,1024,512]{2,1,0:T(8,128)(2,1)S(1)} %copy-done.4), kind=kOutput, calls=%fused_computation.29 | convolution fusion | flops 2147483648 | bytes 9437184 | tf_op jit(solution)/shard_map/ret,de->rtd/dot_general | solution.py:804
  327.7 2.8 add_convert_fusion.4
  335.2 3.0 convolution_convert_fusion.4.refs_0_
  338.2 3.2 shard_map.235
  341.5 4.2 %collective-permute-start.68 = (bf16[128,1024]{1,0:T(8,128)(2,1)S(1)}, bf16[128,1024]{1,0:T(8,128)(2,1)S(1)}, u32[]{:S(2)}, u32[]{:S(2)}) collective-permute-start(bf16[128,1024]{1,0:T(8,128)(2,1)S(1)} %fusion.59), channel_id=1, source_target_pairs={{0,16},{1,17},{2,18},{3,19},{4,20},{5,21},{6,22},{7,23},{8,24},{9,... | collective-permute-start | bytes 786440 | tf_op jit(solution)/shard_map/ppermute | solution.py:61
  350.7 4.7 %collective-permute-start.67 = (f32[1,128]{1,0:T(1,128)S(1)}, f32[1,128]{1,0:T(1,128)S(1)}, u32[]{:S(2)}, u32[]{:S(2)}) collective-permute-start(f32[1,128]{1,0:T(1,128)S(1)} %fusion.111), channel_id=1, source_target_pairs={{0,16},{1,17},{2,18},{3,19},{4,20},{5,21},{6,22},{7,23},{8,24},{9,... | collective-permute-start | bytes 1544 | tf_op jit(solution)/shard_map/ppermute | solution.py:61
  357.6 3.1 fusion.3
  362.6 3.0 collective-permute-start.71
  370.7 2.6 fusion.5
  386.5 2.9 collective-permute-start.81
  (489 shorter events, 170.2 us)
Async XLA Ops:
  2.6 12.1 %collective-permute-start = (bf16[64,1664]{1,0:T(8,128)(2,1)S(1)}, bf16[64,1664]{1,0:T(8,128)(2,1)S(1)}, u32[]{:S(2)}, u32[]{:S(2)}) collective-permute-start(bf16[64,1664]{1,0:T(8,128)(2,1)S(1)} %pad_maximum_fusion.28), channel_id=1, source_target_pairs={{0,8},{1,9},{2,10},{3,11},{4,12},{5,13},{6,14},{7,15},{8,0},{9,1},... | collective-permute-start | bytes 638984 | tf_op jit(solution)/shard_map/ppermute | solution.py:61
  5.7 18.2 %collective-permute-start.1 = (bf16[64,1664]{1,0:T(8,128)(2,1)S(1)}, bf16[64,1664]{1,0:T(8,128)(2,1)S(1)}, u32[]{:S(2)}, u32[]{:S(2)}) collective-permute-start(bf16[64,1664]{1,0:T(8,128)(2,1)S(1)} %pad_maximum_fusion.28), channel_id=1, source_target_pairs={{0,16},{1,17},{2,18},{3,19},{4,20},{5,21},{6,22},{7,23},{8,24},{9,... | collective-permute-start | bytes 638984 | tf_op jit(solution)/shard_map/ppermute | solution.py:61
  8.3 15.6 %collective-permute-start.2 = (bf16[64,1664]{1,0:T(8,128)(2,1)S(1)}, bf16[64,1664]{1,0:T(8,128)(2,1)S(1)}, u32[]{:S(2)}, u32[]{:S(2)}) collective-permute-start(bf16[64,1664]{1,0:T(8,128)(2,1)S(1)} %pad_maximum_fusion.28), channel_id=1, source_target_pairs={{0,24},{1,25},{2,26},{3,27},{4,28},{5,29},{6,30},{7,31},{8,16},{9,... | collective-permute-start | bytes 638984 | tf_op jit(solution)/shard_map/ppermute | solution.py:61
  24.0 22.9 %collective-permute-start.3 = (bf16[128,1664]{1,0:T(8,128)(2,1)S(1)}, bf16[128,1664]{1,0:T(8,128)(2,1)S(1)}, u32[]{:S(2)}, u32[]{:S(2)}) collective-permute-start(bf16[128,1664]{1,0:T(8,128)(2,1)S(1)} %pad_maximum_fusion.18), channel_id=1, source_target_pairs={{0,4},{1,5},{2,6},{3,7},{4,0},{5,1},{6,2},{7,3},{8,12},{9,13},{10,... | collective-permute-start | bytes 1277960 | tf_op jit(solution)/shard_map/ppermute | solution.py:61
  25.6 21.3 %collective-permute-start.4 = (bf16[128,1664]{1,0:T(8,128)(2,1)S(1)}, bf16[128,1664]{1,0:T(8,128)(2,1)S(1)}, u32[]{:S(2)}, u32[]{:S(2)}) collective-permute-start(bf16[128,1664]{1,0:T(8,128)(2,1)S(1)} %pad_maximum_fusion.19), channel_id=1, source_target_pairs={{0,2},{1,3},{2,0},{3,1},{4,6},{5,7},{6,4},{7,5},{8,10},{9,11},{10,... | collective-permute-start | bytes 1277960 | tf_op jit(solution)/shard_map/ppermute | solution.py:61
  30.8 16.1 %collective-permute-start.6 = (bf16[64,1536]{1,0:T(8,128)(2,1)S(1)}, bf16[64,1536]{1,0:T(8,128)(2,1)S(1)}, u32[]{:S(2)}, u32[]{:S(2)}) collective-permute-start(bf16[64,1536]{1,0:T(8,128)(2,1)S(1)} %get-tuple-element.285), channel_id=1, source_target_pairs={{0,16},{1,17},{2,18},{3,19},{4,20},{5,21},{6,22},{7,23},{8,24},{9,... | collective-permute-start | bytes 589832 | tf_op jit(solution)/shard_map/ppermute | solution.py:61
  31.8 15.1 %collective-permute-start.7 = (bf16[64,1536]{1,0:T(8,128)(2,1)S(1)}, bf16[64,1536]{1,0:T(8,128)(2,1)S(1)}, u32[]{:S(2)}, u32[]{:S(2)}) collective-permute-start(bf16[64,1536]{1,0:T(8,128)(2,1)S(1)} %get-tuple-element.285), channel_id=1, source_target_pairs={{0,24},{1,25},{2,26},{3,27},{4,28},{5,29},{6,30},{7,31},{8,16},{9,... | collective-permute-start | bytes 589832 | tf_op jit(solution)/shard_map/ppermute | solution.py:61
  47.0 15.5 %collective-permute-start.8 = (bf16[256,1664]{1,0:T(8,128)(2,1)S(1)}, bf16[256,1664]{1,0:T(8,128)(2,1)S(1)}, u32[]{:S(2)}, u32[]{:S(2)}) collective-permute-start(bf16[256,1664]{1,0:T(8,128)(2,1)S(1)} %pad_maximum_fusion.7.refs_0_), channel_id=1, source_target_pairs={{0,2},{1,3},{2,0},{3,1},{4,6},{5,7},{6,4},{7,5},{8,10},{9,11},{10,... | collective-permute-start | bytes 2555912 | tf_op jit(solution)/shard_map/ppermute | solution.py:61
  47.6 15.3 %collective-permute-start.9 = (bf16[256,1664]{1,0:T(8,128)(2,1)S(1)}, bf16[256,1664]{1,0:T(8,128)(2,1)}, u32[]{:S(2)}, u32[]{:S(2)}) collective-permute-start(bf16[256,1664]{1,0:T(8,128)(2,1)S(1)} %pad_maximum_fusion.8.refs_1_), channel_id=1, source_target_pairs={{0,4},{1,5},{2,6},{3,7},{4,0},{5,1},{6,2},{7,3},{8,12},{9,13},{10,... | collective-permute-start | bytes 2555912 | tf_op jit(solution)/shard_map/ppermute | solution.py:61
  64.4 13.0 %collective-permute-start.13 = (bf16[128,1536]{1,0:T(8,128)(2,1)}, bf16[128,1536]{1,0:T(8,128)(2,1)S(1)}, u32[]{:S(2)}, u32[]{:S(2)}) collective-permute-start(bf16[128,1536]{1,0:T(8,128)(2,1)} %pad_maximum_fusion.20), channel_id=1, source_target_pairs={{0,4},{1,5},{2,6},{3,7},{4,0},{5,1},{6,2},{7,3},{8,12},{9,13},{10,... | collective-permute-start | bytes 1179656 | tf_op jit(solution)/shard_map/ppermute | solution.py:61
  77.8 19.2 %collective-permute-start.19 = (bf16[1,512,512]{2,1,0:T(8,128)(2,1)S(1)}, bf16[1,512,512]{2,1,0:T(8,128)(2,1)S(1)}, u32[]{:S(2)}, u32[]{:S(2)}) collective-permute-start(bf16[1,512,512]{2,1,0:T(8,128)(2,1)S(1)} %pad_maximum_fusion.14), channel_id=1, source_target_pairs={{0,2},{1,3},{2,0},{3,1},{4,6},{5,7},{6,4},{7,5},{8,10},{9,11},{10,... | collective-permute-start | bytes 1572872 | tf_op jit(solution)/shard_map/ppermute | solution.py:61
  79.4 12.9 %collective-permute-start.20 = (bf16[128,1024]{1,0:T(8,128)(2,1)S(1)}, bf16[128,1024]{1,0:T(8,128)(2,1)S(1)}, u32[]{:S(2)}, u32[]{:S(2)}) collective-permute-start(bf16[128,1024]{1,0:T(8,128)(2,1)S(1)} %pad_maximum_fusion.24), channel_id=1, source_target_pairs={{0,4},{1,5},{2,6},{3,7},{4,0},{5,1},{6,2},{7,3},{8,12},{9,13},{10,... | collective-permute-start | bytes 786440 | tf_op jit(solution)/shard_map/ppermute | solution.py:61
  80.9 16.2 %collective-permute-start.21 = (bf16[128,1024]{1,0:T(8,128)(2,1)S(1)}, bf16[128,1024]{1,0:T(8,128)(2,1)S(1)}, u32[]{:S(2)}, u32[]{:S(2)}) collective-permute-start(bf16[128,1024]{1,0:T(8,128)(2,1)S(1)} %pad_maximum_fusion.25), channel_id=1, source_target_pairs={{0,2},{1,3},{2,0},{3,1},{4,6},{5,7},{6,4},{7,5},{8,10},{9,11},{10,... | collective-permute-start | bytes 786440 | tf_op jit(solution)/shard_map/ppermute | solution.py:61
  97.4 32.4 %collective-permute-start.25 = (bf16[256,1536]{1,0:T(8,128)(2,1)S(1)}, bf16[256,1536]{1,0:T(8,128)(2,1)S(1)}, u32[]{:S(2)}, u32[]{:S(2)}) collective-permute-start(bf16[256,1536]{1,0:T(8,128)(2,1)S(1)} %pad_maximum_fusion.9), channel_id=1, source_target_pairs={{0,2},{1,3},{2,0},{3,1},{4,6},{5,7},{6,4},{7,5},{8,10},{9,11},{10,... | collective-permute-start | bytes 2359304 | tf_op jit(solution)/shard_map/ppermute | solution.py:61
  99.0 30.9 %collective-permute-start.26 = (bf16[256,1536]{1,0:T(8,128)(2,1)S(1)}, bf16[256,1536]{1,0:T(8,128)(2,1)S(1)}, u32[]{:S(2)}, u32[]{:S(2)}) collective-permute-start(bf16[256,1536]{1,0:T(8,128)(2,1)S(1)} %pad_maximum_fusion.10), channel_id=1, source_target_pairs={{0,4},{1,5},{2,6},{3,7},{4,0},{5,1},{6,2},{7,3},{8,12},{9,13},{10,... | collective-permute-start | bytes 2359304 | tf_op jit(solution)/shard_map/ppermute | solution.py:61
  99.6 29.0 %collective-permute-start.23 = (bf16[256,1024]{1,0:T(8,128)(2,1)S(1)}, bf16[256,1024]{1,0:T(8,128)(2,1)S(1)}, u32[]{:S(2)}, u32[]{:S(2)}) collective-permute-start(bf16[256,1024]{1,0:T(8,128)(2,1)S(1)} %pad_maximum_fusion.15), channel_id=1, source_target_pairs={{0,2},{1,3},{2,0},{3,1},{4,6},{5,7},{6,4},{7,5},{8,10},{9,11},{10,... | collective-permute-start | bytes 1572872 | tf_op jit(solution)/shard_map/ppermute | solution.py:61
  100.1 29.7 %collective-permute-start.24 = (bf16[256,1024]{1,0:T(8,128)(2,1)S(1)}, bf16[256,1024]{1,0:T(8,128)(2,1)S(1)}, u32[]{:S(2)}, u32[]{:S(2)}) collective-permute-start(bf16[256,1024]{1,0:T(8,128)(2,1)S(1)} %pad_maximum_fusion.16), channel_id=1, source_target_pairs={{0,4},{1,5},{2,6},{3,7},{4,0},{5,1},{6,2},{7,3},{8,12},{9,13},{10,... | collective-permute-start | bytes 1572872 | tf_op jit(solution)/shard_map/ppermute | solution.py:61
  102.2 24.6 %collective-permute-start.27 = (bf16[128,1536]{1,0:T(8,128)(2,1)S(1)}, bf16[128,1536]{1,0:T(8,128)(2,1)S(1)}, u32[]{:S(2)}, u32[]{:S(2)}) collective-permute-start(bf16[128,1536]{1,0:T(8,128)(2,1)S(1)} %pad_maximum_fusion.22), channel_id=1, source_target_pairs={{0,16},{1,17},{2,18},{3,19},{4,20},{5,21},{6,22},{7,23},{8,24},{9,... | collective-permute-start | bytes 1179656 | tf_op jit(solution)/shard_map/ppermute | solution.py:61
  130.5 19.1 %collective-permute-start.29 = (bf16[1024,1536]{1,0:T(8,128)(2,1)S(1)}, bf16[1024,1536]{1,0:T(8,128)(2,1)S(1)}, u32[]{:S(2)}, u32[]{:S(2)}) collective-permute-start(bf16[1024,1536]{1,0:T(8,128)(2,1)S(1)} %pad_maximum_fusion.refs_0_), channel_id=1, source_target_pairs={{0,1},{1,0},{2,3},{3,2},{4,5},{5,4},{6,7},{7,6},{8,9},{9,8},{10,11... | collective-permute-start | bytes 9437192 | tf_op jit(solution)/shard_map/ppermute | solution.py:61
  131.6 17.9 %collective-permute-start.30 = (bf16[128,1536]{1,0:T(8,128)(2,1)S(1)}, bf16[128,1536]{1,0:T(8,128)(2,1)S(1)}, u32[]{:S(2)}, u32[]{:S(2)}) collective-permute-start(bf16[128,1536]{1,0:T(8,128)(2,1)S(1)} %pad_maximum_fusion.22), channel_id=1, source_target_pairs={{0,4},{1,5},{2,6},{3,7},{4,0},{5,1},{6,2},{7,3},{8,12},{9,13},{10,... | collective-permute-start | bytes 1179656 | tf_op jit(solution)/shard_map/ppermute | solution.py:61
  132.3 17.3 %collective-permute-start.31 = (bf16[128,1536]{1,0:T(8,128)(2,1)S(1)}, bf16[128,1536]{1,0:T(8,128)(2,1)S(1)}, u32[]{:S(2)}, u32[]{:S(2)}) collective-permute-start(bf16[128,1536]{1,0:T(8,128)(2,1)S(1)} %collective-permute-done.27), channel_id=1, source_target_pairs={{0,2},{1,3},{2,0},{3,1},{4,6},{5,7},{6,4},{7,5},{8,10},{9,11},{10,... | collective-permute-start | bytes 1179656 | tf_op jit(solution)/shard_map/ppermute | solution.py:61
  149.7 21.0 %collective-permute-start.33 = (bf16[256,1536]{1,0:T(8,128)(2,1)S(1)}, bf16[256,1536]{1,0:T(8,128)(2,1)S(1)}, u32[]{:S(2)}, u32[]{:S(2)}) collective-permute-start(bf16[256,1536]{1,0:T(8,128)(2,1)S(1)} %pad_maximum_fusion.11), channel_id=1, source_target_pairs={{0,2},{1,3},{2,0},{3,1},{4,6},{5,7},{6,4},{7,5},{8,10},{9,11},{10,... | collective-permute-start | bytes 2359304 | tf_op jit(solution)/shard_map/ppermute | solution.py:61
  152.7 19.5 %collective-permute-start.34 = (bf16[256,1536]{1,0:T(8,128)(2,1)S(1)}, bf16[256,1536]{1,0:T(8,128)(2,1)S(1)}, u32[]{:S(2)}, u32[]{:S(2)}) collective-permute-start(bf16[256,1536]{1,0:T(8,128)(2,1)S(1)} %pad_maximum_fusion.12), channel_id=1, source_target_pairs={{0,4},{1,5},{2,6},{3,7},{4,0},{5,1},{6,2},{7,3},{8,12},{9,13},{10,... | collective-permute-start | bytes 2359304 | tf_op jit(solution)/shard_map/ppermute | solution.py:61
  178.2 13.7 %collective-permute-start.36 = (bf16[1024,1536]{1,0:T(8,128)(2,1)S(1)}, bf16[1024,1536]{1,0:T(8,128)(2,1)}, u32[]{:S(2)}, u32[]{:S(2)}) collective-permute-start(bf16[1024,1536]{1,0:T(8,128)(2,1)S(1)} %get-tuple-element.380), channel_id=1, source_target_pairs={{0,1},{1,0},{2,3},{3,2},{4,5},{5,4},{6,7},{7,6},{8,9},{9,8},{10,11... | collective-permute-start | bytes 9437192 | tf_op jit(solution)/shard_map/ppermute | solution.py:61
  195.9 20.8 %collective-permute-start.37 = (bf16[256,1536]{1,0:T(8,128)(2,1)}, bf16[256,1536]{1,0:T(8,128)(2,1)}, u32[]{:S(2)}, u32[]{:S(2)}) collective-permute-start(bf16[256,1536]{1,0:T(8,128)(2,1)} %get-tuple-element.385), channel_id=1, source_target_pairs={{0,2},{1,3},{2,0},{3,1},{4,6},{5,7},{6,4},{7,5},{8,10},{9,11},{10,... | collective-permute-start | bytes 2359304 | tf_op jit(solution)/shard_map/ppermute | solution.py:61
  196.3 20.4 %collective-permute-start.38 = (bf16[256,1536]{1,0:T(8,128)(2,1)}, bf16[256,1536]{1,0:T(8,128)(2,1)}, u32[]{:S(2)}, u32[]{:S(2)}) collective-permute-start(bf16[256,1536]{1,0:T(8,128)(2,1)} %get-tuple-element.386), channel_id=1, source_target_pairs={{0,4},{1,5},{2,6},{3,7},{4,0},{5,1},{6,2},{7,3},{8,12},{9,13},{10,... | collective-permute-start | bytes 2359304 | tf_op jit(solution)/shard_map/ppermute | solution.py:61
  221.0 13.3 %collective-permute-start.41 = (bf16[1024,1536]{1,0:T(8,128)(2,1)}, bf16[1024,1536]{1,0:T(8,128)(2,1)}, u32[]{:S(2)}, u32[]{:S(2)}) collective-permute-start(bf16[1024,1536]{1,0:T(8,128)(2,1)} %get-tuple-element.397), channel_id=1, source_target_pairs={{0,1},{1,0},{2,3},{3,2},{4,5},{5,4},{6,7},{7,6},{8,9},{9,8},{10,11... | collective-permute-start | bytes 9437192 | tf_op jit(solution)/shard_map/ppermute | solution.py:61
  221.0 11.8 %collective-permute-start.39 = (bf16[128,1536]{1,0:T(8,128)(2,1)}, bf16[128,1536]{1,0:T(8,128)(2,1)}, u32[]{:S(2)}, u32[]{:S(2)}) collective-permute-start(bf16[128,1536]{1,0:T(8,128)(2,1)} %slice.651), channel_id=1, source_target_pairs={{0,4},{1,5},{2,6},{3,7},{4,0},{5,1},{6,2},{7,3},{8,12},{9,13},{10,... | collective-permute-start | bytes 1179656 | tf_op jit(solution)/shard_map/ppermute | solution.py:61
  222.7 11.6 %collective-permute-start.40 = (bf16[128,1536]{1,0:T(8,128)(2,1)}, bf16[128,1536]{1,0:T(8,128)(2,1)}, u32[]{:S(2)}, u32[]{:S(2)}) collective-permute-start(bf16[128,1536]{1,0:T(8,128)(2,1)} %slice.650), channel_id=1, source_target_pairs={{0,2},{1,3},{2,0},{3,1},{4,6},{5,7},{6,4},{7,5},{8,10},{9,11},{10,... | collective-permute-start | bytes 1179656 | tf_op jit(solution)/shard_map/ppermute | solution.py:61
  238.7 19.5 %collective-permute-start.45 = (bf16[256,1536]{1,0:T(8,128)(2,1)S(1)}, bf16[256,1536]{1,0:T(8,128)(2,1)S(1)}, u32[]{:S(2)}, u32[]{:S(2)}) collective-permute-start(bf16[256,1536]{1,0:T(8,128)(2,1)S(1)} %get-tuple-element.410), channel_id=1, source_target_pairs={{0,2},{1,3},{2,0},{3,1},{4,6},{5,7},{6,4},{7,5},{8,10},{9,11},{10,... | collective-permute-start | bytes 2359304 | tf_op jit(solution)/shard_map/ppermute | solution.py:61
  241.4 18.9 %collective-permute-start.46 = (bf16[256,1536]{1,0:T(8,128)(2,1)S(1)}, bf16[256,1536]{1,0:T(8,128)(2,1)S(1)}, u32[]{:S(2)}, u32[]{:S(2)}) collective-permute-start(bf16[256,1536]{1,0:T(8,128)(2,1)S(1)} %get-tuple-element.411), channel_id=1, source_target_pairs={{0,4},{1,5},{2,6},{3,7},{4,0},{5,1},{6,2},{7,3},{8,12},{9,13},{10,... | collective-permute-start | bytes 2359304 | tf_op jit(solution)/shard_map/ppermute | solution.py:61
  243.6 14.5 %collective-permute-start.44 = (bf16[64,1536]{1,0:T(8,128)(2,1)S(1)}, bf16[64,1536]{1,0:T(8,128)(2,1)S(1)}, u32[]{:S(2)}, u32[]{:S(2)}) collective-permute-start(bf16[64,1536]{1,0:T(8,128)(2,1)S(1)} %get-tuple-element.409), channel_id=1, source_target_pairs={{0,24},{1,25},{2,26},{3,27},{4,28},{5,29},{6,30},{7,31},{8,16},{9,... | collective-permute-start | bytes 589832 | tf_op jit(solution)/shard_map/ppermute | solution.py:61
  262.5 13.0 %collective-permute-start.49 = (bf16[1024,1024]{1,0:T(8,128)(2,1)S(1)}, bf16[1024,1024]{1,0:T(8,128)(2,1)S(1)}, u32[]{:S(2)}, u32[]{:S(2)}) collective-permute-start(bf16[1024,1024]{1,0:T(8,128)(2,1)S(1)} %copy-done.26), channel_id=1, source_target_pairs={{0,1},{1,0},{2,3},{3,2},{4,5},{5,4},{6,7},{7,6},{8,9},{9,8},{10,11... | collective-permute-start | bytes 6291464 | tf_op jit(solution)/shard_map/ppermute | solution.py:61
  277.7 23.9 %collective-permute-start.53 = (bf16[256,1024]{1,0:T(8,128)(2,1)S(1)}, bf16[256,1024]{1,0:T(8,128)(2,1)S(1)}, u32[]{:S(2)}, u32[]{:S(2)}) collective-permute-start(bf16[256,1024]{1,0:T(8,128)(2,1)S(1)} %get-tuple-element.437), channel_id=1, source_target_pairs={{0,2},{1,3},{2,0},{3,1},{4,6},{5,7},{6,4},{7,5},{8,10},{9,11},{10,... | collective-permute-start | bytes 1572872 | tf_op jit(solution)/shard_map/ppermute | solution.py:61
  281.0 20.6 %collective-permute-start.54 = (bf16[256,1024]{1,0:T(8,128)(2,1)S(1)}, bf16[256,1024]{1,0:T(8,128)(2,1)S(1)}, u32[]{:S(2)}, u32[]{:S(2)}) collective-permute-start(bf16[256,1024]{1,0:T(8,128)(2,1)S(1)} %get-tuple-element.438), channel_id=1, source_target_pairs={{0,4},{1,5},{2,6},{3,7},{4,0},{5,1},{6,2},{7,3},{8,12},{9,13},{10,... | collective-permute-start | bytes 1572872 | tf_op jit(solution)/shard_map/ppermute | solution.py:61
  282.3 12.0 %collective-permute-start.50 = (bf16[64,1536]{1,0:T(8,128)(2,1)S(1)}, bf16[64,1536]{1,0:T(8,128)(2,1)S(1)}, u32[]{:S(2)}, u32[]{:S(2)}) collective-permute-start(bf16[64,1536]{1,0:T(8,128)(2,1)S(1)} %slice.657), channel_id=1, source_target_pairs={{0,8},{1,9},{2,10},{3,11},{4,12},{5,13},{6,14},{7,15},{8,0},{9,1},... | collective-permute-start | bytes 589832 | tf_op jit(solution)/shard_map/ppermute | solution.py:61
  286.7 14.9 %collective-permute-start.52 = (bf16[64,1536]{1,0:T(8,128)(2,1)S(1)}, bf16[64,1536]{1,0:T(8,128)(2,1)S(1)}, u32[]{:S(2)}, u32[]{:S(2)}) collective-permute-start(bf16[64,1536]{1,0:T(8,128)(2,1)S(1)} %get-tuple-element.436), channel_id=1, source_target_pairs={{0,24},{1,25},{2,26},{3,27},{4,28},{5,29},{6,30},{7,31},{8,16},{9,... | collective-permute-start | bytes 589832 | tf_op jit(solution)/shard_map/ppermute | solution.py:61
  303.4 13.9 %collective-permute-start.57 = (bf16[128,1024]{1,0:T(8,128)(2,1)S(1)}, bf16[128,1024]{1,0:T(8,128)(2,1)S(1)}, u32[]{:S(2)}, u32[]{:S(2)}) collective-permute-start(bf16[128,1024]{1,0:T(8,128)(2,1)S(1)} %slice.655), channel_id=1, source_target_pairs={{0,4},{1,5},{2,6},{3,7},{4,0},{5,1},{6,2},{7,3},{8,12},{9,13},{10,... | collective-permute-start | bytes 786440 | tf_op jit(solution)/shard_map/ppermute | solution.py:61
  304.7 12.7 %collective-permute-start.58 = (bf16[128,1024]{1,0:T(8,128)(2,1)S(1)}, bf16[128,1024]{1,0:T(8,128)(2,1)S(1)}, u32[]{:S(2)}, u32[]{:S(2)}) collective-permute-start(bf16[128,1024]{1,0:T(8,128)(2,1)S(1)} %slice.654), channel_id=1, source_target_pairs={{0,2},{1,3},{2,0},{3,1},{4,6},{5,7},{6,4},{7,5},{8,10},{9,11},{10,... | collective-permute-start | bytes 786440 | tf_op jit(solution)/shard_map/ppermute | solution.py:61
  306.6 12.0 %collective-permute-start.56 = (bf16[1,1,1,256,512]{4,3,2,1,0:T(8,128)(2,1)S(1)}, bf16[1,1,1,256,512]{4,3,2,1,0:T(8,128)(2,1)S(1)}, u32[]{:S(2)}, u32[]{:S(2)}) collective-permute-start(bf16[1,1,1,256,512]{4,3,2,1,0:T(8,128)(2,1)S(1)} %get-tuple-element.454), channel_id=1, source_target_pairs={{0,2},{1,3},{2,0},{3,1},{4,6},{5,7},{6,4},{7,5},{8,10},{9,11},{10,... | collective-permute-start | bytes 786440 | tf_op jit(solution)/shard_map/ppermute | solution.py:61
  331.4 14.3 %collective-permute-start.61 = (bf16[256,1024]{1,0:T(8,128)(2,1)}, bf16[256,1024]{1,0:T(8,128)(2,1)S(1)}, u32[]{:S(2)}, u32[]{:S(2)}) collective-permute-start(bf16[256,1024]{1,0:T(8,128)(2,1)} %get-tuple-element.472), channel_id=1, source_target_pairs={{0,2},{1,3},{2,0},{3,1},{4,6},{5,7},{6,4},{7,5},{8,10},{9,11},{10,... | collective-permute-start | bytes 1572872 | tf_op jit(solution)/shard_map/ppermute | solution.py:61
  332.4 13.5 %collective-permute-start.62 = (bf16[256,1024]{1,0:T(8,128)(2,1)}, bf16[256,1024]{1,0:T(8,128)(2,1)S(1)}, u32[]{:S(2)}, u32[]{:S(2)}) collective-permute-start(bf16[256,1024]{1,0:T(8,128)(2,1)} %get-tuple-element.473), channel_id=1, source_target_pairs={{0,4},{1,5},{2,6},{3,7},{4,0},{5,1},{6,2},{7,3},{8,12},{9,13},{10,... | collective-permute-start | bytes 1572872 | tf_op jit(solution)/shard_map/ppermute | solution.py:61
  341.5 19.3 %collective-permute-start.68 = (bf16[128,1024]{1,0:T(8,128)(2,1)S(1)}, bf16[128,1024]{1,0:T(8,128)(2,1)S(1)}, u32[]{:S(2)}, u32[]{:S(2)}) collective-permute-start(bf16[128,1024]{1,0:T(8,128)(2,1)S(1)} %fusion.59), channel_id=1, source_target_pairs={{0,16},{1,17},{2,18},{3,19},{4,20},{5,21},{6,22},{7,23},{8,24},{9,... | collective-permute-start | bytes 786440 | tf_op jit(solution)/shard_map/ppermute | solution.py:61
  347.8 12.9 %collective-permute-start.64 = (bf16[128,1024]{1,0:T(8,128)(2,1)S(1)}, bf16[128,1024]{1,0:T(8,128)(2,1)S(1)}, u32[]{:S(2)}, u32[]{:S(2)}) collective-permute-start(bf16[128,1024]{1,0:T(8,128)(2,1)S(1)} %slice.653), channel_id=1, source_target_pairs={{0,4},{1,5},{2,6},{3,7},{4,0},{5,1},{6,2},{7,3},{8,12},{9,13},{10,... | collective-permute-start | bytes 786440 | tf_op jit(solution)/shard_map/ppermute | solution.py:61
  349.5 11.3 %collective-permute-start.65 = (bf16[128,1024]{1,0:T(8,128)(2,1)S(1)}, bf16[128,1024]{1,0:T(8,128)(2,1)S(1)}, u32[]{:S(2)}, u32[]{:S(2)}) collective-permute-start(bf16[128,1024]{1,0:T(8,128)(2,1)S(1)} %slice.652), channel_id=1, source_target_pairs={{0,2},{1,3},{2,0},{3,1},{4,6},{5,7},{6,4},{7,5},{8,10},{9,11},{10,... | collective-permute-start | bytes 786440 | tf_op jit(solution)/shard_map/ppermute | solution.py:61
  361.2 14.1 %collective-permute-start.69 = (bf16[64,1024]{1,0:T(8,128)(2,1)S(1)}, bf16[64,1024]{1,0:T(8,128)(2,1)S(1)}, u32[]{:S(2)}, u32[]{:S(2)}) collective-permute-start(bf16[64,1024]{1,0:T(8,128)(2,1)S(1)} %slice.662), channel_id=1, source_target_pairs={{0,8},{1,9},{2,10},{3,11},{4,12},{5,13},{6,14},{7,15},{8,0},{9,1},... | collective-permute-start | bytes 393224 | tf_op jit(solution)/shard_map/ppermute | solution.py:61
  361.3 14.1 %collective-permute-start.70 = (bf16[64,1024]{1,0:T(8,128)(2,1)S(1)}, bf16[64,1024]{1,0:T(8,128)(2,1)S(1)}, u32[]{:S(2)}, u32[]{:S(2)}) collective-permute-start(bf16[64,1024]{1,0:T(8,128)(2,1)S(1)} %get-tuple-element.503), channel_id=1, source_target_pairs={{0,16},{1,17},{2,18},{3,19},{4,20},{5,21},{6,22},{7,23},{8,24},{9,... | collective-permute-start | bytes 393224 | tf_op jit(solution)/shard_map/ppermute | solution.py:61
  362.6 12.8 %collective-permute-start.71 = (bf16[64,1024]{1,0:T(8,128)(2,1)S(1)}, bf16[64,1024]{1,0:T(8,128)(2,1)S(1)}, u32[]{:S(2)}, u32[]{:S(2)}) collective-permute-start(bf16[64,1024]{1,0:T(8,128)(2,1)S(1)} %get-tuple-element.504), channel_id=1, source_target_pairs={{0,24},{1,25},{2,26},{3,27},{4,28},{5,29},{6,30},{7,31},{8,16},{9,... | collective-permute-start | bytes 393224 | tf_op jit(solution)/shard_map/ppermute | solution.py:61
  (132 other events, 882.0 us)
